TPU v7x, 128 devices: a whole 4x4x4 slice. The times are simulated.
128 devices in a mesh: seq: 4 (over z), expert: 32 (over y, x, core).
Axes of the slice: x: 4, y: 4, z: 4, core: 2. Of those that a mesh axis runs over, the one named last changes fastest.
Arguments:
- tokens: bfloat16 [2, 4096, 1280], P(None, 'seq'), may hold values from -46.205783 to 46.205783
- slot_embed: bfloat16 [1280, 1024], P(None, 'expert'), may hold values from -0.14115179 to 0.14115179
- combine: bfloat16 [2, 4096, 1024], P(None, 'seq', 'expert'), may hold values from 0.00024414062 to 0.00390625
- w_in: bfloat16 [32, 1280, 5120], P('expert', None, 'seq'), may hold values from -0.15625 to 0.15625
- w_out: bfloat16 [32, 5120, 1280], P('expert', 'seq'), may hold values from -0.078125 to 0.078125
- grad_out: bfloat16 [2, 4096, 1280], P(None, 'seq'), may hold values from -6 to 6
Outputs:
- grad_tokens: bfloat16 [2, 4096, 1280], P(None, ('seq', 'expert'))
- grad_embed: bfloat16 [1280, 1024], P('seq', 'expert')
- grad_w_in: bfloat16 [32, 1280, 5120], P('expert', None, 'seq')
- grad_w_out: bfloat16 [32, 5120, 1280], P('expert', 'seq')
All inputs are finite; a program needn't handle non-finite values.
Results may differ from a plain program's by a relative error of at most 0.028.
Values may be sent and summed in bfloat16 or wider, within the bound.
No kernel may reach another device: no remote copies, remote signals or barrier semaphores. Data moves between devices by JAX's collectives and lax.ppermute only.
A program may use at most 128 MiB of HBM per device.

v0:
```python
import math

import jax
import jax.numpy as jnp
from jax import lax
from jax.sharding import PartitionSpec as P


def gelu_exact(values):
    return 0.5 * values * (1.0 + jax.scipy.special.erf(values / math.sqrt(2.0)))


def gelu_slope(values):
    return 0.5 * (1.0 + jax.scipy.special.erf(values / math.sqrt(2.0))) + values * jnp.exp(
        -0.5 * values * values
    ) / math.sqrt(2.0 * math.pi)


def local(tokens, slot_embed, combine, w_in, w_out, grad_out):
    images, patches, model_width = tokens.shape
    local_experts = w_in.shape[0]
    local_slots = slot_embed.shape[1]
    slots_each = local_slots // local_experts
    logits = jnp.einsum("itd,dj->itj", tokens, slot_embed, preferred_element_type=jnp.float32)
    local_max = jnp.max(logits, axis=1, keepdims=True)
    col_peak = lax.pmax(local_max, "seq")
    exponent = jnp.exp(logits - col_peak)
    col_total = lax.psum(jnp.sum(exponent, axis=1, keepdims=True), "seq")
    dispatch = (exponent / col_total).astype(jnp.bfloat16)
    slot_part = jnp.einsum("itj,itd->ijd", dispatch, tokens, preferred_element_type=jnp.float32)
    out_part = jnp.einsum("itj,itd->ijd", combine, grad_out, preferred_element_type=jnp.float32)
    slot_sum, grad_sum = lax.psum((slot_part, out_part), "seq")
    slot_in = slot_sum.astype(jnp.bfloat16).reshape(images, local_experts, slots_each, model_width)
    grad_slot_out = grad_sum.astype(jnp.bfloat16).reshape(
        images, local_experts, slots_each, model_width
    )
    pre_act = jnp.einsum("iesd,edh->iesh", slot_in, w_in, preferred_element_type=jnp.float32)
    act_value = gelu_exact(pre_act).astype(jnp.bfloat16)
    partial_out = jnp.einsum("iesh,ehd->iesd", act_value, w_out, preferred_element_type=jnp.float32)
    slot_out = lax.psum(partial_out.astype(jnp.bfloat16), "seq")
    slot_out = slot_out.reshape(images, local_slots, model_width)
    grad_combine = jnp.einsum(
        "itd,ijd->itj", grad_out, slot_out, preferred_element_type=jnp.float32
    )
    combine_full = combine.astype(jnp.float32)
    row_dot = lax.psum(jnp.sum(combine_full * grad_combine, axis=2, keepdims=True), "expert")
    grad_act = jnp.einsum(
        "iesd,ehd->iesh", grad_slot_out, w_out, preferred_element_type=jnp.float32
    )
    grad_pre = (grad_act * gelu_slope(pre_act)).astype(jnp.bfloat16)
    grad_w_out = jnp.einsum(
        "iesh,iesd->ehd", act_value, grad_slot_out, preferred_element_type=jnp.float32
    ).astype(jnp.bfloat16)
    grad_w_in = jnp.einsum(
        "iesd,iesh->edh", slot_in, grad_pre, preferred_element_type=jnp.float32
    ).astype(jnp.bfloat16)
    in_part = jnp.einsum("iesh,edh->iesd", grad_pre, w_in, preferred_element_type=jnp.float32)
    grad_slot_in = lax.psum(in_part.astype(jnp.bfloat16), "seq")
    grad_slot_in = grad_slot_in.reshape(images, local_slots, model_width)
    grad_dispatch = jnp.einsum(
        "itd,ijd->itj", tokens, grad_slot_in, preferred_element_type=jnp.float32
    )
    dispatch_full = dispatch.astype(jnp.float32)
    col_dot = lax.psum(jnp.sum(dispatch_full * grad_dispatch, axis=1, keepdims=True), "seq")
    grad_logits = (
        dispatch_full * (grad_dispatch - col_dot) + combine_full * (grad_combine - row_dot)
    ).astype(jnp.bfloat16)
    embed_part = jnp.einsum("itd,itj->dj", tokens, grad_logits, preferred_element_type=jnp.float32)
    grad_embed = lax.psum_scatter(
        embed_part.astype(jnp.bfloat16), "seq", scatter_dimension=0, tiled=True
    )
    term_sum = jnp.einsum(
        "itj,ijd->tid", dispatch, grad_slot_in, preferred_element_type=jnp.float32
    )
    token_sum = lax.psum_scatter(
        (
            term_sum
            + jnp.einsum("itj,dj->tid", grad_logits, slot_embed, preferred_element_type=jnp.float32)
        ).astype(jnp.bfloat16),
        "expert",
        scatter_dimension=0,
        tiled=True,
    ).astype(jnp.float32)
    grad_tokens = jnp.transpose(token_sum, (1, 0, 2)).astype(jnp.bfloat16)
    return (grad_tokens, grad_embed, grad_w_in, grad_w_out)


def solution(mesh):
    return jax.shard_map(
        local,
        mesh=mesh,
        in_specs=(
            P(None, "seq", None),
            P(None, "expert"),
            P(None, "seq", "expert"),
            P("expert", None, "seq"),
            P("expert", "seq", None),
            P(None, "seq", None),
        ),
        out_specs=(
            P(None, ("seq", "expert"), None),
            P("seq", "expert"),
            P("expert", None, "seq"),
            P("expert", "seq", None),
        ),
        check_vma=False,
    )
```

profile of v0, /device:TPU:0, one launch (start us, length us, event | category | flops | bytes accessed | tf_op | source)
XLA Modules:
  0.0 346.9 jit_solution(14374296373742168816)
XLA Ops:
  7.2 4.3 %fusion.55 = (f32[2,32]{1,0:T(2,128)S(1)}, f32[2,1024,32]{1,2,0:T(8,128)S(1)}) fusion(bf16[2,1024,1280]{2,1,0:T(8,128)(2,1)} %param.6, bf16[1280,32]{0,1:T(8,128)(2,1)} %param.7), kind=kOutput, calls=%fused_computation.55 | convolution fusion | flops 167837632 | bytes 5587200 | tf_op jit(solution)/shard_map/itd,dj->itj/dot_general | solution.py:24
  11.6 11.8 %pmax.7 = f32[2,32]{1,0:T(2,128)S(1)} all-reduce(f32[2,32]{1,0:T(2,128)S(1)} %get-tuple-element.16), channel_id=1, replica_groups=mesh['seq'=4,'expert'=32] {'seq'}, use_global_device_ids=true, to_apply=%region_2.0 | all-reduce | flops 64 | bytes 512 | tf_op jit(solution)/shard_map/pmax | solution.py:26
  23.6 7.7 %psum.50 = f32[2,32]{1,0:T(2,128)S(1)} all-reduce(f32[2,32]{1,0:T(2,128)S(1)} %fusion.44), channel_id=1, replica_groups=mesh['seq'=4,'expert'=32] {'seq'}, use_global_device_ids=true, to_apply=%region_4.0 | all-reduce | flops 64 | bytes 512 | tf_op jit(solution)/shard_map/psum | solution.py:28
  31.3 4.4 %fusion.57 = f32[2,32,1280]{2,1,0:T(8,128)} fusion(bf16[2,1024,1280]{2,1,0:T(8,128)(2,1)} %param.6, f32[2,1024,32]{1,2,0:T(8,128)S(1)} %get-tuple-element.17, f32[2,32]{1,0:T(2,128)S(1)} %psum.50, f32[2,32]{1,0:T(2,128)S(1)} %pmax.7), kind=kOutput, calls=%fused_computation.57 | convolution fusion | flops 167968768 | bytes 5833216 | tf_op jit(solution)/shard_map/itj,itd->ijd/dot_general | solution.py:30
  35.8 1.7 fusion.56
  37.5 22.4 %all-reduce.10 = (bf16[2,32,1280]{2,1,0:T(8,128)(2,1)}, bf16[2,32,1280]{2,1,0:T(8,128)(2,1)}) all-reduce(f32[2,32,1280]{2,1,0:T(8,128)} %fusion.57, f32[2,32,1280]{2,1,0:T(8,128)} %fusion.56), channel_id=1, replica_groups=mesh['seq'=4,'expert'=32] {'seq'}, use_global_device_ids=true, to_apply=%region_5.0 | all-reduce | flops 163840 | bytes 983040 | tf_op jit(solution)/shard_map/psum | solution.py:32
  59.9 2.7 fusion.19
  62.7 1.4 fusion.25
  64.1 1.1 fusion.31
  65.9 1.8 fusion.28
  67.7 42.7 %all-reduce.9.cloned.1.call-done = (bf16[2,32,1280]{2,1,0:T(8,128)(2,1)}, bf16[2,32,1280]{2,1,0:T(8,128)(2,1)}) async-done(((bf16[2,32,1280]{2,1,0:T(8,128)(2,1)}, bf16[2,32,1280]{2,1,0:T(8,128)(2,1)}), (bf16[2,32,1280]{2,1,0:T(8,128)(2,1)}, bf16[2,32,1280]{2,1,0:T(8,128)(2,1)})) %all-reduce.9.cloned.1.call-update) | async-done | bytes 327696 | tf_op jit(solution)/shard_map/psum | solution.py:58
  110.5 4.9 %fusion.40 = (f32[2,32]{1,0:T(2,128)S(1)}, f32[2,1024,32]{1,2,0:T(8,128)}) fusion(bf16[2,32,1280]{2,1,0:T(8,128)(2,1)} %get-tuple-element.14, bf16[2,1024,1280]{2,1,0:T(8,128)(2,1)} %param.6, f32[2,32]{1,0:T(2,128)S(1)} %psum.50, f32[2,1024,32]{1,2,0:T(8,128)S(1)} %get-tuple-element.17, f32[2,32]{1,0:T(2,128)S(1)} %pmax.7), kind=kOutput, calls=%fused_computation.39 | convolution fusion | flops 168165312 | bytes 5931776 | tf_op jit(solution)/shard_map/itd,ijd->itj/dot_general | solution.py:60
  115.4 5.6 %fusion.58 = f32[2,1280,1024]{2,1,0:T(8,128)} fusion(bf16[2,32,1280]{2,1,0:T(8,128)(2,1)S(1)} %copy-done.9, f32[2,1024,32]{1,2,0:T(8,128)S(1)} %get-tuple-element.17, f32[2,32]{1,0:T(2,128)S(1)} %psum.50, f32[2,32]{1,0:T(2,128)S(1)} %pmax.7), kind=kOutput, calls=%fused_computation.58 | convolution fusion | flops 167968768 | bytes 10912256 | tf_op jit(solution)/shard_map/itj,ijd->tid/dot_general | solution.py:72
  121.0 9.8 %psum.53 = f32[2,32]{1,0:T(2,128)} all-reduce(f32[2,32]{1,0:T(2,128)S(1)} %get-tuple-element.20), channel_id=1, replica_groups=mesh['seq'=4,'expert'=32] {'seq'}, use_global_device_ids=true, to_apply=%region_8.0 | all-reduce | flops 64 | bytes 512 | tf_op jit(solution)/shard_map/psum | solution.py:64
  130.8 5.4 %fusion.43 = (f32[2,1024]{1,0:T(2,128)}, f32[2,1024,32]{1,2,0:T(8,128)}) fusion(bf16[2,1024,32]{1,2,0:T(8,128)(2,1)} %param.8, bf16[2,32,1280]{2,1,0:T(8,128)(2,1)} %get-tuple-element.15, bf16[2,1024,1280]{2,1,0:T(8,128)(2,1)} %param.11), kind=kOutput, calls=%fused_computation.42 | convolution fusion | flops 167966720 | bytes 5808128 | tf_op jit(solution)/shard_map/itd,ijd->itj/dot_general | solution.py:42
  136.3 64.1 %psum.55 = f32[2,1024]{1,0:T(2,128)S(1)} all-reduce(f32[2,1024]{1,0:T(2,128)} %get-tuple-element.18), channel_id=1, replica_groups=mesh['seq'=4,'expert'=32] {'expert'}, use_global_device_ids=true, to_apply=%region_11.0 | all-reduce | flops 2048 | bytes 16384 | tf_op jit(solution)/shard_map/psum | solution.py:46
  200.4 1.3 fusion.42
  202.3 3.5 %fusion.35 = bf16[1280,32]{0,1:T(8,128)(2,1)S(1)} fusion(bf16[2,1024,32]{1,2,0:T(8,128)(2,1)S(1)} %fusion.42, bf16[2,1024,1280]{2,1,0:T(8,128)(2,1)} %param.6), kind=kOutput, calls=%fused_computation.25 | convolution fusion | flops 167813120 | bytes 5455872 | tf_op jit(solution)/shard_map/itd,itj->dj/dot_general | solution.py:68
  207.0 8.1 %fusion = bf16[1024,2,1280]{0,2,1:T(8,128)(2,1)} fusion(f32[2,1280,1024]{2,1,0:T(8,128)} %fusion.58, bf16[2,1024,32]{1,2,0:T(8,128)(2,1)} %copy-done.4, bf16[1280,32]{0,1:T(8,128)(2,1)S(1)} %copy-done.10), kind=kOutput, calls=%fused_computation.1 | convolution fusion | flops 173015040 | bytes 15941632 | tf_op jit(solution)/shard_map/itj,dj->tid/dot_general | solution.py:78
  215.1 13.8 %copy.13 = bf16[1024,2,1280]{2,1,0:T(2,128)(2,1)} copy(bf16[1024,2,1280]{0,2,1:T(8,128)(2,1)} %fusion) | data formatting | bytes 10485760 | tf_op jit(solution)/shard_map/convert_element_type | solution.py:79
  230.7 3.7 %fusion.4 = bf16[1,1280,1280]{2,1,0:T(8,128)(2,1)} fusion(bf16[2,32,1280]{2,1,0:T(8,128)(2,1)S(1)} %copy-done.7, bf16[2,32,1280]{2,1,0:T(8,128)(2,1)} %get-tuple-element.12), kind=kOutput, calls=%fused_computation.7 | convolution fusion | flops 211353600 | bytes 3604480 | tf_op jit(solution)/shard_map/iesd,iesh->edh/dot_general | solution.py:54
  234.4 3.8 %fusion.3 = bf16[1,1280,1280]{2,1,0:T(8,128)(2,1)} fusion(bf16[2,32,1280]{2,1,0:T(8,128)(2,1)} %get-tuple-element.13, f32[2,1,32,1280]{3,2,0,1:T(8,128)} %copy-done.3), kind=kOutput, calls=%fused_computation.6 | convolution fusion | flops 211763200 | bytes 3768320 | tf_op jit(solution)/shard_map/iesh,iesd->ehd/dot_general | solution.py:51
  238.2 1.6 copy.17
  239.8 98.9 %all-reduce.7.cloned.1.call-done = bf16[1024,2,1280]{2,1,0:T(2,128)(2,1)} async-done(((bf16[1024,2,1280]{2,1,0:T(2,128)(2,1)}), bf16[1024,2,1280]{2,1,0:T(2,128)(2,1)}) %all-reduce.7.cloned.1.call-update) | async-done | bytes 5242896
  (36 shorter events, 5.7 us)
Async XLA Ops:
  7.2 55.5 %copy-start = (bf16[1,1280,1280]{2,1,0:T(8,128)(2,1)S(1)}, bf16[1,1280,1280]{2,1,0:T(8,128)(2,1)}, u32[]{:S(2)}) copy-start(bf16[1,1280,1280]{2,1,0:T(8,128)(2,1)} %param.10) | copy-start | bytes 9830404
  7.2 103.3 %all-reduce.9.cloned.1.call-start = ((), (), s32[]{:S(2)}) async-start(), calls=%async_computation.3 | async-start | bytes 655360 | tf_op jit(solution)/shard_map/psum | solution.py:58
  31.3 4.4 %copy-start.1 = (bf16[2,1024,1280]{2,1,0:T(8,128)(2,1)S(1)}, bf16[2,1024,1280]{2,1,0:T(8,128)(2,1)}, u32[]{:S(2)}) copy-start(bf16[2,1024,1280]{2,1,0:T(8,128)(2,1)} %param.11) | copy-start | bytes 15728644
  31.3 4.4 %copy-start.5 = (bf16[2,1024,32]{1,2,0:T(8,128)(2,1)S(1)}, bf16[2,1024,32]{1,2,0:T(8,128)(2,1)}, u32[]{:S(2)}) copy-start(bf16[2,1024,32]{1,2,0:T(8,128)(2,1)} %param.8) | copy-start | bytes 393220
  59.9 4.2 %copy-start.8 = (bf16[2,32,1280]{2,1,0:T(8,128)(2,1)S(1)}, bf16[2,32,1280]{2,1,0:T(8,128)(2,1)}, u32[]{:S(2)}) copy-start(bf16[2,32,1280]{2,1,0:T(8,128)(2,1)} %get-tuple-element.13) | copy-start | bytes 491524
  62.7 1.4 copy-start.3
  62.7 3.2 copy-start.2
  65.2 0.7 copy-start.6
  67.7 170.5 %reduce-scatter.4.cloned.1.call-start = ((), (), s32[]{:S(2)}) async-start(), calls=%async_computation.1 | async-start | bytes 409600
  110.5 5.0 %copy-start.9 = (bf16[2,32,1280]{2,1,0:T(8,128)(2,1)S(1)}, bf16[2,32,1280]{2,1,0:T(8,128)(2,1)}, u32[]{:S(2)}) copy-start(bf16[2,32,1280]{2,1,0:T(8,128)(2,1)} %get-tuple-element.14) | copy-start | bytes 491524
  201.7 0.7 copy-start.4
  202.3 4.7 %copy-start.10 = (bf16[1280,32]{0,1:T(8,128)(2,1)S(1)}, bf16[1280,32]{0,1:T(8,128)(2,1)}, u32[]{:S(2)}) copy-start(bf16[1280,32]{0,1:T(8,128)(2,1)} %param.7) | copy-start | bytes 245764
  206.8 131.9 %all-reduce.7.cloned.1.call-start = ((), (), s32[]{:S(2)}) async-start(), calls=%async_computation.2 | async-start | bytes 10485760
  228.8 0.7 copy-start.11
  228.8 1.9 copy-start.7
Sparse Core Ops, SparseCore 0:
  67.8 42.6 all-reduce.8
  206.9 15.1 reduce-scatter.3
  229.0 109.6 all-reduce.6
where the time goes:
time: 348 us; the launch traced here: 347 us
  waiting for transfers between devices  142 us (41%)
  blocking collectives  116 us (33%)
  matrix products  52.5 us (15%)
  local copies, waits for them, and re-layouts  20.5 us (6%)
  between operations  14.5 us (4%)
    unnamed x5, waiting for transfers between devices  98.9 us
    psum x1, blocking collectives, local(): lax.psum(jnp.sum(combine_full * grad_combine, axis=2, keepdims=True), 'ex...  64.1 us
    psum x1, waiting for transfers between devices, local(): grad_slot_in = lax.psum(in_part.astype(jnp.bfloat16), 'seq')  42.7 us
    psum x1, blocking collectives, local(): slot_sum, grad_sum = lax.psum((slot_part, out_part), 'seq')  22.4 us
    convert_element_type x1, local copies, waits for them, and re-layouts, local(): token_sum = lax.psum_scatter((term_sum + jnp.einsum('itj,dj->tid', grad_l...  13.8 us
    pmax x1, blocking collectives, local(): col_peak = lax.pmax(local_max, 'seq')  11.8 us
    psum x1, blocking collectives, local(): lax.psum(jnp.sum(dispatch_full * grad_dispatch, axis=1, keepdims=True), '...  9.83 us
    dot_general x1, matrix products, local(): jnp.einsum('itj,dj->tid', grad_logits, slot_embed, preferred_element_type...  8.07 us
  transfers between devices with their start and end apart: 3, of which 2 were waited for; matrix products, arithmetic and copies ran while one was open for 9% of the time, Pallas kernels for 0%

commit v1 on v0

v1 whole, which is shorter than its diff:
```python
import math

import jax
import jax.numpy as jnp
from jax import lax
from jax.sharding import Mesh, PartitionSpec as P

F32 = jnp.float32
BF16 = jnp.bfloat16


def gelu_parts(values):
    cdf = 0.5 * (1.0 + jax.scipy.special.erf(values / math.sqrt(2.0)))
    slope = cdf + values * jnp.exp(-0.5 * values * values) / math.sqrt(2.0 * math.pi)
    return values * cdf, slope


def shift(value, axis, by):
    return lax.ppermute(value, axis, [(i, (i + by) % 4) for i in range(4)])


def swap_cores(value):
    return lax.ppermute(value, "core", [(0, 1), (1, 0)])


def rolled(value, index, size, dim):
    twice = jnp.concatenate([value, value], axis=dim)
    return lax.dynamic_slice_in_dim(twice, index * size, value.shape[dim], axis=dim)


def scatter_terms(blocks, axis):
    return [blocks[0]] + [shift(blocks[k], axis, k) for k in (1, 2, 3)]


def gather_blocks(block, axis):
    return [block] + [shift(block, axis, -k) for k in (1, 2, 3)]


def local(tokens, slot_embed, combine, w_in, w_out, grad_out):
    z = lax.axis_index("seq")
    w_in, w_out = w_in[0], w_out[0]
    embed = rolled(slot_embed.T, z, 8, 0)
    comb = rolled(jnp.transpose(combine, (0, 2, 1)), z, 8, 1)

    logits = jnp.einsum("jd,itd->ijt", embed, tokens, preferred_element_type=F32)
    peak = jnp.max(logits, axis=2, keepdims=True)
    weight = jnp.exp(logits - peak)
    total = jnp.sum(weight, axis=2, keepdims=True)
    lse = peak + jnp.log(total)
    slot_part = jnp.einsum("ijt,itd->ijd", weight.astype(BF16), tokens, preferred_element_type=F32)
    slot_part = (slot_part / total).astype(BF16).reshape(2, 4, 8, 1280)
    out_part = jnp.einsum("ijt,itd->ijd", comb, grad_out, preferred_element_type=F32)
    out_part = out_part.astype(BF16).reshape(2, 4, 8, 1280)
    lses = [lse] + [
        jnp.roll(shift(lse, "seq", k), -8 * k, axis=1) for k in (1, 2, 3)
    ]
    top = jnp.maximum(jnp.maximum(lses[0], lses[1]), jnp.maximum(lses[2], lses[3]))
    lse_all = top + jnp.log(sum(jnp.exp(one - top) for one in lses))
    terms = scatter_terms(
        [jnp.stack([slot_part[:, k], out_part[:, k]]) for k in range(4)], "seq"
    )
    slot_own = sum(
        jnp.exp(lses[k] - lse_all)[:, :8] * terms[k][0].astype(F32) for k in range(4)
    )
    out_own = sum(terms[k][1].astype(F32) for k in range(4))
    both = gather_blocks(jnp.stack([slot_own, out_own]).astype(BF16), "seq")
    both = jnp.stack(both)
    slot_in = both[:, 0].reshape(64, 1280)
    grad_slot_out = both[:, 1].reshape(64, 1280)

    pre_act = jnp.dot(slot_in, w_in, preferred_element_type=F32)
    act, slope = gelu_parts(pre_act)
    act = act.astype(BF16)
    out_sum = jnp.dot(act, w_out, preferred_element_type=F32).astype(BF16)
    grad_act = jnp.einsum("sd,hd->sh", grad_slot_out, w_out, preferred_element_type=F32)
    grad_pre = (grad_act * slope).astype(BF16)
    in_sum = jnp.einsum("sh,dh->sd", grad_pre, w_in, preferred_element_type=F32).astype(BF16)
    pair = jnp.stack([out_sum.reshape(4, 16, 1280), in_sum.reshape(4, 16, 1280)], axis=1)
    terms = scatter_terms([pair[k] for k in range(4)], "seq")
    own = sum(term.astype(F32) for term in terms).astype(BF16)
    pair = jnp.stack(gather_blocks(own, "seq"))
    pair = pair.reshape(4, 2, 2, 8, 1280).transpose(1, 2, 0, 3, 4).reshape(2, 2, 32, 1280)
    slot_out, grad_slot_in = pair[0], pair[1]
    slot_in_f = slot_in.reshape(4, 2, 8, 1280).transpose(1, 0, 2, 3).reshape(2, 32, 1280)

    grad_w_out = jnp.einsum("sh,sd->hd", act, grad_slot_out, preferred_element_type=F32)
    grad_w_in = jnp.einsum("sd,sh->dh", slot_in, grad_pre, preferred_element_type=F32)

    grad_combine = jnp.einsum("ijd,itd->ijt", slot_out, grad_out, preferred_element_type=F32)
    comb_f = comb.astype(F32)
    row_dot = jnp.sum(comb_f * grad_combine, axis=1)
    row_dot = row_dot + swap_cores(row_dot)
    for axis in ("x", "y"):
        row_dot = sum(scatter_terms([row_dot] * 4, axis))
    grad_dispatch = jnp.einsum("ijd,itd->ijt", grad_slot_in, tokens, preferred_element_type=F32)
    col_dot = jnp.sum(
        slot_in_f.astype(F32) * grad_slot_in.astype(F32), axis=2, keepdims=True
    )
    dispatch = jnp.exp(logits - lse_all)
    grad_logits = (
        dispatch * (grad_dispatch - col_dot) + comb_f * (grad_combine - row_dot[:, None, :])
    ).astype(BF16)
    dispatch = dispatch.astype(BF16)

    embed_part = jnp.einsum("ijt,itd->jd", grad_logits, tokens, preferred_element_type=F32)
    embed_part = rolled(embed_part.astype(BF16), (4 - z) % 4, 8, 0)
    embed_part = rolled(embed_part.reshape(32, 4, 320).transpose(1, 0, 2), z, 1, 0)
    terms = scatter_terms([embed_part[k] for k in range(4)], "seq")
    grad_embed = sum(term.astype(F32) for term in terms).astype(BF16).T

    y, x, core = lax.axis_index("y"), lax.axis_index("x"), lax.axis_index("core")
    rows = jnp.concatenate([grad_slot_in.reshape(64, 1280), embed])
    rows = jnp.stack(gather_blocks(rows, "y"))
    weights = jnp.stack([dispatch, grad_logits], axis=1).reshape(2, 2, 32, 4, 256)
    weights = rolled(weights.transpose(3, 0, 1, 2, 4), y, 1, 0)
    weights = scatter_terms([weights[k] for k in range(4)], "y")
    weights = jnp.stack([weights[0], weights[3], weights[2], weights[1]])
    slots = jnp.stack(
        [
            jnp.stack([rows[:, 32 * i : 32 * i + 32], rows[:, 64:96]], axis=1)
            for i in range(2)
        ],
        axis=1,
    )
    part = jnp.einsum("kicjt,kicjd->itd", weights, slots, preferred_element_type=F32)
    part = part.astype(BF16).reshape(2, 4, 2, 32, 1280)
    part = part.transpose(2, 1, 0, 3, 4)
    mine = lax.dynamic_index_in_dim(part, core, 0, keepdims=False)
    other = lax.dynamic_index_in_dim(part, 1 - core, 0, keepdims=False)
    part = (mine.astype(F32) + swap_cores(other).astype(F32)).astype(BF16)
    part = rolled(part, x, 1, 0)
    terms = scatter_terms([part[k] for k in range(4)], "x")
    grad_tokens = sum(term.astype(F32) for term in terms).astype(BF16)
    return (
        grad_tokens,
        grad_embed,
        grad_w_in.astype(BF16)[None],
        grad_w_out.astype(BF16)[None],
    )


def solution(mesh):
    fine = Mesh(mesh.devices.reshape(4, 4, 4, 2), ("seq", "y", "x", "core"))
    expert = ("y", "x", "core")
    return jax.shard_map(
        local,
        mesh=fine,
        in_specs=(
            P(None, "seq", None),
            P(None, expert),
            P(None, "seq", expert),
            P(expert, None, "seq"),
            P(expert, "seq", None),
            P(None, "seq", None),
        ),
        out_specs=(
            P(None, ("seq", *expert), None),
            P("seq", expert),
            P(expert, None, "seq"),
            P(expert, "seq", None),
        ),
        check_vma=False,
    )
```

time: 348 us -> 130 us (0.37)
  waiting for transfers between devices: 142 us -> 22.1 us
  blocking collectives: 116 us -> 0 us
  starting transfers between devices: 0.3 us -> 47.1 us
  matrix products: 52.5 us -> 30.1 us
  other arithmetic: 1.45 us -> 15.7 us
  between operations: 14.5 us -> 1.24 us
  local copies, waits for them, and re-layouts: 20.5 us -> 13.1 us
    psum x4 -> x0, blocking collectives: 104 us -> none  [the longest x1 64.1 us: local(): lax.psum(jnp.sum(combine_full * grad_combine, axis=2, keepdims=True), 'ex...]
    unnamed x5 -> x0, waiting for transfers between devices: 98.9 us -> none
    ppermute x0 -> x35, starting transfers between devices: none -> 47.1 us  [the longest x33 47.1 us: shift(): return lax.ppermute(value, axis, [(i, (i + by) % 4) for i in range(4)])]
    psum x1 -> x0, waiting for transfers between devices: 42.7 us -> none  [local(): grad_slot_in = lax.psum(in_part.astype(jnp.bfloat16), 'seq')]
    dot_general x14 -> x13, matrix products: 52.5 us -> 30.1 us  [the longest x1 4.97 us: local(): jnp.einsum('ijd,itd->ijt', slot_out, grad_out, preferred_element_type=F32)]
    ppermute x0 -> x35, waiting for transfers between devices: none -> 22.1 us  [the longest x33 22.1 us: shift(): return lax.ppermute(value, axis, [(i, (i + by) % 4) for i in range(4)])]
    convert_element_type x2 -> x0, local copies, waits for them, and re-layouts: 14.8 us -> none  [the longest x1 13.8 us: local(): token_sum = lax.psum_scatter((term_sum + jnp.einsum('itj,dj->tid', grad_l...]
    pmax x1 -> x0, blocking collectives: 11.8 us -> none  [local(): col_peak = lax.pmax(local_max, 'seq')]
  transfers between devices with their start and end apart: 3 -> 35, of which waited for: 2 -> 12; matrix products, arithmetic and copies ran while one was open for 9% -> 27% of each run, Pallas kernels for 0% -> 0%
where the time goes in v1:
time: 130 us; the launch traced here: 129 us
  starting transfers between devices  47.1 us (36%)
  matrix products  30.1 us (23%)
  waiting for transfers between devices  22.1 us (17%)
  other arithmetic  15.7 us (12%)
  local copies, waits for them, and re-layouts  13.1 us (10%)
    ppermute x33, starting transfers between devices, shift(): return lax.ppermute(value, axis, [(i, (i + by) % 4) for i in range(4)])  47.1 us
    ppermute x33, waiting for transfers between devices, shift(): return lax.ppermute(value, axis, [(i, (i + by) % 4) for i in range(4)])  22.1 us
    dot_general x1, matrix products, local(): jnp.einsum('ijd,itd->ijt', slot_out, grad_out, preferred_element_type=F32)  4.97 us
    dot_general x1, matrix products, local(): jnp.einsum('ijd,itd->ijt', grad_slot_in, tokens, preferred_element_type=F32)  4.87 us
    dot_general x1, matrix products, local(): jnp.einsum('jd,itd->ijt', embed, tokens, preferred_element_type=F32)  4.62 us
    another operation x4, local copies, waits for them, and re-layouts, local(): jnp.stack([dispatch, grad_logits], axis=1).reshape(2, 2, 32, 4, 256)  4.25 us
    dot_general x1, matrix products, local(): jnp.einsum('sh,sd->hd', act, grad_slot_out, preferred_element_type=F32)  3.79 us
    concatenate x5, local copies, waits for them, and re-layouts, local(): jnp.roll(shift(lse, 'seq', k), -8 * k, axis=1)  2.91 us
  transfers between devices with their start and end apart: 35, of which 12 were waited for; matrix products, arithmetic and copies ran while one was open for 27% of the time, Pallas kernels for 0%

profile of v1, /device:TPU:0, one launch (start us, length us, event | category | flops | bytes accessed | tf_op | source)
XLA Modules:
  0.0 129.4 jit_solution(615550831739574245)
XLA Ops:
  1.8 4.6 %fusion.97 = (f32[2,32]{1,0:T(2,128)S(1)}, f32[2,32,1024]{2,1,0:T(8,128)S(1)}) fusion(bf16[2,1024,1280]{2,1,0:T(8,128)(2,1)} %param.6, bf16[32,1280]{1,0:T(8,128)(2,1)S(1)} %fusion.71), kind=kOutput, calls=%fused_computation.191 | convolution fusion | flops 167837632 | bytes 5587200 | tf_op jit(solution)/shard_map/jd,itd->ijt/dot_general | solution.py:45
  6.6 4.1 %collective-permute-start.2 = (f32[2,32,1]{1,0,2:T(2,128)S(1)}, f32[2,32,1]{1,0,2:T(2,128)}, u32[]{:S(2)}, u32[]{:S(2)}) collective-permute-start(f32[2,32,1]{1,0,2:T(2,128)S(1)} %fusion.91), channel_id=1, source_target_pairs={{0,96},{32,0},{64,32},{96,64},{1,97},{33,1},{65,33},{97,65},{2,98}... | collective-permute-start | bytes 776 | tf_op jit(solution)/shard_map/ppermute | solution.py:19
  16.1 2.0 %collective-permute-start.5 = (bf16[2,2,8,1280]{3,2,1,0:T(8,128)(2,1)}, bf16[2,2,8,1280]{3,2,1,0:T(8,128)(2,1)}, u32[]{:S(2)}, u32[]{:S(2)}) collective-permute-start(bf16[2,2,8,1280]{3,2,1,0:T(8,128)(2,1)} %pad_maximum_fusion.8), channel_id=1, source_target_pairs={{0,96},{32,0},{64,32},{96,64},{1,97},{33,1},{65,33},{97,65},{2,98}... | collective-permute-start | bytes 245768 | tf_op jit(solution)/shard_map/ppermute | solution.py:19
  18.7 2.3 %collective-permute-start.4 = (bf16[2,2,8,1280]{3,2,1,0:T(8,128)(2,1)}, bf16[2,2,8,1280]{3,2,1,0:T(8,128)(2,1)}, u32[]{:S(2)}, u32[]{:S(2)}) collective-permute-start(bf16[2,2,8,1280]{3,2,1,0:T(8,128)(2,1)} %pad_maximum_fusion.7), channel_id=1, source_target_pairs={{0,64},{32,96},{64,0},{96,32},{1,65},{33,97},{65,1},{97,33},{2,66}... | collective-permute-start | bytes 245768 | tf_op jit(solution)/shard_map/ppermute | solution.py:19
  25.8 2.5 %collective-permute-done.3 = bf16[2,2,8,1280]{3,2,1,0:T(8,128)(2,1)S(1)} collective-permute-done((bf16[2,2,8,1280]{3,2,1,0:T(8,128)(2,1)}, bf16[2,2,8,1280]{3,2,1,0:T(8,128)(2,1)S(1)}, u32[]{:S(2)}, u32[]{:S(2)}) %collective-permute-start.3) | collective-permute-done | bytes 81952 | tf_op jit(solution)/shard_map/ppermute | solution.py:19
  29.4 2.1 %collective-permute-start.7 = (bf16[2,2,8,1280]{3,2,1,0:T(8,128)(2,1)S(1)}, bf16[2,2,8,1280]{3,2,1,0:T(8,128)(2,1)S(1)}, u32[]{:S(2)}, u32[]{:S(2)}) collective-permute-start(bf16[2,2,8,1280]{3,2,1,0:T(8,128)(2,1)S(1)} %pad_maximum_fusion.9), channel_id=1, source_target_pairs={{0,64},{32,96},{64,0},{96,32},{1,65},{33,97},{65,1},{97,33},{2,66}... | collective-permute-start | bytes 245768 | tf_op jit(solution)/shard_map/ppermute | solution.py:19
  32.7 3.3 %collective-permute-done.8 = bf16[2,2,8,1280]{3,2,1,0:T(8,128)(2,1)S(1)} collective-permute-done((bf16[2,2,8,1280]{3,2,1,0:T(8,128)(2,1)S(1)}, bf16[2,2,8,1280]{3,2,1,0:T(8,128)(2,1)S(1)}, u32[]{:S(2)}, u32[]{:S(2)}) %collective-permute-start.8) | collective-permute-done | bytes 81952 | tf_op jit(solution)/shard_map/ppermute | solution.py:19
  37.7 2.6 %fusion.8 = f32[64,1280]{1,0:T(8,128)S(1)} fusion(bf16[64,1280]{1,0:T(8,128)(2,1)S(1)} %bitcast.259, bf16[1,1280,1280]{2,1,0:T(8,128)(2,1)} %param.9), kind=kOutput, calls=%fused_computation.10 | convolution fusion | flops 209715200 | bytes 3768320 | tf_op jit(solution)/shard_map/dot_general | solution.py:71
  46.1 2.1 %collective-permute-start.11 = (bf16[2,16,1280]{2,1,0:T(8,128)(2,1)}, bf16[2,16,1280]{2,1,0:T(8,128)(2,1)}, u32[]{:S(2)}, u32[]{:S(2)}) collective-permute-start(bf16[2,16,1280]{2,1,0:T(8,128)(2,1)} %get-tuple-element.19), channel_id=1, source_target_pairs={{0,96},{32,0},{64,32},{96,64},{1,97},{33,1},{65,33},{97,65},{2,98}... | collective-permute-start | bytes 245768 | tf_op jit(solution)/shard_map/ppermute | solution.py:19
  52.8 2.6 %collective-permute-done.10 = bf16[2,16,1280]{2,1,0:T(8,128)(2,1)} collective-permute-done((bf16[2,16,1280]{2,1,0:T(8,128)(2,1)}, bf16[2,16,1280]{2,1,0:T(8,128)(2,1)}, u32[]{:S(2)}, u32[]{:S(2)}) %collective-permute-start.10) | collective-permute-done | bytes 81952 | tf_op jit(solution)/shard_map/ppermute | solution.py:19
  59.8 3.8 %fusion.1 = bf16[1,1280,1280]{2,1,0:T(8,128)(2,1)} fusion(bf16[64,1280]{1,0:T(8,128)(2,1)} %bitcast.266, f32[64,1280]{1,0:T(8,128)} %copy-done.4), kind=kOutput, calls=%fused_computation.3 | convolution fusion | flops 211763200 | bytes 3768320 | tf_op jit(solution)/shard_map/sh,sd->hd/dot_general | solution.py:86
  64.0 5.0 %fusion.43 = (f32[2,1024]{1,0:T(2,128)S(1)}, f32[2,32,1024]{2,1,0:T(8,128)}) fusion(bf16[2,32,1024]{2,1,0:T(8,128)(2,1)S(1)} %copy-done.6, bf16[2,1024,1280]{2,1,0:T(8,128)(2,1)} %param.11, bf16[1,2,4,8,1280]{4,3,1,2,0:T(8,128)(2,1)S(1)} %get-tuple-element.14), kind=kOutput, calls=%fused_computation.71 | convolution fusion | flops 167966720 | bytes 5808128 | tf_op jit(solution)/shard_map/ijd,itd->ijt/dot_general | solution.py:89
  69.0 2.8 %fusion = bf16[1,1280,1280]{2,1,0:T(8,128)(2,1)} fusion(bf16[64,1280]{1,0:T(8,128)(2,1)S(1)} %bitcast.260, bf16[64,1280]{1,0:T(8,128)(2,1)S(1)} %copy-done.12), kind=kOutput, calls=%fused_computation.2 | convolution fusion | flops 211353600 | bytes 3604480 | tf_op jit(solution)/shard_map/sd,sh->dh/dot_general | solution.py:87
  71.8 2.8 %collective-permute-start.18 = (f32[2,1024]{1,0:T(2,128)S(1)}, f32[2,1024]{1,0:T(2,128)S(1)}, u32[]{:S(2)}, u32[]{:S(2)}) collective-permute-start(f32[2,1024]{1,0:T(2,128)S(1)} %add.283), channel_id=1, source_target_pairs={{0,6},{2,0},{4,2},{6,4},{1,7},{3,1},{5,3},{7,5},{8,14},{10,8},{12,... | collective-permute-start | bytes 24584 | tf_op jit(solution)/shard_map/ppermute | solution.py:19
  77.2 2.7 %collective-permute-done.17 = f32[2,1024]{1,0:T(2,128)S(1)} collective-permute-done((f32[2,1024]{1,0:T(2,128)S(1)}, f32[2,1024]{1,0:T(2,128)S(1)}, u32[]{:S(2)}, u32[]{:S(2)}) %collective-permute-start.17) | collective-permute-done | bytes 8224 | tf_op jit(solution)/shard_map/ppermute | solution.py:19
  80.3 3.1 %collective-permute-start.21 = (f32[2,1024]{1,0:T(2,128)S(1)}, f32[2,1024]{1,0:T(2,128)}, u32[]{:S(2)}, u32[]{:S(2)}) collective-permute-start(f32[2,1024]{1,0:T(2,128)S(1)} %add_add_fusion.1), channel_id=1, source_target_pairs={{0,24},{8,0},{16,8},{24,16},{1,25},{9,1},{17,9},{25,17},{2,26},{10... | collective-permute-start | bytes 24584 | tf_op jit(solution)/shard_map/ppermute | solution.py:19
  85.2 2.0 %collective-permute-start.26 = (bf16[96,1280]{1,0:T(8,128)(2,1)}, bf16[96,1280]{1,0:T(8,128)(2,1)}, u32[]{:S(2)}, u32[]{:S(2)}) collective-permute-start(bf16[96,1280]{1,0:T(8,128)(2,1)} %get-tuple-element.28), channel_id=1, source_target_pairs={{0,16},{8,24},{16,0},{24,8},{1,17},{9,25},{17,1},{25,9},{2,18},{10... | collective-permute-start | bytes 737288 | tf_op jit(solution)/shard_map/ppermute | solution.py:19
  87.1 2.6 %collective-permute-start.25 = (bf16[96,1280]{1,0:T(8,128)(2,1)}, bf16[96,1280]{1,0:T(8,128)(2,1)}, u32[]{:S(2)}, u32[]{:S(2)}) collective-permute-start(bf16[96,1280]{1,0:T(8,128)(2,1)} %get-tuple-element.28), channel_id=1, source_target_pairs={{0,24},{8,0},{16,8},{24,16},{1,25},{9,1},{17,9},{25,17},{2,26},{10... | collective-permute-start | bytes 737288 | tf_op jit(solution)/shard_map/ppermute | solution.py:19
  91.2 4.9 %fusion.45 = bf16[2,32,1024]{2,1,0:T(8,128)(2,1)} fusion(bf16[2,32,1024]{2,1,0:T(8,128)(2,1)} %copy-done.5, f32[2,32,1024]{2,1,0:T(8,128)} %get-tuple-element.59, bf16[2,1024,1280]{2,1,0:T(8,128)(2,1)} %param.6, f32[2,32,1024]{2,1,0:T(8,128)S(1)} %get-tuple-element.57, f32[2,1024]{1,0:T(2,128)S(1)} %add_add_fusion, f32[2,32]{1,0:T(2,128)} %sub.212, ...), kind=kOutput, calls=%fused_computation.73 | convolution fusion | flops 168296448 | bytes 6201856 | tf_op jit(solution)/shard_map/ijd,itd->ijt/dot_general | solution.py:95
  98.2 2.2 %collective-permute-start.23 = (bf16[2,2,32,256]{3,2,0,1:T(8,128)(2,1)S(1)}, bf16[2,2,32,256]{3,2,0,1:T(8,128)(2,1)S(1)}, u32[]{:S(2)}, u32[]{:S(2)}) collective-permute-start(bf16[2,2,32,256]{3,2,0,1:T(8,128)(2,1)S(1)} %get-tuple-element.24), channel_id=1, source_target_pairs={{0,16},{8,24},{16,0},{24,8},{1,17},{9,25},{17,1},{25,9},{2,18},{10... | collective-permute-start | bytes 196616 | tf_op jit(solution)/shard_map/ppermute | solution.py:19
  111.1 2.5 %collective-permute-start.34 = (bf16[32,320]{1,0:T(8,128)(2,1)S(1)}, bf16[32,320]{1,0:T(8,128)(2,1)S(1)}, u32[]{:S(2)}, u32[]{:S(2)}) collective-permute-start(bf16[32,320]{1,0:T(8,128)(2,1)S(1)} %bitcast.283), channel_id=1, source_target_pairs={{0,96},{32,0},{64,32},{96,64},{1,97},{33,1},{65,33},{97,65},{2,98}... | collective-permute-start | bytes 61448 | tf_op jit(solution)/shard_map/ppermute | solution.py:19
  113.5 2.2 %collective-permute-start.33 = (bf16[32,320]{1,0:T(8,128)(2,1)S(1)}, bf16[32,320]{1,0:T(8,128)(2,1)S(1)}, u32[]{:S(2)}, u32[]{:S(2)}) collective-permute-start(bf16[32,320]{1,0:T(8,128)(2,1)S(1)} %bitcast.281), channel_id=1, source_target_pairs={{0,64},{32,96},{64,0},{96,32},{1,65},{33,97},{65,1},{97,33},{2,66}... | collective-permute-start | bytes 61448 | tf_op jit(solution)/shard_map/ppermute | solution.py:19
  119.4 2.4 %collective-permute-start.31 = (bf16[2,32,1280]{2,1,0:T(8,128)(2,1)S(1)}, bf16[2,32,1280]{2,1,0:T(8,128)(2,1)S(1)}, u32[]{:S(2)}, u32[]{:S(2)}) collective-permute-start(bf16[2,32,1280]{2,1,0:T(8,128)(2,1)S(1)} %get-tuple-element.13), channel_id=1, source_target_pairs={{0,6},{2,0},{4,2},{6,4},{1,7},{3,1},{5,3},{7,5},{8,14},{10,8},{12,... | collective-permute-start | bytes 491528 | tf_op jit(solution)/shard_map/ppermute | solution.py:19
  122.4 5.7 %collective-permute-done.29 = bf16[2,32,1280]{2,1,0:T(8,128)(2,1)S(1)} collective-permute-done((bf16[2,32,1280]{2,1,0:T(8,128)(2,1)S(1)}, bf16[2,32,1280]{2,1,0:T(8,128)(2,1)S(1)}, u32[]{:S(2)}, u32[]{:S(2)}) %collective-permute-start.29) | collective-permute-done | bytes 163872 | tf_op jit(solution)/shard_map/ppermute | solution.py:19
  (171 shorter events, 55.3 us)
Async XLA Ops:
  6.6 15.9 %collective-permute-start.2 = (f32[2,32,1]{1,0,2:T(2,128)S(1)}, f32[2,32,1]{1,0,2:T(2,128)}, u32[]{:S(2)}, u32[]{:S(2)}) collective-permute-start(f32[2,32,1]{1,0,2:T(2,128)S(1)} %fusion.91), channel_id=1, source_target_pairs={{0,96},{32,0},{64,32},{96,64},{1,97},{33,1},{65,33},{97,65},{2,98}... | collective-permute-start | bytes 776 | tf_op jit(solution)/shard_map/ppermute | solution.py:19
  10.7 14.6 %collective-permute-start.1 = (f32[2,32,1]{1,0,2:T(2,128)S(1)}, f32[2,32,1]{1,0,2:T(2,128)S(1)}, u32[]{:S(2)}, u32[]{:S(2)}) collective-permute-start(f32[2,32,1]{1,0,2:T(2,128)S(1)} %fusion.91), channel_id=1, source_target_pairs={{0,64},{32,96},{64,0},{96,32},{1,65},{33,97},{65,1},{97,33},{2,66}... | collective-permute-start | bytes 776 | tf_op jit(solution)/shard_map/ppermute | solution.py:19
  10.8 13.2 %collective-permute-start = (f32[2,32,1]{1,0,2:T(2,128)S(1)}, f32[2,32,1]{1,0,2:T(2,128)}, u32[]{:S(2)}, u32[]{:S(2)}) collective-permute-start(f32[2,32,1]{1,0,2:T(2,128)S(1)} %fusion.91), channel_id=1, source_target_pairs={{0,32},{32,64},{64,96},{96,0},{1,33},{33,65},{65,97},{97,1},{2,34}... | collective-permute-start | bytes 776 | tf_op jit(solution)/shard_map/ppermute | solution.py:19
  16.1 9.7 %collective-permute-start.5 = (bf16[2,2,8,1280]{3,2,1,0:T(8,128)(2,1)}, bf16[2,2,8,1280]{3,2,1,0:T(8,128)(2,1)}, u32[]{:S(2)}, u32[]{:S(2)}) collective-permute-start(bf16[2,2,8,1280]{3,2,1,0:T(8,128)(2,1)} %pad_maximum_fusion.8), channel_id=1, source_target_pairs={{0,96},{32,0},{64,32},{96,64},{1,97},{33,1},{65,33},{97,65},{2,98}... | collective-permute-start | bytes 245768 | tf_op jit(solution)/shard_map/ppermute | solution.py:19
  18.7 7.1 %collective-permute-start.4 = (bf16[2,2,8,1280]{3,2,1,0:T(8,128)(2,1)}, bf16[2,2,8,1280]{3,2,1,0:T(8,128)(2,1)}, u32[]{:S(2)}, u32[]{:S(2)}) collective-permute-start(bf16[2,2,8,1280]{3,2,1,0:T(8,128)(2,1)} %pad_maximum_fusion.7), channel_id=1, source_target_pairs={{0,64},{32,96},{64,0},{96,32},{1,65},{33,97},{65,1},{97,33},{2,66}... | collective-permute-start | bytes 245768 | tf_op jit(solution)/shard_map/ppermute | solution.py:19
  29.4 6.6 %collective-permute-start.8 = (bf16[2,2,8,1280]{3,2,1,0:T(8,128)(2,1)S(1)}, bf16[2,2,8,1280]{3,2,1,0:T(8,128)(2,1)S(1)}, u32[]{:S(2)}, u32[]{:S(2)}) collective-permute-start(bf16[2,2,8,1280]{3,2,1,0:T(8,128)(2,1)S(1)} %pad_maximum_fusion.9), channel_id=1, source_target_pairs={{0,32},{32,64},{64,96},{96,0},{1,33},{33,65},{65,97},{97,1},{2,34}... | collective-permute-start | bytes 245768 | tf_op jit(solution)/shard_map/ppermute | solution.py:19
  29.4 6.5 %collective-permute-start.7 = (bf16[2,2,8,1280]{3,2,1,0:T(8,128)(2,1)S(1)}, bf16[2,2,8,1280]{3,2,1,0:T(8,128)(2,1)S(1)}, u32[]{:S(2)}, u32[]{:S(2)}) collective-permute-start(bf16[2,2,8,1280]{3,2,1,0:T(8,128)(2,1)S(1)} %pad_maximum_fusion.9), channel_id=1, source_target_pairs={{0,64},{32,96},{64,0},{96,32},{1,65},{33,97},{65,1},{97,33},{2,66}... | collective-permute-start | bytes 245768 | tf_op jit(solution)/shard_map/ppermute | solution.py:19
  44.9 7.9 %collective-permute-start.9 = (bf16[2,16,1280]{2,1,0:T(8,128)(2,1)}, bf16[2,16,1280]{2,1,0:T(8,128)(2,1)}, u32[]{:S(2)}, u32[]{:S(2)}) collective-permute-start(bf16[2,16,1280]{2,1,0:T(8,128)(2,1)} %get-tuple-element.18), channel_id=1, source_target_pairs={{0,32},{32,64},{64,96},{96,0},{1,33},{33,65},{65,97},{97,1},{2,34}... | collective-permute-start | bytes 245768 | tf_op jit(solution)/shard_map/ppermute | solution.py:19
  46.1 6.7 %collective-permute-start.11 = (bf16[2,16,1280]{2,1,0:T(8,128)(2,1)}, bf16[2,16,1280]{2,1,0:T(8,128)(2,1)}, u32[]{:S(2)}, u32[]{:S(2)}) collective-permute-start(bf16[2,16,1280]{2,1,0:T(8,128)(2,1)} %get-tuple-element.19), channel_id=1, source_target_pairs={{0,96},{32,0},{64,32},{96,64},{1,97},{33,1},{65,33},{97,65},{2,98}... | collective-permute-start | bytes 245768 | tf_op jit(solution)/shard_map/ppermute | solution.py:19
  48.2 7.2 %collective-permute-start.10 = (bf16[2,16,1280]{2,1,0:T(8,128)(2,1)}, bf16[2,16,1280]{2,1,0:T(8,128)(2,1)}, u32[]{:S(2)}, u32[]{:S(2)}) collective-permute-start(bf16[2,16,1280]{2,1,0:T(8,128)(2,1)} %get-tuple-element.20), channel_id=1, source_target_pairs={{0,64},{32,96},{64,0},{96,32},{1,65},{33,97},{65,1},{97,33},{2,66}... | collective-permute-start | bytes 245768 | tf_op jit(solution)/shard_map/ppermute | solution.py:19
  56.4 7.1 %collective-permute-start.14 = (bf16[2,16,1280]{2,1,0:T(8,128)(2,1)S(1)}, bf16[2,16,1280]{2,1,0:T(8,128)(2,1)S(1)}, u32[]{:S(2)}, u32[]{:S(2)}) collective-permute-start(bf16[2,16,1280]{2,1,0:T(8,128)(2,1)S(1)} %fusion.59), channel_id=1, source_target_pairs={{0,32},{32,64},{64,96},{96,0},{1,33},{33,65},{65,97},{97,1},{2,34}... | collective-permute-start | bytes 245768 | tf_op jit(solution)/shard_map/ppermute | solution.py:19
  56.5 7.0 %collective-permute-start.13 = (bf16[2,16,1280]{2,1,0:T(8,128)(2,1)S(1)}, bf16[2,16,1280]{2,1,0:T(8,128)(2,1)S(1)}, u32[]{:S(2)}, u32[]{:S(2)}) collective-permute-start(bf16[2,16,1280]{2,1,0:T(8,128)(2,1)S(1)} %fusion.59), channel_id=1, source_target_pairs={{0,64},{32,96},{64,0},{96,32},{1,65},{33,97},{65,1},{97,33},{2,66}... | collective-permute-start | bytes 245768 | tf_op jit(solution)/shard_map/ppermute | solution.py:19
  80.3 10.1 %collective-permute-start.21 = (f32[2,1024]{1,0:T(2,128)S(1)}, f32[2,1024]{1,0:T(2,128)}, u32[]{:S(2)}, u32[]{:S(2)}) collective-permute-start(f32[2,1024]{1,0:T(2,128)S(1)} %add_add_fusion.1), channel_id=1, source_target_pairs={{0,24},{8,0},{16,8},{24,16},{1,25},{9,1},{17,9},{25,17},{2,26},{10... | collective-permute-start | bytes 24584 | tf_op jit(solution)/shard_map/ppermute | solution.py:19
  83.4 7.0 %collective-permute-start.20 = (f32[2,1024]{1,0:T(2,128)S(1)}, f32[2,1024]{1,0:T(2,128)}, u32[]{:S(2)}, u32[]{:S(2)}) collective-permute-start(f32[2,1024]{1,0:T(2,128)S(1)} %add_add_fusion.1), channel_id=1, source_target_pairs={{0,16},{8,24},{16,0},{24,8},{1,17},{9,25},{17,1},{25,9},{2,18},{10... | collective-permute-start | bytes 24584 | tf_op jit(solution)/shard_map/ppermute | solution.py:19
  84.0 6.4 %collective-permute-start.19 = (f32[2,1024]{1,0:T(2,128)S(1)}, f32[2,1024]{1,0:T(2,128)}, u32[]{:S(2)}, u32[]{:S(2)}) collective-permute-start(f32[2,1024]{1,0:T(2,128)S(1)} %add_add_fusion.1), channel_id=1, source_target_pairs={{0,8},{8,16},{16,24},{24,0},{1,9},{9,17},{17,25},{25,1},{2,10},{10... | collective-permute-start | bytes 24584 | tf_op jit(solution)/shard_map/ppermute | solution.py:19
  85.2 16.4 %collective-permute-start.26 = (bf16[96,1280]{1,0:T(8,128)(2,1)}, bf16[96,1280]{1,0:T(8,128)(2,1)}, u32[]{:S(2)}, u32[]{:S(2)}) collective-permute-start(bf16[96,1280]{1,0:T(8,128)(2,1)} %get-tuple-element.28), channel_id=1, source_target_pairs={{0,16},{8,24},{16,0},{24,8},{1,17},{9,25},{17,1},{25,9},{2,18},{10... | collective-permute-start | bytes 737288 | tf_op jit(solution)/shard_map/ppermute | solution.py:19
  87.1 15.3 %collective-permute-start.25 = (bf16[96,1280]{1,0:T(8,128)(2,1)}, bf16[96,1280]{1,0:T(8,128)(2,1)}, u32[]{:S(2)}, u32[]{:S(2)}) collective-permute-start(bf16[96,1280]{1,0:T(8,128)(2,1)} %get-tuple-element.28), channel_id=1, source_target_pairs={{0,24},{8,0},{16,8},{24,16},{1,25},{9,1},{17,9},{25,17},{2,26},{10... | collective-permute-start | bytes 737288 | tf_op jit(solution)/shard_map/ppermute | solution.py:19
  90.4 12.0 %collective-permute-start.27 = (bf16[96,1280]{1,0:T(8,128)(2,1)}, bf16[96,1280]{1,0:T(8,128)(2,1)}, u32[]{:S(2)}, u32[]{:S(2)}) collective-permute-start(bf16[96,1280]{1,0:T(8,128)(2,1)} %get-tuple-element.28), channel_id=1, source_target_pairs={{0,8},{8,16},{16,24},{24,0},{1,9},{9,17},{17,25},{25,1},{2,10},{10... | collective-permute-start | bytes 737288 | tf_op jit(solution)/shard_map/ppermute | solution.py:19
  111.1 8.3 %collective-permute-start.34 = (bf16[32,320]{1,0:T(8,128)(2,1)S(1)}, bf16[32,320]{1,0:T(8,128)(2,1)S(1)}, u32[]{:S(2)}, u32[]{:S(2)}) collective-permute-start(bf16[32,320]{1,0:T(8,128)(2,1)S(1)} %bitcast.283), channel_id=1, source_target_pairs={{0,96},{32,0},{64,32},{96,64},{1,97},{33,1},{65,33},{97,65},{2,98}... | collective-permute-start | bytes 61448 | tf_op jit(solution)/shard_map/ppermute | solution.py:19
  113.5 8.2 %collective-permute-start.32 = (bf16[32,320]{1,0:T(8,128)(2,1)S(1)}, bf16[32,320]{1,0:T(8,128)(2,1)S(1)}, u32[]{:S(2)}, u32[]{:S(2)}) collective-permute-start(bf16[32,320]{1,0:T(8,128)(2,1)S(1)} %bitcast.282), channel_id=1, source_target_pairs={{0,32},{32,64},{64,96},{96,0},{1,33},{33,65},{65,97},{97,1},{2,34}... | collective-permute-start | bytes 61448 | tf_op jit(solution)/shard_map/ppermute | solution.py:19
  113.5 8.2 %collective-permute-start.33 = (bf16[32,320]{1,0:T(8,128)(2,1)S(1)}, bf16[32,320]{1,0:T(8,128)(2,1)S(1)}, u32[]{:S(2)}, u32[]{:S(2)}) collective-permute-start(bf16[32,320]{1,0:T(8,128)(2,1)S(1)} %bitcast.281), channel_id=1, source_target_pairs={{0,64},{32,96},{64,0},{96,32},{1,65},{33,97},{65,1},{97,33},{2,66}... | collective-permute-start | bytes 61448 | tf_op jit(solution)/shard_map/ppermute | solution.py:19
  117.5 10.5 %collective-permute-start.29 = (bf16[2,32,1280]{2,1,0:T(8,128)(2,1)S(1)}, bf16[2,32,1280]{2,1,0:T(8,128)(2,1)S(1)}, u32[]{:S(2)}, u32[]{:S(2)}) collective-permute-start(bf16[2,32,1280]{2,1,0:T(8,128)(2,1)S(1)} %get-tuple-element.11), channel_id=1, source_target_pairs={{0,2},{2,4},{4,6},{6,0},{1,3},{3,5},{5,7},{7,1},{8,10},{10,12},{12... | collective-permute-start | bytes 491528 | tf_op jit(solution)/shard_map/ppermute | solution.py:19
  117.6 10.5 %collective-permute-start.30 = (bf16[2,32,1280]{2,1,0:T(8,128)(2,1)S(1)}, bf16[2,32,1280]{2,1,0:T(8,128)(2,1)S(1)}, u32[]{:S(2)}, u32[]{:S(2)}) collective-permute-start(bf16[2,32,1280]{2,1,0:T(8,128)(2,1)S(1)} %get-tuple-element.12), channel_id=1, source_target_pairs={{0,4},{2,6},{4,0},{6,2},{1,5},{3,7},{5,1},{7,3},{8,12},{10,14},{12... | collective-permute-start | bytes 491528 | tf_op jit(solution)/shard_map/ppermute | solution.py:19
  119.4 9.3 %collective-permute-start.31 = (bf16[2,32,1280]{2,1,0:T(8,128)(2,1)S(1)}, bf16[2,32,1280]{2,1,0:T(8,128)(2,1)S(1)}, u32[]{:S(2)}, u32[]{:S(2)}) collective-permute-start(bf16[2,32,1280]{2,1,0:T(8,128)(2,1)S(1)} %get-tuple-element.13), channel_id=1, source_target_pairs={{0,6},{2,0},{4,2},{6,4},{1,7},{3,1},{5,3},{7,5},{8,14},{10,8},{12,... | collective-permute-start | bytes 491528 | tf_op jit(solution)/shard_map/ppermute | solution.py:19
  (36 other events, 219.1 us)

commit v2 on v1

v2 whole, which is shorter than its diff:
```python
import math

import jax
import jax.numpy as jnp
from jax import lax
from jax.experimental import pallas as pl
from jax.experimental.pallas import tpu as pltpu
from jax.sharding import Mesh, PartitionSpec as P

F32 = jnp.float32
BF16 = jnp.bfloat16
NT = (((1,), (1,)), ((), ()))
TN = (((0,), (0,)), ((), ()))
PARAMS = pltpu.CompilerParams(vmem_limit_bytes=24 * 1024 * 1024)


def shape(dims, dtype):
    return jax.ShapeDtypeStruct(dims, dtype)


def gelu_parts(values):
    cdf = 0.5 * (1.0 + jax.scipy.special.erf(values / math.sqrt(2.0)))
    slope = cdf + values * jnp.exp(-0.5 * values * values) / math.sqrt(2.0 * math.pi)
    return values * cdf, slope


def shift(value, axis, by):
    return lax.ppermute(value, axis, [(i, (i + by) % 4) for i in range(4)])


def swap_cores(value):
    return lax.ppermute(value, "core", [(0, 1), (1, 0)])


def near(value):
    return lax.ppermute(value, "seq", [(0, 1), (1, 0), (2, 3), (3, 2)])


def far(value):
    return lax.ppermute(value, "seq", [(0, 3), (3, 0), (1, 2), (2, 1)])


def add(one, two):
    return (one.astype(F32) + two.astype(F32)).astype(BF16)


def merge(part_a, lse_a, part_b, lse_b):
    top = jnp.maximum(lse_a, lse_b)
    weight_a, weight_b = jnp.exp(lse_a - top), jnp.exp(lse_b - top)
    total = weight_a + weight_b
    share_a, share_b = (weight_a / total)[:, :1], (weight_b / total)[:, :1]
    part = share_a * part_a.astype(F32) + share_b * part_b.astype(F32)
    return part.astype(BF16), top + jnp.log(total)


def scatter_terms(blocks, axis):
    return [blocks[0]] + [shift(blocks[k], axis, k) for k in (1, 2, 3)]


def gather_blocks(block, axis):
    return [block] + [shift(block, axis, -k) for k in (1, 2, 3)]


def chunk(axis, k, size):
    return pl.multiple_of(((lax.axis_index(axis) + k) & 3) * size, size)


def softmax_kernel(tok, embed, logits, part, lse):
    patches = tok[0]
    scores = lax.dot_general(patches, embed[...], NT, preferred_element_type=F32).T
    peak = jnp.max(scores, axis=1, keepdims=True)
    weight = jnp.exp(scores - peak)
    total = jnp.sum(weight, axis=1, keepdims=True)
    sums = jnp.dot(weight.astype(BF16), patches, preferred_element_type=F32)
    logits[...] = scores
    part[...] = (sums / total).astype(BF16)
    lse[...] = jnp.broadcast_to(peak + jnp.log(total), lse.shape)


def local_softmax(tokens, embed):
    return pl.pallas_call(
        softmax_kernel,
        grid=(2,),
        in_specs=[
            pl.BlockSpec((1, 1024, 1280), lambda i: (i, 0, 0)),
            pl.BlockSpec((32, 1280), lambda i: (0, 0)),
        ],
        out_specs=[
            pl.BlockSpec((32, 1024), lambda i: (i, 0)),
            pl.BlockSpec((32, 1280), lambda i: (i, 0)),
            pl.BlockSpec((32, 128), lambda i: (i, 0)),
        ],
        out_shape=[shape((64, 1024), F32), shape((64, 1280), BF16), shape((64, 128), F32)],
        cost_estimate=pl.CostEstimate(flops=700_000_000, bytes_accessed=6_000_000, transcendentals=65536),
        compiler_params=PARAMS,
        name="local_softmax",
    )(tokens, embed)


def combine_grad_kernel(gout, sum_a, sum_b, comb, grad, row):
    slot_out = add(sum_a[...], sum_b[...])
    value = lax.dot_general(gout[0], slot_out, NT, preferred_element_type=F32).T
    grad[...] = value
    row[0] = jnp.sum(comb[...].astype(F32) * value, axis=0, keepdims=True)


def combine_grad(grad_out, sum_a, sum_b, comb):
    return pl.pallas_call(
        combine_grad_kernel,
        grid=(2,),
        in_specs=[
            pl.BlockSpec((1, 1024, 1280), lambda i: (i, 0, 0)),
            pl.BlockSpec((32, 1280), lambda i: (i, 0)),
            pl.BlockSpec((32, 1280), lambda i: (i, 0)),
            pl.BlockSpec((32, 1024), lambda i: (i, 0)),
        ],
        out_specs=[
            pl.BlockSpec((32, 1024), lambda i: (i, 0)),
            pl.BlockSpec((1, 1, 1024), lambda i: (i, 0, 0)),
        ],
        out_shape=[shape((64, 1024), F32), shape((2, 1, 1024), F32)],
        cost_estimate=pl.CostEstimate(flops=350_000_000, bytes_accessed=6_000_000, transcendentals=0),
        compiler_params=PARAMS,
        name="combine_grad",
    )(grad_out, sum_a, sum_b, comb)


def dispatch_grad_kernel(tok, gslot, slot_in, logits, lse, comb, gcomb, full, c0, c1, c2, c3):
    rows = gslot[...]
    col_dot = jnp.sum(slot_in[...].astype(F32) * rows.astype(F32), axis=1, keepdims=True)
    grad = lax.dot_general(tok[0], rows, NT, preferred_element_type=F32).T
    weight = jnp.exp(logits[...] - lse[:, :1])
    full[...] = weight * (grad - col_dot) + comb[...].astype(F32) * gcomb[...]
    for k, out in enumerate((c0, c1, c2, c3)):
        out[...] = full[:, pl.ds(chunk("y", k, 256), 256)].astype(BF16)


def dispatch_grad(tokens, gslot, slot_in, logits, lse, comb, gcomb):
    rows = pl.BlockSpec((32, 1280), lambda i: (i, 0))
    wide = pl.BlockSpec((32, 1024), lambda i: (i, 0))
    part = pl.BlockSpec((32, 256), lambda i: (i, 0))
    return pl.pallas_call(
        dispatch_grad_kernel,
        grid=(2,),
        in_specs=[
            pl.BlockSpec((1, 1024, 1280), lambda i: (i, 0, 0)),
            rows,
            rows,
            wide,
            pl.BlockSpec((32, 128), lambda i: (i, 0)),
            wide,
            wide,
        ],
        out_specs=[wide] + [part] * 4,
        out_shape=[shape((64, 1024), F32)] + [shape((64, 256), BF16)] * 4,
        cost_estimate=pl.CostEstimate(flops=350_000_000, bytes_accessed=7_000_000, transcendentals=65536),
        compiler_params=PARAMS,
        name="dispatch_grad",
    )(tokens, gslot, slot_in, logits, lse, comb, gcomb)


def weights_kernel(logits, lse, o0, o1, o2, o3):
    for k, out in enumerate((o0, o1, o2, o3)):
        piece = logits[:, pl.ds(chunk("y", k, 256), 256)]
        out[...] = jnp.exp(piece - lse[:, :1]).astype(BF16)


def dispatch_chunks(logits, lse):
    return pl.pallas_call(
        weights_kernel,
        out_shape=[shape((64, 256), BF16)] * 4,
        cost_estimate=pl.CostEstimate(flops=65536, bytes_accessed=400_000, transcendentals=65536),
        compiler_params=PARAMS,
        name="dispatch_chunks",
    )(logits, lse)


def split_kernel(value, o0, o1, o2, o3):
    for k, out in enumerate((o0, o1, o2, o3)):
        out[...] = value[:, pl.ds(chunk("y", k, 256), 256)]


def y_chunks(value):
    return pl.pallas_call(
        split_kernel,
        out_shape=[shape((64, 256), BF16)] * 4,
        cost_estimate=pl.CostEstimate(flops=0, bytes_accessed=262_144, transcendentals=0),
        compiler_params=PARAMS,
        name="y_chunks",
    )(value)


def rows_kernel(kinds, *refs):
    ins, (m0, m1, m2, m3, other, scratch) = refs[:-6], refs[-6:]
    for i in range(2):
        weights, rows = [], []
        for kind in range(kinds):
            for k in range(4):
                weight, row = ins[8 * kind + k], ins[8 * kind + 4 + k]
                weights.append(weight[32 * i : 32 * i + 32, :])
                rows.append(row[32 * i : 32 * i + 32, :] if row.shape[0] == 64 else row[...])
        scratch[i] = lax.dot_general(
            jnp.concatenate(weights), jnp.concatenate(rows), TN, preferred_element_type=F32
        )
        core = lax.axis_index("core")
        for k, mine in enumerate((m0, m1, m2, m3)):
            base = ((lax.axis_index("x") + k) & 3) * 64
            here = pl.multiple_of(base + core * 32, 32)
            there = pl.multiple_of(base + (1 - core) * 32, 32)
            mine[i] = scratch[i, pl.ds(here, 32), :].astype(BF16)
            other[k, i] = scratch[i, pl.ds(there, 32), :].astype(BF16)


def patch_rows(kinds):
    refs = [one for weights, rows in kinds for one in (*weights, *rows)]
    block = shape((2, 32, 1280), BF16)
    *mine, other = pl.pallas_call(
        lambda *refs: rows_kernel(len(kinds), *refs),
        out_shape=[block] * 4 + [shape((4, 2, 32, 1280), BF16)],
        scratch_shapes=[pltpu.VMEM((2, 256, 1280), F32)],
        cost_estimate=pl.CostEstimate(flops=170_000_000 * len(kinds), bytes_accessed=3_000_000, transcendentals=0),
        compiler_params=PARAMS,
        name="patch_rows",
    )(*refs)
    return mine, other


def add_kernel(m0, m1, m2, m3, other, o0, o1, o2, o3):
    for k, (mine, out) in enumerate(((m0, o0), (m1, o1), (m2, o2), (m3, o3))):
        out[...] = add(mine[...], other[k])


def add_cores(mine, other):
    return pl.pallas_call(
        add_kernel,
        out_shape=[shape((2, 32, 1280), BF16)] * 4,
        cost_estimate=pl.CostEstimate(flops=327_680, bytes_accessed=2_000_000, transcendentals=0),
        compiler_params=PARAMS,
        name="add_cores",
    )(*mine, other)


def reduce_rows(kinds):
    mine, other = patch_rows(kinds)
    return scatter_terms(add_cores(mine, swap_cores(other)), "x")


def sources(terms):
    return [terms[0], terms[3], terms[2], terms[1]]


def local(tokens, slot_embed, combine, w_in, w_out, grad_out):
    w_in, w_out = w_in[0], w_out[0]
    embed = slot_embed.T
    comb = jnp.transpose(combine, (0, 2, 1)).reshape(64, 1024)
    comb_f = comb.astype(F32)

    out_part = jnp.einsum(
        "ijt,itd->ijd", comb.reshape(2, 32, 1024), grad_out, preferred_element_type=F32
    )
    out_part = out_part.astype(BF16).reshape(64, 1280)
    out_part = add(out_part, far(out_part))
    grad_slot_out = add(out_part, near(out_part))

    logits, part, lse = local_softmax(tokens, embed)
    part, lse = merge(part, lse, near(part), near(lse))
    slot_in, lse = merge(part, lse, far(part), far(lse))

    embeds = gather_blocks(embed, "y")
    combs = sources(scatter_terms(y_chunks(comb), "y"))
    v_terms = reduce_rows([(combs, embeds)])

    pre_act = jnp.dot(slot_in, w_in, preferred_element_type=F32)
    act, slope = gelu_parts(pre_act)
    act = act.astype(BF16)
    out_sum = jnp.dot(act, w_out, preferred_element_type=F32).astype(BF16)
    out_sum = add(out_sum, near(out_sum))
    out_other = far(out_sum)
    grad_act = jnp.einsum("sd,hd->sh", grad_slot_out, w_out, preferred_element_type=F32)
    grad_pre = (grad_act * slope).astype(BF16)
    in_sum = jnp.einsum("sh,dh->sd", grad_pre, w_in, preferred_element_type=F32).astype(BF16)
    in_sum = add(in_sum, far(in_sum))
    grad_slot_in = add(in_sum, near(in_sum))
    grad_w_out = jnp.einsum("sh,sd->hd", act, grad_slot_out, preferred_element_type=F32)
    grad_w_in = jnp.einsum("sd,sh->dh", slot_in, grad_pre, preferred_element_type=F32)

    grad_combine, row_dot = combine_grad(grad_out, out_sum, out_other, comb)
    row_dot = row_dot + swap_cores(row_dot)
    for axis in ("x", "y"):
        row_dot = sum(scatter_terms([row_dot] * 4, axis))

    dispatch = sources(scatter_terms(dispatch_chunks(logits, lse), "y"))
    rows = gather_blocks(grad_slot_in, "y")
    partial_logits, *chunks = dispatch_grad(
        tokens, grad_slot_in, slot_in, logits, lse, comb, grad_combine
    )
    chunks = sources(scatter_terms(chunks, "y"))
    u_terms = reduce_rows([(dispatch, rows), (chunks, embeds)])

    grad_logits = partial_logits - comb_f * jnp.repeat(row_dot, 32, axis=1).reshape(64, 1024)
    grad_logits = grad_logits.astype(BF16).reshape(2, 32, 1024)
    embed_part = jnp.einsum("ijt,itd->jd", grad_logits, tokens, preferred_element_type=F32)
    embed_part = embed_part.astype(BF16)
    embed_part = add(embed_part, near(embed_part))
    embed_sum = add(embed_part, far(embed_part))
    z = lax.axis_index("seq")
    grad_embed = lax.dynamic_slice_in_dim(embed_sum, z * 320, 320, axis=1).T

    place = (lax.axis_index("y") * 4 + lax.axis_index("x")) * 2 + lax.axis_index("core")
    own = lax.dynamic_slice_in_dim(row_dot, place * 32, 32, axis=2).reshape(2, 32, 1)
    grad_tokens = sum(term.astype(F32) for term in u_terms) - own * sum(
        term.astype(F32) for term in v_terms
    )
    return (
        grad_tokens.astype(BF16),
        grad_embed,
        grad_w_in.astype(BF16)[None],
        grad_w_out.astype(BF16)[None],
    )


def solution(mesh):
    fine = Mesh(mesh.devices.reshape(4, 4, 4, 2), ("seq", "y", "x", "core"))
    expert = ("y", "x", "core")
    return jax.shard_map(
        local,
        mesh=fine,
        in_specs=(
            P(None, "seq", None),
            P(None, expert),
            P(None, "seq", expert),
            P(expert, None, "seq"),
            P(expert, "seq", None),
            P(None, "seq", None),
        ),
        out_specs=(
            P(None, ("seq", *expert), None),
            P("seq", expert),
            P(expert, None, "seq"),
            P(expert, "seq", None),
        ),
        check_vma=False,
    )
```

time: 130 us -> 128 us (0.985)
  matrix products: 30.1 us -> 12 us
  Pallas kernels: 0 us -> 13.3 us
  other arithmetic: 15.7 us -> 4.7 us
  waiting for transfers between devices: 22.1 us -> 31.5 us
  starting transfers between devices: 47.1 us -> 54.1 us
  local copies, waits for them, and re-layouts: 13.1 us -> 11.2 us
    dot_general x6 -> x1, matrix products: 17.1 us -> 1.87 us  [local(): jnp.einsum('ijt,itd->ijd', comb.reshape(2, 32, 1024), grad_out, preferred...]
    ppermute x0 -> x12, starting transfers between devices: none -> 14.4 us  [the longest x6 9.9 us: far(): return lax.ppermute(value, 'seq', [(0, 3), (3, 0), (1, 2), (2, 1)])]
    pallas_call x0 -> x9, Pallas kernels: none -> 13.3 us  [the longest x1 5.06 us: local_softmax(): pl.pallas_call(softmax_kernel, grid=(2,), in_specs=[pl.BlockSpec((1, 1024...]
    ppermute x0 -> x12, waiting for transfers between devices: none -> 12.8 us  [the longest x6 11.4 us: far(): return lax.ppermute(value, 'seq', [(0, 3), (3, 0), (1, 2), (2, 1)])]
    unnamed x54 -> x51, local copies, waits for them, and re-layouts: 2.67 us -> 11.1 us
    ppermute x33 -> x27, starting transfers between devices: 47.1 us -> 39.6 us  [shift(): return lax.ppermute(value, axis, [(i, (i + by) % 4) for i in range(4)])]
    another operation x10 -> x0, other arithmetic: 6.11 us -> none  [the longest x3 2.72 us: local(): jnp.stack([slot_part[:, k], out_part[:, k]])]
    another operation x7 -> x0, local copies, waits for them, and re-layouts: 5.58 us -> none  [the longest x4 4.25 us: local(): jnp.stack([dispatch, grad_logits], axis=1).reshape(2, 2, 32, 4, 256)]
  transfers between devices with their start and end apart: 35 -> 42, of which waited for: 12 -> 13; matrix products, arithmetic and copies ran while one was open for 27% -> 12% of each run, Pallas kernels for 0% -> 6%
where the time goes in v2:
time: 128 us
  starting transfers between devices  54.1 us (42%)
  waiting for transfers between devices  31.5 us (25%)
  Pallas kernels  13.3 us (10%)
  matrix products  12 us (9%)
  local copies, waits for them, and re-layouts  11.2 us (9%)
  other arithmetic  4.7 us (4%)
    ppermute x27, starting transfers between devices, shift(): return lax.ppermute(value, axis, [(i, (i + by) % 4) for i in range(4)])  39.6 us
    ppermute x27, waiting for transfers between devices, shift(): return lax.ppermute(value, axis, [(i, (i + by) % 4) for i in range(4)])  18.7 us
    ppermute x6, waiting for transfers between devices, far(): return lax.ppermute(value, 'seq', [(0, 3), (3, 0), (1, 2), (2, 1)])  11.4 us
    unnamed x51, local copies, waits for them, and re-layouts  11.1 us
    ppermute x6, starting transfers between devices, far(): return lax.ppermute(value, 'seq', [(0, 3), (3, 0), (1, 2), (2, 1)])  9.9 us
    pallas_call x1, Pallas kernels, local_softmax(): pl.pallas_call(softmax_kernel, grid=(2,), in_specs=[pl.BlockSpec((1, 1024...  5.06 us
    ppermute x6, starting transfers between devices, near(): return lax.ppermute(value, 'seq', [(0, 1), (1, 0), (2, 3), (3, 2)])  4.53 us
    pallas_call x2, Pallas kernels, patch_rows(): pl.pallas_call(lambda *refs: rows_kernel(len(kinds), *refs), out_shape=[b...  3.21 us
  transfers between devices with their start and end apart: 42, of which 13 were waited for; matrix products, arithmetic and copies ran while one was open for 12% of the time, Pallas kernels for 6%

profile of v2, /device:TPU:0, one launch (start us, length us, event | category | flops | bytes accessed | tf_op | source)
XLA Modules:
  0.0 128.0 jit_solution(10400055124692089712)
XLA Ops:
  0.7 2.6 %copy-done.1 = bf16[2,1024,1280]{2,1,0:T(8,128)(2,1)S(1)} copy-done((bf16[2,1024,1280]{2,1,0:T(8,128)(2,1)S(1)}, bf16[2,1024,1280]{2,1,0:T(8,128)(2,1)}, u32[]{:S(2)}) %copy-start.1) | copy-done | bytes 5242904
  3.3 5.1 %local_softmax.1 = (f32[64,1024]{1,0:T(8,128)S(1)}, bf16[64,1280]{1,0:T(8,128)(2,1)S(1)}, f32[64,128]{1,0:T(8,128)S(1)}) custom-call(bf16[2,1024,1280]{2,1,0:T(8,128)(2,1)S(1)} %copy-done.1, bf16[32,1280]{1,0:T(8,128)(2,1)} %bitcast.embed.refs_12_.refs_4_), custom_call_target="tpu_custom_call" | custom-call | flops 700000000 | bytes 6000000 | tf_op jit(solution)/shard_map/local_softmax/pallas_call | solution.py:81
  12.3 2.9 %collective-permute-start.5 = (bf16[64,1280]{1,0:T(8,128)(2,1)S(1)}, bf16[64,1280]{1,0:T(8,128)(2,1)S(1)}, u32[]{:S(2)}, u32[]{:S(2)}) collective-permute-start(bf16[64,1280]{1,0:T(8,128)(2,1)S(1)} %bitcast.57), channel_id=1, source_target_pairs={{0,96},{96,0},{32,64},{64,32},{1,97},{97,1},{33,65},{65,33},{2,98}... | collective-permute-start | bytes 491528 | tf_op jit(solution)/shard_map/ppermute | solution.py:40
  16.8 4.3 %collective-permute-done.1 = f32[64,128]{1,0:T(8,128)S(1)} collective-permute-done((f32[64,128]{1,0:T(8,128)S(1)}, f32[64,128]{1,0:T(8,128)S(1)}, u32[]{:S(2)}, u32[]{:S(2)}) %collective-permute-start.1) | collective-permute-done | bytes 32800 | tf_op jit(solution)/shard_map/ppermute | solution.py:40
  23.2 4.9 %collective-permute-done.8 = bf16[64,1280]{1,0:T(8,128)(2,1)S(1)} collective-permute-done((bf16[64,1280]{1,0:T(8,128)(2,1)S(1)}, bf16[64,1280]{1,0:T(8,128)(2,1)S(1)}, u32[]{:S(2)}, u32[]{:S(2)}) %collective-permute-start.8) | collective-permute-done | bytes 163872 | tf_op jit(solution)/shard_map/ppermute | solution.py:40
  37.9 2.3 %collective-permute-done.9 = bf16[64,1280]{1,0:T(8,128)(2,1)S(1)} collective-permute-done((bf16[64,1280]{1,0:T(8,128)(2,1)S(1)}, bf16[64,1280]{1,0:T(8,128)(2,1)S(1)}, u32[]{:S(2)}, u32[]{:S(2)}) %collective-permute-start.9) | collective-permute-done | bytes 163872 | tf_op jit(solution)/shard_map/ppermute | solution.py:40
  41.5 3.0 %collective-permute-start.33 = (bf16[64,256]{1,0:T(8,128)(2,1)S(1)}, bf16[64,256]{1,0:T(8,128)(2,1)S(1)}, u32[]{:S(2)}, u32[]{:S(2)}) collective-permute-start(bf16[64,256]{1,0:T(8,128)(2,1)S(1)} %get-tuple-element.63), channel_id=1, source_target_pairs={{0,24},{8,0},{16,8},{24,16},{1,25},{9,1},{17,9},{25,17},{2,26},{10... | collective-permute-start | bytes 98312 | tf_op jit(solution)/shard_map/ppermute | solution.py:28
  47.2 2.3 %collective-permute-start.20 = (bf16[32,1280]{1,0:T(8,128)(2,1)}, bf16[32,1280]{1,0:T(8,128)(2,1)}, u32[]{:S(2)}, u32[]{:S(2)}) collective-permute-start(bf16[32,1280]{1,0:T(8,128)(2,1)} %bitcast.embed.refs_12_.refs_4_), channel_id=1, source_target_pairs={{0,16},{8,24},{16,0},{24,8},{1,17},{9,25},{17,1},{25,9},{2,18},{10... | collective-permute-start | bytes 245768 | tf_op jit(solution)/shard_map/ppermute | solution.py:28
  53.8 2.5 %copy-done.4 = bf16[2,1024,1280]{2,1,0:T(8,128)(2,1)S(1)} copy-done((bf16[2,1024,1280]{2,1,0:T(8,128)(2,1)S(1)}, bf16[2,1024,1280]{2,1,0:T(8,128)(2,1)}, u32[]{:S(2)}) %copy-start.4) | copy-done | bytes 5242904
  56.3 2.8 %combine_grad.1 = (f32[64,1024]{1,0:T(8,128)S(1)}, f32[2,1,1024]{2,1,0:T(1,128)S(1)}) custom-call(bf16[2,1024,1280]{2,1,0:T(8,128)(2,1)S(1)} %copy-done.4, bf16[64,1280]{1,0:T(8,128)(2,1)} %add_convert_fusion.sum_a, bf16[64,1280]{1,0:T(8,128)(2,1)} %collective-permute-done.15.sum_b, bf16[64,1024]{1,0:T(8,128)(2,1)S(1)} %bitcast.55), custom_call_target="tpu_custom_call" | custom-call | flops 350000000 | bytes 6000000 | tf_op jit(solution)/shard_map/combine_grad/pallas_call | solution.py:108
  59.0 2.6 %collective-permute-start.2 = (bf16[64,256]{1,0:T(8,128)(2,1)S(1)}, bf16[64,256]{1,0:T(8,128)(2,1)S(1)}, u32[]{:S(2)}, u32[]{:S(2)}) collective-permute-start(bf16[64,256]{1,0:T(8,128)(2,1)S(1)} %get-tuple-element.43), channel_id=1, source_target_pairs={{0,24},{8,0},{16,8},{24,16},{1,25},{9,1},{17,9},{25,17},{2,26},{10... | collective-permute-start | bytes 98312 | tf_op jit(solution)/shard_map/ppermute | solution.py:28
  64.6 2.8 %collective-permute-start.29 = (f32[2,1,1024]{2,1,0:T(1,128)S(1)}, f32[2,1,1024]{2,1,0:T(1,128)S(1)}, u32[]{:S(2)}, u32[]{:S(2)}) collective-permute-start(f32[2,1,1024]{2,1,0:T(1,128)S(1)} %add.118), channel_id=1, source_target_pairs={{0,6},{2,0},{4,2},{6,4},{1,7},{3,1},{5,3},{7,5},{8,14},{10,8},{12,... | collective-permute-start | bytes 24584 | tf_op jit(solution)/shard_map/ppermute | solution.py:28
  70.1 2.4 %collective-permute-done.28 = f32[2,1,1024]{2,1,0:T(1,128)S(1)} collective-permute-done((f32[2,1,1024]{2,1,0:T(1,128)S(1)}, f32[2,1,1024]{2,1,0:T(1,128)S(1)}, u32[]{:S(2)}, u32[]{:S(2)}) %collective-permute-start.28) | collective-permute-done | bytes 8224 | tf_op jit(solution)/shard_map/ppermute | solution.py:28
  76.8 2.5 %copy-done.2 = bf16[2,1024,1280]{2,1,0:T(8,128)(2,1)S(1)} copy-done((bf16[2,1024,1280]{2,1,0:T(8,128)(2,1)S(1)}, bf16[2,1024,1280]{2,1,0:T(8,128)(2,1)}, u32[]{:S(2)}) %copy-start.2) | copy-done | bytes 5242904
  82.0 2.6 %collective-permute-start.16 = (bf16[64,256]{1,0:T(8,128)(2,1)S(1)}, bf16[64,256]{1,0:T(8,128)(2,1)S(1)}, u32[]{:S(2)}, u32[]{:S(2)}) collective-permute-start(bf16[64,256]{1,0:T(8,128)(2,1)S(1)} %get-tuple-element.49), channel_id=1, source_target_pairs={{0,24},{8,0},{16,8},{24,16},{1,25},{9,1},{17,9},{25,17},{2,26},{10... | collective-permute-start | bytes 98312 | tf_op jit(solution)/shard_map/ppermute | solution.py:28
  88.4 2.5 %collective-permute-start.11 = (bf16[64,1280]{1,0:T(8,128)(2,1)S(1)}, bf16[64,1280]{1,0:T(8,128)(2,1)S(1)}, u32[]{:S(2)}, u32[]{:S(2)}) collective-permute-start(bf16[64,1280]{1,0:T(8,128)(2,1)S(1)} %add_convert_fusion.1.gslot.refs_4_), channel_id=1, source_target_pairs={{0,24},{8,0},{16,8},{24,16},{1,25},{9,1},{17,9},{25,17},{2,26},{10... | collective-permute-start | bytes 491528 | tf_op jit(solution)/shard_map/ppermute | solution.py:28
  92.0 5.8 %collective-permute-done.18.refs_11_ = bf16[64,256]{1,0:T(8,128)(2,1)S(1)} collective-permute-done((bf16[64,256]{1,0:T(8,128)(2,1)S(1)}, bf16[64,256]{1,0:T(8,128)(2,1)S(1)}, u32[]{:S(2)}, u32[]{:S(2)}) %collective-permute-start.18) | collective-permute-done | bytes 32800 | tf_op jit(solution)/shard_map/ppermute | solution.py:28
  101.1 2.8 %fusion.1 = bf16[1,1280,1280]{2,1,0:T(8,128)(2,1)} fusion(bf16[64,1280]{1,0:T(8,128)(2,1)S(1)} %copy-done.24, bf16[64,1280]{1,0:T(8,128)(2,1)S(1)} %copy-done.22, f32[64,1280]{1,0:T(8,128)S(1)} %copy-done.18), kind=kOutput, calls=%fused_computation.3 | convolution fusion | flops 212090880 | bytes 3932160 | tf_op jit(solution)/shard_map/sh,sd->hd/dot_general | solution.py:284
  105.7 2.8 %fusion = bf16[1,1280,1280]{2,1,0:T(8,128)(2,1)} fusion(bf16[64,1280]{1,0:T(8,128)(2,1)S(1)} %copy-done.7, bf16[64,1280]{1,0:T(8,128)(2,1)S(1)} %copy-done.20), kind=kOutput, calls=%fused_computation.2 | convolution fusion | flops 211353600 | bytes 3604480 | tf_op jit(solution)/shard_map/sd,sh->dh/dot_general | solution.py:285
  110.2 2.4 %collective-permute-start.39 = (bf16[2,32,1280]{2,1,0:T(8,128)(2,1)S(1)}, bf16[2,32,1280]{2,1,0:T(8,128)(2,1)S(1)}, u32[]{:S(2)}, u32[]{:S(2)}) collective-permute-start(bf16[2,32,1280]{2,1,0:T(8,128)(2,1)S(1)} %get-tuple-element.74), channel_id=1, source_target_pairs={{0,6},{2,0},{4,2},{6,4},{1,7},{3,1},{5,3},{7,5},{8,14},{10,8},{12,... | collective-permute-start | bytes 491528 | tf_op jit(solution)/shard_map/ppermute | solution.py:28
  115.0 2.5 %collective-permute-start.25 = (bf16[2,32,1280]{2,1,0:T(8,128)(2,1)S(1)}, bf16[2,32,1280]{2,1,0:T(8,128)(2,1)S(1)}, u32[]{:S(2)}, u32[]{:S(2)}) collective-permute-start(bf16[2,32,1280]{2,1,0:T(8,128)(2,1)S(1)} %get-tuple-element.60), channel_id=1, source_target_pairs={{0,6},{2,0},{4,2},{6,4},{1,7},{3,1},{5,3},{7,5},{8,14},{10,8},{12,... | collective-permute-start | bytes 491528 | tf_op jit(solution)/shard_map/ppermute | solution.py:28
  118.3 2.9 %collective-permute-done.39 = bf16[2,32,1280]{2,1,0:T(8,128)(2,1)S(1)} collective-permute-done((bf16[2,32,1280]{2,1,0:T(8,128)(2,1)S(1)}, bf16[2,32,1280]{2,1,0:T(8,128)(2,1)S(1)}, u32[]{:S(2)}, u32[]{:S(2)}) %collective-permute-start.39) | collective-permute-done | bytes 163872 | tf_op jit(solution)/shard_map/ppermute | solution.py:28
  121.2 2.4 %collective-permute-done.23 = bf16[2,32,1280]{2,1,0:T(8,128)(2,1)S(1)} collective-permute-done((bf16[2,32,1280]{2,1,0:T(8,128)(2,1)S(1)}, bf16[2,32,1280]{2,1,0:T(8,128)(2,1)S(1)}, u32[]{:S(2)}, u32[]{:S(2)}) %collective-permute-start.23) | collective-permute-done | bytes 163872 | tf_op jit(solution)/shard_map/ppermute | solution.py:28
  123.5 3.6 %collective-permute-done.25 = bf16[2,32,1280]{2,1,0:T(8,128)(2,1)S(1)} collective-permute-done((bf16[2,32,1280]{2,1,0:T(8,128)(2,1)S(1)}, bf16[2,32,1280]{2,1,0:T(8,128)(2,1)S(1)}, u32[]{:S(2)}, u32[]{:S(2)}) %collective-permute-start.25) | collective-permute-done | bytes 163872 | tf_op jit(solution)/shard_map/ppermute | solution.py:28
  (146 shorter events, 53.7 us)
Async XLA Ops:
  8.4 7.5 %collective-permute-start = (f32[64,128]{1,0:T(8,128)S(1)}, f32[64,128]{1,0:T(8,128)S(1)}, u32[]{:S(2)}, u32[]{:S(2)}) collective-permute-start(f32[64,128]{1,0:T(8,128)S(1)} %get-tuple-element.41), channel_id=1, source_target_pairs={{0,32},{32,0},{64,96},{96,64},{1,33},{33,1},{65,97},{97,65},{2,34}... | collective-permute-start | bytes 98312 | tf_op jit(solution)/shard_map/ppermute | solution.py:36
  12.3 10.7 %collective-permute-start.5 = (bf16[64,1280]{1,0:T(8,128)(2,1)S(1)}, bf16[64,1280]{1,0:T(8,128)(2,1)S(1)}, u32[]{:S(2)}, u32[]{:S(2)}) collective-permute-start(bf16[64,1280]{1,0:T(8,128)(2,1)S(1)} %bitcast.57), channel_id=1, source_target_pairs={{0,96},{96,0},{32,64},{64,32},{1,97},{97,1},{33,65},{65,33},{2,98}... | collective-permute-start | bytes 491528 | tf_op jit(solution)/shard_map/ppermute | solution.py:40
  36.4 16.6 %collective-permute-start.15 = (bf16[64,1280]{1,0:T(8,128)(2,1)}, bf16[64,1280]{1,0:T(8,128)(2,1)}, u32[]{:S(2)}, u32[]{:S(2)}) collective-permute-start(bf16[64,1280]{1,0:T(8,128)(2,1)} %add_convert_fusion.sum_a), channel_id=1, source_target_pairs={{0,96},{96,0},{32,64},{64,32},{1,97},{97,1},{33,65},{65,33},{2,98}... | collective-permute-start | bytes 491528 | tf_op jit(solution)/shard_map/ppermute | solution.py:40
  40.8 27.4 %collective-permute-start.10 = (bf16[64,1280]{1,0:T(8,128)(2,1)}, bf16[64,1280]{1,0:T(8,128)(2,1)}, u32[]{:S(2)}, u32[]{:S(2)}) collective-permute-start(bf16[64,1280]{1,0:T(8,128)(2,1)} %add_convert_fusion.2), channel_id=1, source_target_pairs={{0,32},{32,0},{64,96},{96,64},{1,33},{33,1},{65,97},{97,65},{2,34}... | collective-permute-start | bytes 491528 | tf_op jit(solution)/shard_map/ppermute | solution.py:36
  45.2 16.5 %collective-permute-start.21 = (bf16[32,1280]{1,0:T(8,128)(2,1)}, bf16[32,1280]{1,0:T(8,128)(2,1)S(1)}, u32[]{:S(2)}, u32[]{:S(2)}) collective-permute-start(bf16[32,1280]{1,0:T(8,128)(2,1)} %bitcast.embed.refs_12_.refs_4_), channel_id=1, source_target_pairs={{0,8},{8,16},{16,24},{24,0},{1,9},{9,17},{17,25},{25,1},{2,10},{10... | collective-permute-start | bytes 245768 | tf_op jit(solution)/shard_map/ppermute | solution.py:28
  47.2 15.7 %collective-permute-start.20 = (bf16[32,1280]{1,0:T(8,128)(2,1)}, bf16[32,1280]{1,0:T(8,128)(2,1)}, u32[]{:S(2)}, u32[]{:S(2)}) collective-permute-start(bf16[32,1280]{1,0:T(8,128)(2,1)} %bitcast.embed.refs_12_.refs_4_), channel_id=1, source_target_pairs={{0,16},{8,24},{16,0},{24,8},{1,17},{9,25},{17,1},{25,9},{2,18},{10... | collective-permute-start | bytes 245768 | tf_op jit(solution)/shard_map/ppermute | solution.py:28
  50.6 12.4 %collective-permute-start.19 = (bf16[32,1280]{1,0:T(8,128)(2,1)}, bf16[32,1280]{1,0:T(8,128)(2,1)}, u32[]{:S(2)}, u32[]{:S(2)}) collective-permute-start(bf16[32,1280]{1,0:T(8,128)(2,1)} %bitcast.embed.refs_12_.refs_4_), channel_id=1, source_target_pairs={{0,24},{8,0},{16,8},{24,16},{1,25},{9,1},{17,9},{25,17},{2,26},{10... | collective-permute-start | bytes 245768 | tf_op jit(solution)/shard_map/ppermute | solution.py:28
  59.0 22.2 %collective-permute-start.2 = (bf16[64,256]{1,0:T(8,128)(2,1)S(1)}, bf16[64,256]{1,0:T(8,128)(2,1)S(1)}, u32[]{:S(2)}, u32[]{:S(2)}) collective-permute-start(bf16[64,256]{1,0:T(8,128)(2,1)S(1)} %get-tuple-element.43), channel_id=1, source_target_pairs={{0,24},{8,0},{16,8},{24,16},{1,25},{9,1},{17,9},{25,17},{2,26},{10... | collective-permute-start | bytes 98312 | tf_op jit(solution)/shard_map/ppermute | solution.py:28
  61.6 24.3 %collective-permute-start.3 = (bf16[64,256]{1,0:T(8,128)(2,1)S(1)}, bf16[64,256]{1,0:T(8,128)(2,1)S(1)}, u32[]{:S(2)}, u32[]{:S(2)}) collective-permute-start(bf16[64,256]{1,0:T(8,128)(2,1)S(1)} %get-tuple-element.44), channel_id=1, source_target_pairs={{0,16},{8,24},{16,0},{24,8},{1,17},{9,25},{17,1},{25,9},{2,18},{10... | collective-permute-start | bytes 98312 | tf_op jit(solution)/shard_map/ppermute | solution.py:28
  73.1 8.9 %collective-permute-start.32 = (f32[2,1,1024]{2,1,0:T(1,128)S(1)}, f32[2,1,1024]{2,1,0:T(1,128)S(1)}, u32[]{:S(2)}, u32[]{:S(2)}) collective-permute-start(f32[2,1,1024]{2,1,0:T(1,128)S(1)} %add_add_fusion.1), channel_id=1, source_target_pairs={{0,24},{8,0},{16,8},{24,16},{1,25},{9,1},{17,9},{25,17},{2,26},{10... | collective-permute-start | bytes 24584 | tf_op jit(solution)/shard_map/ppermute | solution.py:28
  74.0 8.0 %collective-permute-start.31 = (f32[2,1,1024]{2,1,0:T(1,128)S(1)}, f32[2,1,1024]{2,1,0:T(1,128)S(1)}, u32[]{:S(2)}, u32[]{:S(2)}) collective-permute-start(f32[2,1,1024]{2,1,0:T(1,128)S(1)} %add_add_fusion.1), channel_id=1, source_target_pairs={{0,16},{8,24},{16,0},{24,8},{1,17},{9,25},{17,1},{25,9},{2,18},{10... | collective-permute-start | bytes 24584 | tf_op jit(solution)/shard_map/ppermute | solution.py:28
  75.5 9.1 %collective-permute-start.30 = (f32[2,1,1024]{2,1,0:T(1,128)S(1)}, f32[2,1,1024]{2,1,0:T(1,128)S(1)}, u32[]{:S(2)}, u32[]{:S(2)}) collective-permute-start(f32[2,1,1024]{2,1,0:T(1,128)S(1)} %add_add_fusion.1), channel_id=1, source_target_pairs={{0,8},{8,16},{16,24},{24,0},{1,9},{9,17},{17,25},{25,1},{2,10},{10... | collective-permute-start | bytes 24584 | tf_op jit(solution)/shard_map/ppermute | solution.py:28
  82.0 21.9 %collective-permute-start.36 = (bf16[4,2,32,1280]{3,2,1,0:T(8,128)(2,1)S(1)}, bf16[4,2,32,1280]{3,2,1,0:T(8,128)(2,1)S(1)}, u32[]{:S(2)}, u32[]{:S(2)}) collective-permute-start(bf16[4,2,32,1280]{3,2,1,0:T(8,128)(2,1)S(1)} %get-tuple-element.70), channel_id=1, source_target_pairs={{0,1},{1,0},{2,3},{3,2},{4,5},{5,4},{6,7},{7,6},{8,9},{9,8},{10,11... | collective-permute-start | bytes 1966088 | tf_op jit(solution)/shard_map/ppermute | solution.py:32
  86.0 13.4 %collective-permute-start.13 = (bf16[64,1280]{1,0:T(8,128)(2,1)S(1)}, bf16[64,1280]{1,0:T(8,128)(2,1)S(1)}, u32[]{:S(2)}, u32[]{:S(2)}) collective-permute-start(bf16[64,1280]{1,0:T(8,128)(2,1)S(1)} %add_convert_fusion.1.gslot.refs_4_), channel_id=1, source_target_pairs={{0,8},{8,16},{16,24},{24,0},{1,9},{9,17},{17,25},{25,1},{2,10},{10... | collective-permute-start | bytes 491528 | tf_op jit(solution)/shard_map/ppermute | solution.py:28
  86.4 12.9 %collective-permute-start.12 = (bf16[64,1280]{1,0:T(8,128)(2,1)S(1)}, bf16[64,1280]{1,0:T(8,128)(2,1)S(1)}, u32[]{:S(2)}, u32[]{:S(2)}) collective-permute-start(bf16[64,1280]{1,0:T(8,128)(2,1)S(1)} %add_convert_fusion.1.gslot.refs_4_), channel_id=1, source_target_pairs={{0,16},{8,24},{16,0},{24,8},{1,17},{9,25},{17,1},{25,9},{2,18},{10... | collective-permute-start | bytes 491528 | tf_op jit(solution)/shard_map/ppermute | solution.py:28
  88.4 10.9 %collective-permute-start.11 = (bf16[64,1280]{1,0:T(8,128)(2,1)S(1)}, bf16[64,1280]{1,0:T(8,128)(2,1)S(1)}, u32[]{:S(2)}, u32[]{:S(2)}) collective-permute-start(bf16[64,1280]{1,0:T(8,128)(2,1)S(1)} %add_convert_fusion.1.gslot.refs_4_), channel_id=1, source_target_pairs={{0,24},{8,0},{16,8},{24,16},{1,25},{9,1},{17,9},{25,17},{2,26},{10... | collective-permute-start | bytes 491528 | tf_op jit(solution)/shard_map/ppermute | solution.py:28
  101.0 11.6 %collective-permute-start.22 = (bf16[4,2,32,1280]{3,2,1,0:T(8,128)(2,1)S(1)}, bf16[4,2,32,1280]{3,2,1,0:T(8,128)(2,1)S(1)}, u32[]{:S(2)}, u32[]{:S(2)}) collective-permute-start(bf16[4,2,32,1280]{3,2,1,0:T(8,128)(2,1)S(1)} %get-tuple-element.56), channel_id=1, source_target_pairs={{0,1},{1,0},{2,3},{3,2},{4,5},{5,4},{6,7},{7,6},{8,9},{9,8},{10,11... | collective-permute-start | bytes 1966088 | tf_op jit(solution)/shard_map/ppermute | solution.py:32
  104.1 10.9 %collective-permute-start.37 = (bf16[2,32,1280]{2,1,0:T(8,128)(2,1)S(1)}, bf16[2,32,1280]{2,1,0:T(8,128)(2,1)S(1)}, u32[]{:S(2)}, u32[]{:S(2)}) collective-permute-start(bf16[2,32,1280]{2,1,0:T(8,128)(2,1)S(1)} %get-tuple-element.72), channel_id=1, source_target_pairs={{0,2},{2,4},{4,6},{6,0},{1,3},{3,5},{5,7},{7,1},{8,10},{10,12},{12... | collective-permute-start | bytes 491528 | tf_op jit(solution)/shard_map/ppermute | solution.py:28
  104.2 8.7 %collective-permute-start.41 = (bf16[32,1280]{1,0:T(8,128)(2,1)S(1)}, bf16[32,1280]{1,0:T(8,128)(2,1)S(1)}, u32[]{:S(2)}, u32[]{:S(2)}) collective-permute-start(bf16[32,1280]{1,0:T(8,128)(2,1)S(1)} %add_convert_fusion.7), channel_id=1, source_target_pairs={{0,96},{96,0},{32,64},{64,32},{1,97},{97,1},{33,65},{65,33},{2,98}... | collective-permute-start | bytes 245768 | tf_op jit(solution)/shard_map/ppermute | solution.py:40
  108.5 9.8 %collective-permute-start.38 = (bf16[2,32,1280]{2,1,0:T(8,128)(2,1)S(1)}, bf16[2,32,1280]{2,1,0:T(8,128)(2,1)S(1)}, u32[]{:S(2)}, u32[]{:S(2)}) collective-permute-start(bf16[2,32,1280]{2,1,0:T(8,128)(2,1)S(1)} %get-tuple-element.73), channel_id=1, source_target_pairs={{0,4},{2,6},{4,0},{6,2},{1,5},{3,7},{5,1},{7,3},{8,12},{10,14},{12... | collective-permute-start | bytes 491528 | tf_op jit(solution)/shard_map/ppermute | solution.py:28
  110.2 10.9 %collective-permute-start.39 = (bf16[2,32,1280]{2,1,0:T(8,128)(2,1)S(1)}, bf16[2,32,1280]{2,1,0:T(8,128)(2,1)S(1)}, u32[]{:S(2)}, u32[]{:S(2)}) collective-permute-start(bf16[2,32,1280]{2,1,0:T(8,128)(2,1)S(1)} %get-tuple-element.74), channel_id=1, source_target_pairs={{0,6},{2,0},{4,2},{6,4},{1,7},{3,1},{5,3},{7,5},{8,14},{10,8},{12,... | collective-permute-start | bytes 491528 | tf_op jit(solution)/shard_map/ppermute | solution.py:28
  112.8 10.8 %collective-permute-start.23 = (bf16[2,32,1280]{2,1,0:T(8,128)(2,1)S(1)}, bf16[2,32,1280]{2,1,0:T(8,128)(2,1)S(1)}, u32[]{:S(2)}, u32[]{:S(2)}) collective-permute-start(bf16[2,32,1280]{2,1,0:T(8,128)(2,1)S(1)} %get-tuple-element.58), channel_id=1, source_target_pairs={{0,2},{2,4},{4,6},{6,0},{1,3},{3,5},{5,7},{7,1},{8,10},{10,12},{12... | collective-permute-start | bytes 491528 | tf_op jit(solution)/shard_map/ppermute | solution.py:28
  112.9 10.7 %collective-permute-start.24 = (bf16[2,32,1280]{2,1,0:T(8,128)(2,1)S(1)}, bf16[2,32,1280]{2,1,0:T(8,128)(2,1)S(1)}, u32[]{:S(2)}, u32[]{:S(2)}) collective-permute-start(bf16[2,32,1280]{2,1,0:T(8,128)(2,1)S(1)} %get-tuple-element.59), channel_id=1, source_target_pairs={{0,4},{2,6},{4,0},{6,2},{1,5},{3,7},{5,1},{7,3},{8,12},{10,14},{12... | collective-permute-start | bytes 491528 | tf_op jit(solution)/shard_map/ppermute | solution.py:28
  115.0 12.2 %collective-permute-start.25 = (bf16[2,32,1280]{2,1,0:T(8,128)(2,1)S(1)}, bf16[2,32,1280]{2,1,0:T(8,128)(2,1)S(1)}, u32[]{:S(2)}, u32[]{:S(2)}) collective-permute-start(bf16[2,32,1280]{2,1,0:T(8,128)(2,1)S(1)} %get-tuple-element.60), channel_id=1, source_target_pairs={{0,6},{2,0},{4,2},{6,4},{1,7},{3,1},{5,3},{7,5},{8,14},{10,8},{12,... | collective-permute-start | bytes 491528 | tf_op jit(solution)/shard_map/ppermute | solution.py:28
  (43 other events, 311.3 us)

commit v3 on v2

v3 whole, which is shorter than its diff:
```python
import math

import jax
import jax.numpy as jnp
from jax import lax
from jax.experimental import pallas as pl
from jax.experimental.pallas import tpu as pltpu
from jax.sharding import Mesh, PartitionSpec as P

F32 = jnp.float32
BF16 = jnp.bfloat16
NT = (((1,), (1,)), ((), ()))
TN = (((0,), (0,)), ((), ()))
PARAMS = pltpu.CompilerParams(vmem_limit_bytes=24 * 1024 * 1024)


def shape(dims, dtype):
    return jax.ShapeDtypeStruct(dims, dtype)


def gelu_parts(values):
    cdf = 0.5 * (1.0 + jax.scipy.special.erf(values / math.sqrt(2.0)))
    slope = cdf + values * jnp.exp(-0.5 * values * values) / math.sqrt(2.0 * math.pi)
    return values * cdf, slope


def shift(value, axis, by):
    return lax.ppermute(value, axis, [(i, (i + by) % 4) for i in range(4)])


def swap_cores(value):
    return lax.ppermute(value, "core", [(0, 1), (1, 0)])


def near(value):
    return lax.ppermute(value, "seq", [(0, 1), (1, 0), (2, 3), (3, 2)])


def far(value):
    return lax.ppermute(value, "seq", [(0, 3), (3, 0), (1, 2), (2, 1)])


def add(one, two):
    return (one.astype(F32) + two.astype(F32)).astype(BF16)


def scatter_terms(blocks, axis):
    return [blocks[0]] + [shift(blocks[k], axis, k) for k in (1, 2, 3)]


def gather_blocks(block, axis):
    return [block] + [shift(block, axis, -k) for k in (1, 2, 3)]


def chunk(axis, k, size):
    return pl.multiple_of(((lax.axis_index(axis) + k) & 3) * size, size)


def lse_lanes(lse):
    high = lse.astype(BF16).astype(F32)
    middle = (lse - high).astype(BF16).astype(F32)
    low = lse - high - middle
    lane = lax.broadcasted_iota(jnp.int32, (lse.shape[0], 128), 1)
    lanes = jnp.where(lane == 0, high, jnp.where(lane == 1, middle, low))
    return jnp.where(lane < 3, lanes, 0.0).astype(BF16)


def lse_column(lanes):
    lanes = lanes.astype(F32)
    return lanes[:, 0:1] + lanes[:, 1:2] + lanes[:, 2:3]


def softmax_kernel(tok, embed, logits, part, peak, total, sums):
    step = pl.program_id(1)
    patches = tok[0]
    scores = lax.dot_general(patches, embed[...], NT, preferred_element_type=F32).T
    logits[...] = scores

    @pl.when(step == 0)
    def _():
        peak[...] = jnp.full_like(peak, -jnp.inf)
        total[...] = jnp.zeros_like(total)
        sums[...] = jnp.zeros_like(sums)

    top = jnp.maximum(peak[:, :1], jnp.max(scores, axis=1, keepdims=True))
    scale = jnp.exp(peak[:, :1] - top)
    weight = jnp.exp(scores - top)
    new_total = total[:, :1] * scale + jnp.sum(weight, axis=1, keepdims=True)
    new_sums = sums[...] * scale + jnp.dot(
        weight.astype(BF16), patches, preferred_element_type=F32
    )
    peak[...] = jnp.broadcast_to(top, peak.shape)
    total[...] = jnp.broadcast_to(new_total, total.shape)
    sums[...] = new_sums

    @pl.when(step == pl.num_programs(1) - 1)
    def _():
        part[:, :1280] = (new_sums / new_total).astype(BF16)
        part[:, 1280:] = lse_lanes(top + jnp.log(new_total))


def in_hbm(value):
    return pltpu.with_memory_space_constraint(value, pltpu.HBM)


def local_softmax(tokens, embed):
    return pl.pallas_call(
        softmax_kernel,
        grid=(2, 2),
        in_specs=[
            pl.BlockSpec((1, 512, 1280), lambda i, t: (i, t, 0)),
            pl.BlockSpec((32, 1280), lambda i, t: (0, 0)),
        ],
        out_specs=[
            pl.BlockSpec((32, 512), lambda i, t: (i, t)),
            pl.BlockSpec((32, 1408), lambda i, t: (i, 0)),
        ],
        out_shape=[shape((64, 1024), F32), shape((64, 1408), BF16)],
        scratch_shapes=[
            pltpu.VMEM((32, 128), F32),
            pltpu.VMEM((32, 128), F32),
            pltpu.VMEM((32, 1280), F32),
        ],
        cost_estimate=pl.CostEstimate(flops=700_000_000, bytes_accessed=6_000_000, transcendentals=65536),
        compiler_params=PARAMS,
        name="local_softmax",
    )(in_hbm(tokens), embed)


def merge_kernel(one, two, sums, lse):
    lse_a, lse_b = lse_column(one[:, 1280:]), lse_column(two[:, 1280:])
    top = jnp.maximum(lse_a, lse_b)
    weight_a, weight_b = jnp.exp(lse_a - top), jnp.exp(lse_b - top)
    total = weight_a + weight_b
    part = (weight_a / total) * one[:, :1280].astype(F32)
    part = part + (weight_b / total) * two[:, :1280].astype(F32)
    lse_all = top + jnp.log(total)
    sums[:, :1280] = part.astype(BF16)
    if lse is None:
        sums[:, 1280:] = lse_lanes(lse_all)
    else:
        lse[...] = jnp.broadcast_to(lse_all, lse.shape)


def merge_pair(one, two):
    return pl.pallas_call(
        lambda a, b, out: merge_kernel(a, b, out, None),
        out_shape=shape((64, 1408), BF16),
        cost_estimate=pl.CostEstimate(flops=300_000, bytes_accessed=540_000, transcendentals=256),
        compiler_params=PARAMS,
        name="merge_pair",
    )(one, two)


def merge_last(one, two):
    return pl.pallas_call(
        merge_kernel,
        out_shape=[shape((64, 1280), BF16), shape((64, 128), F32)],
        cost_estimate=pl.CostEstimate(flops=300_000, bytes_accessed=540_000, transcendentals=256),
        compiler_params=PARAMS,
        name="merge_last",
    )(one, two)


def combine_grad_kernel(gout, sum_a, sum_b, comb, grad, row):
    slot_out = add(sum_a[...], sum_b[...])
    value = lax.dot_general(gout[0], slot_out, NT, preferred_element_type=F32).T
    grad[...] = value
    row[0] = jnp.sum(comb[...].astype(F32) * value, axis=0, keepdims=True)


def combine_grad(grad_out, sum_a, sum_b, comb):
    return pl.pallas_call(
        combine_grad_kernel,
        grid=(2, 2),
        in_specs=[
            pl.BlockSpec((1, 512, 1280), lambda i, t: (i, t, 0)),
            pl.BlockSpec((32, 1280), lambda i, t: (i, 0)),
            pl.BlockSpec((32, 1280), lambda i, t: (i, 0)),
            pl.BlockSpec((32, 512), lambda i, t: (i, t)),
        ],
        out_specs=[
            pl.BlockSpec((32, 512), lambda i, t: (i, t)),
            pl.BlockSpec((1, 1, 512), lambda i, t: (i, 0, t)),
        ],
        out_shape=[shape((64, 1024), F32), shape((2, 1, 1024), F32)],
        cost_estimate=pl.CostEstimate(flops=350_000_000, bytes_accessed=6_000_000, transcendentals=0),
        compiler_params=PARAMS,
        name="combine_grad",
    )(in_hbm(grad_out), sum_a, sum_b, comb)


def dispatch_grad_kernel(tok, gslot, slot_in, logits, lse, comb, gcomb, full, c0, c1, c2, c3, all_grad, all_weight):
    step = pl.program_id(1)
    rows = gslot[...]
    col_dot = jnp.sum(slot_in[...].astype(F32) * rows.astype(F32), axis=1, keepdims=True)
    grad = lax.dot_general(tok[0], rows, NT, preferred_element_type=F32).T
    weight = jnp.exp(logits[...] - lse[:, :1])
    value = weight * (grad - col_dot) + comb[...].astype(F32) * gcomb[...]
    full[...] = value
    span = pl.ds(pl.multiple_of(step * 512, 512), 512)
    all_grad[:, span] = value
    all_weight[:, span] = weight

    @pl.when(step == pl.num_programs(1) - 1)
    def _():
        for k, out in enumerate((c0, c1, c2, c3)):
            piece = pl.ds(chunk("y", k, 256), 256)
            out[:, :256] = all_grad[:, piece].astype(BF16)
            out[:, 256:] = all_weight[:, piece].astype(BF16)


def dispatch_grad(tokens, gslot, slot_in, logits, lse, comb, gcomb):
    rows = pl.BlockSpec((32, 1280), lambda i, t: (i, 0))
    wide = pl.BlockSpec((32, 512), lambda i, t: (i, t))
    part = pl.BlockSpec((32, 512), lambda i, t: (i, 0))
    return pl.pallas_call(
        dispatch_grad_kernel,
        grid=(2, 2),
        in_specs=[
            pl.BlockSpec((1, 512, 1280), lambda i, t: (i, t, 0)),
            rows,
            rows,
            wide,
            pl.BlockSpec((32, 128), lambda i, t: (i, 0)),
            wide,
            wide,
        ],
        out_specs=[wide] + [part] * 4,
        out_shape=[shape((64, 1024), F32)] + [shape((64, 512), BF16)] * 4,
        scratch_shapes=[pltpu.VMEM((32, 1024), F32), pltpu.VMEM((32, 1024), F32)],
        cost_estimate=pl.CostEstimate(flops=350_000_000, bytes_accessed=7_000_000, transcendentals=65536),
        compiler_params=PARAMS,
        name="dispatch_grad",
    )(in_hbm(tokens), gslot, slot_in, logits, lse, comb, gcomb)


def inputs_kernel(comb, embed, o0, o1, o2, o3):
    for k, out in enumerate((o0, o1, o2, o3)):
        out[:64, :] = comb[:, pl.ds(chunk("y", k, 256), 256)]
        for n in range(5):
            out[64 + 32 * n : 96 + 32 * n, :] = embed[:, 256 * n : 256 * n + 256]


def input_blocks(comb, embed):
    return pl.pallas_call(
        inputs_kernel,
        out_shape=[shape((224, 256), BF16)] * 4,
        cost_estimate=pl.CostEstimate(flops=0, bytes_accessed=700_000, transcendentals=0),
        compiler_params=PARAMS,
        name="input_blocks",
    )(comb, embed)


def rows_kernel(*refs):
    slots, parts, inputs = (refs[4 * n : 4 * n + 4] for n in range(3))
    row_dot, m0, m1, m2, m3, other, scratch = refs[12:]
    core = lax.axis_index("core")
    embeds = [
        jnp.concatenate([one[64 + 32 * n : 96 + 32 * n, :] for n in range(5)], axis=1)
        for one in inputs
    ]
    for i in range(2):
        half = slice(32 * i, 32 * i + 32)
        dots = row_dot[i, :, pl.ds(chunk("y", 0, 256), 256)]
        weights = [one[half, 256:] for one in parts] + [
            (p[half, :256].astype(F32) - c[half, :].astype(F32) * dots).astype(BF16)
            for p, c in zip(parts, inputs)
        ]
        rows = [one[half, :] for one in slots] + embeds
        scratch[i] = lax.dot_general(
            jnp.concatenate(weights), jnp.concatenate(rows), TN, preferred_element_type=F32
        )
        for k, mine in enumerate((m0, m1, m2, m3)):
            base = ((lax.axis_index("x") + k) & 3) * 64
            here = pl.multiple_of(base + core * 32, 32)
            there = pl.multiple_of(base + (1 - core) * 32, 32)
            mine[i] = scratch[i, pl.ds(here, 32), :].astype(BF16)
            other[k, i] = scratch[i, pl.ds(there, 32), :].astype(BF16)


def patch_rows(slots, parts, inputs, row_dot):
    block = shape((2, 32, 1280), BF16)
    *mine, other = pl.pallas_call(
        rows_kernel,
        out_shape=[block] * 4 + [shape((4, 2, 32, 1280), BF16)],
        scratch_shapes=[pltpu.VMEM((2, 256, 1280), F32)],
        cost_estimate=pl.CostEstimate(flops=335_000_000, bytes_accessed=3_000_000, transcendentals=0),
        compiler_params=PARAMS,
        name="patch_rows",
    )(*slots, *parts, *inputs, row_dot)
    return mine, other


def add_kernel(m0, m1, m2, m3, other, o0, o1, o2, o3):
    for k, (mine, out) in enumerate(((m0, o0), (m1, o1), (m2, o2), (m3, o3))):
        out[...] = add(mine[...], other[k])


def add_cores(mine, other):
    return pl.pallas_call(
        add_kernel,
        out_shape=[shape((2, 32, 1280), BF16)] * 4,
        cost_estimate=pl.CostEstimate(flops=327_680, bytes_accessed=2_000_000, transcendentals=0),
        compiler_params=PARAMS,
        name="add_cores",
    )(*mine, other)


def after(value, *others):
    return lax.optimization_barrier((value, *others))[0]


def sources(terms):
    return [terms[0], terms[3], terms[2], terms[1]]


def local(tokens, slot_embed, combine, w_in, w_out, grad_out):
    w_in, w_out = w_in[0], w_out[0]
    embed = slot_embed.T
    comb = jnp.transpose(combine, (0, 2, 1)).reshape(64, 1024)
    comb_f = comb.astype(F32)
    inputs = sources(scatter_terms(input_blocks(comb, embed), "y"))

    logits, part = local_softmax(tokens, embed)
    part = merge_pair(part, near(part))

    out_part = jnp.einsum(
        "ijt,itd->ijd", comb.reshape(2, 32, 1024), grad_out, preferred_element_type=F32
    )
    out_part = out_part.astype(BF16).reshape(64, 1280)
    out_part = add(out_part, far(out_part))
    grad_slot_out = add(out_part, near(out_part))
    slot_in, lse = merge_last(part, far(part))
    slot_in = after(slot_in, *inputs)

    pre_act = jnp.dot(slot_in, w_in, preferred_element_type=F32)
    act, slope = gelu_parts(pre_act)
    act = act.astype(BF16)
    out_sum = jnp.dot(act, w_out, preferred_element_type=F32).astype(BF16)
    out_sum = add(out_sum, near(out_sum))
    out_other = far(out_sum)
    grad_act = jnp.einsum("sd,hd->sh", grad_slot_out, w_out, preferred_element_type=F32)
    grad_pre = (grad_act * slope).astype(BF16)
    in_sum = jnp.einsum("sh,dh->sd", grad_pre, w_in, preferred_element_type=F32).astype(BF16)
    in_sum = add(in_sum, far(in_sum))
    grad_slot_in = add(in_sum, near(in_sum))

    grad_combine, row_dot = combine_grad(grad_out, out_sum, out_other, comb)
    row_dot = row_dot + swap_cores(row_dot)
    for axis in ("x", "y"):
        row_dot = sum(scatter_terms([row_dot] * 4, axis))

    rows = gather_blocks(grad_slot_in, "y")
    partial_logits, *chunks = dispatch_grad(
        tokens, grad_slot_in, slot_in, logits, lse, comb, grad_combine
    )
    chunks = sources(scatter_terms(chunks, "y"))

    mine, other = patch_rows(rows, chunks, inputs, row_dot)
    sums = add_cores(mine, swap_cores(other))
    terms = scatter_terms(sums, "x")
    grad_tokens = sum(term.astype(F32) for term in terms).astype(BF16)

    grad_logits = partial_logits - comb_f * jnp.repeat(row_dot, 32, axis=1).reshape(64, 1024)
    grad_logits = grad_logits.astype(BF16).reshape(2, 32, 1024)
    embed_part = jnp.einsum("ijt,itd->jd", grad_logits, tokens, preferred_element_type=F32)
    embed_part = embed_part.astype(BF16)
    embed_part = add(embed_part, near(embed_part))
    embed_sum = add(embed_part, far(embed_part))
    z = lax.axis_index("seq")
    grad_embed = lax.dynamic_slice_in_dim(embed_sum, z * 320, 320, axis=1).T

    act_late, slot_late = lax.optimization_barrier((act, slot_in, sums[0]))[:2]
    grad_w_out = jnp.einsum("sh,sd->hd", act_late, grad_slot_out, preferred_element_type=F32)
    grad_w_in = jnp.einsum("sd,sh->dh", slot_late, grad_pre, preferred_element_type=F32)
    return (
        grad_tokens,
        grad_embed,
        grad_w_in.astype(BF16)[None],
        grad_w_out.astype(BF16)[None],
    )


def solution(mesh):
    fine = Mesh(mesh.devices.reshape(4, 4, 4, 2), ("seq", "y", "x", "core"))
    expert = ("y", "x", "core")
    return jax.shard_map(
        local,
        mesh=fine,
        in_specs=(
            P(None, "seq", None),
            P(None, expert),
            P(None, "seq", expert),
            P(expert, None, "seq"),
            P(expert, "seq", None),
            P(None, "seq", None),
        ),
        out_specs=(
            P(None, ("seq", *expert), None),
            P("seq", expert),
            P(expert, None, "seq"),
            P(expert, "seq", None),
        ),
        check_vma=False,
    )
```

time: 128 us -> 108 us (0.84)
  starting transfers between devices: 54.1 us -> 35.1 us
  Pallas kernels: 13.3 us -> 19 us
  local copies, waits for them, and re-layouts: 11.2 us -> 7.45 us
  waiting for transfers between devices: 31.5 us -> 27.9 us
  matrix products: 12 us -> 14.5 us
  other arithmetic: 4.7 us -> 2.49 us
    ppermute x27 -> x18, starting transfers between devices: 39.6 us -> 26.1 us  [shift(): return lax.ppermute(value, axis, [(i, (i + by) % 4) for i in range(4)])]
    ppermute x27 -> x18, waiting for transfers between devices: 18.7 us -> 8.03 us  [shift(): return lax.ppermute(value, axis, [(i, (i + by) % 4) for i in range(4)])]
    ppermute x6 -> x5, waiting for transfers between devices: 11.4 us -> 16.8 us  [far(): return lax.ppermute(value, 'seq', [(0, 3), (3, 0), (1, 2), (2, 1)])]
    pallas_call x7, Pallas kernels: 13 us -> 17.7 us  [the longest x1 6.75 us: local_softmax(): pl.pallas_call(softmax_kernel, grid=(2, 2), in_specs=[pl.BlockSpec((1, 51...]
    ppermute x6 -> x5, starting transfers between devices: 9.9 us -> 5.96 us  [far(): return lax.ppermute(value, 'seq', [(0, 3), (3, 0), (1, 2), (2, 1)])]
    unnamed x51 -> x43, local copies, waits for them, and re-layouts: 11.1 us -> 7.45 us
    convert_element_type x5, other arithmetic: 2.53 us -> 0.2 us  [add(): return (one.astype(F32) + two.astype(F32)).astype(BF16)]
    ppermute x6 -> x5, starting transfers between devices: 4.53 us -> 2.92 us  [near(): return lax.ppermute(value, 'seq', [(0, 1), (1, 0), (2, 3), (3, 2)])]
  transfers between devices with their start and end apart: 42 -> 30, of which waited for: 13 -> 10; matrix products, arithmetic and copies ran while one was open for 12% -> 15% of each run, Pallas kernels for 6% -> 10%
where the time goes in v3:
time: 108 us; the launch traced here: 107 us
  starting transfers between devices  35.1 us (32%)
  waiting for transfers between devices  27.9 us (26%)
  Pallas kernels  19 us (18%)
  matrix products  14.5 us (13%)
  local copies, waits for them, and re-layouts  7.45 us (7%)
  other arithmetic  2.49 us (2%)
    ppermute x18, starting transfers between devices, shift(): return lax.ppermute(value, axis, [(i, (i + by) % 4) for i in range(4)])  26.1 us
    ppermute x5, waiting for transfers between devices, far(): return lax.ppermute(value, 'seq', [(0, 3), (3, 0), (1, 2), (2, 1)])  16.8 us
    ppermute x18, waiting for transfers between devices, shift(): return lax.ppermute(value, axis, [(i, (i + by) % 4) for i in range(4)])  8.03 us
    unnamed x43, local copies, waits for them, and re-layouts  7.45 us
    pallas_call x1, Pallas kernels, local_softmax(): pl.pallas_call(softmax_kernel, grid=(2, 2), in_specs=[pl.BlockSpec((1, 51...  6.75 us
    ppermute x5, starting transfers between devices, far(): return lax.ppermute(value, 'seq', [(0, 3), (3, 0), (1, 2), (2, 1)])  5.96 us
    pallas_call x1, Pallas kernels, dispatch_grad(): pl.pallas_call(dispatch_grad_kernel, grid=(2, 2), in_specs=[pl.BlockSpec(...  4.53 us
    pallas_call x1, Pallas kernels, combine_grad(): pl.pallas_call(combine_grad_kernel, grid=(2, 2), in_specs=[pl.BlockSpec((...  4.4 us
  transfers between devices with their start and end apart: 30, of which 10 were waited for; matrix products, arithmetic and copies ran while one was open for 15% of the time, Pallas kernels for 10%

profile of v3, /device:TPU:0, one launch (start us, length us, event | category | flops | bytes accessed | tf_op | source)
XLA Modules:
  0.0 107.4 jit_solution(12414773760539581469)
XLA Ops:
  1.7 6.7 %local_softmax.1 = (f32[64,1024]{1,0:T(8,128)S(1)}, bf16[64,1408]{1,0:T(8,128)(2,1)S(1)}) custom-call(bf16[2,1024,1280]{2,1,0:T(8,128)(2,1)} %tok.3, bf16[32,1280]{1,0:T(8,128)(2,1)S(1)} %bitcast.60), custom_call_target="tpu_custom_call" | custom-call | flops 700000000 | bytes 6000000 | tf_op jit(solution)/shard_map/local_softmax/pallas_call | solution.py:107
  8.5 2.1 %collective-permute-start.2 = (bf16[64,1408]{1,0:T(8,128)(2,1)S(1)}, bf16[64,1408]{1,0:T(8,128)(2,1)S(1)}, u32[]{:S(2)}, u32[]{:S(2)}) collective-permute-start(bf16[64,1408]{1,0:T(8,128)(2,1)S(1)} %get-tuple-element.31.a), channel_id=1, source_target_pairs={{0,32},{32,0},{64,96},{96,64},{1,33},{33,1},{65,97},{97,65},{2,34}... | collective-permute-start | bytes 540680 | tf_op jit(solution)/shard_map/ppermute | solution.py:36
  10.6 3.5 %convolution_convert_fusion.2 = bf16[2,32,1280]{2,1,0:T(8,128)(2,1)S(1)} fusion(bf16[2,1024,32]{1,2,0:T(8,128)(2,1)S(1)} %copy-done.1, bf16[2,1024,1280]{2,1,0:T(8,128)(2,1)} %gout.1), kind=kOutput, calls=%fused_computation.16 | convolution fusion | flops 167854080 | bytes 5537792 | tf_op jit(solution)/shard_map/ijt,itd->ijd/dot_general | solution.py:328
  14.0 2.6 %collective-permute-start = (bf16[64,1280]{1,0:T(8,128)(2,1)S(1)}, bf16[64,1280]{1,0:T(8,128)(2,1)S(1)}, u32[]{:S(2)}, u32[]{:S(2)}) collective-permute-start(bf16[64,1280]{1,0:T(8,128)(2,1)S(1)} %bitcast.64), channel_id=1, source_target_pairs={{0,96},{96,0},{32,64},{64,32},{1,97},{97,1},{33,65},{65,33},{2,98}... | collective-permute-start | bytes 491528 | tf_op jit(solution)/shard_map/ppermute | solution.py:40
  16.7 3.1 %collective-permute-start.4 = (bf16[224,256]{1,0:T(8,128)(2,1)S(1)}, bf16[224,256]{1,0:T(8,128)(2,1)S(1)}, u32[]{:S(2)}, u32[]{:S(2)}) collective-permute-start(bf16[224,256]{1,0:T(8,128)(2,1)S(1)} %get-tuple-element.34), channel_id=1, source_target_pairs={{0,24},{8,0},{16,8},{24,16},{1,25},{9,1},{17,9},{25,17},{2,26},{10... | collective-permute-start | bytes 344072 | tf_op jit(solution)/shard_map/ppermute | solution.py:28
  22.9 5.5 %collective-permute-done.3.two = bf16[64,1408]{1,0:T(8,128)(2,1)S(1)} collective-permute-done((bf16[64,1408]{1,0:T(8,128)(2,1)S(1)}, bf16[64,1408]{1,0:T(8,128)(2,1)S(1)}, u32[]{:S(2)}, u32[]{:S(2)}) %collective-permute-start.3) | collective-permute-done | bytes 180256 | tf_op jit(solution)/shard_map/ppermute | solution.py:40
  33.6 1.9 %collective-permute-done.12 = bf16[64,1280]{1,0:T(8,128)(2,1)S(1)} collective-permute-done((bf16[64,1280]{1,0:T(8,128)(2,1)S(1)}, bf16[64,1280]{1,0:T(8,128)(2,1)S(1)}, u32[]{:S(2)}, u32[]{:S(2)}) %collective-permute-start.12) | collective-permute-done | bytes 163872 | tf_op jit(solution)/shard_map/ppermute | solution.py:36
  36.3 4.3 %collective-permute-done.7 = bf16[64,1280]{1,0:T(8,128)(2,1)S(1)} collective-permute-done((bf16[64,1280]{1,0:T(8,128)(2,1)S(1)}, bf16[64,1280]{1,0:T(8,128)(2,1)S(1)}, u32[]{:S(2)}, u32[]{:S(2)}) %collective-permute-start.7) | collective-permute-done | bytes 163872 | tf_op jit(solution)/shard_map/ppermute | solution.py:40
  40.7 1.6 %collective-permute-done.13.sum_b = bf16[64,1280]{1,0:T(8,128)(2,1)S(1)} collective-permute-done((bf16[64,1280]{1,0:T(8,128)(2,1)S(1)}, bf16[64,1280]{1,0:T(8,128)(2,1)S(1)}, u32[]{:S(2)}, u32[]{:S(2)}) %collective-permute-start.13) | collective-permute-done | bytes 163872 | tf_op jit(solution)/shard_map/ppermute | solution.py:40
  42.3 4.4 %combine_grad.1 = (f32[64,1024]{1,0:T(8,128)S(1)}, f32[2,1,1024]{2,1,0:T(1,128)S(1)}) custom-call(bf16[2,1024,1280]{2,1,0:T(8,128)(2,1)} %gout.1, bf16[64,1280]{1,0:T(8,128)(2,1)S(1)} %add_convert_fusion.1.sum_a, bf16[64,1280]{1,0:T(8,128)(2,1)S(1)} %collective-permute-done.13.sum_b, bf16[64,1024]{1,0:T(8,128)(2,1)S(1)} %bitcast.58), custom_call_target="tpu_custom_call" | custom-call | flops 350000000 | bytes 6000000 | tf_op jit(solution)/shard_map/combine_grad/pallas_call | solution.py:173
  48.0 2.8 %collective-permute-start.20 = (f32[2,1,1024]{2,1,0:T(1,128)S(1)}, f32[2,1,1024]{2,1,0:T(1,128)S(1)}, u32[]{:S(2)}, u32[]{:S(2)}) collective-permute-start(f32[2,1,1024]{2,1,0:T(1,128)S(1)} %add.73), channel_id=1, source_target_pairs={{0,6},{2,0},{4,2},{6,4},{1,7},{3,1},{5,3},{7,5},{8,14},{10,8},{12,... | collective-permute-start | bytes 24584 | tf_op jit(solution)/shard_map/ppermute | solution.py:28
  52.6 1.8 %collective-permute-start.11 = (bf16[64,1280]{1,0:T(8,128)(2,1)S(1)}, bf16[64,1280]{1,0:T(8,128)(2,1)S(1)}, u32[]{:S(2)}, u32[]{:S(2)}) collective-permute-start(bf16[64,1280]{1,0:T(8,128)(2,1)S(1)} %add_convert_fusion.2.gslot.refs_0_), channel_id=1, source_target_pairs={{0,8},{8,16},{16,24},{24,0},{1,9},{9,17},{17,25},{25,1},{2,10},{10... | collective-permute-start | bytes 491528 | tf_op jit(solution)/shard_map/ppermute | solution.py:28
  54.3 1.8 %collective-permute-start.10 = (bf16[64,1280]{1,0:T(8,128)(2,1)S(1)}, bf16[64,1280]{1,0:T(8,128)(2,1)S(1)}, u32[]{:S(2)}, u32[]{:S(2)}) collective-permute-start(bf16[64,1280]{1,0:T(8,128)(2,1)S(1)} %add_convert_fusion.2.gslot.refs_0_), channel_id=1, source_target_pairs={{0,16},{8,24},{16,0},{24,8},{1,17},{9,25},{17,1},{25,9},{2,18},{10... | collective-permute-start | bytes 491528 | tf_op jit(solution)/shard_map/ppermute | solution.py:28
  56.5 2.1 %collective-permute-start.23 = (f32[2,1,1024]{2,1,0:T(1,128)S(1)}, f32[2,1,1024]{2,1,0:T(1,128)S(1)}, u32[]{:S(2)}, u32[]{:S(2)}) collective-permute-start(f32[2,1,1024]{2,1,0:T(1,128)S(1)} %add_add_fusion.1), channel_id=1, source_target_pairs={{0,24},{8,0},{16,8},{24,16},{1,25},{9,1},{17,9},{25,17},{2,26},{10... | collective-permute-start | bytes 24584 | tf_op jit(solution)/shard_map/ppermute | solution.py:28
  58.7 1.7 %collective-permute-start.22 = (f32[2,1,1024]{2,1,0:T(1,128)S(1)}, f32[2,1,1024]{2,1,0:T(1,128)S(1)}, u32[]{:S(2)}, u32[]{:S(2)}) collective-permute-start(f32[2,1,1024]{2,1,0:T(1,128)S(1)} %add_add_fusion.1), channel_id=1, source_target_pairs={{0,16},{8,24},{16,0},{24,8},{1,17},{9,25},{17,1},{25,9},{2,18},{10... | collective-permute-start | bytes 24584 | tf_op jit(solution)/shard_map/ppermute | solution.py:28
  60.4 4.5 %dispatch_grad.1 = (f32[64,1024]{1,0:T(8,128)S(1)}, bf16[64,512]{1,0:T(8,128)(2,1)S(1)}, bf16[64,512]{1,0:T(8,128)(2,1)S(1)}, bf16[64,512]{1,0:T(8,128)(2,1)S(1)}, bf16[64,512]{1,0:T(8,128)(2,1)S(1)}) custom-call(bf16[2,1024,1280]{2,1,0:T(8,128)(2,1)} %tok.3, bf16[64,1280]{1,0:T(8,128)(2,1)S(1)} %add_convert_fusion.2.gslot.refs_0_, ...), custom_call_target="tpu_custom_call" | custom-call | flops 350000000 | bytes 7000000 | tf_op jit(solution)/shard_map/dispatch_grad/pallas_call | solution.py:217
  64.9 3.3 %collective-permute-start.9 = (bf16[64,1280]{1,0:T(8,128)(2,1)S(1)}, bf16[64,1280]{1,0:T(8,128)(2,1)S(1)}, u32[]{:S(2)}, u32[]{:S(2)}) collective-permute-start(bf16[64,1280]{1,0:T(8,128)(2,1)S(1)} %add_convert_fusion.2.gslot.refs_0_), channel_id=1, source_target_pairs={{0,24},{8,0},{16,8},{24,16},{1,25},{9,1},{17,9},{25,17},{2,26},{10... | collective-permute-start | bytes 491528 | tf_op jit(solution)/shard_map/ppermute | solution.py:28
  69.2 3.5 %collective-permute-done.14.refs_5_ = bf16[64,512]{1,0:T(8,128)(2,1)S(1)} collective-permute-done((bf16[64,512]{1,0:T(8,128)(2,1)S(1)}, bf16[64,512]{1,0:T(8,128)(2,1)S(1)}, u32[]{:S(2)}, u32[]{:S(2)}) %collective-permute-start.14) | collective-permute-done | bytes 65568 | tf_op jit(solution)/shard_map/ppermute | solution.py:28
  74.7 3.9 %collective-permute-done.16.refs_7_ = bf16[64,512]{1,0:T(8,128)(2,1)S(1)} collective-permute-done((bf16[64,512]{1,0:T(8,128)(2,1)S(1)}, bf16[64,512]{1,0:T(8,128)(2,1)S(1)}, u32[]{:S(2)}, u32[]{:S(2)}) %collective-permute-start.16) | collective-permute-done | bytes 65568 | tf_op jit(solution)/shard_map/ppermute | solution.py:28
  83.6 5.5 %collective-permute-done.29 = bf16[32,1280]{1,0:T(8,128)(2,1)} collective-permute-done((bf16[32,1280]{1,0:T(8,128)(2,1)S(1)}, bf16[32,1280]{1,0:T(8,128)(2,1)}, u32[]{:S(2)}, u32[]{:S(2)}) %collective-permute-start.29) | collective-permute-done | bytes 81952 | tf_op jit(solution)/shard_map/ppermute | solution.py:40
  96.0 2.0 %collective-permute-start.26 = (bf16[2,32,1280]{2,1,0:T(8,128)(2,1)S(1)}, bf16[2,32,1280]{2,1,0:T(8,128)(2,1)S(1)}, u32[]{:S(2)}, u32[]{:S(2)}) collective-permute-start(bf16[2,32,1280]{2,1,0:T(8,128)(2,1)S(1)} %get-tuple-element.53), channel_id=1, source_target_pairs={{0,4},{2,6},{4,0},{6,2},{1,5},{3,7},{5,1},{7,3},{8,12},{10,14},{12... | collective-permute-start | bytes 491528 | tf_op jit(solution)/shard_map/ppermute | solution.py:28
  98.0 1.9 %collective-permute-start.27 = (bf16[2,32,1280]{2,1,0:T(8,128)(2,1)S(1)}, bf16[2,32,1280]{2,1,0:T(8,128)(2,1)S(1)}, u32[]{:S(2)}, u32[]{:S(2)}) collective-permute-start(bf16[2,32,1280]{2,1,0:T(8,128)(2,1)S(1)} %get-tuple-element.54), channel_id=1, source_target_pairs={{0,6},{2,0},{4,2},{6,4},{1,7},{3,1},{5,3},{7,5},{8,14},{10,8},{12,... | collective-permute-start | bytes 491528 | tf_op jit(solution)/shard_map/ppermute | solution.py:28
  99.9 3.7 %fusion = bf16[1,1280,1280]{2,1,0:T(8,128)(2,1)} fusion(bf16[64,1280]{1,0:T(8,128)(2,1)S(1)} %get-tuple-element.56.slot_in, bf16[64,1280]{1,0:T(8,128)(2,1)} %copy-done.12), kind=kOutput, calls=%fused_computation.2 | convolution fusion | flops 211353600 | bytes 3604480 | tf_op jit(solution)/shard_map/sd,sh->dh/dot_general | solution.py:376
  103.6 2.8 %fusion.1 = bf16[1,1280,1280]{2,1,0:T(8,128)(2,1)} fusion(bf16[64,1280]{1,0:T(8,128)(2,1)S(1)} %copy-done.16, bf16[64,1280]{1,0:T(8,128)(2,1)S(1)} %copy-done.18, bf16[64,1280]{1,0:T(8,128)(2,1)S(1)} %copy-done.14), kind=kOutput, calls=%fused_computation.3 | convolution fusion | flops 211681280 | bytes 3768320 | tf_op jit(solution)/shard_map/sh,sd->hd/dot_general | solution.py:375
  (107 shorter events, 29.5 us)
Async XLA Ops:
  8.5 12.9 %collective-permute-start.2 = (bf16[64,1408]{1,0:T(8,128)(2,1)S(1)}, bf16[64,1408]{1,0:T(8,128)(2,1)S(1)}, u32[]{:S(2)}, u32[]{:S(2)}) collective-permute-start(bf16[64,1408]{1,0:T(8,128)(2,1)S(1)} %get-tuple-element.31.a), channel_id=1, source_target_pairs={{0,32},{32,0},{64,96},{96,64},{1,33},{33,1},{65,97},{97,65},{2,34}... | collective-permute-start | bytes 540680 | tf_op jit(solution)/shard_map/ppermute | solution.py:36
  14.0 8.4 %collective-permute-start = (bf16[64,1280]{1,0:T(8,128)(2,1)S(1)}, bf16[64,1280]{1,0:T(8,128)(2,1)S(1)}, u32[]{:S(2)}, u32[]{:S(2)}) collective-permute-start(bf16[64,1280]{1,0:T(8,128)(2,1)S(1)} %bitcast.64), channel_id=1, source_target_pairs={{0,96},{96,0},{32,64},{64,32},{1,97},{97,1},{33,65},{65,33},{2,98}... | collective-permute-start | bytes 491528 | tf_op jit(solution)/shard_map/ppermute | solution.py:40
  16.7 11.9 %collective-permute-start.4 = (bf16[224,256]{1,0:T(8,128)(2,1)S(1)}, bf16[224,256]{1,0:T(8,128)(2,1)S(1)}, u32[]{:S(2)}, u32[]{:S(2)}) collective-permute-start(bf16[224,256]{1,0:T(8,128)(2,1)S(1)} %get-tuple-element.34), channel_id=1, source_target_pairs={{0,24},{8,0},{16,8},{24,16},{1,25},{9,1},{17,9},{25,17},{2,26},{10... | collective-permute-start | bytes 344072 | tf_op jit(solution)/shard_map/ppermute | solution.py:28
  19.7 8.9 %collective-permute-start.5 = (bf16[224,256]{1,0:T(8,128)(2,1)S(1)}, bf16[224,256]{1,0:T(8,128)(2,1)S(1)}, u32[]{:S(2)}, u32[]{:S(2)}) collective-permute-start(bf16[224,256]{1,0:T(8,128)(2,1)S(1)} %get-tuple-element.35), channel_id=1, source_target_pairs={{0,16},{8,24},{16,0},{24,8},{1,17},{9,25},{17,1},{25,9},{2,18},{10... | collective-permute-start | bytes 344072 | tf_op jit(solution)/shard_map/ppermute | solution.py:28
  20.4 8.3 %collective-permute-start.6 = (bf16[224,256]{1,0:T(8,128)(2,1)S(1)}, bf16[224,256]{1,0:T(8,128)(2,1)S(1)}, u32[]{:S(2)}, u32[]{:S(2)}) collective-permute-start(bf16[224,256]{1,0:T(8,128)(2,1)S(1)} %get-tuple-element.36), channel_id=1, source_target_pairs={{0,8},{8,16},{16,24},{24,0},{1,9},{9,17},{17,25},{25,1},{2,10},{10... | collective-permute-start | bytes 344072 | tf_op jit(solution)/shard_map/ppermute | solution.py:28
  21.6 6.8 %collective-permute-start.3 = (bf16[64,1408]{1,0:T(8,128)(2,1)S(1)}, bf16[64,1408]{1,0:T(8,128)(2,1)S(1)}, u32[]{:S(2)}, u32[]{:S(2)}) collective-permute-start(bf16[64,1408]{1,0:T(8,128)(2,1)S(1)} %merge_pair.1.one), channel_id=1, source_target_pairs={{0,96},{96,0},{32,64},{64,32},{1,97},{97,1},{33,65},{65,33},{2,98}... | collective-permute-start | bytes 540680 | tf_op jit(solution)/shard_map/ppermute | solution.py:40
  22.5 7.8 %collective-permute-start.1 = (bf16[64,1280]{1,0:T(8,128)(2,1)S(1)}, bf16[64,1280]{1,0:T(8,128)(2,1)S(1)}, u32[]{:S(2)}, u32[]{:S(2)}) collective-permute-start(bf16[64,1280]{1,0:T(8,128)(2,1)S(1)} %add_convert_fusion.5), channel_id=1, source_target_pairs={{0,32},{32,0},{64,96},{96,64},{1,33},{33,1},{65,97},{97,65},{2,34}... | collective-permute-start | bytes 491528 | tf_op jit(solution)/shard_map/ppermute | solution.py:36
  32.6 8.0 %collective-permute-start.7 = (bf16[64,1280]{1,0:T(8,128)(2,1)S(1)}, bf16[64,1280]{1,0:T(8,128)(2,1)S(1)}, u32[]{:S(2)}, u32[]{:S(2)}) collective-permute-start(bf16[64,1280]{1,0:T(8,128)(2,1)S(1)} %fusion.19), channel_id=1, source_target_pairs={{0,96},{96,0},{32,64},{64,32},{1,97},{97,1},{33,65},{65,33},{2,98}... | collective-permute-start | bytes 491528 | tf_op jit(solution)/shard_map/ppermute | solution.py:40
  35.5 6.8 %collective-permute-start.13 = (bf16[64,1280]{1,0:T(8,128)(2,1)S(1)}, bf16[64,1280]{1,0:T(8,128)(2,1)S(1)}, u32[]{:S(2)}, u32[]{:S(2)}) collective-permute-start(bf16[64,1280]{1,0:T(8,128)(2,1)S(1)} %add_convert_fusion.1.sum_a), channel_id=1, source_target_pairs={{0,96},{96,0},{32,64},{64,32},{1,97},{97,1},{33,65},{65,33},{2,98}... | collective-permute-start | bytes 491528 | tf_op jit(solution)/shard_map/ppermute | solution.py:40
  40.6 11.9 %collective-permute-start.8 = (bf16[64,1280]{1,0:T(8,128)(2,1)S(1)}, bf16[64,1280]{1,0:T(8,128)(2,1)S(1)}, u32[]{:S(2)}, u32[]{:S(2)}) collective-permute-start(bf16[64,1280]{1,0:T(8,128)(2,1)S(1)} %add_convert_fusion.3), channel_id=1, source_target_pairs={{0,32},{32,0},{64,96},{96,64},{1,33},{33,1},{65,97},{97,65},{2,34}... | collective-permute-start | bytes 491528 | tf_op jit(solution)/shard_map/ppermute | solution.py:36
  48.0 8.2 %collective-permute-start.20 = (f32[2,1,1024]{2,1,0:T(1,128)S(1)}, f32[2,1,1024]{2,1,0:T(1,128)S(1)}, u32[]{:S(2)}, u32[]{:S(2)}) collective-permute-start(f32[2,1,1024]{2,1,0:T(1,128)S(1)} %add.73), channel_id=1, source_target_pairs={{0,6},{2,0},{4,2},{6,4},{1,7},{3,1},{5,3},{7,5},{8,14},{10,8},{12,... | collective-permute-start | bytes 24584 | tf_op jit(solution)/shard_map/ppermute | solution.py:28
  52.6 26.0 %collective-permute-start.11 = (bf16[64,1280]{1,0:T(8,128)(2,1)S(1)}, bf16[64,1280]{1,0:T(8,128)(2,1)S(1)}, u32[]{:S(2)}, u32[]{:S(2)}) collective-permute-start(bf16[64,1280]{1,0:T(8,128)(2,1)S(1)} %add_convert_fusion.2.gslot.refs_0_), channel_id=1, source_target_pairs={{0,8},{8,16},{16,24},{24,0},{1,9},{9,17},{17,25},{25,1},{2,10},{10... | collective-permute-start | bytes 491528 | tf_op jit(solution)/shard_map/ppermute | solution.py:28
  54.3 24.2 %collective-permute-start.10 = (bf16[64,1280]{1,0:T(8,128)(2,1)S(1)}, bf16[64,1280]{1,0:T(8,128)(2,1)S(1)}, u32[]{:S(2)}, u32[]{:S(2)}) collective-permute-start(bf16[64,1280]{1,0:T(8,128)(2,1)S(1)} %add_convert_fusion.2.gslot.refs_0_), channel_id=1, source_target_pairs={{0,16},{8,24},{16,0},{24,8},{1,17},{9,25},{17,1},{25,9},{2,18},{10... | collective-permute-start | bytes 491528 | tf_op jit(solution)/shard_map/ppermute | solution.py:28
  56.5 8.4 %collective-permute-start.23 = (f32[2,1,1024]{2,1,0:T(1,128)S(1)}, f32[2,1,1024]{2,1,0:T(1,128)S(1)}, u32[]{:S(2)}, u32[]{:S(2)}) collective-permute-start(f32[2,1,1024]{2,1,0:T(1,128)S(1)} %add_add_fusion.1), channel_id=1, source_target_pairs={{0,24},{8,0},{16,8},{24,16},{1,25},{9,1},{17,9},{25,17},{2,26},{10... | collective-permute-start | bytes 24584 | tf_op jit(solution)/shard_map/ppermute | solution.py:28
  58.7 9.6 %collective-permute-start.22 = (f32[2,1,1024]{2,1,0:T(1,128)S(1)}, f32[2,1,1024]{2,1,0:T(1,128)S(1)}, u32[]{:S(2)}, u32[]{:S(2)}) collective-permute-start(f32[2,1,1024]{2,1,0:T(1,128)S(1)} %add_add_fusion.1), channel_id=1, source_target_pairs={{0,16},{8,24},{16,0},{24,8},{1,17},{9,25},{17,1},{25,9},{2,18},{10... | collective-permute-start | bytes 24584 | tf_op jit(solution)/shard_map/ppermute | solution.py:28
  60.4 8.0 %collective-permute-start.21 = (f32[2,1,1024]{2,1,0:T(1,128)S(1)}, f32[2,1,1024]{2,1,0:T(1,128)S(1)}, u32[]{:S(2)}, u32[]{:S(2)}) collective-permute-start(f32[2,1,1024]{2,1,0:T(1,128)S(1)} %add_add_fusion.1), channel_id=1, source_target_pairs={{0,8},{8,16},{16,24},{24,0},{1,9},{9,17},{17,25},{25,1},{2,10},{10... | collective-permute-start | bytes 24584 | tf_op jit(solution)/shard_map/ppermute | solution.py:28
  64.9 13.7 %collective-permute-start.9 = (bf16[64,1280]{1,0:T(8,128)(2,1)S(1)}, bf16[64,1280]{1,0:T(8,128)(2,1)S(1)}, u32[]{:S(2)}, u32[]{:S(2)}) collective-permute-start(bf16[64,1280]{1,0:T(8,128)(2,1)S(1)} %add_convert_fusion.2.gslot.refs_0_), channel_id=1, source_target_pairs={{0,24},{8,0},{16,8},{24,16},{1,25},{9,1},{17,9},{25,17},{2,26},{10... | collective-permute-start | bytes 491528 | tf_op jit(solution)/shard_map/ppermute | solution.py:28
  68.3 6.2 %collective-permute-start.15 = (bf16[64,512]{1,0:T(8,128)(2,1)S(1)}, bf16[64,512]{1,0:T(8,128)(2,1)S(1)}, u32[]{:S(2)}, u32[]{:S(2)}) collective-permute-start(bf16[64,512]{1,0:T(8,128)(2,1)S(1)} %get-tuple-element.43), channel_id=1, source_target_pairs={{0,16},{8,24},{16,0},{24,8},{1,17},{9,25},{17,1},{25,9},{2,18},{10... | collective-permute-start | bytes 196616 | tf_op jit(solution)/shard_map/ppermute | solution.py:28
  74.5 8.2 %collective-permute-start.28 = (bf16[32,1280]{1,0:T(8,128)(2,1)S(1)}, bf16[32,1280]{1,0:T(8,128)(2,1)S(1)}, u32[]{:S(2)}, u32[]{:S(2)}) collective-permute-start(bf16[32,1280]{1,0:T(8,128)(2,1)S(1)} %fusion.22), channel_id=1, source_target_pairs={{0,32},{32,0},{64,96},{96,64},{1,33},{33,1},{65,97},{97,65},{2,34}... | collective-permute-start | bytes 245768 | tf_op jit(solution)/shard_map/ppermute | solution.py:36
  82.7 7.7 %collective-permute-start.24 = (bf16[4,2,32,1280]{3,2,1,0:T(8,128)(2,1)}, bf16[4,2,32,1280]{3,2,1,0:T(8,128)(2,1)}, u32[]{:S(2)}, u32[]{:S(2)}) collective-permute-start(bf16[4,2,32,1280]{3,2,1,0:T(8,128)(2,1)} %get-tuple-element.50), channel_id=1, source_target_pairs={{0,1},{1,0},{2,3},{3,2},{4,5},{5,4},{6,7},{7,6},{8,9},{9,8},{10,11... | collective-permute-start | bytes 1966088 | tf_op jit(solution)/shard_map/ppermute | solution.py:32
  82.8 6.3 %collective-permute-start.29 = (bf16[32,1280]{1,0:T(8,128)(2,1)S(1)}, bf16[32,1280]{1,0:T(8,128)(2,1)}, u32[]{:S(2)}, u32[]{:S(2)}) collective-permute-start(bf16[32,1280]{1,0:T(8,128)(2,1)S(1)} %add_convert_fusion.6), channel_id=1, source_target_pairs={{0,96},{96,0},{32,64},{64,32},{1,97},{97,1},{33,65},{65,33},{2,98}... | collective-permute-start | bytes 245768 | tf_op jit(solution)/shard_map/ppermute | solution.py:40
  95.5 10.9 %collective-permute-start.25 = (bf16[2,32,1280]{2,1,0:T(8,128)(2,1)S(1)}, bf16[2,32,1280]{2,1,0:T(8,128)(2,1)S(1)}, u32[]{:S(2)}, u32[]{:S(2)}) collective-permute-start(bf16[2,32,1280]{2,1,0:T(8,128)(2,1)S(1)} %get-tuple-element.52), channel_id=1, source_target_pairs={{0,2},{2,4},{4,6},{6,0},{1,3},{3,5},{5,7},{7,1},{8,10},{10,12},{12... | collective-permute-start | bytes 491528 | tf_op jit(solution)/shard_map/ppermute | solution.py:28
  96.0 10.4 %collective-permute-start.26 = (bf16[2,32,1280]{2,1,0:T(8,128)(2,1)S(1)}, bf16[2,32,1280]{2,1,0:T(8,128)(2,1)S(1)}, u32[]{:S(2)}, u32[]{:S(2)}) collective-permute-start(bf16[2,32,1280]{2,1,0:T(8,128)(2,1)S(1)} %get-tuple-element.53), channel_id=1, source_target_pairs={{0,4},{2,6},{4,0},{6,2},{1,5},{3,7},{5,1},{7,3},{8,12},{10,14},{12... | collective-permute-start | bytes 491528 | tf_op jit(solution)/shard_map/ppermute | solution.py:28
  98.0 8.7 %collective-permute-start.27 = (bf16[2,32,1280]{2,1,0:T(8,128)(2,1)S(1)}, bf16[2,32,1280]{2,1,0:T(8,128)(2,1)S(1)}, u32[]{:S(2)}, u32[]{:S(2)}) collective-permute-start(bf16[2,32,1280]{2,1,0:T(8,128)(2,1)S(1)} %get-tuple-element.54), channel_id=1, source_target_pairs={{0,6},{2,0},{4,2},{6,4},{1,7},{3,1},{5,3},{7,5},{8,14},{10,8},{12,... | collective-permute-start | bytes 491528 | tf_op jit(solution)/shard_map/ppermute | solution.py:28
  (27 other events, 232.3 us)

commit v4 on v3

--- a/solution.py
+++ b/solution.py
@@ -11,7 +11,9 @@
 BF16 = jnp.bfloat16
 NT = (((1,), (1,)), ((), ()))
 TN = (((0,), (0,)), ((), ()))
-PARAMS = pltpu.CompilerParams(vmem_limit_bytes=24 * 1024 * 1024)
+LARGE = pltpu.CompilerParams(vmem_limit_bytes=16 * 1024 * 1024)
+MEDIUM = pltpu.CompilerParams(vmem_limit_bytes=10 * 1024 * 1024)
+SMALL = pltpu.CompilerParams(vmem_limit_bytes=4 * 1024 * 1024)
 
 
 def shape(dims, dtype):
@@ -32,12 +34,12 @@
     return lax.ppermute(value, "core", [(0, 1), (1, 0)])
 
 
-def near(value):
-    return lax.ppermute(value, "seq", [(0, 1), (1, 0), (2, 3), (3, 2)])
-
-
-def far(value):
-    return lax.ppermute(value, "seq", [(0, 3), (3, 0), (1, 2), (2, 1)])
+def near(value, axis="seq"):
+    return lax.ppermute(value, axis, [(0, 1), (1, 0), (2, 3), (3, 2)])
+
+
+def far(value, axis="seq"):
+    return lax.ppermute(value, axis, [(0, 3), (3, 0), (1, 2), (2, 1)])
 
 
 def add(one, two):
@@ -71,10 +73,7 @@
 
 
 def softmax_kernel(tok, embed, logits, part, peak, total, sums):
-    step = pl.program_id(1)
-    patches = tok[0]
-    scores = lax.dot_general(patches, embed[...], NT, preferred_element_type=F32).T
-    logits[...] = scores
+    step = pl.program_id(0)
 
     @pl.when(step == 0)
     def _():
@@ -82,21 +81,28 @@
         total[...] = jnp.zeros_like(total)
         sums[...] = jnp.zeros_like(sums)
 
-    top = jnp.maximum(peak[:, :1], jnp.max(scores, axis=1, keepdims=True))
-    scale = jnp.exp(peak[:, :1] - top)
-    weight = jnp.exp(scores - top)
-    new_total = total[:, :1] * scale + jnp.sum(weight, axis=1, keepdims=True)
-    new_sums = sums[...] * scale + jnp.dot(
-        weight.astype(BF16), patches, preferred_element_type=F32
-    )
-    peak[...] = jnp.broadcast_to(top, peak.shape)
-    total[...] = jnp.broadcast_to(new_total, total.shape)
-    sums[...] = new_sums
-
-    @pl.when(step == pl.num_programs(1) - 1)
-    def _():
-        part[:, :1280] = (new_sums / new_total).astype(BF16)
-        part[:, 1280:] = lse_lanes(top + jnp.log(new_total))
+    scores = [
+        lax.dot_general(tok[i], embed[...], NT, preferred_element_type=F32).T for i in range(2)
+    ]
+    for i in range(2):
+        half = slice(32 * i, 32 * i + 32)
+        logits[half, :] = scores[i]
+        before = peak[half, :1]
+        top = jnp.maximum(before, jnp.max(scores[i], axis=1, keepdims=True))
+        scale = jnp.exp(before - top)
+        weight = jnp.exp(scores[i] - top)
+        new_total = total[half, :1] * scale + jnp.sum(weight, axis=1, keepdims=True)
+        new_sums = sums[half, :] * scale + jnp.dot(
+            weight.astype(BF16), tok[i], preferred_element_type=F32
+        )
+        peak[half, :] = jnp.broadcast_to(top, (32, 128))
+        total[half, :] = jnp.broadcast_to(new_total, (32, 128))
+        sums[half, :] = new_sums
+
+        @pl.when(step == pl.num_programs(0) - 1)
+        def _():
+            part[half, :1280] = (new_sums / new_total).astype(BF16)
+            part[half, 1280:] = lse_lanes(top + jnp.log(new_total))
 
 
 def in_hbm(value):
@@ -106,23 +112,23 @@
 def local_softmax(tokens, embed):
     return pl.pallas_call(
         softmax_kernel,
-        grid=(2, 2),
+        grid=(2,),
         in_specs=[
-            pl.BlockSpec((1, 512, 1280), lambda i, t: (i, t, 0)),
-            pl.BlockSpec((32, 1280), lambda i, t: (0, 0)),
+            pl.BlockSpec((2, 512, 1280), lambda t: (0, t, 0)),
+            pl.BlockSpec((32, 1280), lambda t: (0, 0)),
         ],
         out_specs=[
-            pl.BlockSpec((32, 512), lambda i, t: (i, t)),
-            pl.BlockSpec((32, 1408), lambda i, t: (i, 0)),
+            pl.BlockSpec((64, 512), lambda t: (0, t)),
+            pl.BlockSpec((64, 1408), lambda t: (0, 0)),
         ],
         out_shape=[shape((64, 1024), F32), shape((64, 1408), BF16)],
         scratch_shapes=[
-            pltpu.VMEM((32, 128), F32),
-            pltpu.VMEM((32, 128), F32),
-            pltpu.VMEM((32, 1280), F32),
+            pltpu.VMEM((64, 128), F32),
+            pltpu.VMEM((64, 128), F32),
+            pltpu.VMEM((64, 1280), F32),
         ],
         cost_estimate=pl.CostEstimate(flops=700_000_000, bytes_accessed=6_000_000, transcendentals=65536),
-        compiler_params=PARAMS,
+        compiler_params=LARGE,
         name="local_softmax",
     )(in_hbm(tokens), embed)
 
@@ -147,7 +153,7 @@
         lambda a, b, out: merge_kernel(a, b, out, None),
         out_shape=shape((64, 1408), BF16),
         cost_estimate=pl.CostEstimate(flops=300_000, bytes_accessed=540_000, transcendentals=256),
-        compiler_params=PARAMS,
+        compiler_params=SMALL,
         name="merge_pair",
     )(one, two)
 
@@ -157,7 +163,7 @@
         merge_kernel,
         out_shape=[shape((64, 1280), BF16), shape((64, 128), F32)],
         cost_estimate=pl.CostEstimate(flops=300_000, bytes_accessed=540_000, transcendentals=256),
-        compiler_params=PARAMS,
+        compiler_params=SMALL,
         name="merge_last",
     )(one, two)
 
@@ -185,9 +191,9 @@
         ],
         out_shape=[shape((64, 1024), F32), shape((2, 1, 1024), F32)],
         cost_estimate=pl.CostEstimate(flops=350_000_000, bytes_accessed=6_000_000, transcendentals=0),
-        compiler_params=PARAMS,
+        compiler_params=MEDIUM,
         name="combine_grad",
-    )(in_hbm(grad_out), sum_a, sum_b, comb)
+    )(grad_out, sum_a, sum_b, comb)
 
 
 def dispatch_grad_kernel(tok, gslot, slot_in, logits, lse, comb, gcomb, full, c0, c1, c2, c3, all_grad, all_weight):
@@ -230,42 +236,31 @@
         out_shape=[shape((64, 1024), F32)] + [shape((64, 512), BF16)] * 4,
         scratch_shapes=[pltpu.VMEM((32, 1024), F32), pltpu.VMEM((32, 1024), F32)],
         cost_estimate=pl.CostEstimate(flops=350_000_000, bytes_accessed=7_000_000, transcendentals=65536),
-        compiler_params=PARAMS,
+        compiler_params=MEDIUM,
         name="dispatch_grad",
-    )(in_hbm(tokens), gslot, slot_in, logits, lse, comb, gcomb)
-
-
-def inputs_kernel(comb, embed, o0, o1, o2, o3):
-    for k, out in enumerate((o0, o1, o2, o3)):
-        out[:64, :] = comb[:, pl.ds(chunk("y", k, 256), 256)]
-        for n in range(5):
-            out[64 + 32 * n : 96 + 32 * n, :] = embed[:, 256 * n : 256 * n + 256]
-
-
-def input_blocks(comb, embed):
-    return pl.pallas_call(
-        inputs_kernel,
-        out_shape=[shape((224, 256), BF16)] * 4,
-        cost_estimate=pl.CostEstimate(flops=0, bytes_accessed=700_000, transcendentals=0),
-        compiler_params=PARAMS,
-        name="input_blocks",
-    )(comb, embed)
+    )(tokens, gslot, slot_in, logits, lse, comb, gcomb)
 
 
 def rows_kernel(*refs):
-    slots, parts, inputs = (refs[4 * n : 4 * n + 4] for n in range(3))
-    row_dot, m0, m1, m2, m3, other, scratch = refs[12:]
-    core = lax.axis_index("core")
+    slots, parts = refs[:4], refs[4:8]
+    inputs, row_dot, m0, m1, m2, m3, other, scratch = refs[8:]
+    core, y = lax.axis_index("core"), lax.axis_index("y")
+    mine_span = pl.ds(chunk("y", 0, 256), 256)
     embeds = [
-        jnp.concatenate([one[64 + 32 * n : 96 + 32 * n, :] for n in range(5)], axis=1)
-        for one in inputs
+        jnp.concatenate(
+            [inputs[(y + k) & 3, 32 * n : 32 * n + 32, 1024:1664] for n in range(2)], axis=1
+        )
+        for k in range(4)
     ]
     for i in range(2):
         half = slice(32 * i, 32 * i + 32)
-        dots = row_dot[i, :, pl.ds(chunk("y", 0, 256), 256)]
+        dots = row_dot[i, :, mine_span]
         weights = [one[half, 256:] for one in parts] + [
-            (p[half, :256].astype(F32) - c[half, :].astype(F32) * dots).astype(BF16)
-            for p, c in zip(parts, inputs)
+            (
+                part[half, :256].astype(F32)
+                - inputs[(y + k) & 3, half, mine_span].astype(F32) * dots
+            ).astype(BF16)
+            for k, part in enumerate(parts)
         ]
         rows = [one[half, :] for one in slots] + embeds
         scratch[i] = lax.dot_general(
@@ -286,9 +281,9 @@
         out_shape=[block] * 4 + [shape((4, 2, 32, 1280), BF16)],
         scratch_shapes=[pltpu.VMEM((2, 256, 1280), F32)],
         cost_estimate=pl.CostEstimate(flops=335_000_000, bytes_accessed=3_000_000, transcendentals=0),
-        compiler_params=PARAMS,
+        compiler_params=MEDIUM,
         name="patch_rows",
-    )(*slots, *parts, *inputs, row_dot)
+    )(*slots, *parts, inputs, row_dot)
     return mine, other
 
 
@@ -302,7 +297,7 @@
         add_kernel,
         out_shape=[shape((2, 32, 1280), BF16)] * 4,
         cost_estimate=pl.CostEstimate(flops=327_680, bytes_accessed=2_000_000, transcendentals=0),
-        compiler_params=PARAMS,
+        compiler_params=SMALL,
         name="add_cores",
     )(*mine, other)
 
@@ -320,40 +315,47 @@
     embed = slot_embed.T
     comb = jnp.transpose(combine, (0, 2, 1)).reshape(64, 1024)
     comb_f = comb.astype(F32)
-    inputs = sources(scatter_terms(input_blocks(comb, embed), "y"))
+    inputs = jnp.concatenate([embed[:, :640], embed[:, 640:]], axis=0)
+    inputs = jnp.concatenate([comb, inputs, jnp.zeros((64, 896), BF16)], axis=1)
+    inputs = lax.all_gather(inputs, "y")
 
     logits, part = local_softmax(tokens, embed)
+    comb_late = after(comb, part)
     part = merge_pair(part, near(part))
 
     out_part = jnp.einsum(
-        "ijt,itd->ijd", comb.reshape(2, 32, 1024), grad_out, preferred_element_type=F32
+        "ijt,itd->ijd", comb_late.reshape(2, 32, 1024), grad_out, preferred_element_type=F32
     )
     out_part = out_part.astype(BF16).reshape(64, 1280)
     out_part = add(out_part, far(out_part))
     grad_slot_out = add(out_part, near(out_part))
     slot_in, lse = merge_last(part, far(part))
-    slot_in = after(slot_in, *inputs)
 
     pre_act = jnp.dot(slot_in, w_in, preferred_element_type=F32)
     act, slope = gelu_parts(pre_act)
     act = act.astype(BF16)
     out_sum = jnp.dot(act, w_out, preferred_element_type=F32).astype(BF16)
+    grad_slot_out = after(grad_slot_out, out_sum)
     out_sum = add(out_sum, near(out_sum))
     out_other = far(out_sum)
     grad_act = jnp.einsum("sd,hd->sh", grad_slot_out, w_out, preferred_element_type=F32)
     grad_pre = (grad_act * slope).astype(BF16)
     in_sum = jnp.einsum("sh,dh->sd", grad_pre, w_in, preferred_element_type=F32).astype(BF16)
     in_sum = add(in_sum, far(in_sum))
-    grad_slot_in = add(in_sum, near(in_sum))
+    in_other = near(in_sum)
 
     grad_combine, row_dot = combine_grad(grad_out, out_sum, out_other, comb)
+    grad_slot_in = add(after(in_sum, row_dot), in_other)
     row_dot = row_dot + swap_cores(row_dot)
-    for axis in ("x", "y"):
-        row_dot = sum(scatter_terms([row_dot] * 4, axis))
+    row_dot = row_dot + near(row_dot, "x")
+    act_late, late, row_dot = lax.optimization_barrier((act, grad_slot_in, row_dot))
+    row_dot = row_dot + far(row_dot, "x")
+    row_dot = row_dot + near(row_dot, "y")
+    row_dot = row_dot + far(row_dot, "y")
 
     rows = gather_blocks(grad_slot_in, "y")
     partial_logits, *chunks = dispatch_grad(
-        tokens, grad_slot_in, slot_in, logits, lse, comb, grad_combine
+        tokens, late, slot_in, logits, lse, comb, grad_combine
     )
     chunks = sources(scatter_terms(chunks, "y"))
 
@@ -367,11 +369,12 @@
     embed_part = jnp.einsum("ijt,itd->jd", grad_logits, tokens, preferred_element_type=F32)
     embed_part = embed_part.astype(BF16)
     embed_part = add(embed_part, near(embed_part))
+    embed_part = after(embed_part, sums[0])
     embed_sum = add(embed_part, far(embed_part))
     z = lax.axis_index("seq")
     grad_embed = lax.dynamic_slice_in_dim(embed_sum, z * 320, 320, axis=1).T
 
-    act_late, slot_late = lax.optimization_barrier((act, slot_in, sums[0]))[:2]
+    slot_late = after(slot_in, sums[0])
     grad_w_out = jnp.einsum("sh,sd->hd", act_late, grad_slot_out, preferred_element_type=F32)
     grad_w_in = jnp.einsum("sd,sh->dh", slot_late, grad_pre, preferred_element_type=F32)
     return (

time: 108 us -> 122 us (1.13)
  between operations: 0.94 us -> 14.4 us
  other arithmetic: 2.49 us -> 7.17 us
  local copies, waits for them, and re-layouts: 7.45 us -> 3.88 us
  Pallas kernels: 19 us -> 16.7 us
  waiting for transfers between devices: 27.9 us -> 29.7 us
    ppermute x18 -> x9, starting transfers between devices: 26.1 us -> 11.6 us  [shift(): return lax.ppermute(value, axis, [(i, (i + by) % 4) for i in range(4)])]
    ppermute x10 -> x14, starting transfers between devices: 8.87 us -> 23.1 us  [the longest x7 15.9 us: far(): return lax.ppermute(value, axis, [(0, 3), (3, 0), (1, 2), (2, 1)])]
    unnamed x43 -> x47, local copies, waits for them, and re-layouts: 7.45 us -> 3.86 us
    ppermute x10 -> x14, waiting for transfers between devices: 18.7 us -> 21.5 us  [the longest x7 17.2 us: far(): return lax.ppermute(value, axis, [(0, 3), (3, 0), (1, 2), (2, 1)])]
    dot_general x1, matrix products: 0.98 us -> 3.54 us  [local(): jnp.einsum('ijt,itd->jd', grad_logits, tokens, preferred_element_type=F32)]
    convert_element_type x5 -> x6, other arithmetic: 0.2 us -> 2.57 us  [add(): return (one.astype(F32) + two.astype(F32)).astype(BF16)]
    pallas_call x1, Pallas kernels: 4.4 us -> 2.25 us  [combine_grad(): pl.pallas_call(combine_grad_kernel, grid=(2, 2), in_specs=[pl.BlockSpec((...]
    convert_element_type x1, other arithmetic: 0.05 us -> 1.64 us  [local(): grad_logits = grad_logits.astype(BF16).reshape(2, 32, 1024)]
  transfers between devices with their start and end apart: 30 -> 26, of which waited for: 10 -> 16; matrix products, arithmetic and copies ran while one was open for 15% -> 17% of each run, Pallas kernels for 10% -> 7%
where the time goes in v4:
time: 122 us
  starting transfers between devices  35.1 us (29%)
  waiting for transfers between devices  29.7 us (24%)
  Pallas kernels  16.7 us (14%)
  matrix products  14.6 us (12%)
  between operations  14.4 us (12%)
  other arithmetic  7.17 us (6%)
  local copies, waits for them, and re-layouts  3.88 us (3%)
    ppermute x7, waiting for transfers between devices, far(): return lax.ppermute(value, axis, [(0, 3), (3, 0), (1, 2), (2, 1)])  17.2 us
    ppermute x7, starting transfers between devices, far(): return lax.ppermute(value, axis, [(0, 3), (3, 0), (1, 2), (2, 1)])  15.9 us
    ppermute x9, starting transfers between devices, shift(): return lax.ppermute(value, axis, [(i, (i + by) % 4) for i in range(4)])  11.6 us
    ppermute x7, starting transfers between devices, near(): return lax.ppermute(value, axis, [(0, 1), (1, 0), (2, 3), (3, 2)])  7.2 us
    ppermute x9, waiting for transfers between devices, shift(): return lax.ppermute(value, axis, [(i, (i + by) % 4) for i in range(4)])  7.06 us
    pallas_call x1, Pallas kernels, local_softmax(): pl.pallas_call(softmax_kernel, grid=(2,), in_specs=[pl.BlockSpec((2, 512,...  6.73 us
    ppermute x7, waiting for transfers between devices, near(): return lax.ppermute(value, axis, [(0, 1), (1, 0), (2, 3), (3, 2)])  4.28 us
    pallas_call x1, Pallas kernels, dispatch_grad(): pl.pallas_call(dispatch_grad_kernel, grid=(2, 2), in_specs=[pl.BlockSpec(...  4.17 us
  transfers between devices with their start and end apart: 26, of which 16 were waited for; matrix products, arithmetic and copies ran while one was open for 17% of the time, Pallas kernels for 7%

profile of v4, /device:TPU:0, one launch (start us, length us, event | category | flops | bytes accessed | tf_op | source)
XLA Modules:
  0.0 121.6 jit_solution(4720725655013438300)
XLA Ops:
  8.3 6.7 %local_softmax.1 = (f32[64,1024]{1,0:T(8,128)S(1)}, bf16[64,1408]{1,0:T(8,128)(2,1)}) custom-call(bf16[2,1024,1280]{2,1,0:T(8,128)(2,1)} %tok.3, bf16[32,1280]{1,0:T(8,128)(2,1)S(1)} %bitcast.70), custom_call_target="tpu_custom_call" | custom-call | flops 700000000 | bytes 6000000 | tf_op jit(solution)/shard_map/local_softmax/pallas_call | solution.py:113
  15.7 2.0 %collective-permute-start.2 = (bf16[64,1408]{1,0:T(8,128)(2,1)}, bf16[64,1408]{1,0:T(8,128)(2,1)}, u32[]{:S(2)}, u32[]{:S(2)}) collective-permute-start(bf16[64,1408]{1,0:T(8,128)(2,1)} %get-tuple-element.32.a), channel_id=1, source_target_pairs={{0,32},{32,0},{64,96},{96,64},{1,33},{33,1},{65,97},{97,65},{2,34}... | collective-permute-start | bytes 540680 | tf_op jit(solution)/shard_map/ppermute | solution.py:38
  19.6 2.5 %collective-permute-start = (bf16[64,1280]{1,0:T(8,128)(2,1)S(1)}, bf16[64,1280]{1,0:T(8,128)(2,1)S(1)}, u32[]{:S(2)}, u32[]{:S(2)}) collective-permute-start(bf16[64,1280]{1,0:T(8,128)(2,1)S(1)} %bitcast.72), channel_id=1, source_target_pairs={{0,96},{96,0},{32,64},{64,32},{1,97},{97,1},{33,65},{65,33},{2,98}... | collective-permute-start | bytes 491528 | tf_op jit(solution)/shard_map/ppermute | solution.py:42
  22.2 4.3 %collective-permute-done = bf16[64,1280]{1,0:T(8,128)(2,1)S(1)} collective-permute-done((bf16[64,1280]{1,0:T(8,128)(2,1)S(1)}, bf16[64,1280]{1,0:T(8,128)(2,1)S(1)}, u32[]{:S(2)}, u32[]{:S(2)}) %collective-permute-start) | collective-permute-done | bytes 163872 | tf_op jit(solution)/shard_map/ppermute | solution.py:42
  30.1 2.4 %collective-permute-start.3 = (bf16[64,1408]{1,0:T(8,128)(2,1)S(1)}, bf16[64,1408]{1,0:T(8,128)(2,1)S(1)}, u32[]{:S(2)}, u32[]{:S(2)}) collective-permute-start(bf16[64,1408]{1,0:T(8,128)(2,1)S(1)} %merge_pair.1.one), channel_id=1, source_target_pairs={{0,96},{96,0},{32,64},{64,32},{1,97},{97,1},{33,65},{65,33},{2,98}... | collective-permute-start | bytes 540680 | tf_op jit(solution)/shard_map/ppermute | solution.py:42
  33.9 2.9 %collective-permute-done.3.two = bf16[64,1408]{1,0:T(8,128)(2,1)S(1)} collective-permute-done((bf16[64,1408]{1,0:T(8,128)(2,1)S(1)}, bf16[64,1408]{1,0:T(8,128)(2,1)S(1)}, u32[]{:S(2)}, u32[]{:S(2)}) %collective-permute-start.3) | collective-permute-done | bytes 180256 | tf_op jit(solution)/shard_map/ppermute | solution.py:42
  41.1 2.6 %collective-permute-start.4 = (bf16[64,1280]{1,0:T(8,128)(2,1)S(1)}, bf16[64,1280]{1,0:T(8,128)(2,1)S(1)}, u32[]{:S(2)}, u32[]{:S(2)}) collective-permute-start(bf16[64,1280]{1,0:T(8,128)(2,1)S(1)} %fusion.16), channel_id=1, source_target_pairs={{0,96},{96,0},{32,64},{64,32},{1,97},{97,1},{33,65},{65,33},{2,98}... | collective-permute-start | bytes 491528 | tf_op jit(solution)/shard_map/ppermute | solution.py:42
  44.0 2.4 %collective-permute-start.6 = (bf16[64,1280]{1,0:T(8,128)(2,1)S(1)}, bf16[64,1280]{1,0:T(8,128)(2,1)S(1)}, u32[]{:S(2)}, u32[]{:S(2)}) collective-permute-start(bf16[64,1280]{1,0:T(8,128)(2,1)S(1)} %add_convert_fusion.2.sum_a), channel_id=1, source_target_pairs={{0,96},{96,0},{32,64},{64,32},{1,97},{97,1},{33,65},{65,33},{2,98}... | collective-permute-start | bytes 491528 | tf_op jit(solution)/shard_map/ppermute | solution.py:42
  48.5 2.2 %collective-permute-done.6.sum_b = bf16[64,1280]{1,0:T(8,128)(2,1)S(1)} collective-permute-done((bf16[64,1280]{1,0:T(8,128)(2,1)S(1)}, bf16[64,1280]{1,0:T(8,128)(2,1)S(1)}, u32[]{:S(2)}, u32[]{:S(2)}) %collective-permute-start.6) | collective-permute-done | bytes 163872 | tf_op jit(solution)/shard_map/ppermute | solution.py:42
  50.6 2.2 %combine_grad.1 = (f32[64,1024]{1,0:T(8,128)S(1)}, f32[2,1,1024]{2,1,0:T(1,128)S(1)}) custom-call(bf16[2,1024,1280]{2,1,0:T(8,128)(2,1)S(1)} %bitcast.64, bf16[64,1280]{1,0:T(8,128)(2,1)S(1)} %add_convert_fusion.2.sum_a, bf16[64,1280]{1,0:T(8,128)(2,1)S(1)} %collective-permute-done.6.sum_b, bf16[64,1024]{1,0:T(8,128)(2,1)S(1)} %bitcast.67), custom_call_target="tpu_custom_call" | custom-call | flops 350000000 | bytes 6000000 | tf_op jit(solution)/shard_map/combine_grad/pallas_call | solution.py:179
  58.0 2.9 %collective-permute-start.9 = (bf16[64,1280]{1,0:T(8,128)(2,1)}, bf16[64,1280]{1,0:T(8,128)(2,1)}, u32[]{:S(2)}, u32[]{:S(2)}) collective-permute-start(bf16[64,1280]{1,0:T(8,128)(2,1)} %add_convert_fusion.1.gslot.refs_0_), channel_id=1, source_target_pairs={{0,16},{8,24},{16,0},{24,8},{1,17},{9,25},{17,1},{25,9},{2,18},{10... | collective-permute-start | bytes 491528 | tf_op jit(solution)/shard_map/ppermute | solution.py:30
  62.3 4.2 %dispatch_grad.1 = (f32[64,1024]{1,0:T(8,128)S(1)}, bf16[64,512]{1,0:T(8,128)(2,1)S(1)}, bf16[64,512]{1,0:T(8,128)(2,1)}, bf16[64,512]{1,0:T(8,128)(2,1)}, bf16[64,512]{1,0:T(8,128)(2,1)S(1)}) custom-call(bf16[2,1024,1280]{2,1,0:T(8,128)(2,1)S(1)} %bitcast.62, bf16[64,1280]{1,0:T(8,128)(2,1)} %add_convert_fusion.1.gslot.refs_0_, ...), custom_call_target="tpu_custom_call" | custom-call | flops 350000000 | bytes 7000000 | tf_op jit(solution)/shard_map/dispatch_grad/pallas_call | solution.py:223
  67.2 2.1 %collective-permute-start.16 = (f32[2,1,1024]{2,1,0:T(1,128)S(1)}, f32[2,1,1024]{2,1,0:T(1,128)S(1)}, u32[]{:S(2)}, u32[]{:S(2)}) collective-permute-start(f32[2,1,1024]{2,1,0:T(1,128)S(1)} %add.68), channel_id=1, source_target_pairs={{0,6},{6,0},{2,4},{4,2},{1,7},{7,1},{3,5},{5,3},{8,14},{14,8},{10,... | collective-permute-start | bytes 24584 | tf_op jit(solution)/shard_map/ppermute | solution.py:42
  69.3 2.8 %collective-permute-done.16 = f32[2,1,1024]{2,1,0:T(1,128)S(1)} collective-permute-done((f32[2,1,1024]{2,1,0:T(1,128)S(1)}, f32[2,1,1024]{2,1,0:T(1,128)S(1)}, u32[]{:S(2)}, u32[]{:S(2)}) %collective-permute-start.16) | collective-permute-done | bytes 8224 | tf_op jit(solution)/shard_map/ppermute | solution.py:42
  72.1 2.1 %collective-permute-start.17 = (f32[2,1,1024]{2,1,0:T(1,128)S(1)}, f32[2,1,1024]{2,1,0:T(1,128)S(1)}, u32[]{:S(2)}, u32[]{:S(2)}) collective-permute-start(f32[2,1,1024]{2,1,0:T(1,128)S(1)} %add.69), channel_id=1, source_target_pairs={{0,8},{8,0},{16,24},{24,16},{1,9},{9,1},{17,25},{25,17},{2,10},{10... | collective-permute-start | bytes 24584 | tf_op jit(solution)/shard_map/ppermute | solution.py:38
  77.2 3.6 %collective-permute-done.18 = f32[2,1,1024]{2,1,0:T(1,128)S(1)} collective-permute-done((f32[2,1,1024]{2,1,0:T(1,128)S(1)}, f32[2,1,1024]{2,1,0:T(1,128)S(1)}, u32[]{:S(2)}, u32[]{:S(2)}) %collective-permute-start.18) | collective-permute-done | bytes 8224 | tf_op jit(solution)/shard_map/ppermute | solution.py:42
  80.8 2.0 %collective-permute-start.14 = (bf16[64,512]{1,0:T(8,128)(2,1)}, bf16[64,512]{1,0:T(8,128)(2,1)}, u32[]{:S(2)}, u32[]{:S(2)}) collective-permute-start(bf16[64,512]{1,0:T(8,128)(2,1)} %get-tuple-element.44), channel_id=1, source_target_pairs={{0,16},{8,24},{16,0},{24,8},{1,17},{9,25},{17,1},{25,9},{2,18},{10... | collective-permute-start | bytes 196616 | tf_op jit(solution)/shard_map/ppermute | solution.py:30
  92.1 3.5 %fusion.22 = bf16[32,1280]{1,0:T(8,128)(2,1)S(1)} fusion(bf16[2,32,1024]{2,1,0:T(8,128)(2,1)} %bitcast.73, bf16[2,1024,1280]{2,1,0:T(8,128)(2,1)} %tok.3), kind=kOutput, calls=%fused_computation.18 | convolution fusion | flops 167813120 | bytes 5455872 | tf_op jit(solution)/shard_map/ijt,itd->jd/dot_general | solution.py:369
  95.8 2.8 %fusion.1 = bf16[1,1280,1280]{2,1,0:T(8,128)(2,1)} fusion(bf16[64,1280]{1,0:T(8,128)(2,1)S(1)} %copy-done.15, bf16[64,1280]{1,0:T(8,128)(2,1)S(1)} %copy-done.17), kind=kOutput, calls=%fused_computation.3 | convolution fusion | flops 211353600 | bytes 3604480 | tf_op jit(solution)/shard_map/sh,sd->hd/dot_general | solution.py:378
  98.5 2.1 %collective-permute-done.23 = bf16[32,1280]{1,0:T(8,128)(2,1)S(1)} collective-permute-done((bf16[32,1280]{1,0:T(8,128)(2,1)S(1)}, bf16[32,1280]{1,0:T(8,128)(2,1)S(1)}, u32[]{:S(2)}, u32[]{:S(2)}) %collective-permute-start.23) | collective-permute-done | bytes 81952 | tf_op jit(solution)/shard_map/ppermute | solution.py:38
  100.8 2.4 %collective-permute-start.24 = (bf16[32,1280]{1,0:T(8,128)(2,1)S(1)}, bf16[32,1280]{1,0:T(8,128)(2,1)S(1)}, u32[]{:S(2)}, u32[]{:S(2)}) collective-permute-start(bf16[32,1280]{1,0:T(8,128)(2,1)S(1)} %add_convert_fusion.6), channel_id=1, source_target_pairs={{0,96},{96,0},{32,64},{64,32},{1,97},{97,1},{33,65},{65,33},{2,98}... | collective-permute-start | bytes 245768 | tf_op jit(solution)/shard_map/ppermute | solution.py:42
  103.2 3.6 %collective-permute-start.21 = (bf16[2,32,1280]{2,1,0:T(8,128)(2,1)S(1)}, bf16[2,32,1280]{2,1,0:T(8,128)(2,1)S(1)}, u32[]{:S(2)}, u32[]{:S(2)}) collective-permute-start(bf16[2,32,1280]{2,1,0:T(8,128)(2,1)S(1)} %get-tuple-element.54), channel_id=1, source_target_pairs={{0,4},{2,6},{4,0},{6,2},{1,5},{3,7},{5,1},{7,3},{8,12},{10,14},{12... | collective-permute-start | bytes 491528 | tf_op jit(solution)/shard_map/ppermute | solution.py:30
  106.8 2.8 %fusion = bf16[1,1280,1280]{2,1,0:T(8,128)(2,1)} fusion(bf16[64,1280]{1,0:T(8,128)(2,1)S(1)} %copy-done.4, bf16[64,1280]{1,0:T(8,128)(2,1)S(1)} %copy-done.13), kind=kOutput, calls=%fused_computation.2 | convolution fusion | flops 211353600 | bytes 3604480 | tf_op jit(solution)/shard_map/sd,sh->dh/dot_general | solution.py:379
  111.2 2.6 %collective-permute-done.21 = bf16[2,32,1280]{2,1,0:T(8,128)(2,1)S(1)} collective-permute-done((bf16[2,32,1280]{2,1,0:T(8,128)(2,1)S(1)}, bf16[2,32,1280]{2,1,0:T(8,128)(2,1)S(1)}, u32[]{:S(2)}, u32[]{:S(2)}) %collective-permute-start.21) | collective-permute-done | bytes 163872 | tf_op jit(solution)/shard_map/ppermute | solution.py:30
  (111 shorter events, 37.6 us)
Async XLA Ops:
  7.2 81.4 %all-gather.3.cloned.1.call-start = ((), (), s32[]{:S(2)}) async-start(), calls=%async_computation | async-start | bytes 1638400 | tf_op jit(solution)/shard_map/all_gather | solution.py:320
  15.7 12.9 %collective-permute-start.2 = (bf16[64,1408]{1,0:T(8,128)(2,1)}, bf16[64,1408]{1,0:T(8,128)(2,1)}, u32[]{:S(2)}, u32[]{:S(2)}) collective-permute-start(bf16[64,1408]{1,0:T(8,128)(2,1)} %get-tuple-element.32.a), channel_id=1, source_target_pairs={{0,32},{32,0},{64,96},{96,64},{1,33},{33,1},{65,97},{97,65},{2,34}... | collective-permute-start | bytes 540680 | tf_op jit(solution)/shard_map/ppermute | solution.py:38
  19.6 6.9 %collective-permute-start = (bf16[64,1280]{1,0:T(8,128)(2,1)S(1)}, bf16[64,1280]{1,0:T(8,128)(2,1)S(1)}, u32[]{:S(2)}, u32[]{:S(2)}) collective-permute-start(bf16[64,1280]{1,0:T(8,128)(2,1)S(1)} %bitcast.72), channel_id=1, source_target_pairs={{0,96},{96,0},{32,64},{64,32},{1,97},{97,1},{33,65},{65,33},{2,98}... | collective-permute-start | bytes 491528 | tf_op jit(solution)/shard_map/ppermute | solution.py:42
  27.2 5.6 %collective-permute-start.1 = (bf16[64,1280]{1,0:T(8,128)(2,1)}, bf16[64,1280]{1,0:T(8,128)(2,1)}, u32[]{:S(2)}, u32[]{:S(2)}) collective-permute-start(bf16[64,1280]{1,0:T(8,128)(2,1)} %add_convert_fusion.5), channel_id=1, source_target_pairs={{0,32},{32,0},{64,96},{96,64},{1,33},{33,1},{65,97},{97,65},{2,34}... | collective-permute-start | bytes 491528 | tf_op jit(solution)/shard_map/ppermute | solution.py:38
  30.1 6.8 %collective-permute-start.3 = (bf16[64,1408]{1,0:T(8,128)(2,1)S(1)}, bf16[64,1408]{1,0:T(8,128)(2,1)S(1)}, u32[]{:S(2)}, u32[]{:S(2)}) collective-permute-start(bf16[64,1408]{1,0:T(8,128)(2,1)S(1)} %merge_pair.1.one), channel_id=1, source_target_pairs={{0,96},{96,0},{32,64},{64,32},{1,97},{97,1},{33,65},{65,33},{2,98}... | collective-permute-start | bytes 540680 | tf_op jit(solution)/shard_map/ppermute | solution.py:42
  38.6 5.4 %collective-permute-start.5 = (bf16[64,1280]{1,0:T(8,128)(2,1)S(1)}, bf16[64,1280]{1,0:T(8,128)(2,1)S(1)}, u32[]{:S(2)}, u32[]{:S(2)}) collective-permute-start(bf16[64,1280]{1,0:T(8,128)(2,1)S(1)} %fusion.19), channel_id=1, source_target_pairs={{0,32},{32,0},{64,96},{96,64},{1,33},{33,1},{65,97},{97,65},{2,34}... | collective-permute-start | bytes 491528 | tf_op jit(solution)/shard_map/ppermute | solution.py:38
  41.1 6.7 %collective-permute-start.4 = (bf16[64,1280]{1,0:T(8,128)(2,1)S(1)}, bf16[64,1280]{1,0:T(8,128)(2,1)S(1)}, u32[]{:S(2)}, u32[]{:S(2)}) collective-permute-start(bf16[64,1280]{1,0:T(8,128)(2,1)S(1)} %fusion.16), channel_id=1, source_target_pairs={{0,96},{96,0},{32,64},{64,32},{1,97},{97,1},{33,65},{65,33},{2,98}... | collective-permute-start | bytes 491528 | tf_op jit(solution)/shard_map/ppermute | solution.py:42
  44.0 6.6 %collective-permute-start.6 = (bf16[64,1280]{1,0:T(8,128)(2,1)S(1)}, bf16[64,1280]{1,0:T(8,128)(2,1)S(1)}, u32[]{:S(2)}, u32[]{:S(2)}) collective-permute-start(bf16[64,1280]{1,0:T(8,128)(2,1)S(1)} %add_convert_fusion.2.sum_a), channel_id=1, source_target_pairs={{0,96},{96,0},{32,64},{64,32},{1,97},{97,1},{33,65},{65,33},{2,98}... | collective-permute-start | bytes 491528 | tf_op jit(solution)/shard_map/ppermute | solution.py:42
  47.9 7.8 %collective-permute-start.7 = (bf16[64,1280]{1,0:T(8,128)(2,1)S(1)}, bf16[64,1280]{1,0:T(8,128)(2,1)S(1)}, u32[]{:S(2)}, u32[]{:S(2)}) collective-permute-start(bf16[64,1280]{1,0:T(8,128)(2,1)S(1)} %add_convert_fusion.3), channel_id=1, source_target_pairs={{0,32},{32,0},{64,96},{96,64},{1,33},{33,1},{65,97},{97,65},{2,34}... | collective-permute-start | bytes 491528 | tf_op jit(solution)/shard_map/ppermute | solution.py:38
  54.2 8.1 %collective-permute-start.12 = (f32[2,1,1024]{2,1,0:T(1,128)S(1)}, f32[2,1,1024]{2,1,0:T(1,128)S(1)}, u32[]{:S(2)}, u32[]{:S(2)}) collective-permute-start(f32[2,1,1024]{2,1,0:T(1,128)S(1)} %add.67), channel_id=1, source_target_pairs={{0,2},{2,0},{4,6},{6,4},{1,3},{3,1},{5,7},{7,5},{8,10},{10,8},{12,... | collective-permute-start | bytes 24584 | tf_op jit(solution)/shard_map/ppermute | solution.py:38
  56.4 32.2 %collective-permute-start.10 = (bf16[64,1280]{1,0:T(8,128)(2,1)}, bf16[64,1280]{1,0:T(8,128)(2,1)}, u32[]{:S(2)}, u32[]{:S(2)}) collective-permute-start(bf16[64,1280]{1,0:T(8,128)(2,1)} %add_convert_fusion.1.gslot.refs_0_), channel_id=1, source_target_pairs={{0,8},{8,16},{16,24},{24,0},{1,9},{9,17},{17,25},{25,1},{2,10},{10... | collective-permute-start | bytes 491528 | tf_op jit(solution)/shard_map/ppermute | solution.py:30
  58.0 30.6 %collective-permute-start.9 = (bf16[64,1280]{1,0:T(8,128)(2,1)}, bf16[64,1280]{1,0:T(8,128)(2,1)}, u32[]{:S(2)}, u32[]{:S(2)}) collective-permute-start(bf16[64,1280]{1,0:T(8,128)(2,1)} %add_convert_fusion.1.gslot.refs_0_), channel_id=1, source_target_pairs={{0,16},{8,24},{16,0},{24,8},{1,17},{9,25},{17,1},{25,9},{2,18},{10... | collective-permute-start | bytes 491528 | tf_op jit(solution)/shard_map/ppermute | solution.py:30
  60.9 27.7 %collective-permute-start.8 = (bf16[64,1280]{1,0:T(8,128)(2,1)}, bf16[64,1280]{1,0:T(8,128)(2,1)}, u32[]{:S(2)}, u32[]{:S(2)}) collective-permute-start(bf16[64,1280]{1,0:T(8,128)(2,1)} %add_convert_fusion.1.gslot.refs_0_), channel_id=1, source_target_pairs={{0,24},{8,0},{16,8},{24,16},{1,25},{9,1},{17,9},{25,17},{2,26},{10... | collective-permute-start | bytes 491528 | tf_op jit(solution)/shard_map/ppermute | solution.py:30
  67.2 15.6 %collective-permute-start.13 = (bf16[64,512]{1,0:T(8,128)(2,1)S(1)}, bf16[64,512]{1,0:T(8,128)(2,1)S(1)}, u32[]{:S(2)}, u32[]{:S(2)}) collective-permute-start(bf16[64,512]{1,0:T(8,128)(2,1)S(1)} %get-tuple-element.43), channel_id=1, source_target_pairs={{0,24},{8,0},{16,8},{24,16},{1,25},{9,1},{17,9},{25,17},{2,26},{10... | collective-permute-start | bytes 196616 | tf_op jit(solution)/shard_map/ppermute | solution.py:30
  67.2 4.9 %collective-permute-start.16 = (f32[2,1,1024]{2,1,0:T(1,128)S(1)}, f32[2,1,1024]{2,1,0:T(1,128)S(1)}, u32[]{:S(2)}, u32[]{:S(2)}) collective-permute-start(f32[2,1,1024]{2,1,0:T(1,128)S(1)} %add.68), channel_id=1, source_target_pairs={{0,6},{6,0},{2,4},{4,2},{1,7},{7,1},{3,5},{5,3},{8,14},{14,8},{10,... | collective-permute-start | bytes 24584 | tf_op jit(solution)/shard_map/ppermute | solution.py:42
  75.8 5.0 %collective-permute-start.18 = (f32[2,1,1024]{2,1,0:T(1,128)S(1)}, f32[2,1,1024]{2,1,0:T(1,128)S(1)}, u32[]{:S(2)}, u32[]{:S(2)}) collective-permute-start(f32[2,1,1024]{2,1,0:T(1,128)S(1)} %add.70), channel_id=1, source_target_pairs={{0,24},{24,0},{8,16},{16,8},{1,25},{25,1},{9,17},{17,9},{2,26},{26... | collective-permute-start | bytes 24584 | tf_op jit(solution)/shard_map/ppermute | solution.py:42
  80.8 6.1 %collective-permute-start.14 = (bf16[64,512]{1,0:T(8,128)(2,1)}, bf16[64,512]{1,0:T(8,128)(2,1)}, u32[]{:S(2)}, u32[]{:S(2)}) collective-permute-start(bf16[64,512]{1,0:T(8,128)(2,1)} %get-tuple-element.44), channel_id=1, source_target_pairs={{0,16},{8,24},{16,0},{24,8},{1,17},{9,25},{17,1},{25,9},{2,18},{10... | collective-permute-start | bytes 196616 | tf_op jit(solution)/shard_map/ppermute | solution.py:30
  82.8 5.8 %collective-permute-start.15 = (bf16[64,512]{1,0:T(8,128)(2,1)}, bf16[64,512]{1,0:T(8,128)(2,1)}, u32[]{:S(2)}, u32[]{:S(2)}) collective-permute-start(bf16[64,512]{1,0:T(8,128)(2,1)} %get-tuple-element.45), channel_id=1, source_target_pairs={{0,8},{8,16},{16,24},{24,0},{1,9},{9,17},{17,25},{25,1},{2,10},{10... | collective-permute-start | bytes 196616 | tf_op jit(solution)/shard_map/ppermute | solution.py:30
  91.8 8.8 %collective-permute-start.19 = (bf16[4,2,32,1280]{3,2,1,0:T(8,128)(2,1)S(1)}, bf16[4,2,32,1280]{3,2,1,0:T(8,128)(2,1)S(1)}, u32[]{:S(2)}, u32[]{:S(2)}) collective-permute-start(bf16[4,2,32,1280]{3,2,1,0:T(8,128)(2,1)S(1)} %get-tuple-element.51), channel_id=1, source_target_pairs={{0,1},{1,0},{2,3},{3,2},{4,5},{5,4},{6,7},{7,6},{8,9},{9,8},{10,11... | collective-permute-start | bytes 1966088 | tf_op jit(solution)/shard_map/ppermute | solution.py:34
  95.6 4.9 %collective-permute-start.23 = (bf16[32,1280]{1,0:T(8,128)(2,1)S(1)}, bf16[32,1280]{1,0:T(8,128)(2,1)S(1)}, u32[]{:S(2)}, u32[]{:S(2)}) collective-permute-start(bf16[32,1280]{1,0:T(8,128)(2,1)S(1)} %fusion.22), channel_id=1, source_target_pairs={{0,32},{32,0},{64,96},{96,64},{1,33},{33,1},{65,97},{97,65},{2,34}... | collective-permute-start | bytes 245768 | tf_op jit(solution)/shard_map/ppermute | solution.py:38
  100.8 8.8 %collective-permute-start.24 = (bf16[32,1280]{1,0:T(8,128)(2,1)S(1)}, bf16[32,1280]{1,0:T(8,128)(2,1)S(1)}, u32[]{:S(2)}, u32[]{:S(2)}) collective-permute-start(bf16[32,1280]{1,0:T(8,128)(2,1)S(1)} %add_convert_fusion.6), channel_id=1, source_target_pairs={{0,96},{96,0},{32,64},{64,32},{1,97},{97,1},{33,65},{65,33},{2,98}... | collective-permute-start | bytes 245768 | tf_op jit(solution)/shard_map/ppermute | solution.py:42
  103.2 8.0 %collective-permute-start.20 = (bf16[2,32,1280]{2,1,0:T(8,128)(2,1)S(1)}, bf16[2,32,1280]{2,1,0:T(8,128)(2,1)S(1)}, u32[]{:S(2)}, u32[]{:S(2)}) collective-permute-start(bf16[2,32,1280]{2,1,0:T(8,128)(2,1)S(1)} %get-tuple-element.53), channel_id=1, source_target_pairs={{0,2},{2,4},{4,6},{6,0},{1,3},{3,5},{5,7},{7,1},{8,10},{10,12},{12... | collective-permute-start | bytes 491528 | tf_op jit(solution)/shard_map/ppermute | solution.py:30
  103.2 10.6 %collective-permute-start.21 = (bf16[2,32,1280]{2,1,0:T(8,128)(2,1)S(1)}, bf16[2,32,1280]{2,1,0:T(8,128)(2,1)S(1)}, u32[]{:S(2)}, u32[]{:S(2)}) collective-permute-start(bf16[2,32,1280]{2,1,0:T(8,128)(2,1)S(1)} %get-tuple-element.54), channel_id=1, source_target_pairs={{0,4},{2,6},{4,0},{6,2},{1,5},{3,7},{5,1},{7,3},{8,12},{10,14},{12... | collective-permute-start | bytes 491528 | tf_op jit(solution)/shard_map/ppermute | solution.py:30
  106.7 7.3 %collective-permute-start.22 = (bf16[2,32,1280]{2,1,0:T(8,128)(2,1)S(1)}, bf16[2,32,1280]{2,1,0:T(8,128)(2,1)S(1)}, u32[]{:S(2)}, u32[]{:S(2)}) collective-permute-start(bf16[2,32,1280]{2,1,0:T(8,128)(2,1)S(1)} %get-tuple-element.55), channel_id=1, source_target_pairs={{0,6},{2,0},{4,2},{6,4},{1,7},{3,1},{5,3},{7,5},{8,14},{10,8},{12,... | collective-permute-start | bytes 491528 | tf_op jit(solution)/shard_map/ppermute | solution.py:30
  (25 other events, 252.2 us)
Sparse Core Ops, SparseCore 0:
  28.7 26.6 all-gather.2

commit v5 on v4

--- a/solution.py
+++ b/solution.py
@@ -72,7 +72,7 @@
     return lanes[:, 0:1] + lanes[:, 1:2] + lanes[:, 2:3]
 
 
-def softmax_kernel(tok, embed, logits, part, peak, total, sums):
+def softmax_kernel(t00, t01, t10, t11, embed, logits, part, peak, total, sums):
     step = pl.program_id(0)
 
     @pl.when(step == 0)
@@ -81,8 +81,14 @@
         total[...] = jnp.zeros_like(total)
         sums[...] = jnp.zeros_like(sums)
 
+    slots = embed[...]
+    blocks = [[t00[0], t01[0]], [t10[0], t11[0]]]
     scores = [
-        lax.dot_general(tok[i], embed[...], NT, preferred_element_type=F32).T for i in range(2)
+        jnp.concatenate(
+            [lax.dot_general(one, slots, NT, preferred_element_type=F32).T for one in pair],
+            axis=1,
+        )
+        for pair in blocks
     ]
     for i in range(2):
         half = slice(32 * i, 32 * i + 32)
@@ -92,9 +98,12 @@
         scale = jnp.exp(before - top)
         weight = jnp.exp(scores[i] - top)
         new_total = total[half, :1] * scale + jnp.sum(weight, axis=1, keepdims=True)
-        new_sums = sums[half, :] * scale + jnp.dot(
-            weight.astype(BF16), tok[i], preferred_element_type=F32
-        )
+        weight = weight.astype(BF16)
+        new_sums = sums[half, :] * scale
+        for n in range(2):
+            new_sums = new_sums + jnp.dot(
+                weight[:, 256 * n : 256 * n + 256], blocks[i][n], preferred_element_type=F32
+            )
         peak[half, :] = jnp.broadcast_to(top, (32, 128))
         total[half, :] = jnp.broadcast_to(new_total, (32, 128))
         sums[half, :] = new_sums
@@ -114,7 +123,10 @@
         softmax_kernel,
         grid=(2,),
         in_specs=[
-            pl.BlockSpec((2, 512, 1280), lambda t: (0, t, 0)),
+            pl.BlockSpec((1, 256, 1280), lambda t: (0, 2 * t, 0)),
+            pl.BlockSpec((1, 256, 1280), lambda t: (0, 2 * t + 1, 0)),
+            pl.BlockSpec((1, 256, 1280), lambda t: (1, 2 * t, 0)),
+            pl.BlockSpec((1, 256, 1280), lambda t: (1, 2 * t + 1, 0)),
             pl.BlockSpec((32, 1280), lambda t: (0, 0)),
         ],
         out_specs=[
@@ -130,7 +142,7 @@
         cost_estimate=pl.CostEstimate(flops=700_000_000, bytes_accessed=6_000_000, transcendentals=65536),
         compiler_params=LARGE,
         name="local_softmax",
-    )(in_hbm(tokens), embed)
+    )(*[in_hbm(tokens)] * 4, embed)
 
 
 def merge_kernel(one, two, sums, lse):
@@ -196,100 +208,136 @@
     )(grad_out, sum_a, sum_b, comb)
 
 
-def dispatch_grad_kernel(tok, gslot, slot_in, logits, lse, comb, gcomb, full, c0, c1, c2, c3, all_grad, all_weight):
-    step = pl.program_id(1)
+def dispatch_grad_kernel(tok, gslot, slot_in, logits, lse, comb, gcomb, full, c0, c1, c2, c3, all_weight):
     rows = gslot[...]
     col_dot = jnp.sum(slot_in[...].astype(F32) * rows.astype(F32), axis=1, keepdims=True)
     grad = lax.dot_general(tok[0], rows, NT, preferred_element_type=F32).T
     weight = jnp.exp(logits[...] - lse[:, :1])
-    value = weight * (grad - col_dot) + comb[...].astype(F32) * gcomb[...]
-    full[...] = value
-    span = pl.ds(pl.multiple_of(step * 512, 512), 512)
-    all_grad[:, span] = value
-    all_weight[:, span] = weight
-
-    @pl.when(step == pl.num_programs(1) - 1)
-    def _():
-        for k, out in enumerate((c0, c1, c2, c3)):
-            piece = pl.ds(chunk("y", k, 256), 256)
-            out[:, :256] = all_grad[:, piece].astype(BF16)
-            out[:, 256:] = all_weight[:, piece].astype(BF16)
+    full[...] = weight * (grad - col_dot) + comb[...].astype(F32) * gcomb[...]
+    all_weight[...] = weight
+    for k, out in enumerate((c0, c1, c2, c3)):
+        piece = pl.ds(chunk("y", k, 256), 256)
+        out[:, :1280] = rows
+        out[:, 1280:1536] = full[:, piece].astype(BF16)
+        out[:, 1536:] = all_weight[:, piece].astype(BF16)
 
 
 def dispatch_grad(tokens, gslot, slot_in, logits, lse, comb, gcomb):
-    rows = pl.BlockSpec((32, 1280), lambda i, t: (i, 0))
-    wide = pl.BlockSpec((32, 512), lambda i, t: (i, t))
-    part = pl.BlockSpec((32, 512), lambda i, t: (i, 0))
+    rows = pl.BlockSpec((32, 1280), lambda i: (i, 0))
+    wide = pl.BlockSpec((32, 1024), lambda i: (i, 0))
+    part = pl.BlockSpec((32, 1792), lambda i: (i, 0))
     return pl.pallas_call(
         dispatch_grad_kernel,
-        grid=(2, 2),
+        grid=(2,),
         in_specs=[
-            pl.BlockSpec((1, 512, 1280), lambda i, t: (i, t, 0)),
+            pl.BlockSpec((1, 1024, 1280), lambda i: (i, 0, 0)),
             rows,
             rows,
             wide,
-            pl.BlockSpec((32, 128), lambda i, t: (i, 0)),
+            pl.BlockSpec((32, 128), lambda i: (i, 0)),
             wide,
             wide,
         ],
         out_specs=[wide] + [part] * 4,
-        out_shape=[shape((64, 1024), F32)] + [shape((64, 512), BF16)] * 4,
-        scratch_shapes=[pltpu.VMEM((32, 1024), F32), pltpu.VMEM((32, 1024), F32)],
+        out_shape=[shape((64, 1024), F32)] + [shape((64, 1792), BF16)] * 4,
+        scratch_shapes=[pltpu.VMEM((32, 1024), F32)],
         cost_estimate=pl.CostEstimate(flops=350_000_000, bytes_accessed=7_000_000, transcendentals=65536),
         compiler_params=MEDIUM,
         name="dispatch_grad",
     )(tokens, gslot, slot_in, logits, lse, comb, gcomb)
 
 
+def inputs_kernel(comb, embed, o0, o1, o2, o3):
+    for k, out in enumerate((o0, o1, o2, o3)):
+        out[:64, :] = comb[:, pl.ds(chunk("y", k, 256), 256)]
+        for n in range(5):
+            out[64 + 32 * n : 96 + 32 * n, :] = embed[:, 256 * n : 256 * n + 256]
+
+
+def input_blocks(comb, embed):
+    return pl.pallas_call(
+        inputs_kernel,
+        out_shape=[shape((224, 256), BF16)] * 4,
+        cost_estimate=pl.CostEstimate(flops=0, bytes_accessed=700_000, transcendentals=0),
+        compiler_params=SMALL,
+        name="input_blocks",
+    )(comb, embed)
+
+
+def embed_grad_kernel(tok, partial_logits, comb, row_dot, out, sums):
+    grad = partial_logits[...] - comb[...].astype(F32) * row_dot[0]
+    value = jnp.dot(grad.astype(BF16), tok[0], preferred_element_type=F32)
+
+    @pl.when(pl.program_id(0) == 0)
+    def _():
+        sums[...] = value
+
+    @pl.when(pl.program_id(0) == 1)
+    def _():
+        out[...] = (sums[...] + value).astype(BF16)
+
+
+def embed_grad(tokens, partial_logits, comb, row_dot):
+    wide = pl.BlockSpec((32, 1024), lambda i: (i, 0))
+    return pl.pallas_call(
+        embed_grad_kernel,
+        grid=(2,),
+        in_specs=[
+            pl.BlockSpec((1, 1024, 1280), lambda i: (i, 0, 0)),
+            wide,
+            wide,
+            pl.BlockSpec((1, 1, 1024), lambda i: (i, 0, 0)),
+        ],
+        out_specs=pl.BlockSpec((32, 1280), lambda i: (0, 0)),
+        out_shape=shape((32, 1280), BF16),
+        scratch_shapes=[pltpu.VMEM((32, 1280), F32)],
+        cost_estimate=pl.CostEstimate(flops=170_000_000, bytes_accessed=6_000_000, transcendentals=0),
+        compiler_params=MEDIUM,
+        name="embed_grad",
+    )(tokens, partial_logits, comb, row_dot)
+
+
 def rows_kernel(*refs):
-    slots, parts = refs[:4], refs[4:8]
-    inputs, row_dot, m0, m1, m2, m3, other, scratch = refs[8:]
-    core, y = lax.axis_index("core"), lax.axis_index("y")
-    mine_span = pl.ds(chunk("y", 0, 256), 256)
+    parts, inputs = refs[:4], refs[4:8]
+    row_dot, mine, other, scratch = refs[8:]
+    core = lax.axis_index("core")
     embeds = [
-        jnp.concatenate(
-            [inputs[(y + k) & 3, 32 * n : 32 * n + 32, 1024:1664] for n in range(2)], axis=1
-        )
-        for k in range(4)
+        jnp.concatenate([one[64 + 32 * n : 96 + 32 * n, :] for n in range(5)], axis=1)
+        for one in inputs
     ]
     for i in range(2):
         half = slice(32 * i, 32 * i + 32)
-        dots = row_dot[i, :, mine_span]
-        weights = [one[half, 256:] for one in parts] + [
-            (
-                part[half, :256].astype(F32)
-                - inputs[(y + k) & 3, half, mine_span].astype(F32) * dots
-            ).astype(BF16)
-            for k, part in enumerate(parts)
+        dots = row_dot[i, :, pl.ds(chunk("y", 0, 256), 256)]
+        weights = [one[half, 1536:] for one in parts] + [
+            (p[half, 1280:1536].astype(F32) - c[half, :].astype(F32) * dots).astype(BF16)
+            for p, c in zip(parts, inputs)
         ]
-        rows = [one[half, :] for one in slots] + embeds
+        rows = [one[half, :1280] for one in parts] + embeds
         scratch[i] = lax.dot_general(
             jnp.concatenate(weights), jnp.concatenate(rows), TN, preferred_element_type=F32
         )
-        for k, mine in enumerate((m0, m1, m2, m3)):
+        for k in range(4):
             base = ((lax.axis_index("x") + k) & 3) * 64
             here = pl.multiple_of(base + core * 32, 32)
             there = pl.multiple_of(base + (1 - core) * 32, 32)
-            mine[i] = scratch[i, pl.ds(here, 32), :].astype(BF16)
+            mine[k, i] = scratch[i, pl.ds(here, 32), :].astype(BF16)
             other[k, i] = scratch[i, pl.ds(there, 32), :].astype(BF16)
 
 
-def patch_rows(slots, parts, inputs, row_dot):
-    block = shape((2, 32, 1280), BF16)
-    *mine, other = pl.pallas_call(
+def patch_rows(parts, inputs, row_dot):
+    return pl.pallas_call(
         rows_kernel,
-        out_shape=[block] * 4 + [shape((4, 2, 32, 1280), BF16)],
+        out_shape=[shape((4, 2, 32, 1280), BF16)] * 2,
         scratch_shapes=[pltpu.VMEM((2, 256, 1280), F32)],
         cost_estimate=pl.CostEstimate(flops=335_000_000, bytes_accessed=3_000_000, transcendentals=0),
         compiler_params=MEDIUM,
         name="patch_rows",
-    )(*slots, *parts, inputs, row_dot)
-    return mine, other
-
-
-def add_kernel(m0, m1, m2, m3, other, o0, o1, o2, o3):
-    for k, (mine, out) in enumerate(((m0, o0), (m1, o1), (m2, o2), (m3, o3))):
-        out[...] = add(mine[...], other[k])
+    )(*parts, *inputs, row_dot)
+
+
+def add_kernel(mine, other, o0, o1, o2, o3):
+    for k, out in enumerate((o0, o1, o2, o3)):
+        out[...] = add(mine[k], other[k])
 
 
 def add_cores(mine, other):
@@ -299,7 +347,7 @@
         cost_estimate=pl.CostEstimate(flops=327_680, bytes_accessed=2_000_000, transcendentals=0),
         compiler_params=SMALL,
         name="add_cores",
-    )(*mine, other)
+    )(mine, other)
 
 
 def after(value, *others):
@@ -314,22 +362,20 @@
     w_in, w_out = w_in[0], w_out[0]
     embed = slot_embed.T
     comb = jnp.transpose(combine, (0, 2, 1)).reshape(64, 1024)
-    comb_f = comb.astype(F32)
-    inputs = jnp.concatenate([embed[:, :640], embed[:, 640:]], axis=0)
-    inputs = jnp.concatenate([comb, inputs, jnp.zeros((64, 896), BF16)], axis=1)
-    inputs = lax.all_gather(inputs, "y")
 
     logits, part = local_softmax(tokens, embed)
     comb_late = after(comb, part)
-    part = merge_pair(part, near(part))
-
     out_part = jnp.einsum(
         "ijt,itd->ijd", comb_late.reshape(2, 32, 1024), grad_out, preferred_element_type=F32
     )
     out_part = out_part.astype(BF16).reshape(64, 1280)
-    out_part = add(out_part, far(out_part))
+    part = merge_pair(part, near(part))
+    out_other = far(out_part)
+    comb_late = after(comb_late, part)
+    slot_in, lse = merge_last(part, far(part))
+    out_part = add(after(out_part, slot_in), out_other)
+    inputs = sources(scatter_terms(input_blocks(comb_late, embed), "y"))
     grad_slot_out = add(out_part, near(out_part))
-    slot_in, lse = merge_last(part, far(part))
 
     pre_act = jnp.dot(slot_in, w_in, preferred_element_type=F32)
     act, slope = gelu_parts(pre_act)
@@ -337,44 +383,43 @@
     out_sum = jnp.dot(act, w_out, preferred_element_type=F32).astype(BF16)
     grad_slot_out = after(grad_slot_out, out_sum)
     out_sum = add(out_sum, near(out_sum))
-    out_other = far(out_sum)
+    out_sum = after(out_sum, *inputs)
+    sum_other = far(out_sum)
     grad_act = jnp.einsum("sd,hd->sh", grad_slot_out, w_out, preferred_element_type=F32)
     grad_pre = (grad_act * slope).astype(BF16)
     in_sum = jnp.einsum("sh,dh->sd", grad_pre, w_in, preferred_element_type=F32).astype(BF16)
     in_sum = add(in_sum, far(in_sum))
     in_other = near(in_sum)
 
-    grad_combine, row_dot = combine_grad(grad_out, out_sum, out_other, comb)
+    grad_combine, row_dot = combine_grad(grad_out, out_sum, sum_other, comb)
     grad_slot_in = add(after(in_sum, row_dot), in_other)
     row_dot = row_dot + swap_cores(row_dot)
+    late, row_dot = lax.optimization_barrier((grad_slot_in, row_dot))
     row_dot = row_dot + near(row_dot, "x")
-    act_late, late, row_dot = lax.optimization_barrier((act, grad_slot_in, row_dot))
     row_dot = row_dot + far(row_dot, "x")
     row_dot = row_dot + near(row_dot, "y")
     row_dot = row_dot + far(row_dot, "y")
 
-    rows = gather_blocks(grad_slot_in, "y")
-    partial_logits, *chunks = dispatch_grad(
+    partial_logits, *parts = dispatch_grad(
         tokens, late, slot_in, logits, lse, comb, grad_combine
     )
-    chunks = sources(scatter_terms(chunks, "y"))
-
-    mine, other = patch_rows(rows, chunks, inputs, row_dot)
-    sums = add_cores(mine, swap_cores(other))
+    parts = sources(scatter_terms(parts, "y"))
+
+    mine, other = patch_rows(parts, inputs, row_dot)
+    other_core = swap_cores(other)
+
+    partial_logits, mine = lax.optimization_barrier((partial_logits, mine))
+    embed_part = embed_grad(tokens, partial_logits, comb, row_dot)
+    embed_other = near(embed_part)
+    sums = add_cores(mine, other_core)
     terms = scatter_terms(sums, "x")
     grad_tokens = sum(term.astype(F32) for term in terms).astype(BF16)
-
-    grad_logits = partial_logits - comb_f * jnp.repeat(row_dot, 32, axis=1).reshape(64, 1024)
-    grad_logits = grad_logits.astype(BF16).reshape(2, 32, 1024)
-    embed_part = jnp.einsum("ijt,itd->jd", grad_logits, tokens, preferred_element_type=F32)
-    embed_part = embed_part.astype(BF16)
-    embed_part = add(embed_part, near(embed_part))
-    embed_part = after(embed_part, sums[0])
+    embed_part = add(after(embed_part, sums[0]), embed_other)
     embed_sum = add(embed_part, far(embed_part))
     z = lax.axis_index("seq")
     grad_embed = lax.dynamic_slice_in_dim(embed_sum, z * 320, 320, axis=1).T
 
-    slot_late = after(slot_in, sums[0])
+    act_late, slot_late = lax.optimization_barrier((act, slot_in, sums[0]))[:2]
     grad_w_out = jnp.einsum("sh,sd->hd", act_late, grad_slot_out, preferred_element_type=F32)
     grad_w_in = jnp.einsum("sd,sh->dh", slot_late, grad_pre, preferred_element_type=F32)
     return (

time: 122 us -> 94.5 us (0.77)
  between operations: 14.4 us -> 0.99 us
  other arithmetic: 7.17 us -> 2.61 us
  matrix products: 14.6 us -> 11.1 us
  waiting for transfers between devices: 29.7 us -> 26.3 us
  Pallas kernels: 16.7 us -> 13.8 us
  starting transfers between devices: 35.1 us -> 36.4 us
    ppermute x7, waiting for transfers between devices: 4.28 us -> 11.8 us  [near(): return lax.ppermute(value, axis, [(0, 1), (1, 0), (2, 3), (3, 2)])]
    ppermute x9, waiting for transfers between devices: 7.06 us -> 0.02 us  [shift(): return lax.ppermute(value, axis, [(i, (i + by) % 4) for i in range(4)])]
    ppermute x7, waiting for transfers between devices: 17.2 us -> 12.2 us  [far(): return lax.ppermute(value, axis, [(0, 3), (3, 0), (1, 2), (2, 1)])]
    dot_general x1 -> x0, matrix products: 3.54 us -> none  [local(): jnp.einsum('ijt,itd->jd', grad_logits, tokens, preferred_element_type=F32)]
    pallas_call x3 -> x5, Pallas kernels: 12.7 us -> 9.81 us  [the longest x1 5.29 us: local_softmax(): pl.pallas_call(softmax_kernel, grid=(2,), in_specs=[pl.BlockSpec((1, 256,...]
    ppermute x9, starting transfers between devices: 11.6 us -> 13.8 us  [shift(): return lax.ppermute(value, axis, [(i, (i + by) % 4) for i in range(4)])]
    convert_element_type x1 -> x0, other arithmetic: 1.64 us -> none  [local(): grad_logits = grad_logits.astype(BF16).reshape(2, 32, 1024)]
    convert_element_type x6, other arithmetic: 2.57 us -> 1.11 us  [add(): return (one.astype(F32) + two.astype(F32)).astype(BF16)]
  transfers between devices with their start and end apart: 26 -> 25, of which waited for: 16 -> 12; matrix products, arithmetic and copies ran while one was open for 17% -> 13% of each run, Pallas kernels for 7% -> 5%
where the time goes in v5:
time: 94.5 us; the launch traced here: 94 us
  starting transfers between devices  36.4 us (39%)
  waiting for transfers between devices  26.3 us (28%)
  Pallas kernels  13.8 us (15%)
  matrix products  11.1 us (12%)
  local copies, waits for them, and re-layouts  2.84 us (3%)
  other arithmetic  2.61 us (3%)
  between operations  0.99 us (1%)
    ppermute x7, starting transfers between devices, far(): return lax.ppermute(value, axis, [(0, 3), (3, 0), (1, 2), (2, 1)])  14.5 us
    ppermute x9, starting transfers between devices, shift(): return lax.ppermute(value, axis, [(i, (i + by) % 4) for i in range(4)])  13.8 us
    ppermute x7, waiting for transfers between devices, far(): return lax.ppermute(value, axis, [(0, 3), (3, 0), (1, 2), (2, 1)])  12.2 us
    ppermute x7, waiting for transfers between devices, near(): return lax.ppermute(value, axis, [(0, 1), (1, 0), (2, 3), (3, 2)])  11.8 us
    ppermute x7, starting transfers between devices, near(): return lax.ppermute(value, axis, [(0, 1), (1, 0), (2, 3), (3, 2)])  7.99 us
    pallas_call x1, Pallas kernels, local_softmax(): pl.pallas_call(softmax_kernel, grid=(2,), in_specs=[pl.BlockSpec((1, 256,...  5.29 us
    dot_general x1, matrix products, local(): jnp.einsum('sd,sh->dh', slot_late, grad_pre, preferred_element_type=F32)  3.68 us
    unnamed x30, local copies, waits for them, and re-layouts  2.84 us
  transfers between devices with their start and end apart: 25, of which 12 were waited for; matrix products, arithmetic and copies ran while one was open for 13% of the time, Pallas kernels for 5%

profile of v5, /device:TPU:0, one launch (start us, length us, event | category | flops | bytes accessed | tf_op | source)
XLA Modules:
  0.0 94.0 jit_solution(5551552345578674615)
XLA Ops:
  1.7 5.3 %local_softmax.1 = (f32[64,1024]{1,0:T(8,128)S(1)}, bf16[64,1408]{1,0:T(8,128)(2,1)S(1)}) custom-call(bf16[2,1024,1280]{2,1,0:T(8,128)(2,1)} %tok.3, bf16[2,1024,1280]{2,1,0:T(8,128)(2,1)} %tok.3, bf16[2,1024,1280]{2,1,0:T(8,128)(2,1)} %tok.3, bf16[2,1024,1280]{2,1,0:T(8,128)(2,1)} %tok.3, bf16[32,1280]{1,0:T(8,128)(2,1)S(1)} %bitcast.49), custom_call_target="tpu_custom_call" | custom-call | flops 700000000 | bytes 6000000 | tf_op jit(solution)/shard_map/local_softmax/pallas_call | solution.py:122
  7.0 2.1 %collective-permute-start = (bf16[64,1408]{1,0:T(8,128)(2,1)S(1)}, bf16[64,1408]{1,0:T(8,128)(2,1)S(1)}, u32[]{:S(2)}, u32[]{:S(2)}) collective-permute-start(bf16[64,1408]{1,0:T(8,128)(2,1)S(1)} %get-tuple-element.38.a), channel_id=1, source_target_pairs={{0,32},{32,0},{64,96},{96,64},{1,33},{33,1},{65,97},{97,65},{2,34}... | collective-permute-start | bytes 540680 | tf_op jit(solution)/shard_map/ppermute | solution.py:38
  9.1 4.6 %collective-permute-done.b = bf16[64,1408]{1,0:T(8,128)(2,1)S(1)} collective-permute-done((bf16[64,1408]{1,0:T(8,128)(2,1)S(1)}, bf16[64,1408]{1,0:T(8,128)(2,1)S(1)}, u32[]{:S(2)}, u32[]{:S(2)}) %collective-permute-start) | collective-permute-done | bytes 180256 | tf_op jit(solution)/shard_map/ppermute | solution.py:38
  13.9 3.9 %collective-permute-start.1 = (bf16[64,1408]{1,0:T(8,128)(2,1)S(1)}, bf16[64,1408]{1,0:T(8,128)(2,1)S(1)}, u32[]{:S(2)}, u32[]{:S(2)}) collective-permute-start(bf16[64,1408]{1,0:T(8,128)(2,1)S(1)} %merge_pair.1.one), channel_id=1, source_target_pairs={{0,96},{96,0},{32,64},{64,32},{1,97},{97,1},{33,65},{65,33},{2,98}... | collective-permute-start | bytes 540680 | tf_op jit(solution)/shard_map/ppermute | solution.py:42
  18.9 3.1 %collective-permute-start.6 = (bf16[224,256]{1,0:T(8,128)(2,1)S(1)}, bf16[224,256]{1,0:T(8,128)(2,1)S(1)}, u32[]{:S(2)}, u32[]{:S(2)}) collective-permute-start(bf16[224,256]{1,0:T(8,128)(2,1)S(1)} %get-tuple-element.45), channel_id=1, source_target_pairs={{0,24},{8,0},{16,8},{24,16},{1,25},{9,1},{17,9},{25,17},{2,26},{10... | collective-permute-start | bytes 344072 | tf_op jit(solution)/shard_map/ppermute | solution.py:30
  27.0 2.1 %collective-permute-start.5 = (bf16[64,1280]{1,0:T(8,128)(2,1)S(1)}, bf16[64,1280]{1,0:T(8,128)(2,1)S(1)}, u32[]{:S(2)}, u32[]{:S(2)}) collective-permute-start(bf16[64,1280]{1,0:T(8,128)(2,1)S(1)} %fusion.19), channel_id=1, source_target_pairs={{0,32},{32,0},{64,96},{96,64},{1,33},{33,1},{65,97},{97,65},{2,34}... | collective-permute-start | bytes 491528 | tf_op jit(solution)/shard_map/ppermute | solution.py:38
  29.1 2.0 %collective-permute-done.3 = bf16[64,1280]{1,0:T(8,128)(2,1)S(1)} collective-permute-done((bf16[64,1280]{1,0:T(8,128)(2,1)S(1)}, bf16[64,1280]{1,0:T(8,128)(2,1)S(1)}, u32[]{:S(2)}, u32[]{:S(2)}) %collective-permute-start.3) | collective-permute-done | bytes 163872 | tf_op jit(solution)/shard_map/ppermute | solution.py:38
  34.0 3.0 %collective-permute-start.4 = (bf16[64,1280]{1,0:T(8,128)(2,1)S(1)}, bf16[64,1280]{1,0:T(8,128)(2,1)S(1)}, u32[]{:S(2)}, u32[]{:S(2)}) collective-permute-start(bf16[64,1280]{1,0:T(8,128)(2,1)S(1)} %fusion.16), channel_id=1, source_target_pairs={{0,96},{96,0},{32,64},{64,32},{1,97},{97,1},{33,65},{65,33},{2,98}... | collective-permute-start | bytes 491528 | tf_op jit(solution)/shard_map/ppermute | solution.py:42
  37.5 3.3 %collective-permute-done.4 = bf16[64,1280]{1,0:T(8,128)(2,1)S(1)} collective-permute-done((bf16[64,1280]{1,0:T(8,128)(2,1)S(1)}, bf16[64,1280]{1,0:T(8,128)(2,1)S(1)}, u32[]{:S(2)}, u32[]{:S(2)}) %collective-permute-start.4) | collective-permute-done | bytes 163872 | tf_op jit(solution)/shard_map/ppermute | solution.py:42
  41.1 2.7 %collective-permute-done.9.sum_b = bf16[64,1280]{1,0:T(8,128)(2,1)S(1)} collective-permute-done((bf16[64,1280]{1,0:T(8,128)(2,1)S(1)}, bf16[64,1280]{1,0:T(8,128)(2,1)S(1)}, u32[]{:S(2)}, u32[]{:S(2)}) %collective-permute-start.9) | collective-permute-done | bytes 163872 | tf_op jit(solution)/shard_map/ppermute | solution.py:42
  43.7 2.2 %combine_grad.1 = (f32[64,1024]{1,0:T(8,128)S(1)}, f32[2,1,1024]{2,1,0:T(1,128)S(1)}) custom-call(bf16[2,1024,1280]{2,1,0:T(8,128)(2,1)S(1)} %copy-done.1, bf16[64,1280]{1,0:T(8,128)(2,1)S(1)} %add_convert_fusion.2.sum_a, bf16[64,1280]{1,0:T(8,128)(2,1)S(1)} %collective-permute-done.9.sum_b, bf16[64,1024]{1,0:T(8,128)(2,1)S(1)} %bitcast.46), custom_call_target="tpu_custom_call" | custom-call | flops 350000000 | bytes 6000000 | tf_op jit(solution)/shard_map/combine_grad/pallas_call | solution.py:191
  47.3 1.9 %dispatch_grad.1 = (f32[64,1024]{1,0:T(8,128)S(1)}, bf16[64,1792]{1,0:T(8,128)(2,1)S(1)}, bf16[64,1792]{1,0:T(8,128)(2,1)S(1)}, bf16[64,1792]{1,0:T(8,128)(2,1)S(1)}, bf16[64,1792]{1,0:T(8,128)(2,1)S(1)}) custom-call(bf16[2,1024,1280]{2,1,0:T(8,128)(2,1)S(1)} %bitcast.43, bf16[64,1280]{1,0:T(8,128)(2,1)S(1)} %add_convert_fusion.1.gslot, ...), custom_call_target="tpu_custom_call" | custom-call | flops 350000000 | bytes 7000000 | tf_op jit(solution)/shard_map/dispatch_grad/pallas_call | solution.py:229
  49.2 3.1 %collective-permute-start.12 = (bf16[64,1792]{1,0:T(8,128)(2,1)S(1)}, bf16[64,1792]{1,0:T(8,128)(2,1)S(1)}, u32[]{:S(2)}, u32[]{:S(2)}) collective-permute-start(bf16[64,1792]{1,0:T(8,128)(2,1)S(1)} %get-tuple-element.57), channel_id=1, source_target_pairs={{0,24},{8,0},{16,8},{24,16},{1,25},{9,1},{17,9},{25,17},{2,26},{10... | collective-permute-start | bytes 688136 | tf_op jit(solution)/shard_map/ppermute | solution.py:30
  55.4 2.1 %collective-permute-done.15 = f32[2,1,1024]{2,1,0:T(1,128)S(1)} collective-permute-done((f32[2,1,1024]{2,1,0:T(1,128)S(1)}, f32[2,1,1024]{2,1,0:T(1,128)S(1)}, u32[]{:S(2)}, u32[]{:S(2)}) %collective-permute-start.15) | collective-permute-done | bytes 8224 | tf_op jit(solution)/shard_map/ppermute | solution.py:38
  57.5 2.9 %collective-permute-start.16 = (f32[2,1,1024]{2,1,0:T(1,128)S(1)}, f32[2,1,1024]{2,1,0:T(1,128)S(1)}, u32[]{:S(2)}, u32[]{:S(2)}) collective-permute-start(f32[2,1,1024]{2,1,0:T(1,128)S(1)} %add.66), channel_id=1, source_target_pairs={{0,6},{6,0},{2,4},{4,2},{1,7},{7,1},{3,5},{5,3},{8,14},{14,8},{10,... | collective-permute-start | bytes 24584 | tf_op jit(solution)/shard_map/ppermute | solution.py:42
  60.4 2.1 %collective-permute-done.16 = f32[2,1,1024]{2,1,0:T(1,128)S(1)} collective-permute-done((f32[2,1,1024]{2,1,0:T(1,128)S(1)}, f32[2,1,1024]{2,1,0:T(1,128)S(1)}, u32[]{:S(2)}, u32[]{:S(2)}) %collective-permute-start.16) | collective-permute-done | bytes 8224 | tf_op jit(solution)/shard_map/ppermute | solution.py:42
  62.5 2.0 %collective-permute-start.17 = (f32[2,1,1024]{2,1,0:T(1,128)S(1)}, f32[2,1,1024]{2,1,0:T(1,128)S(1)}, u32[]{:S(2)}, u32[]{:S(2)}) collective-permute-start(f32[2,1,1024]{2,1,0:T(1,128)S(1)} %add.67), channel_id=1, source_target_pairs={{0,8},{8,0},{16,24},{24,16},{1,9},{9,1},{17,25},{25,17},{2,10},{10... | collective-permute-start | bytes 24584 | tf_op jit(solution)/shard_map/ppermute | solution.py:38
  64.4 1.8 %collective-permute-done.17 = f32[2,1,1024]{2,1,0:T(1,128)S(1)} collective-permute-done((f32[2,1,1024]{2,1,0:T(1,128)S(1)}, f32[2,1,1024]{2,1,0:T(1,128)S(1)}, u32[]{:S(2)}, u32[]{:S(2)}) %collective-permute-start.17) | collective-permute-done | bytes 8224 | tf_op jit(solution)/shard_map/ppermute | solution.py:38
  66.2 2.4 %collective-permute-start.18 = (f32[2,1,1024]{2,1,0:T(1,128)S(1)}, f32[2,1,1024]{2,1,0:T(1,128)S(1)}, u32[]{:S(2)}, u32[]{:S(2)}) collective-permute-start(f32[2,1,1024]{2,1,0:T(1,128)S(1)} %add.68), channel_id=1, source_target_pairs={{0,24},{24,0},{8,16},{16,8},{1,25},{25,1},{9,17},{17,9},{2,26},{26... | collective-permute-start | bytes 24584 | tf_op jit(solution)/shard_map/ppermute | solution.py:42
  68.6 2.5 %collective-permute-done.18 = f32[2,1,1024]{2,1,0:T(1,128)S(1)} collective-permute-done((f32[2,1,1024]{2,1,0:T(1,128)S(1)}, f32[2,1,1024]{2,1,0:T(1,128)S(1)}, u32[]{:S(2)}, u32[]{:S(2)}) %collective-permute-start.18) | collective-permute-done | bytes 8224 | tf_op jit(solution)/shard_map/ppermute | solution.py:42
  79.8 1.9 %collective-permute-start.24 = (bf16[32,1280]{1,0:T(8,128)(2,1)S(1)}, bf16[32,1280]{1,0:T(8,128)(2,1)S(1)}, u32[]{:S(2)}, u32[]{:S(2)}) collective-permute-start(bf16[32,1280]{1,0:T(8,128)(2,1)S(1)} %add_convert_fusion.6), channel_id=1, source_target_pairs={{0,96},{96,0},{32,64},{64,32},{1,97},{97,1},{33,65},{65,33},{2,98}... | collective-permute-start | bytes 245768 | tf_op jit(solution)/shard_map/ppermute | solution.py:42
  82.0 3.9 %collective-permute-start.21 = (bf16[2,32,1280]{2,1,0:T(8,128)(2,1)S(1)}, bf16[2,32,1280]{2,1,0:T(8,128)(2,1)S(1)}, u32[]{:S(2)}, u32[]{:S(2)}) collective-permute-start(bf16[2,32,1280]{2,1,0:T(8,128)(2,1)S(1)} %get-tuple-element.66), channel_id=1, source_target_pairs={{0,4},{2,6},{4,0},{6,2},{1,5},{3,7},{5,1},{7,3},{8,12},{10,14},{12... | collective-permute-start | bytes 491528 | tf_op jit(solution)/shard_map/ppermute | solution.py:30
  86.1 3.7 %fusion = bf16[1,1280,1280]{2,1,0:T(8,128)(2,1)} fusion(bf16[64,1280]{1,0:T(8,128)(2,1)S(1)} %get-tuple-element.70.slot_in, bf16[64,1280]{1,0:T(8,128)(2,1)} %copy-done.10), kind=kOutput, calls=%fused_computation.2 | convolution fusion | flops 211353600 | bytes 3604480 | tf_op jit(solution)/shard_map/sd,sh->dh/dot_general | solution.py:424
  89.8 2.8 %fusion.1 = bf16[1,1280,1280]{2,1,0:T(8,128)(2,1)} fusion(bf16[64,1280]{1,0:T(8,128)(2,1)S(1)} %copy-done.9, bf16[64,1280]{1,0:T(8,128)(2,1)S(1)} %copy-done.12), kind=kOutput, calls=%fused_computation.3 | convolution fusion | flops 211353600 | bytes 3604480 | tf_op jit(solution)/shard_map/sh,sd->hd/dot_general | solution.py:423
  (86 shorter events, 26.0 us)
Async XLA Ops:
  7.0 6.6 %collective-permute-start = (bf16[64,1408]{1,0:T(8,128)(2,1)S(1)}, bf16[64,1408]{1,0:T(8,128)(2,1)S(1)}, u32[]{:S(2)}, u32[]{:S(2)}) collective-permute-start(bf16[64,1408]{1,0:T(8,128)(2,1)S(1)} %get-tuple-element.38.a), channel_id=1, source_target_pairs={{0,32},{32,0},{64,96},{96,64},{1,33},{33,1},{65,97},{97,65},{2,34}... | collective-permute-start | bytes 540680 | tf_op jit(solution)/shard_map/ppermute | solution.py:38
  13.9 9.8 %collective-permute-start.1 = (bf16[64,1408]{1,0:T(8,128)(2,1)S(1)}, bf16[64,1408]{1,0:T(8,128)(2,1)S(1)}, u32[]{:S(2)}, u32[]{:S(2)}) collective-permute-start(bf16[64,1408]{1,0:T(8,128)(2,1)S(1)} %merge_pair.1.one), channel_id=1, source_target_pairs={{0,96},{96,0},{32,64},{64,32},{1,97},{97,1},{33,65},{65,33},{2,98}... | collective-permute-start | bytes 540680 | tf_op jit(solution)/shard_map/ppermute | solution.py:42
  18.8 6.6 %collective-permute-start.2 = (bf16[64,1280]{1,0:T(8,128)(2,1)S(1)}, bf16[64,1280]{1,0:T(8,128)(2,1)S(1)}, u32[]{:S(2)}, u32[]{:S(2)}) collective-permute-start(bf16[64,1280]{1,0:T(8,128)(2,1)S(1)} %bitcast.51), channel_id=1, source_target_pairs={{0,96},{96,0},{32,64},{64,32},{1,97},{97,1},{33,65},{65,33},{2,98}... | collective-permute-start | bytes 491528 | tf_op jit(solution)/shard_map/ppermute | solution.py:42
  18.9 18.1 %collective-permute-start.6 = (bf16[224,256]{1,0:T(8,128)(2,1)S(1)}, bf16[224,256]{1,0:T(8,128)(2,1)S(1)}, u32[]{:S(2)}, u32[]{:S(2)}) collective-permute-start(bf16[224,256]{1,0:T(8,128)(2,1)S(1)} %get-tuple-element.45), channel_id=1, source_target_pairs={{0,24},{8,0},{16,8},{24,16},{1,25},{9,1},{17,9},{25,17},{2,26},{10... | collective-permute-start | bytes 344072 | tf_op jit(solution)/shard_map/ppermute | solution.py:30
  22.0 15.1 %collective-permute-start.7 = (bf16[224,256]{1,0:T(8,128)(2,1)S(1)}, bf16[224,256]{1,0:T(8,128)(2,1)S(1)}, u32[]{:S(2)}, u32[]{:S(2)}) collective-permute-start(bf16[224,256]{1,0:T(8,128)(2,1)S(1)} %get-tuple-element.46), channel_id=1, source_target_pairs={{0,16},{8,24},{16,0},{24,8},{1,17},{9,25},{17,1},{25,9},{2,18},{10... | collective-permute-start | bytes 344072 | tf_op jit(solution)/shard_map/ppermute | solution.py:30
  22.7 14.4 %collective-permute-start.8 = (bf16[224,256]{1,0:T(8,128)(2,1)S(1)}, bf16[224,256]{1,0:T(8,128)(2,1)S(1)}, u32[]{:S(2)}, u32[]{:S(2)}) collective-permute-start(bf16[224,256]{1,0:T(8,128)(2,1)S(1)} %get-tuple-element.47), channel_id=1, source_target_pairs={{0,8},{8,16},{16,24},{24,0},{1,9},{9,17},{17,25},{25,1},{2,10},{10... | collective-permute-start | bytes 344072 | tf_op jit(solution)/shard_map/ppermute | solution.py:30
  25.4 5.6 %collective-permute-start.3 = (bf16[64,1280]{1,0:T(8,128)(2,1)S(1)}, bf16[64,1280]{1,0:T(8,128)(2,1)S(1)}, u32[]{:S(2)}, u32[]{:S(2)}) collective-permute-start(bf16[64,1280]{1,0:T(8,128)(2,1)S(1)} %add_convert_fusion.5), channel_id=1, source_target_pairs={{0,32},{32,0},{64,96},{96,64},{1,33},{33,1},{65,97},{97,65},{2,34}... | collective-permute-start | bytes 491528 | tf_op jit(solution)/shard_map/ppermute | solution.py:38
  27.0 10.0 %collective-permute-start.5 = (bf16[64,1280]{1,0:T(8,128)(2,1)S(1)}, bf16[64,1280]{1,0:T(8,128)(2,1)S(1)}, u32[]{:S(2)}, u32[]{:S(2)}) collective-permute-start(bf16[64,1280]{1,0:T(8,128)(2,1)S(1)} %fusion.19), channel_id=1, source_target_pairs={{0,32},{32,0},{64,96},{96,64},{1,33},{33,1},{65,97},{97,65},{2,34}... | collective-permute-start | bytes 491528 | tf_op jit(solution)/shard_map/ppermute | solution.py:38
  34.0 6.8 %collective-permute-start.4 = (bf16[64,1280]{1,0:T(8,128)(2,1)S(1)}, bf16[64,1280]{1,0:T(8,128)(2,1)S(1)}, u32[]{:S(2)}, u32[]{:S(2)}) collective-permute-start(bf16[64,1280]{1,0:T(8,128)(2,1)S(1)} %fusion.16), channel_id=1, source_target_pairs={{0,96},{96,0},{32,64},{64,32},{1,97},{97,1},{33,65},{65,33},{2,98}... | collective-permute-start | bytes 491528 | tf_op jit(solution)/shard_map/ppermute | solution.py:42
  37.1 6.6 %collective-permute-start.9 = (bf16[64,1280]{1,0:T(8,128)(2,1)S(1)}, bf16[64,1280]{1,0:T(8,128)(2,1)S(1)}, u32[]{:S(2)}, u32[]{:S(2)}) collective-permute-start(bf16[64,1280]{1,0:T(8,128)(2,1)S(1)} %add_convert_fusion.2.sum_a), channel_id=1, source_target_pairs={{0,96},{96,0},{32,64},{64,32},{1,97},{97,1},{33,65},{65,33},{2,98}... | collective-permute-start | bytes 491528 | tf_op jit(solution)/shard_map/ppermute | solution.py:42
  40.9 6.3 %collective-permute-start.10 = (bf16[64,1280]{1,0:T(8,128)(2,1)S(1)}, bf16[64,1280]{1,0:T(8,128)(2,1)S(1)}, u32[]{:S(2)}, u32[]{:S(2)}) collective-permute-start(bf16[64,1280]{1,0:T(8,128)(2,1)S(1)} %add_convert_fusion.3), channel_id=1, source_target_pairs={{0,32},{32,0},{64,96},{96,64},{1,33},{33,1},{65,97},{97,65},{2,34}... | collective-permute-start | bytes 491528 | tf_op jit(solution)/shard_map/ppermute | solution.py:38
  49.2 22.0 %collective-permute-start.12 = (bf16[64,1792]{1,0:T(8,128)(2,1)S(1)}, bf16[64,1792]{1,0:T(8,128)(2,1)S(1)}, u32[]{:S(2)}, u32[]{:S(2)}) collective-permute-start(bf16[64,1792]{1,0:T(8,128)(2,1)S(1)} %get-tuple-element.57), channel_id=1, source_target_pairs={{0,24},{8,0},{16,8},{24,16},{1,25},{9,1},{17,9},{25,17},{2,26},{10... | collective-permute-start | bytes 688136 | tf_op jit(solution)/shard_map/ppermute | solution.py:30
  52.2 18.9 %collective-permute-start.13 = (bf16[64,1792]{1,0:T(8,128)(2,1)S(1)}, bf16[64,1792]{1,0:T(8,128)(2,1)S(1)}, u32[]{:S(2)}, u32[]{:S(2)}) collective-permute-start(bf16[64,1792]{1,0:T(8,128)(2,1)S(1)} %get-tuple-element.58), channel_id=1, source_target_pairs={{0,16},{8,24},{16,0},{24,8},{1,17},{9,25},{17,1},{25,9},{2,18},{10... | collective-permute-start | bytes 688136 | tf_op jit(solution)/shard_map/ppermute | solution.py:30
  52.9 18.3 %collective-permute-start.14 = (bf16[64,1792]{1,0:T(8,128)(2,1)S(1)}, bf16[64,1792]{1,0:T(8,128)(2,1)S(1)}, u32[]{:S(2)}, u32[]{:S(2)}) collective-permute-start(bf16[64,1792]{1,0:T(8,128)(2,1)S(1)} %get-tuple-element.59), channel_id=1, source_target_pairs={{0,8},{8,16},{16,24},{24,0},{1,9},{9,17},{17,25},{25,1},{2,10},{10... | collective-permute-start | bytes 688136 | tf_op jit(solution)/shard_map/ppermute | solution.py:30
  53.8 3.7 %collective-permute-start.15 = (f32[2,1,1024]{2,1,0:T(1,128)S(1)}, f32[2,1,1024]{2,1,0:T(1,128)S(1)}, u32[]{:S(2)}, u32[]{:S(2)}) collective-permute-start(f32[2,1,1024]{2,1,0:T(1,128)S(1)} %add.65), channel_id=1, source_target_pairs={{0,2},{2,0},{4,6},{6,4},{1,3},{3,1},{5,7},{7,5},{8,10},{10,8},{12,... | collective-permute-start | bytes 24584 | tf_op jit(solution)/shard_map/ppermute | solution.py:38
  57.5 4.9 %collective-permute-start.16 = (f32[2,1,1024]{2,1,0:T(1,128)S(1)}, f32[2,1,1024]{2,1,0:T(1,128)S(1)}, u32[]{:S(2)}, u32[]{:S(2)}) collective-permute-start(f32[2,1,1024]{2,1,0:T(1,128)S(1)} %add.66), channel_id=1, source_target_pairs={{0,6},{6,0},{2,4},{4,2},{1,7},{7,1},{3,5},{5,3},{8,14},{14,8},{10,... | collective-permute-start | bytes 24584 | tf_op jit(solution)/shard_map/ppermute | solution.py:42
  62.5 3.7 %collective-permute-start.17 = (f32[2,1,1024]{2,1,0:T(1,128)S(1)}, f32[2,1,1024]{2,1,0:T(1,128)S(1)}, u32[]{:S(2)}, u32[]{:S(2)}) collective-permute-start(f32[2,1,1024]{2,1,0:T(1,128)S(1)} %add.67), channel_id=1, source_target_pairs={{0,8},{8,0},{16,24},{24,16},{1,9},{9,1},{17,25},{25,17},{2,10},{10... | collective-permute-start | bytes 24584 | tf_op jit(solution)/shard_map/ppermute | solution.py:38
  66.2 4.9 %collective-permute-start.18 = (f32[2,1,1024]{2,1,0:T(1,128)S(1)}, f32[2,1,1024]{2,1,0:T(1,128)S(1)}, u32[]{:S(2)}, u32[]{:S(2)}) collective-permute-start(f32[2,1,1024]{2,1,0:T(1,128)S(1)} %add.68), channel_id=1, source_target_pairs={{0,24},{24,0},{8,16},{16,8},{1,25},{25,1},{9,17},{17,9},{2,26},{26... | collective-permute-start | bytes 24584 | tf_op jit(solution)/shard_map/ppermute | solution.py:42
  72.7 2.4 %collective-permute-start.19 = (bf16[4,2,32,1280]{3,2,1,0:T(8,128)(2,1)}, bf16[4,2,32,1280]{3,2,1,0:T(8,128)(2,1)}, u32[]{:S(2)}, u32[]{:S(2)}) collective-permute-start(bf16[4,2,32,1280]{3,2,1,0:T(8,128)(2,1)} %get-tuple-element.63), channel_id=1, source_target_pairs={{0,1},{1,0},{2,3},{3,2},{4,5},{5,4},{6,7},{7,6},{8,9},{9,8},{10,11... | collective-permute-start | bytes 1966088 | tf_op jit(solution)/shard_map/ppermute | solution.py:34
  73.8 5.0 %collective-permute-start.23 = (bf16[32,1280]{1,0:T(8,128)(2,1)S(1)}, bf16[32,1280]{1,0:T(8,128)(2,1)}, u32[]{:S(2)}, u32[]{:S(2)}) collective-permute-start(bf16[32,1280]{1,0:T(8,128)(2,1)S(1)} %embed_grad.1), channel_id=1, source_target_pairs={{0,32},{32,0},{64,96},{96,64},{1,33},{33,1},{65,97},{97,65},{2,34}... | collective-permute-start | bytes 245768 | tf_op jit(solution)/shard_map/ppermute | solution.py:38
  79.8 12.8 %collective-permute-start.24 = (bf16[32,1280]{1,0:T(8,128)(2,1)S(1)}, bf16[32,1280]{1,0:T(8,128)(2,1)S(1)}, u32[]{:S(2)}, u32[]{:S(2)}) collective-permute-start(bf16[32,1280]{1,0:T(8,128)(2,1)S(1)} %add_convert_fusion.6), channel_id=1, source_target_pairs={{0,96},{96,0},{32,64},{64,32},{1,97},{97,1},{33,65},{65,33},{2,98}... | collective-permute-start | bytes 245768 | tf_op jit(solution)/shard_map/ppermute | solution.py:42
  81.7 11.6 %collective-permute-start.20 = (bf16[2,32,1280]{2,1,0:T(8,128)(2,1)S(1)}, bf16[2,32,1280]{2,1,0:T(8,128)(2,1)S(1)}, u32[]{:S(2)}, u32[]{:S(2)}) collective-permute-start(bf16[2,32,1280]{2,1,0:T(8,128)(2,1)S(1)} %get-tuple-element.65), channel_id=1, source_target_pairs={{0,2},{2,4},{4,6},{6,0},{1,3},{3,5},{5,7},{7,1},{8,10},{10,12},{12... | collective-permute-start | bytes 491528 | tf_op jit(solution)/shard_map/ppermute | solution.py:30
  82.0 11.3 %collective-permute-start.21 = (bf16[2,32,1280]{2,1,0:T(8,128)(2,1)S(1)}, bf16[2,32,1280]{2,1,0:T(8,128)(2,1)S(1)}, u32[]{:S(2)}, u32[]{:S(2)}) collective-permute-start(bf16[2,32,1280]{2,1,0:T(8,128)(2,1)S(1)} %get-tuple-element.66), channel_id=1, source_target_pairs={{0,4},{2,6},{4,0},{6,2},{1,5},{3,7},{5,1},{7,3},{8,12},{10,14},{12... | collective-permute-start | bytes 491528 | tf_op jit(solution)/shard_map/ppermute | solution.py:30
  85.9 7.4 %collective-permute-start.22 = (bf16[2,32,1280]{2,1,0:T(8,128)(2,1)S(1)}, bf16[2,32,1280]{2,1,0:T(8,128)(2,1)S(1)}, u32[]{:S(2)}, u32[]{:S(2)}) collective-permute-start(bf16[2,32,1280]{2,1,0:T(8,128)(2,1)S(1)} %get-tuple-element.67), channel_id=1, source_target_pairs={{0,6},{2,0},{4,2},{6,4},{1,7},{3,1},{5,3},{7,5},{8,14},{10,8},{12,... | collective-permute-start | bytes 491528 | tf_op jit(solution)/shard_map/ppermute | solution.py:30
  (16 other events, 184.7 us)

commit v6 on v5

--- a/solution.py
+++ b/solution.py
@@ -369,12 +369,15 @@
         "ijt,itd->ijd", comb_late.reshape(2, 32, 1024), grad_out, preferred_element_type=F32
     )
     out_part = out_part.astype(BF16).reshape(64, 1280)
-    part = merge_pair(part, near(part))
+    part_other = near(part)
+    part, out_part = lax.optimization_barrier((part, out_part))
     out_other = far(out_part)
+    part = merge_pair(part, part_other)
     comb_late = after(comb_late, part)
     slot_in, lse = merge_last(part, far(part))
-    out_part = add(after(out_part, slot_in), out_other)
-    inputs = sources(scatter_terms(input_blocks(comb_late, embed), "y"))
+    inputs = input_blocks(comb_late, embed)
+    out_part = add(after(out_part, inputs[0]), out_other)
+    inputs = sources(scatter_terms(inputs, "y"))
     grad_slot_out = add(out_part, near(out_part))
 
     pre_act = jnp.dot(slot_in, w_in, preferred_element_type=F32)
@@ -388,6 +391,7 @@
     grad_act = jnp.einsum("sd,hd->sh", grad_slot_out, w_out, preferred_element_type=F32)
     grad_pre = (grad_act * slope).astype(BF16)
     in_sum = jnp.einsum("sh,dh->sd", grad_pre, w_in, preferred_element_type=F32).astype(BF16)
+    in_sum = after(in_sum, out_sum)
     in_sum = add(in_sum, far(in_sum))
     in_other = near(in_sum)
 
@@ -414,19 +418,20 @@
     sums = add_cores(mine, other_core)
     terms = scatter_terms(sums, "x")
     grad_tokens = sum(term.astype(F32) for term in terms).astype(BF16)
-    embed_part = add(after(embed_part, sums[0]), embed_other)
+    act_late, slot_late = lax.optimization_barrier((act, slot_in, sums[0]))[:2]
+    grad_w_out = jnp.einsum("sh,sd->hd", act_late, grad_slot_out, preferred_element_type=F32)
+    grad_w_out = grad_w_out.astype(BF16)
+    grad_w_in = jnp.einsum("sd,sh->dh", slot_late, grad_pre, preferred_element_type=F32)
+
+    embed_part = add(after(embed_part, grad_w_out), embed_other)
     embed_sum = add(embed_part, far(embed_part))
     z = lax.axis_index("seq")
     grad_embed = lax.dynamic_slice_in_dim(embed_sum, z * 320, 320, axis=1).T
-
-    act_late, slot_late = lax.optimization_barrier((act, slot_in, sums[0]))[:2]
-    grad_w_out = jnp.einsum("sh,sd->hd", act_late, grad_slot_out, preferred_element_type=F32)
-    grad_w_in = jnp.einsum("sd,sh->dh", slot_late, grad_pre, preferred_element_type=F32)
     return (
         grad_tokens,
         grad_embed,
         grad_w_in.astype(BF16)[None],
-        grad_w_out.astype(BF16)[None],
+        grad_w_out[None],
     )
 
 

time: 94.5 us -> 91.4 us (0.967)
  waiting for transfers between devices: 26.3 us -> 21.7 us
  local copies, waits for them, and re-layouts: 2.84 us -> 5.39 us
    ppermute x7, waiting for transfers between devices: 11.8 us -> 6.91 us  [near(): return lax.ppermute(value, axis, [(0, 1), (1, 0), (2, 3), (3, 2)])]
    unnamed x30 -> x42, local copies, waits for them, and re-layouts: 2.84 us -> 5.39 us
    ppermute x7, waiting for transfers between devices: 12.2 us -> 13.6 us  [far(): return lax.ppermute(value, axis, [(0, 3), (3, 0), (1, 2), (2, 1)])]
    ppermute x7, starting transfers between devices: 14.5 us -> 15.8 us  [far(): return lax.ppermute(value, axis, [(0, 3), (3, 0), (1, 2), (2, 1)])]
    ppermute x2, waiting for transfers between devices: 2.33 us -> 1.16 us  [swap_cores(): return lax.ppermute(value, 'core', [(0, 1), (1, 0)])]
  transfers between devices with their start and end apart: 25 -> 25, of which waited for: 12 -> 11; matrix products, arithmetic and copies ran while one was open for 13% -> 12% of each run, Pallas kernels for 5% -> 6%
where the time goes in v6:
time: 91.4 us; the launch traced here: 90.9 us
  starting transfers between devices  37.2 us (41%)
  waiting for transfers between devices  21.7 us (24%)
  Pallas kernels  13.8 us (15%)
  matrix products  10.2 us (11%)
  local copies, waits for them, and re-layouts  5.39 us (6%)
  other arithmetic  1.73 us (2%)
  between operations  1.04 us (1%)
    ppermute x7, starting transfers between devices, far(): return lax.ppermute(value, axis, [(0, 3), (3, 0), (1, 2), (2, 1)])  15.8 us
    ppermute x9, starting transfers between devices, shift(): return lax.ppermute(value, axis, [(i, (i + by) % 4) for i in range(4)])  13.8 us
    ppermute x7, waiting for transfers between devices, far(): return lax.ppermute(value, axis, [(0, 3), (3, 0), (1, 2), (2, 1)])  13.6 us
    ppermute x7, starting transfers between devices, near(): return lax.ppermute(value, axis, [(0, 1), (1, 0), (2, 3), (3, 2)])  7.45 us
    ppermute x7, waiting for transfers between devices, near(): return lax.ppermute(value, axis, [(0, 1), (1, 0), (2, 3), (3, 2)])  6.91 us
    unnamed x42, local copies, waits for them, and re-layouts  5.39 us
    pallas_call x1, Pallas kernels, local_softmax(): pl.pallas_call(softmax_kernel, grid=(2,), in_specs=[pl.BlockSpec((1, 256,...  5.29 us
    dot_general x1, matrix products, local(): jnp.einsum('sd,sh->dh', slot_late, grad_pre, preferred_element_type=F32)  2.76 us
  transfers between devices with their start and end apart: 25, of which 11 were waited for; matrix products, arithmetic and copies ran while one was open for 12% of the time, Pallas kernels for 6%

profile of v6, /device:TPU:0, one launch (start us, length us, event | category | flops | bytes accessed | tf_op | source)
XLA Modules:
  0.0 90.9 jit_solution(4448108821837562811)
XLA Ops:
  1.7 5.3 %local_softmax.1 = (f32[64,1024]{1,0:T(8,128)S(1)}, bf16[64,1408]{1,0:T(8,128)(2,1)S(1)}) custom-call(bf16[2,1024,1280]{2,1,0:T(8,128)(2,1)} %tok.3, bf16[2,1024,1280]{2,1,0:T(8,128)(2,1)} %tok.3, bf16[2,1024,1280]{2,1,0:T(8,128)(2,1)} %tok.3, bf16[2,1024,1280]{2,1,0:T(8,128)(2,1)} %tok.3, bf16[32,1280]{1,0:T(8,128)(2,1)S(1)} %bitcast.48), custom_call_target="tpu_custom_call" | custom-call | flops 700000000 | bytes 6000000 | tf_op jit(solution)/shard_map/local_softmax/pallas_call | solution.py:122
  7.0 2.1 %collective-permute-start = (bf16[64,1408]{1,0:T(8,128)(2,1)S(1)}, bf16[64,1408]{1,0:T(8,128)(2,1)S(1)}, u32[]{:S(2)}, u32[]{:S(2)}) collective-permute-start(bf16[64,1408]{1,0:T(8,128)(2,1)S(1)} %get-tuple-element.44.a), channel_id=1, source_target_pairs={{0,32},{32,0},{64,96},{96,64},{1,33},{33,1},{65,97},{97,65},{2,34}... | collective-permute-start | bytes 540680 | tf_op jit(solution)/shard_map/ppermute | solution.py:38
  10.1 2.6 %collective-permute-start.1 = (bf16[64,1280]{1,0:T(8,128)(2,1)S(1)}, bf16[64,1280]{1,0:T(8,128)(2,1)S(1)}, u32[]{:S(2)}, u32[]{:S(2)}) collective-permute-start(bf16[64,1280]{1,0:T(8,128)(2,1)S(1)} %bitcast.51), channel_id=1, source_target_pairs={{0,96},{96,0},{32,64},{64,32},{1,97},{97,1},{33,65},{65,33},{2,98}... | collective-permute-start | bytes 491528 | tf_op jit(solution)/shard_map/ppermute | solution.py:42
  13.9 3.1 %collective-permute-done.1 = bf16[64,1280]{1,0:T(8,128)(2,1)S(1)} collective-permute-done((bf16[64,1280]{1,0:T(8,128)(2,1)S(1)}, bf16[64,1280]{1,0:T(8,128)(2,1)S(1)}, u32[]{:S(2)}, u32[]{:S(2)}) %collective-permute-start.1) | collective-permute-done | bytes 163872 | tf_op jit(solution)/shard_map/ppermute | solution.py:42
  17.7 2.3 %collective-permute-start.3 = (bf16[64,1408]{1,0:T(8,128)(2,1)S(1)}, bf16[64,1408]{1,0:T(8,128)(2,1)S(1)}, u32[]{:S(2)}, u32[]{:S(2)}) collective-permute-start(bf16[64,1408]{1,0:T(8,128)(2,1)S(1)} %merge_pair.1.one), channel_id=1, source_target_pairs={{0,96},{96,0},{32,64},{64,32},{1,97},{97,1},{33,65},{65,33},{2,98}... | collective-permute-start | bytes 540680 | tf_op jit(solution)/shard_map/ppermute | solution.py:42
  20.1 3.0 %collective-permute-start.5 = (bf16[224,256]{1,0:T(8,128)(2,1)S(1)}, bf16[224,256]{1,0:T(8,128)(2,1)S(1)}, u32[]{:S(2)}, u32[]{:S(2)}) collective-permute-start(bf16[224,256]{1,0:T(8,128)(2,1)S(1)} %get-tuple-element.50), channel_id=1, source_target_pairs={{0,24},{8,0},{16,8},{24,16},{1,25},{9,1},{17,9},{25,17},{2,26},{10... | collective-permute-start | bytes 344072 | tf_op jit(solution)/shard_map/ppermute | solution.py:30
  29.8 2.0 %collective-permute-done.4 = bf16[64,1280]{1,0:T(8,128)(2,1)S(1)} collective-permute-done((bf16[64,1280]{1,0:T(8,128)(2,1)S(1)}, bf16[64,1280]{1,0:T(8,128)(2,1)S(1)}, u32[]{:S(2)}, u32[]{:S(2)}) %collective-permute-start.4) | collective-permute-done | bytes 163872 | tf_op jit(solution)/shard_map/ppermute | solution.py:38
  31.9 2.1 %collective-permute-start.8 = (bf16[64,1280]{1,0:T(8,128)(2,1)S(1)}, bf16[64,1280]{1,0:T(8,128)(2,1)S(1)}, u32[]{:S(2)}, u32[]{:S(2)}) collective-permute-start(bf16[64,1280]{1,0:T(8,128)(2,1)S(1)} %fusion.15), channel_id=1, source_target_pairs={{0,96},{96,0},{32,64},{64,32},{1,97},{97,1},{33,65},{65,33},{2,98}... | collective-permute-start | bytes 491528 | tf_op jit(solution)/shard_map/ppermute | solution.py:42
  35.3 3.3 %collective-permute-done.8 = bf16[64,1280]{1,0:T(8,128)(2,1)S(1)} collective-permute-done((bf16[64,1280]{1,0:T(8,128)(2,1)S(1)}, bf16[64,1280]{1,0:T(8,128)(2,1)S(1)}, u32[]{:S(2)}, u32[]{:S(2)}) %collective-permute-start.8) | collective-permute-done | bytes 163872 | tf_op jit(solution)/shard_map/ppermute | solution.py:42
  38.7 1.9 %collective-permute-done.9.sum_b = bf16[64,1280]{1,0:T(8,128)(2,1)S(1)} collective-permute-done((bf16[64,1280]{1,0:T(8,128)(2,1)S(1)}, bf16[64,1280]{1,0:T(8,128)(2,1)S(1)}, u32[]{:S(2)}, u32[]{:S(2)}) %collective-permute-start.9) | collective-permute-done | bytes 163872 | tf_op jit(solution)/shard_map/ppermute | solution.py:42
  40.6 2.2 %combine_grad.1 = (f32[64,1024]{1,0:T(8,128)S(1)}, f32[2,1,1024]{2,1,0:T(1,128)S(1)}) custom-call(bf16[2,1024,1280]{2,1,0:T(8,128)(2,1)S(1)} %copy-done.2, bf16[64,1280]{1,0:T(8,128)(2,1)S(1)} %add_convert_fusion.3.sum_a, bf16[64,1280]{1,0:T(8,128)(2,1)S(1)} %collective-permute-done.9.sum_b, bf16[64,1024]{1,0:T(8,128)(2,1)S(1)} %bitcast.45), custom_call_target="tpu_custom_call" | custom-call | flops 350000000 | bytes 6000000 | tf_op jit(solution)/shard_map/combine_grad/pallas_call | solution.py:191
  44.2 1.9 %dispatch_grad.1 = (f32[64,1024]{1,0:T(8,128)S(1)}, bf16[64,1792]{1,0:T(8,128)(2,1)S(1)}, bf16[64,1792]{1,0:T(8,128)(2,1)S(1)}, bf16[64,1792]{1,0:T(8,128)(2,1)S(1)}, bf16[64,1792]{1,0:T(8,128)(2,1)S(1)}) custom-call(bf16[2,1024,1280]{2,1,0:T(8,128)(2,1)S(1)} %bitcast.42, bf16[64,1280]{1,0:T(8,128)(2,1)S(1)} %add_convert_fusion.1.gslot, ...), custom_call_target="tpu_custom_call" | custom-call | flops 350000000 | bytes 7000000 | tf_op jit(solution)/shard_map/dispatch_grad/pallas_call | solution.py:229
  46.1 3.1 %collective-permute-start.12 = (bf16[64,1792]{1,0:T(8,128)(2,1)S(1)}, bf16[64,1792]{1,0:T(8,128)(2,1)S(1)}, u32[]{:S(2)}, u32[]{:S(2)}) collective-permute-start(bf16[64,1792]{1,0:T(8,128)(2,1)S(1)} %get-tuple-element.63), channel_id=1, source_target_pairs={{0,24},{8,0},{16,8},{24,16},{1,25},{9,1},{17,9},{25,17},{2,26},{10... | collective-permute-start | bytes 688136 | tf_op jit(solution)/shard_map/ppermute | solution.py:30
  52.3 2.2 %collective-permute-done.15 = f32[2,1,1024]{2,1,0:T(1,128)S(1)} collective-permute-done((f32[2,1,1024]{2,1,0:T(1,128)S(1)}, f32[2,1,1024]{2,1,0:T(1,128)S(1)}, u32[]{:S(2)}, u32[]{:S(2)}) %collective-permute-start.15) | collective-permute-done | bytes 8224 | tf_op jit(solution)/shard_map/ppermute | solution.py:38
  54.4 2.8 %collective-permute-start.16 = (f32[2,1,1024]{2,1,0:T(1,128)S(1)}, f32[2,1,1024]{2,1,0:T(1,128)S(1)}, u32[]{:S(2)}, u32[]{:S(2)}) collective-permute-start(f32[2,1,1024]{2,1,0:T(1,128)S(1)} %add.66), channel_id=1, source_target_pairs={{0,6},{6,0},{2,4},{4,2},{1,7},{7,1},{3,5},{5,3},{8,14},{14,8},{10,... | collective-permute-start | bytes 24584 | tf_op jit(solution)/shard_map/ppermute | solution.py:42
  57.3 2.1 %collective-permute-done.16 = f32[2,1,1024]{2,1,0:T(1,128)S(1)} collective-permute-done((f32[2,1,1024]{2,1,0:T(1,128)S(1)}, f32[2,1,1024]{2,1,0:T(1,128)S(1)}, u32[]{:S(2)}, u32[]{:S(2)}) %collective-permute-start.16) | collective-permute-done | bytes 8224 | tf_op jit(solution)/shard_map/ppermute | solution.py:42
  59.4 2.0 %collective-permute-start.17 = (f32[2,1,1024]{2,1,0:T(1,128)S(1)}, f32[2,1,1024]{2,1,0:T(1,128)S(1)}, u32[]{:S(2)}, u32[]{:S(2)}) collective-permute-start(f32[2,1,1024]{2,1,0:T(1,128)S(1)} %add.67), channel_id=1, source_target_pairs={{0,8},{8,0},{16,24},{24,16},{1,9},{9,1},{17,25},{25,17},{2,10},{10... | collective-permute-start | bytes 24584 | tf_op jit(solution)/shard_map/ppermute | solution.py:38
  63.1 2.5 %collective-permute-start.18 = (f32[2,1,1024]{2,1,0:T(1,128)S(1)}, f32[2,1,1024]{2,1,0:T(1,128)S(1)}, u32[]{:S(2)}, u32[]{:S(2)}) collective-permute-start(f32[2,1,1024]{2,1,0:T(1,128)S(1)} %add.68), channel_id=1, source_target_pairs={{0,24},{24,0},{8,16},{16,8},{1,25},{25,1},{9,17},{17,9},{2,26},{26... | collective-permute-start | bytes 24584 | tf_op jit(solution)/shard_map/ppermute | solution.py:42
  65.7 2.4 %collective-permute-done.18 = f32[2,1,1024]{2,1,0:T(1,128)S(1)} collective-permute-done((f32[2,1,1024]{2,1,0:T(1,128)S(1)}, f32[2,1,1024]{2,1,0:T(1,128)S(1)}, u32[]{:S(2)}, u32[]{:S(2)}) %collective-permute-start.18) | collective-permute-done | bytes 8224 | tf_op jit(solution)/shard_map/ppermute | solution.py:42
  70.4 2.5 %copy-done.1 = bf16[2,1024,1280]{2,1,0:T(8,128)(2,1)S(1)} copy-done((bf16[2,1024,1280]{2,1,0:T(8,128)(2,1)S(1)}, bf16[2,1024,1280]{2,1,0:T(8,128)(2,1)}, u32[]{:S(2)}) %copy-start.1) | copy-done | bytes 5242904
  76.8 3.9 %collective-permute-start.21 = (bf16[2,32,1280]{2,1,0:T(8,128)(2,1)S(1)}, bf16[2,32,1280]{2,1,0:T(8,128)(2,1)S(1)}, u32[]{:S(2)}, u32[]{:S(2)}) collective-permute-start(bf16[2,32,1280]{2,1,0:T(8,128)(2,1)S(1)} %get-tuple-element.72), channel_id=1, source_target_pairs={{0,4},{2,6},{4,0},{6,2},{1,5},{3,7},{5,1},{7,3},{8,12},{10,14},{12... | collective-permute-start | bytes 491528 | tf_op jit(solution)/shard_map/ppermute | solution.py:30
  81.0 2.8 %convolution_convert_fusion.1 = bf16[1280,1280]{1,0:T(8,128)(2,1)} fusion(bf16[64,1280]{1,0:T(8,128)(2,1)S(1)} %copy-done.16, bf16[64,1280]{1,0:T(8,128)(2,1)S(1)} %copy-done.18), kind=kOutput, calls=%fused_computation.1 | convolution fusion | flops 211353600 | bytes 3604480 | tf_op jit(solution)/shard_map/sh,sd->hd/dot_general | solution.py:422
  83.7 2.2 %collective-permute-start.24 = (bf16[32,1280]{1,0:T(8,128)(2,1)S(1)}, bf16[32,1280]{1,0:T(8,128)(2,1)S(1)}, u32[]{:S(2)}, u32[]{:S(2)}) collective-permute-start(bf16[32,1280]{1,0:T(8,128)(2,1)S(1)} %add_convert_fusion.6), channel_id=1, source_target_pairs={{0,96},{96,0},{32,64},{64,32},{1,97},{97,1},{33,65},{65,33},{2,98}... | collective-permute-start | bytes 245768 | tf_op jit(solution)/shard_map/ppermute | solution.py:42
  85.9 2.8 %fusion = bf16[1,1280,1280]{2,1,0:T(8,128)(2,1)} fusion(bf16[64,1280]{1,0:T(8,128)(2,1)S(1)} %copy-done.5, bf16[64,1280]{1,0:T(8,128)(2,1)S(1)} %copy-done.14), kind=kOutput, calls=%fused_computation.2 | convolution fusion | flops 211353600 | bytes 3604480 | tf_op jit(solution)/shard_map/sd,sh->dh/dot_general | solution.py:424
  (98 shorter events, 26.8 us)
Async XLA Ops:
  7.0 6.6 %collective-permute-start = (bf16[64,1408]{1,0:T(8,128)(2,1)S(1)}, bf16[64,1408]{1,0:T(8,128)(2,1)S(1)}, u32[]{:S(2)}, u32[]{:S(2)}) collective-permute-start(bf16[64,1408]{1,0:T(8,128)(2,1)S(1)} %get-tuple-element.44.a), channel_id=1, source_target_pairs={{0,32},{32,0},{64,96},{96,64},{1,33},{33,1},{65,97},{97,65},{2,34}... | collective-permute-start | bytes 540680 | tf_op jit(solution)/shard_map/ppermute | solution.py:38
  10.1 7.0 %collective-permute-start.1 = (bf16[64,1280]{1,0:T(8,128)(2,1)S(1)}, bf16[64,1280]{1,0:T(8,128)(2,1)S(1)}, u32[]{:S(2)}, u32[]{:S(2)}) collective-permute-start(bf16[64,1280]{1,0:T(8,128)(2,1)S(1)} %bitcast.51), channel_id=1, source_target_pairs={{0,96},{96,0},{32,64},{64,32},{1,97},{97,1},{33,65},{65,33},{2,98}... | collective-permute-start | bytes 491528 | tf_op jit(solution)/shard_map/ppermute | solution.py:42
  17.1 7.6 %collective-permute-start.2 = (bf16[64,1280]{1,0:T(8,128)(2,1)S(1)}, bf16[64,1280]{1,0:T(8,128)(2,1)S(1)}, u32[]{:S(2)}, u32[]{:S(2)}) collective-permute-start(bf16[64,1280]{1,0:T(8,128)(2,1)S(1)} %add_convert_fusion.5), channel_id=1, source_target_pairs={{0,32},{32,0},{64,96},{96,64},{1,33},{33,1},{65,97},{97,65},{2,34}... | collective-permute-start | bytes 491528 | tf_op jit(solution)/shard_map/ppermute | solution.py:38
  17.7 7.0 %collective-permute-start.3 = (bf16[64,1408]{1,0:T(8,128)(2,1)S(1)}, bf16[64,1408]{1,0:T(8,128)(2,1)S(1)}, u32[]{:S(2)}, u32[]{:S(2)}) collective-permute-start(bf16[64,1408]{1,0:T(8,128)(2,1)S(1)} %merge_pair.1.one), channel_id=1, source_target_pairs={{0,96},{96,0},{32,64},{64,32},{1,97},{97,1},{33,65},{65,33},{2,98}... | collective-permute-start | bytes 540680 | tf_op jit(solution)/shard_map/ppermute | solution.py:42
  20.1 11.8 %collective-permute-start.5 = (bf16[224,256]{1,0:T(8,128)(2,1)S(1)}, bf16[224,256]{1,0:T(8,128)(2,1)S(1)}, u32[]{:S(2)}, u32[]{:S(2)}) collective-permute-start(bf16[224,256]{1,0:T(8,128)(2,1)S(1)} %get-tuple-element.50), channel_id=1, source_target_pairs={{0,24},{8,0},{16,8},{24,16},{1,25},{9,1},{17,9},{25,17},{2,26},{10... | collective-permute-start | bytes 344072 | tf_op jit(solution)/shard_map/ppermute | solution.py:30
  23.1 8.8 %collective-permute-start.6 = (bf16[224,256]{1,0:T(8,128)(2,1)S(1)}, bf16[224,256]{1,0:T(8,128)(2,1)S(1)}, u32[]{:S(2)}, u32[]{:S(2)}) collective-permute-start(bf16[224,256]{1,0:T(8,128)(2,1)S(1)} %get-tuple-element.51), channel_id=1, source_target_pairs={{0,16},{8,24},{16,0},{24,8},{1,17},{9,25},{17,1},{25,9},{2,18},{10... | collective-permute-start | bytes 344072 | tf_op jit(solution)/shard_map/ppermute | solution.py:30
  23.7 8.2 %collective-permute-start.7 = (bf16[224,256]{1,0:T(8,128)(2,1)S(1)}, bf16[224,256]{1,0:T(8,128)(2,1)S(1)}, u32[]{:S(2)}, u32[]{:S(2)}) collective-permute-start(bf16[224,256]{1,0:T(8,128)(2,1)S(1)} %get-tuple-element.52), channel_id=1, source_target_pairs={{0,8},{8,16},{16,24},{24,0},{1,9},{9,17},{17,25},{25,1},{2,10},{10... | collective-permute-start | bytes 344072 | tf_op jit(solution)/shard_map/ppermute | solution.py:30
  26.5 5.4 %collective-permute-start.4 = (bf16[64,1280]{1,0:T(8,128)(2,1)S(1)}, bf16[64,1280]{1,0:T(8,128)(2,1)S(1)}, u32[]{:S(2)}, u32[]{:S(2)}) collective-permute-start(bf16[64,1280]{1,0:T(8,128)(2,1)S(1)} %fusion.18), channel_id=1, source_target_pairs={{0,32},{32,0},{64,96},{96,64},{1,33},{33,1},{65,97},{97,65},{2,34}... | collective-permute-start | bytes 491528 | tf_op jit(solution)/shard_map/ppermute | solution.py:38
  31.9 6.6 %collective-permute-start.8 = (bf16[64,1280]{1,0:T(8,128)(2,1)S(1)}, bf16[64,1280]{1,0:T(8,128)(2,1)S(1)}, u32[]{:S(2)}, u32[]{:S(2)}) collective-permute-start(bf16[64,1280]{1,0:T(8,128)(2,1)S(1)} %fusion.15), channel_id=1, source_target_pairs={{0,96},{96,0},{32,64},{64,32},{1,97},{97,1},{33,65},{65,33},{2,98}... | collective-permute-start | bytes 491528 | tf_op jit(solution)/shard_map/ppermute | solution.py:42
  34.0 6.5 %collective-permute-start.9 = (bf16[64,1280]{1,0:T(8,128)(2,1)S(1)}, bf16[64,1280]{1,0:T(8,128)(2,1)S(1)}, u32[]{:S(2)}, u32[]{:S(2)}) collective-permute-start(bf16[64,1280]{1,0:T(8,128)(2,1)S(1)} %add_convert_fusion.3.sum_a), channel_id=1, source_target_pairs={{0,96},{96,0},{32,64},{64,32},{1,97},{97,1},{33,65},{65,33},{2,98}... | collective-permute-start | bytes 491528 | tf_op jit(solution)/shard_map/ppermute | solution.py:42
  38.6 5.5 %collective-permute-start.10 = (bf16[64,1280]{1,0:T(8,128)(2,1)S(1)}, bf16[64,1280]{1,0:T(8,128)(2,1)S(1)}, u32[]{:S(2)}, u32[]{:S(2)}) collective-permute-start(bf16[64,1280]{1,0:T(8,128)(2,1)S(1)} %add_convert_fusion.2), channel_id=1, source_target_pairs={{0,32},{32,0},{64,96},{96,64},{1,33},{33,1},{65,97},{97,65},{2,34}... | collective-permute-start | bytes 491528 | tf_op jit(solution)/shard_map/ppermute | solution.py:38
  46.1 22.0 %collective-permute-start.12 = (bf16[64,1792]{1,0:T(8,128)(2,1)S(1)}, bf16[64,1792]{1,0:T(8,128)(2,1)S(1)}, u32[]{:S(2)}, u32[]{:S(2)}) collective-permute-start(bf16[64,1792]{1,0:T(8,128)(2,1)S(1)} %get-tuple-element.63), channel_id=1, source_target_pairs={{0,24},{8,0},{16,8},{24,16},{1,25},{9,1},{17,9},{25,17},{2,26},{10... | collective-permute-start | bytes 688136 | tf_op jit(solution)/shard_map/ppermute | solution.py:30
  49.2 18.9 %collective-permute-start.13 = (bf16[64,1792]{1,0:T(8,128)(2,1)S(1)}, bf16[64,1792]{1,0:T(8,128)(2,1)S(1)}, u32[]{:S(2)}, u32[]{:S(2)}) collective-permute-start(bf16[64,1792]{1,0:T(8,128)(2,1)S(1)} %get-tuple-element.64), channel_id=1, source_target_pairs={{0,16},{8,24},{16,0},{24,8},{1,17},{9,25},{17,1},{25,9},{2,18},{10... | collective-permute-start | bytes 688136 | tf_op jit(solution)/shard_map/ppermute | solution.py:30
  50.0 18.1 %collective-permute-start.14 = (bf16[64,1792]{1,0:T(8,128)(2,1)S(1)}, bf16[64,1792]{1,0:T(8,128)(2,1)S(1)}, u32[]{:S(2)}, u32[]{:S(2)}) collective-permute-start(bf16[64,1792]{1,0:T(8,128)(2,1)S(1)} %get-tuple-element.65), channel_id=1, source_target_pairs={{0,8},{8,16},{16,24},{24,0},{1,9},{9,17},{17,25},{25,1},{2,10},{10... | collective-permute-start | bytes 688136 | tf_op jit(solution)/shard_map/ppermute | solution.py:30
  50.8 3.7 %collective-permute-start.15 = (f32[2,1,1024]{2,1,0:T(1,128)S(1)}, f32[2,1,1024]{2,1,0:T(1,128)S(1)}, u32[]{:S(2)}, u32[]{:S(2)}) collective-permute-start(f32[2,1,1024]{2,1,0:T(1,128)S(1)} %add.65), channel_id=1, source_target_pairs={{0,2},{2,0},{4,6},{6,4},{1,3},{3,1},{5,7},{7,5},{8,10},{10,8},{12,... | collective-permute-start | bytes 24584 | tf_op jit(solution)/shard_map/ppermute | solution.py:38
  54.4 4.9 %collective-permute-start.16 = (f32[2,1,1024]{2,1,0:T(1,128)S(1)}, f32[2,1,1024]{2,1,0:T(1,128)S(1)}, u32[]{:S(2)}, u32[]{:S(2)}) collective-permute-start(f32[2,1,1024]{2,1,0:T(1,128)S(1)} %add.66), channel_id=1, source_target_pairs={{0,6},{6,0},{2,4},{4,2},{1,7},{7,1},{3,5},{5,3},{8,14},{14,8},{10,... | collective-permute-start | bytes 24584 | tf_op jit(solution)/shard_map/ppermute | solution.py:42
  59.4 3.7 %collective-permute-start.17 = (f32[2,1,1024]{2,1,0:T(1,128)S(1)}, f32[2,1,1024]{2,1,0:T(1,128)S(1)}, u32[]{:S(2)}, u32[]{:S(2)}) collective-permute-start(f32[2,1,1024]{2,1,0:T(1,128)S(1)} %add.67), channel_id=1, source_target_pairs={{0,8},{8,0},{16,24},{24,16},{1,9},{9,1},{17,25},{25,17},{2,10},{10... | collective-permute-start | bytes 24584 | tf_op jit(solution)/shard_map/ppermute | solution.py:38
  63.1 4.9 %collective-permute-start.18 = (f32[2,1,1024]{2,1,0:T(1,128)S(1)}, f32[2,1,1024]{2,1,0:T(1,128)S(1)}, u32[]{:S(2)}, u32[]{:S(2)}) collective-permute-start(f32[2,1,1024]{2,1,0:T(1,128)S(1)} %add.68), channel_id=1, source_target_pairs={{0,24},{24,0},{8,16},{16,8},{1,25},{25,1},{9,17},{17,9},{2,26},{26... | collective-permute-start | bytes 24584 | tf_op jit(solution)/shard_map/ppermute | solution.py:42
  70.4 4.7 %collective-permute-start.19 = (bf16[4,2,32,1280]{3,2,1,0:T(8,128)(2,1)}, bf16[4,2,32,1280]{3,2,1,0:T(8,128)(2,1)}, u32[]{:S(2)}, u32[]{:S(2)}) collective-permute-start(bf16[4,2,32,1280]{3,2,1,0:T(8,128)(2,1)} %get-tuple-element.69), channel_id=1, source_target_pairs={{0,1},{1,0},{2,3},{3,2},{4,5},{5,4},{6,7},{7,6},{8,9},{9,8},{10,11... | collective-permute-start | bytes 1966088 | tf_op jit(solution)/shard_map/ppermute | solution.py:34
  75.0 8.7 %collective-permute-start.23 = (bf16[32,1280]{1,0:T(8,128)(2,1)S(1)}, bf16[32,1280]{1,0:T(8,128)(2,1)S(1)}, u32[]{:S(2)}, u32[]{:S(2)}) collective-permute-start(bf16[32,1280]{1,0:T(8,128)(2,1)S(1)} %embed_grad.1), channel_id=1, source_target_pairs={{0,32},{32,0},{64,96},{96,64},{1,33},{33,1},{65,97},{97,65},{2,34}... | collective-permute-start | bytes 245768 | tf_op jit(solution)/shard_map/ppermute | solution.py:38
  76.4 13.7 %collective-permute-start.20 = (bf16[2,32,1280]{2,1,0:T(8,128)(2,1)S(1)}, bf16[2,32,1280]{2,1,0:T(8,128)(2,1)S(1)}, u32[]{:S(2)}, u32[]{:S(2)}) collective-permute-start(bf16[2,32,1280]{2,1,0:T(8,128)(2,1)S(1)} %get-tuple-element.71), channel_id=1, source_target_pairs={{0,2},{2,4},{4,6},{6,0},{1,3},{3,5},{5,7},{7,1},{8,10},{10,12},{12... | collective-permute-start | bytes 491528 | tf_op jit(solution)/shard_map/ppermute | solution.py:30
  76.8 13.4 %collective-permute-start.21 = (bf16[2,32,1280]{2,1,0:T(8,128)(2,1)S(1)}, bf16[2,32,1280]{2,1,0:T(8,128)(2,1)S(1)}, u32[]{:S(2)}, u32[]{:S(2)}) collective-permute-start(bf16[2,32,1280]{2,1,0:T(8,128)(2,1)S(1)} %get-tuple-element.72), channel_id=1, source_target_pairs={{0,4},{2,6},{4,0},{6,2},{1,5},{3,7},{5,1},{7,3},{8,12},{10,14},{12... | collective-permute-start | bytes 491528 | tf_op jit(solution)/shard_map/ppermute | solution.py:30
  80.7 9.4 %collective-permute-start.22 = (bf16[2,32,1280]{2,1,0:T(8,128)(2,1)S(1)}, bf16[2,32,1280]{2,1,0:T(8,128)(2,1)S(1)}, u32[]{:S(2)}, u32[]{:S(2)}) collective-permute-start(bf16[2,32,1280]{2,1,0:T(8,128)(2,1)S(1)} %get-tuple-element.73), channel_id=1, source_target_pairs={{0,6},{2,0},{4,2},{6,4},{1,7},{3,1},{5,3},{7,5},{8,14},{10,8},{12,... | collective-permute-start | bytes 491528 | tf_op jit(solution)/shard_map/ppermute | solution.py:30
  83.7 5.7 %collective-permute-start.24 = (bf16[32,1280]{1,0:T(8,128)(2,1)S(1)}, bf16[32,1280]{1,0:T(8,128)(2,1)S(1)}, u32[]{:S(2)}, u32[]{:S(2)}) collective-permute-start(bf16[32,1280]{1,0:T(8,128)(2,1)S(1)} %add_convert_fusion.6), channel_id=1, source_target_pairs={{0,96},{96,0},{32,64},{64,32},{1,97},{97,1},{33,65},{65,33},{2,98}... | collective-permute-start | bytes 245768 | tf_op jit(solution)/shard_map/ppermute | solution.py:42
  (22 other events, 199.0 us)

commit v7 on v6

--- a/solution.py
+++ b/solution.py
@@ -123,10 +123,7 @@
         softmax_kernel,
         grid=(2,),
         in_specs=[
-            pl.BlockSpec((1, 256, 1280), lambda t: (0, 2 * t, 0)),
-            pl.BlockSpec((1, 256, 1280), lambda t: (0, 2 * t + 1, 0)),
-            pl.BlockSpec((1, 256, 1280), lambda t: (1, 2 * t, 0)),
-            pl.BlockSpec((1, 256, 1280), lambda t: (1, 2 * t + 1, 0)),
+            *patch_streams(),
             pl.BlockSpec((32, 1280), lambda t: (0, 0)),
         ],
         out_specs=[
@@ -142,7 +139,7 @@
         cost_estimate=pl.CostEstimate(flops=700_000_000, bytes_accessed=6_000_000, transcendentals=65536),
         compiler_params=LARGE,
         name="local_softmax",
-    )(*[in_hbm(tokens)] * 4, embed)
+    )(*[in_hbm(tokens)] * 4, in_hbm(embed))
 
 
 def merge_kernel(one, two, sums, lse):
@@ -264,9 +261,16 @@
     )(comb, embed)
 
 
-def embed_grad_kernel(tok, partial_logits, comb, row_dot, out, sums):
-    grad = partial_logits[...] - comb[...].astype(F32) * row_dot[0]
-    value = jnp.dot(grad.astype(BF16), tok[0], preferred_element_type=F32)
+def embed_grad_kernel(t00, t01, t10, t11, partial_logits, comb, row_dot, out, sums):
+    value = 0.0
+    for i, pair in enumerate(((t00, t01), (t10, t11))):
+        half = slice(32 * i, 32 * i + 32)
+        grad = partial_logits[half, :] - comb[half, :].astype(F32) * row_dot[i]
+        grad = grad.astype(BF16)
+        for n in range(2):
+            value = value + jnp.dot(
+                grad[:, 256 * n : 256 * n + 256], pair[n][0], preferred_element_type=F32
+            )
 
     @pl.when(pl.program_id(0) == 0)
     def _():
@@ -277,24 +281,27 @@
         out[...] = (sums[...] + value).astype(BF16)
 
 
+def patch_streams():
+    return [
+        pl.BlockSpec((1, 256, 1280), lambda t, i=i, n=n: (i, 2 * t + n, 0))
+        for i in range(2)
+        for n in range(2)
+    ]
+
+
 def embed_grad(tokens, partial_logits, comb, row_dot):
-    wide = pl.BlockSpec((32, 1024), lambda i: (i, 0))
+    wide = pl.BlockSpec((64, 512), lambda t: (0, t))
     return pl.pallas_call(
         embed_grad_kernel,
         grid=(2,),
-        in_specs=[
-            pl.BlockSpec((1, 1024, 1280), lambda i: (i, 0, 0)),
-            wide,
-            wide,
-            pl.BlockSpec((1, 1, 1024), lambda i: (i, 0, 0)),
-        ],
-        out_specs=pl.BlockSpec((32, 1280), lambda i: (0, 0)),
+        in_specs=[*patch_streams(), wide, wide, pl.BlockSpec((2, 1, 512), lambda t: (0, 0, t))],
+        out_specs=pl.BlockSpec((32, 1280), lambda t: (0, 0)),
         out_shape=shape((32, 1280), BF16),
         scratch_shapes=[pltpu.VMEM((32, 1280), F32)],
         cost_estimate=pl.CostEstimate(flops=170_000_000, bytes_accessed=6_000_000, transcendentals=0),
         compiler_params=MEDIUM,
         name="embed_grad",
-    )(tokens, partial_logits, comb, row_dot)
+    )(*[in_hbm(tokens)] * 4, partial_logits, comb, row_dot)
 
 
 def rows_kernel(*refs):
@@ -371,14 +378,13 @@
     out_part = out_part.astype(BF16).reshape(64, 1280)
     part_other = near(part)
     part, out_part = lax.optimization_barrier((part, out_part))
-    out_other = far(out_part)
+    out_other = near(out_part)
     part = merge_pair(part, part_other)
     comb_late = after(comb_late, part)
     slot_in, lse = merge_last(part, far(part))
-    inputs = input_blocks(comb_late, embed)
-    out_part = add(after(out_part, inputs[0]), out_other)
-    inputs = sources(scatter_terms(inputs, "y"))
-    grad_slot_out = add(out_part, near(out_part))
+    inputs = sources(scatter_terms(input_blocks(comb_late, embed), "y"))
+    out_part = add(after(out_part, slot_in), out_other)
+    grad_slot_out = add(out_part, far(out_part))
 
     pre_act = jnp.dot(slot_in, w_in, preferred_element_type=F32)
     act, slope = gelu_parts(pre_act)
@@ -391,9 +397,14 @@
     grad_act = jnp.einsum("sd,hd->sh", grad_slot_out, w_out, preferred_element_type=F32)
     grad_pre = (grad_act * slope).astype(BF16)
     in_sum = jnp.einsum("sh,dh->sd", grad_pre, w_in, preferred_element_type=F32).astype(BF16)
-    in_sum = after(in_sum, out_sum)
-    in_sum = add(in_sum, far(in_sum))
+    in_sum, act_late, slots_late = lax.optimization_barrier(
+        (in_sum, act, grad_slot_out, out_sum)
+    )[:3]
     in_other = near(in_sum)
+    grad_w_out = jnp.einsum("sh,sd->hd", act_late, slots_late, preferred_element_type=F32)
+    grad_w_out = grad_w_out.astype(BF16)
+    in_sum = add(after(in_sum, grad_w_out), in_other)
+    in_other = far(in_sum)
 
     grad_combine, row_dot = combine_grad(grad_out, out_sum, sum_other, comb)
     grad_slot_in = add(after(in_sum, row_dot), in_other)
@@ -415,22 +426,21 @@
     partial_logits, mine = lax.optimization_barrier((partial_logits, mine))
     embed_part = embed_grad(tokens, partial_logits, comb, row_dot)
     embed_other = near(embed_part)
-    sums = add_cores(mine, other_core)
+    sums = add_cores(after(mine, embed_part), other_core)
     terms = scatter_terms(sums, "x")
     grad_tokens = sum(term.astype(F32) for term in terms).astype(BF16)
-    act_late, slot_late = lax.optimization_barrier((act, slot_in, sums[0]))[:2]
-    grad_w_out = jnp.einsum("sh,sd->hd", act_late, grad_slot_out, preferred_element_type=F32)
-    grad_w_out = grad_w_out.astype(BF16)
+    slot_late = after(slot_in, sums[0])
     grad_w_in = jnp.einsum("sd,sh->dh", slot_late, grad_pre, preferred_element_type=F32)
-
-    embed_part = add(after(embed_part, grad_w_out), embed_other)
+    grad_w_in = grad_w_in.astype(BF16)
+
+    embed_part = add(after(embed_part, terms[1]), embed_other)
     embed_sum = add(embed_part, far(embed_part))
     z = lax.axis_index("seq")
     grad_embed = lax.dynamic_slice_in_dim(embed_sum, z * 320, 320, axis=1).T
     return (
         grad_tokens,
         grad_embed,
-        grad_w_in.astype(BF16)[None],
+        grad_w_in[None],
         grad_w_out[None],
     )
 

time: 91.4 us -> 92.2 us (level)
  local copies, waits for them, and re-layouts: 5.39 us -> 2.08 us
  waiting for transfers between devices: 21.7 us -> 23.9 us
    ppermute x7, waiting for transfers between devices: 13.6 us -> 9.41 us  [far(): return lax.ppermute(value, axis, [(0, 3), (3, 0), (1, 2), (2, 1)])]
    ppermute x7, waiting for transfers between devices: 6.91 us -> 10.7 us  [near(): return lax.ppermute(value, axis, [(0, 1), (1, 0), (2, 3), (3, 2)])]
    unnamed x42 -> x24, local copies, waits for them, and re-layouts: 5.39 us -> 2.08 us
    ppermute x9, waiting for transfers between devices: 0.02 us -> 2.65 us  [shift(): return lax.ppermute(value, axis, [(i, (i + by) % 4) for i in range(4)])]
    pallas_call x2, Pallas kernels: 6.41 us -> 8.59 us  [the longest x1 5.48 us: local_softmax(): pl.pallas_call(softmax_kernel, grid=(2,), in_specs=[*patch_streams(), pl....]
    ppermute x7, starting transfers between devices: 7.45 us -> 6.18 us  [near(): return lax.ppermute(value, axis, [(0, 1), (1, 0), (2, 3), (3, 2)])]
  transfers between devices with their start and end apart: 25 -> 25, of which waited for: 11 -> 12; matrix products, arithmetic and copies ran while one was open for 12% -> 14% of each run, Pallas kernels for 6% -> 6%
where the time goes in v7:
time: 92.2 us; the launch traced here: 91.5 us
  starting transfers between devices  36.3 us (39%)
  waiting for transfers between devices  23.9 us (26%)
  Pallas kernels  14.6 us (16%)
  matrix products  11.1 us (12%)
  other arithmetic  2.64 us (3%)
  local copies, waits for them, and re-layouts  2.08 us (2%)
  between operations  0.95 us (1%)
    ppermute x7, starting transfers between devices, far(): return lax.ppermute(value, axis, [(0, 3), (3, 0), (1, 2), (2, 1)])  16.1 us
    ppermute x9, starting transfers between devices, shift(): return lax.ppermute(value, axis, [(i, (i + by) % 4) for i in range(4)])  13.8 us
    ppermute x7, waiting for transfers between devices, near(): return lax.ppermute(value, axis, [(0, 1), (1, 0), (2, 3), (3, 2)])  10.7 us
    ppermute x7, waiting for transfers between devices, far(): return lax.ppermute(value, axis, [(0, 3), (3, 0), (1, 2), (2, 1)])  9.41 us
    ppermute x7, starting transfers between devices, near(): return lax.ppermute(value, axis, [(0, 1), (1, 0), (2, 3), (3, 2)])  6.18 us
    pallas_call x1, Pallas kernels, local_softmax(): pl.pallas_call(softmax_kernel, grid=(2,), in_specs=[*patch_streams(), pl....  5.48 us
    dot_general x1, matrix products, local(): jnp.einsum('sd,sh->dh', slot_late, grad_pre, preferred_element_type=F32)  3.67 us
    pallas_call x1, Pallas kernels, embed_grad(): pl.pallas_call(embed_grad_kernel, grid=(2,), in_specs=[*patch_streams(),...  3.11 us
  transfers between devices with their start and end apart: 25, of which 12 were waited for; matrix products, arithmetic and copies ran while one was open for 14% of the time, Pallas kernels for 6%

profile of v7, /device:TPU:0, one launch (start us, length us, event | category | flops | bytes accessed | tf_op | source)
XLA Modules:
  0.0 91.5 jit_solution(437834457382716711)
XLA Ops:
  0.7 5.5 %local_softmax.1 = (f32[64,1024]{1,0:T(8,128)S(1)}, bf16[64,1408]{1,0:T(8,128)(2,1)S(1)}) custom-call(bf16[2,1024,1280]{2,1,0:T(8,128)(2,1)} %t11.3, bf16[2,1024,1280]{2,1,0:T(8,128)(2,1)} %t11.3, bf16[2,1024,1280]{2,1,0:T(8,128)(2,1)} %t11.3, bf16[2,1024,1280]{2,1,0:T(8,128)(2,1)} %t11.3, bf16[32,1280]{1,0:T(8,128)(2,1)} %bitcast.48), custom_call_target="tpu_custom_call" | custom-call | flops 700000000 | bytes 6000000 | tf_op jit(solution)/shard_map/local_softmax/pallas_call | solution.py:122
  6.2 2.1 %collective-permute-start = (bf16[64,1408]{1,0:T(8,128)(2,1)S(1)}, bf16[64,1408]{1,0:T(8,128)(2,1)S(1)}, u32[]{:S(2)}, u32[]{:S(2)}) collective-permute-start(bf16[64,1408]{1,0:T(8,128)(2,1)S(1)} %get-tuple-element.47.a), channel_id=1, source_target_pairs={{0,32},{32,0},{64,96},{96,64},{1,33},{33,1},{65,97},{97,65},{2,34}... | collective-permute-start | bytes 540680 | tf_op jit(solution)/shard_map/ppermute | solution.py:38
  9.2 3.6 %collective-permute-done.b = bf16[64,1408]{1,0:T(8,128)(2,1)S(1)} collective-permute-done((bf16[64,1408]{1,0:T(8,128)(2,1)S(1)}, bf16[64,1408]{1,0:T(8,128)(2,1)S(1)}, u32[]{:S(2)}, u32[]{:S(2)}) %collective-permute-start) | collective-permute-done | bytes 180256 | tf_op jit(solution)/shard_map/ppermute | solution.py:38
  13.0 3.9 %collective-permute-start.1 = (bf16[64,1408]{1,0:T(8,128)(2,1)S(1)}, bf16[64,1408]{1,0:T(8,128)(2,1)S(1)}, u32[]{:S(2)}, u32[]{:S(2)}) collective-permute-start(bf16[64,1408]{1,0:T(8,128)(2,1)S(1)} %merge_pair.1.one), channel_id=1, source_target_pairs={{0,96},{96,0},{32,64},{64,32},{1,97},{97,1},{33,65},{65,33},{2,98}... | collective-permute-start | bytes 540680 | tf_op jit(solution)/shard_map/ppermute | solution.py:42
  17.0 3.1 %collective-permute-start.5 = (bf16[224,256]{1,0:T(8,128)(2,1)S(1)}, bf16[224,256]{1,0:T(8,128)(2,1)S(1)}, u32[]{:S(2)}, u32[]{:S(2)}) collective-permute-start(bf16[224,256]{1,0:T(8,128)(2,1)S(1)} %get-tuple-element.53), channel_id=1, source_target_pairs={{0,24},{8,0},{16,8},{24,16},{1,25},{9,1},{17,9},{25,17},{2,26},{10... | collective-permute-start | bytes 344072 | tf_op jit(solution)/shard_map/ppermute | solution.py:30
  22.4 1.7 %collective-permute-start.3 = (bf16[64,1280]{1,0:T(8,128)(2,1)S(1)}, bf16[64,1280]{1,0:T(8,128)(2,1)S(1)}, u32[]{:S(2)}, u32[]{:S(2)}) collective-permute-start(bf16[64,1280]{1,0:T(8,128)(2,1)S(1)} %add_convert_fusion.5), channel_id=1, source_target_pairs={{0,96},{96,0},{32,64},{64,32},{1,97},{97,1},{33,65},{65,33},{2,98}... | collective-permute-start | bytes 491528 | tf_op jit(solution)/shard_map/ppermute | solution.py:42
  25.7 3.3 %collective-permute-done.3 = bf16[64,1280]{1,0:T(8,128)(2,1)S(1)} collective-permute-done((bf16[64,1280]{1,0:T(8,128)(2,1)S(1)}, bf16[64,1280]{1,0:T(8,128)(2,1)S(1)}, u32[]{:S(2)}, u32[]{:S(2)}) %collective-permute-start.3) | collective-permute-done | bytes 163872 | tf_op jit(solution)/shard_map/ppermute | solution.py:42
  34.3 2.8 %convolution_convert_fusion.1 = bf16[1280,1280]{1,0:T(8,128)(2,1)} fusion(bf16[64,1280]{1,0:T(8,128)(2,1)S(1)} %get-tuple-element.58, bf16[64,1280]{1,0:T(8,128)(2,1)S(1)} %add_convert_fusion.4), kind=kOutput, calls=%fused_computation.1 | convolution fusion | flops 211353600 | bytes 3604480 | tf_op jit(solution)/shard_map/sh,sd->hd/dot_general | solution.py:404
  37.1 2.1 %collective-permute-done.8 = bf16[64,1280]{1,0:T(8,128)(2,1)S(1)} collective-permute-done((bf16[64,1280]{1,0:T(8,128)(2,1)S(1)}, bf16[64,1280]{1,0:T(8,128)(2,1)S(1)}, u32[]{:S(2)}, u32[]{:S(2)}) %collective-permute-start.8) | collective-permute-done | bytes 163872 | tf_op jit(solution)/shard_map/ppermute | solution.py:38
  39.2 1.7 %collective-permute-start.10 = (bf16[64,1280]{1,0:T(8,128)(2,1)S(1)}, bf16[64,1280]{1,0:T(8,128)(2,1)S(1)}, u32[]{:S(2)}, u32[]{:S(2)}) collective-permute-start(bf16[64,1280]{1,0:T(8,128)(2,1)S(1)} %add_convert_fusion.2), channel_id=1, source_target_pairs={{0,96},{96,0},{32,64},{64,32},{1,97},{97,1},{33,65},{65,33},{2,98}... | collective-permute-start | bytes 491528 | tf_op jit(solution)/shard_map/ppermute | solution.py:42
  40.9 2.2 %combine_grad.1 = (f32[64,1024]{1,0:T(8,128)S(1)}, f32[2,1,1024]{2,1,0:T(1,128)S(1)}) custom-call(bf16[2,1024,1280]{2,1,0:T(8,128)(2,1)S(1)} %copy-done.1, bf16[64,1280]{1,0:T(8,128)(2,1)S(1)} %add_convert_fusion.3.sum_a, bf16[64,1280]{1,0:T(8,128)(2,1)S(1)} %collective-permute-done.9.sum_b, bf16[64,1024]{1,0:T(8,128)(2,1)S(1)} %bitcast.45), custom_call_target="tpu_custom_call" | custom-call | flops 350000000 | bytes 6000000 | tf_op jit(solution)/shard_map/combine_grad/pallas_call | solution.py:188
  45.9 1.9 %dispatch_grad.1 = (f32[64,1024]{1,0:T(8,128)S(1)}, bf16[64,1792]{1,0:T(8,128)(2,1)S(1)}, bf16[64,1792]{1,0:T(8,128)(2,1)S(1)}, bf16[64,1792]{1,0:T(8,128)(2,1)S(1)}, bf16[64,1792]{1,0:T(8,128)(2,1)S(1)}) custom-call(bf16[2,1024,1280]{2,1,0:T(8,128)(2,1)S(1)} %bitcast.42, bf16[64,1280]{1,0:T(8,128)(2,1)S(1)} %add_convert_fusion.1.gslot, ...), custom_call_target="tpu_custom_call" | custom-call | flops 350000000 | bytes 7000000 | tf_op jit(solution)/shard_map/dispatch_grad/pallas_call | solution.py:226
  47.7 3.1 %collective-permute-start.12 = (bf16[64,1792]{1,0:T(8,128)(2,1)S(1)}, bf16[64,1792]{1,0:T(8,128)(2,1)S(1)}, u32[]{:S(2)}, u32[]{:S(2)}) collective-permute-start(bf16[64,1792]{1,0:T(8,128)(2,1)S(1)} %get-tuple-element.69), channel_id=1, source_target_pairs={{0,24},{8,0},{16,8},{24,16},{1,25},{9,1},{17,9},{25,17},{2,26},{10... | collective-permute-start | bytes 688136 | tf_op jit(solution)/shard_map/ppermute | solution.py:30
  53.9 2.2 %collective-permute-done.15 = f32[2,1,1024]{2,1,0:T(1,128)S(1)} collective-permute-done((f32[2,1,1024]{2,1,0:T(1,128)S(1)}, f32[2,1,1024]{2,1,0:T(1,128)S(1)}, u32[]{:S(2)}, u32[]{:S(2)}) %collective-permute-start.15) | collective-permute-done | bytes 8224 | tf_op jit(solution)/shard_map/ppermute | solution.py:38
  56.1 2.8 %collective-permute-start.16 = (f32[2,1,1024]{2,1,0:T(1,128)S(1)}, f32[2,1,1024]{2,1,0:T(1,128)S(1)}, u32[]{:S(2)}, u32[]{:S(2)}) collective-permute-start(f32[2,1,1024]{2,1,0:T(1,128)S(1)} %add.66), channel_id=1, source_target_pairs={{0,6},{6,0},{2,4},{4,2},{1,7},{7,1},{3,5},{5,3},{8,14},{14,8},{10,... | collective-permute-start | bytes 24584 | tf_op jit(solution)/shard_map/ppermute | solution.py:42
  58.9 2.1 %collective-permute-done.16 = f32[2,1,1024]{2,1,0:T(1,128)S(1)} collective-permute-done((f32[2,1,1024]{2,1,0:T(1,128)S(1)}, f32[2,1,1024]{2,1,0:T(1,128)S(1)}, u32[]{:S(2)}, u32[]{:S(2)}) %collective-permute-start.16) | collective-permute-done | bytes 8224 | tf_op jit(solution)/shard_map/ppermute | solution.py:42
  61.1 2.0 %collective-permute-start.17 = (f32[2,1,1024]{2,1,0:T(1,128)S(1)}, f32[2,1,1024]{2,1,0:T(1,128)S(1)}, u32[]{:S(2)}, u32[]{:S(2)}) collective-permute-start(f32[2,1,1024]{2,1,0:T(1,128)S(1)} %add.67), channel_id=1, source_target_pairs={{0,8},{8,0},{16,24},{24,16},{1,9},{9,1},{17,25},{25,17},{2,10},{10... | collective-permute-start | bytes 24584 | tf_op jit(solution)/shard_map/ppermute | solution.py:38
  63.0 1.8 %collective-permute-done.17 = f32[2,1,1024]{2,1,0:T(1,128)S(1)} collective-permute-done((f32[2,1,1024]{2,1,0:T(1,128)S(1)}, f32[2,1,1024]{2,1,0:T(1,128)S(1)}, u32[]{:S(2)}, u32[]{:S(2)}) %collective-permute-start.17) | collective-permute-done | bytes 8224 | tf_op jit(solution)/shard_map/ppermute | solution.py:38
  64.8 2.5 %collective-permute-start.18 = (f32[2,1,1024]{2,1,0:T(1,128)S(1)}, f32[2,1,1024]{2,1,0:T(1,128)S(1)}, u32[]{:S(2)}, u32[]{:S(2)}) collective-permute-start(f32[2,1,1024]{2,1,0:T(1,128)S(1)} %add.68), channel_id=1, source_target_pairs={{0,24},{24,0},{8,16},{16,8},{1,25},{25,1},{9,17},{17,9},{2,26},{26... | collective-permute-start | bytes 24584 | tf_op jit(solution)/shard_map/ppermute | solution.py:42
  67.3 2.6 %collective-permute-done.18 = f32[2,1,1024]{2,1,0:T(1,128)S(1)} collective-permute-done((f32[2,1,1024]{2,1,0:T(1,128)S(1)}, f32[2,1,1024]{2,1,0:T(1,128)S(1)}, u32[]{:S(2)}, u32[]{:S(2)}) %collective-permute-start.18) | collective-permute-done | bytes 8224 | tf_op jit(solution)/shard_map/ppermute | solution.py:42
  70.7 3.1 %embed_grad.1 = bf16[32,1280]{1,0:T(8,128)(2,1)S(1)} custom-call(bf16[2,1024,1280]{2,1,0:T(8,128)(2,1)} %t11.3, bf16[2,1024,1280]{2,1,0:T(8,128)(2,1)} %t11.3, bf16[2,1024,1280]{2,1,0:T(8,128)(2,1)} %t11.3, bf16[2,1024,1280]{2,1,0:T(8,128)(2,1)} %t11.3, f32[64,1024]{1,0:T(8,128)S(1)} %get-tuple-element.75.partial_logits, bf16[64,1024]{1,0:T(8,128)(2,1)S(1)} %bitcast.47, ...), custom_call_target="tpu_custom_call" | custom-call | flops 170000000 | bytes 6000000 | tf_op jit(solution)/shard_map/embed_grad/pallas_call | solution.py:294
  76.9 4.0 %collective-permute-start.21 = (bf16[2,32,1280]{2,1,0:T(8,128)(2,1)}, bf16[2,32,1280]{2,1,0:T(8,128)(2,1)S(1)}, u32[]{:S(2)}, u32[]{:S(2)}) collective-permute-start(bf16[2,32,1280]{2,1,0:T(8,128)(2,1)} %copy-done.7), channel_id=1, source_target_pairs={{0,4},{2,6},{4,0},{6,2},{1,5},{3,7},{5,1},{7,3},{8,12},{10,14},{12... | collective-permute-start | bytes 491528 | tf_op jit(solution)/shard_map/ppermute | solution.py:30
  81.1 3.7 %fusion = bf16[1,1280,1280]{2,1,0:T(8,128)(2,1)} fusion(bf16[64,1280]{1,0:T(8,128)(2,1)S(1)} %get-tuple-element.83.slot_in, bf16[64,1280]{1,0:T(8,128)(2,1)} %copy-done.9), kind=kOutput, calls=%fused_computation.2 | convolution fusion | flops 211353600 | bytes 3604480 | tf_op jit(solution)/shard_map/sd,sh->dh/dot_general | solution.py:433
  86.5 2.6 %collective-permute-done.21 = bf16[2,32,1280]{2,1,0:T(8,128)(2,1)S(1)} collective-permute-done((bf16[2,32,1280]{2,1,0:T(8,128)(2,1)}, bf16[2,32,1280]{2,1,0:T(8,128)(2,1)S(1)}, u32[]{:S(2)}, u32[]{:S(2)}) %collective-permute-start.21) | collective-permute-done | bytes 163872 | tf_op jit(solution)/shard_map/ppermute | solution.py:30
  (80 shorter events, 24.3 us)
Async XLA Ops:
  6.2 6.6 %collective-permute-start = (bf16[64,1408]{1,0:T(8,128)(2,1)S(1)}, bf16[64,1408]{1,0:T(8,128)(2,1)S(1)}, u32[]{:S(2)}, u32[]{:S(2)}) collective-permute-start(bf16[64,1408]{1,0:T(8,128)(2,1)S(1)} %get-tuple-element.47.a), channel_id=1, source_target_pairs={{0,32},{32,0},{64,96},{96,64},{1,33},{33,1},{65,97},{97,65},{2,34}... | collective-permute-start | bytes 540680 | tf_op jit(solution)/shard_map/ppermute | solution.py:38
  13.0 8.7 %collective-permute-start.1 = (bf16[64,1408]{1,0:T(8,128)(2,1)S(1)}, bf16[64,1408]{1,0:T(8,128)(2,1)S(1)}, u32[]{:S(2)}, u32[]{:S(2)}) collective-permute-start(bf16[64,1408]{1,0:T(8,128)(2,1)S(1)} %merge_pair.1.one), channel_id=1, source_target_pairs={{0,96},{96,0},{32,64},{64,32},{1,97},{97,1},{33,65},{65,33},{2,98}... | collective-permute-start | bytes 540680 | tf_op jit(solution)/shard_map/ppermute | solution.py:42
  17.0 5.3 %collective-permute-start.2 = (bf16[64,1280]{1,0:T(8,128)(2,1)S(1)}, bf16[64,1280]{1,0:T(8,128)(2,1)S(1)}, u32[]{:S(2)}, u32[]{:S(2)}) collective-permute-start(bf16[64,1280]{1,0:T(8,128)(2,1)S(1)} %bitcast.51), channel_id=1, source_target_pairs={{0,32},{32,0},{64,96},{96,64},{1,33},{33,1},{65,97},{97,65},{2,34}... | collective-permute-start | bytes 491528 | tf_op jit(solution)/shard_map/ppermute | solution.py:38
  17.0 15.1 %collective-permute-start.5 = (bf16[224,256]{1,0:T(8,128)(2,1)S(1)}, bf16[224,256]{1,0:T(8,128)(2,1)S(1)}, u32[]{:S(2)}, u32[]{:S(2)}) collective-permute-start(bf16[224,256]{1,0:T(8,128)(2,1)S(1)} %get-tuple-element.53), channel_id=1, source_target_pairs={{0,24},{8,0},{16,8},{24,16},{1,25},{9,1},{17,9},{25,17},{2,26},{10... | collective-permute-start | bytes 344072 | tf_op jit(solution)/shard_map/ppermute | solution.py:30
  20.1 12.0 %collective-permute-start.6 = (bf16[224,256]{1,0:T(8,128)(2,1)S(1)}, bf16[224,256]{1,0:T(8,128)(2,1)S(1)}, u32[]{:S(2)}, u32[]{:S(2)}) collective-permute-start(bf16[224,256]{1,0:T(8,128)(2,1)S(1)} %get-tuple-element.54), channel_id=1, source_target_pairs={{0,16},{8,24},{16,0},{24,8},{1,17},{9,25},{17,1},{25,9},{2,18},{10... | collective-permute-start | bytes 344072 | tf_op jit(solution)/shard_map/ppermute | solution.py:30
  20.7 11.4 %collective-permute-start.7 = (bf16[224,256]{1,0:T(8,128)(2,1)S(1)}, bf16[224,256]{1,0:T(8,128)(2,1)S(1)}, u32[]{:S(2)}, u32[]{:S(2)}) collective-permute-start(bf16[224,256]{1,0:T(8,128)(2,1)S(1)} %get-tuple-element.55), channel_id=1, source_target_pairs={{0,8},{8,16},{16,24},{24,0},{1,9},{9,17},{17,25},{25,1},{2,10},{10... | collective-permute-start | bytes 344072 | tf_op jit(solution)/shard_map/ppermute | solution.py:30
  22.4 6.6 %collective-permute-start.3 = (bf16[64,1280]{1,0:T(8,128)(2,1)S(1)}, bf16[64,1280]{1,0:T(8,128)(2,1)S(1)}, u32[]{:S(2)}, u32[]{:S(2)}) collective-permute-start(bf16[64,1280]{1,0:T(8,128)(2,1)S(1)} %add_convert_fusion.5), channel_id=1, source_target_pairs={{0,96},{96,0},{32,64},{64,32},{1,97},{97,1},{33,65},{65,33},{2,98}... | collective-permute-start | bytes 491528 | tf_op jit(solution)/shard_map/ppermute | solution.py:42
  25.5 5.4 %collective-permute-start.4 = (bf16[64,1280]{1,0:T(8,128)(2,1)S(1)}, bf16[64,1280]{1,0:T(8,128)(2,1)S(1)}, u32[]{:S(2)}, u32[]{:S(2)}) collective-permute-start(bf16[64,1280]{1,0:T(8,128)(2,1)S(1)} %fusion.18), channel_id=1, source_target_pairs={{0,32},{32,0},{64,96},{96,64},{1,33},{33,1},{65,97},{97,65},{2,34}... | collective-permute-start | bytes 491528 | tf_op jit(solution)/shard_map/ppermute | solution.py:38
  32.1 8.8 %collective-permute-start.9 = (bf16[64,1280]{1,0:T(8,128)(2,1)S(1)}, bf16[64,1280]{1,0:T(8,128)(2,1)S(1)}, u32[]{:S(2)}, u32[]{:S(2)}) collective-permute-start(bf16[64,1280]{1,0:T(8,128)(2,1)S(1)} %add_convert_fusion.3.sum_a), channel_id=1, source_target_pairs={{0,96},{96,0},{32,64},{64,32},{1,97},{97,1},{33,65},{65,33},{2,98}... | collective-permute-start | bytes 491528 | tf_op jit(solution)/shard_map/ppermute | solution.py:42
  33.8 5.3 %collective-permute-start.8 = (bf16[64,1280]{1,0:T(8,128)(2,1)S(1)}, bf16[64,1280]{1,0:T(8,128)(2,1)S(1)}, u32[]{:S(2)}, u32[]{:S(2)}) collective-permute-start(bf16[64,1280]{1,0:T(8,128)(2,1)S(1)} %fusion.15), channel_id=1, source_target_pairs={{0,32},{32,0},{64,96},{96,64},{1,33},{33,1},{65,97},{97,65},{2,34}... | collective-permute-start | bytes 491528 | tf_op jit(solution)/shard_map/ppermute | solution.py:38
  39.2 6.6 %collective-permute-start.10 = (bf16[64,1280]{1,0:T(8,128)(2,1)S(1)}, bf16[64,1280]{1,0:T(8,128)(2,1)S(1)}, u32[]{:S(2)}, u32[]{:S(2)}) collective-permute-start(bf16[64,1280]{1,0:T(8,128)(2,1)S(1)} %add_convert_fusion.2), channel_id=1, source_target_pairs={{0,96},{96,0},{32,64},{64,32},{1,97},{97,1},{33,65},{65,33},{2,98}... | collective-permute-start | bytes 491528 | tf_op jit(solution)/shard_map/ppermute | solution.py:42
  47.7 22.2 %collective-permute-start.12 = (bf16[64,1792]{1,0:T(8,128)(2,1)S(1)}, bf16[64,1792]{1,0:T(8,128)(2,1)S(1)}, u32[]{:S(2)}, u32[]{:S(2)}) collective-permute-start(bf16[64,1792]{1,0:T(8,128)(2,1)S(1)} %get-tuple-element.69), channel_id=1, source_target_pairs={{0,24},{8,0},{16,8},{24,16},{1,25},{9,1},{17,9},{25,17},{2,26},{10... | collective-permute-start | bytes 688136 | tf_op jit(solution)/shard_map/ppermute | solution.py:30
  50.8 19.1 %collective-permute-start.13 = (bf16[64,1792]{1,0:T(8,128)(2,1)S(1)}, bf16[64,1792]{1,0:T(8,128)(2,1)S(1)}, u32[]{:S(2)}, u32[]{:S(2)}) collective-permute-start(bf16[64,1792]{1,0:T(8,128)(2,1)S(1)} %get-tuple-element.70), channel_id=1, source_target_pairs={{0,16},{8,24},{16,0},{24,8},{1,17},{9,25},{17,1},{25,9},{2,18},{10... | collective-permute-start | bytes 688136 | tf_op jit(solution)/shard_map/ppermute | solution.py:30
  51.5 18.5 %collective-permute-start.14 = (bf16[64,1792]{1,0:T(8,128)(2,1)S(1)}, bf16[64,1792]{1,0:T(8,128)(2,1)S(1)}, u32[]{:S(2)}, u32[]{:S(2)}) collective-permute-start(bf16[64,1792]{1,0:T(8,128)(2,1)S(1)} %get-tuple-element.71), channel_id=1, source_target_pairs={{0,8},{8,16},{16,24},{24,0},{1,9},{9,17},{17,25},{25,1},{2,10},{10... | collective-permute-start | bytes 688136 | tf_op jit(solution)/shard_map/ppermute | solution.py:30
  52.4 3.7 %collective-permute-start.15 = (f32[2,1,1024]{2,1,0:T(1,128)S(1)}, f32[2,1,1024]{2,1,0:T(1,128)S(1)}, u32[]{:S(2)}, u32[]{:S(2)}) collective-permute-start(f32[2,1,1024]{2,1,0:T(1,128)S(1)} %add.65), channel_id=1, source_target_pairs={{0,2},{2,0},{4,6},{6,4},{1,3},{3,1},{5,7},{7,5},{8,10},{10,8},{12,... | collective-permute-start | bytes 24584 | tf_op jit(solution)/shard_map/ppermute | solution.py:38
  56.1 4.9 %collective-permute-start.16 = (f32[2,1,1024]{2,1,0:T(1,128)S(1)}, f32[2,1,1024]{2,1,0:T(1,128)S(1)}, u32[]{:S(2)}, u32[]{:S(2)}) collective-permute-start(f32[2,1,1024]{2,1,0:T(1,128)S(1)} %add.66), channel_id=1, source_target_pairs={{0,6},{6,0},{2,4},{4,2},{1,7},{7,1},{3,5},{5,3},{8,14},{14,8},{10,... | collective-permute-start | bytes 24584 | tf_op jit(solution)/shard_map/ppermute | solution.py:42
  61.1 3.7 %collective-permute-start.17 = (f32[2,1,1024]{2,1,0:T(1,128)S(1)}, f32[2,1,1024]{2,1,0:T(1,128)S(1)}, u32[]{:S(2)}, u32[]{:S(2)}) collective-permute-start(f32[2,1,1024]{2,1,0:T(1,128)S(1)} %add.67), channel_id=1, source_target_pairs={{0,8},{8,0},{16,24},{24,16},{1,9},{9,1},{17,25},{25,17},{2,10},{10... | collective-permute-start | bytes 24584 | tf_op jit(solution)/shard_map/ppermute | solution.py:38
  64.8 5.1 %collective-permute-start.18 = (f32[2,1,1024]{2,1,0:T(1,128)S(1)}, f32[2,1,1024]{2,1,0:T(1,128)S(1)}, u32[]{:S(2)}, u32[]{:S(2)}) collective-permute-start(f32[2,1,1024]{2,1,0:T(1,128)S(1)} %add.68), channel_id=1, source_target_pairs={{0,24},{24,0},{8,16},{16,8},{1,25},{25,1},{9,17},{17,9},{2,26},{26... | collective-permute-start | bytes 24584 | tf_op jit(solution)/shard_map/ppermute | solution.py:42
  70.6 3.2 %collective-permute-start.19 = (bf16[4,2,32,1280]{3,2,1,0:T(8,128)(2,1)S(1)}, bf16[4,2,32,1280]{3,2,1,0:T(8,128)(2,1)S(1)}, u32[]{:S(2)}, u32[]{:S(2)}) collective-permute-start(bf16[4,2,32,1280]{3,2,1,0:T(8,128)(2,1)S(1)} %get-tuple-element.77), channel_id=1, source_target_pairs={{0,1},{1,0},{2,3},{3,2},{4,5},{5,4},{6,7},{7,6},{8,9},{9,8},{10,11... | collective-permute-start | bytes 1966088 | tf_op jit(solution)/shard_map/ppermute | solution.py:34
  76.6 8.1 %collective-permute-start.20 = (bf16[2,32,1280]{2,1,0:T(8,128)(2,1)}, bf16[2,32,1280]{2,1,0:T(8,128)(2,1)}, u32[]{:S(2)}, u32[]{:S(2)}) collective-permute-start(bf16[2,32,1280]{2,1,0:T(8,128)(2,1)} %get-tuple-element.79), channel_id=1, source_target_pairs={{0,2},{2,4},{4,6},{6,0},{1,3},{3,5},{5,7},{7,1},{8,10},{10,12},{12... | collective-permute-start | bytes 491528 | tf_op jit(solution)/shard_map/ppermute | solution.py:30
  76.9 7.9 %collective-permute-start.23 = (bf16[32,1280]{1,0:T(8,128)(2,1)S(1)}, bf16[32,1280]{1,0:T(8,128)(2,1)S(1)}, u32[]{:S(2)}, u32[]{:S(2)}) collective-permute-start(bf16[32,1280]{1,0:T(8,128)(2,1)S(1)} %embed_grad.1), channel_id=1, source_target_pairs={{0,32},{32,0},{64,96},{96,64},{1,33},{33,1},{65,97},{97,65},{2,34}... | collective-permute-start | bytes 245768 | tf_op jit(solution)/shard_map/ppermute | solution.py:38
  76.9 12.2 %collective-permute-start.21 = (bf16[2,32,1280]{2,1,0:T(8,128)(2,1)}, bf16[2,32,1280]{2,1,0:T(8,128)(2,1)S(1)}, u32[]{:S(2)}, u32[]{:S(2)}) collective-permute-start(bf16[2,32,1280]{2,1,0:T(8,128)(2,1)} %copy-done.7), channel_id=1, source_target_pairs={{0,4},{2,6},{4,0},{6,2},{1,5},{3,7},{5,1},{7,3},{8,12},{10,14},{12... | collective-permute-start | bytes 491528 | tf_op jit(solution)/shard_map/ppermute | solution.py:30
  80.8 8.3 %collective-permute-start.22 = (bf16[2,32,1280]{2,1,0:T(8,128)(2,1)}, bf16[2,32,1280]{2,1,0:T(8,128)(2,1)S(1)}, u32[]{:S(2)}, u32[]{:S(2)}) collective-permute-start(bf16[2,32,1280]{2,1,0:T(8,128)(2,1)} %copy-done.6), channel_id=1, source_target_pairs={{0,6},{2,0},{4,2},{6,4},{1,7},{3,1},{5,3},{7,5},{8,14},{10,8},{12,... | collective-permute-start | bytes 491528 | tf_op jit(solution)/shard_map/ppermute | solution.py:30
  84.8 6.0 %collective-permute-start.24 = (bf16[32,1280]{1,0:T(8,128)(2,1)S(1)}, bf16[32,1280]{1,0:T(8,128)(2,1)S(1)}, u32[]{:S(2)}, u32[]{:S(2)}) collective-permute-start(bf16[32,1280]{1,0:T(8,128)(2,1)S(1)} %add_convert_fusion.6), channel_id=1, source_target_pairs={{0,96},{96,0},{32,64},{64,32},{1,97},{97,1},{33,65},{65,33},{2,98}... | collective-permute-start | bytes 245768 | tf_op jit(solution)/shard_map/ppermute | solution.py:42
  (13 other events, 111.1 us)

commit v8 on v7

--- a/solution.py
+++ b/solution.py
@@ -350,7 +350,7 @@
 def add_cores(mine, other):
     return pl.pallas_call(
         add_kernel,
-        out_shape=[shape((2, 32, 1280), BF16)] * 4,
+        out_shape=[pltpu.HBM((2, 32, 1280), BF16)] * 4,
         cost_estimate=pl.CostEstimate(flops=327_680, bytes_accessed=2_000_000, transcendentals=0),
         compiler_params=SMALL,
         name="add_cores",
@@ -382,7 +382,7 @@
     part = merge_pair(part, part_other)
     comb_late = after(comb_late, part)
     slot_in, lse = merge_last(part, far(part))
-    inputs = sources(scatter_terms(input_blocks(comb_late, embed), "y"))
+    inputs = list(input_blocks(comb_late, embed))
     out_part = add(after(out_part, slot_in), out_other)
     grad_slot_out = add(out_part, far(out_part))
 
@@ -391,6 +391,8 @@
     act = act.astype(BF16)
     out_sum = jnp.dot(act, w_out, preferred_element_type=F32).astype(BF16)
     grad_slot_out = after(grad_slot_out, out_sum)
+    inputs[3] = after(inputs[3], out_sum)
+    inputs = sources(scatter_terms(inputs, "y"))
     out_sum = add(out_sum, near(out_sum))
     out_sum = after(out_sum, *inputs)
     sum_other = far(out_sum)

time: 92.2 us -> 90.4 us (0.980)
  waiting for transfers between devices: 23.9 us -> 21.7 us
  starting transfers between devices: 36.3 us -> 38.4 us
  local copies, waits for them, and re-layouts: 2.08 us -> 0.06 us
    ppermute x7, waiting for transfers between devices: 9.41 us -> 6.39 us  [far(): return lax.ppermute(value, axis, [(0, 3), (3, 0), (1, 2), (2, 1)])]
    ppermute x9, starting transfers between devices: 13.8 us -> 16.2 us  [shift(): return lax.ppermute(value, axis, [(i, (i + by) % 4) for i in range(4)])]
    unnamed x24 -> x18, local copies, waits for them, and re-layouts: 2.08 us -> 0.06 us
where the time goes in v8:
time: 90.4 us; the launch traced here: 89.6 us
  starting transfers between devices  38.4 us (42%)
  waiting for transfers between devices  21.7 us (24%)
  Pallas kernels  14.7 us (16%)
  matrix products  11.1 us (12%)
  other arithmetic  2.64 us (3%)
  between operations  0.95 us (1%)
    ppermute x9, starting transfers between devices, shift(): return lax.ppermute(value, axis, [(i, (i + by) % 4) for i in range(4)])  16.2 us
    ppermute x7, starting transfers between devices, far(): return lax.ppermute(value, axis, [(0, 3), (3, 0), (1, 2), (2, 1)])  16.1 us
    ppermute x7, waiting for transfers between devices, near(): return lax.ppermute(value, axis, [(0, 1), (1, 0), (2, 3), (3, 2)])  11.5 us
    ppermute x7, waiting for transfers between devices, far(): return lax.ppermute(value, axis, [(0, 3), (3, 0), (1, 2), (2, 1)])  6.39 us
    ppermute x7, starting transfers between devices, near(): return lax.ppermute(value, axis, [(0, 1), (1, 0), (2, 3), (3, 2)])  5.96 us
    pallas_call x1, Pallas kernels, local_softmax(): pl.pallas_call(softmax_kernel, grid=(2,), in_specs=[*patch_streams(), pl....  5.48 us
    dot_general x1, matrix products, local(): jnp.einsum('sd,sh->dh', slot_late, grad_pre, preferred_element_type=F32)  3.68 us
    pallas_call x1, Pallas kernels, embed_grad(): pl.pallas_call(embed_grad_kernel, grid=(2,), in_specs=[*patch_streams(),...  3.11 us
  transfers between devices with their start and end apart: 25, of which 12 were waited for; matrix products, arithmetic and copies ran while one was open for 14% of the time, Pallas kernels for 6%

profile of v8, /device:TPU:0, one launch (start us, length us, event | category | flops | bytes accessed | tf_op | source)
XLA Modules:
  0.0 89.6 jit_solution(7691540778372962897)
XLA Ops:
  0.7 5.5 %local_softmax.1 = (f32[64,1024]{1,0:T(8,128)S(1)}, bf16[64,1408]{1,0:T(8,128)(2,1)S(1)}) custom-call(bf16[2,1024,1280]{2,1,0:T(8,128)(2,1)} %t11.3, bf16[2,1024,1280]{2,1,0:T(8,128)(2,1)} %t11.3, bf16[2,1024,1280]{2,1,0:T(8,128)(2,1)} %t11.3, bf16[2,1024,1280]{2,1,0:T(8,128)(2,1)} %t11.3, bf16[32,1280]{1,0:T(8,128)(2,1)} %bitcast.48), custom_call_target="tpu_custom_call" | custom-call | flops 700000000 | bytes 6000000 | tf_op jit(solution)/shard_map/local_softmax/pallas_call | solution.py:122
  6.2 2.1 %collective-permute-start = (bf16[64,1408]{1,0:T(8,128)(2,1)S(1)}, bf16[64,1408]{1,0:T(8,128)(2,1)S(1)}, u32[]{:S(2)}, u32[]{:S(2)}) collective-permute-start(bf16[64,1408]{1,0:T(8,128)(2,1)S(1)} %get-tuple-element.48.a), channel_id=1, source_target_pairs={{0,32},{32,0},{64,96},{96,64},{1,33},{33,1},{65,97},{97,65},{2,34}... | collective-permute-start | bytes 540680 | tf_op jit(solution)/shard_map/ppermute | solution.py:38
  9.2 3.6 %collective-permute-done.b = bf16[64,1408]{1,0:T(8,128)(2,1)S(1)} collective-permute-done((bf16[64,1408]{1,0:T(8,128)(2,1)S(1)}, bf16[64,1408]{1,0:T(8,128)(2,1)S(1)}, u32[]{:S(2)}, u32[]{:S(2)}) %collective-permute-start) | collective-permute-done | bytes 180256 | tf_op jit(solution)/shard_map/ppermute | solution.py:38
  13.0 3.9 %collective-permute-start.1 = (bf16[64,1408]{1,0:T(8,128)(2,1)S(1)}, bf16[64,1408]{1,0:T(8,128)(2,1)S(1)}, u32[]{:S(2)}, u32[]{:S(2)}) collective-permute-start(bf16[64,1408]{1,0:T(8,128)(2,1)S(1)} %merge_pair.1.one), channel_id=1, source_target_pairs={{0,96},{96,0},{32,64},{64,32},{1,97},{97,1},{33,65},{65,33},{2,98}... | collective-permute-start | bytes 540680 | tf_op jit(solution)/shard_map/ppermute | solution.py:42
  17.0 3.3 %collective-permute-start.6 = (bf16[224,256]{1,0:T(8,128)(2,1)S(1)}, bf16[224,256]{1,0:T(8,128)(2,1)S(1)}, u32[]{:S(2)}, u32[]{:S(2)}) collective-permute-start(bf16[224,256]{1,0:T(8,128)(2,1)S(1)} %get-tuple-element.56), channel_id=1, source_target_pairs={{0,16},{8,24},{16,0},{24,8},{1,17},{9,25},{17,1},{25,9},{2,18},{10... | collective-permute-start | bytes 344072 | tf_op jit(solution)/shard_map/ppermute | solution.py:30
  22.4 1.7 %collective-permute-start.3 = (bf16[64,1280]{1,0:T(8,128)(2,1)S(1)}, bf16[64,1280]{1,0:T(8,128)(2,1)S(1)}, u32[]{:S(2)}, u32[]{:S(2)}) collective-permute-start(bf16[64,1280]{1,0:T(8,128)(2,1)S(1)} %add_convert_fusion.5), channel_id=1, source_target_pairs={{0,96},{96,0},{32,64},{64,32},{1,97},{97,1},{33,65},{65,33},{2,98}... | collective-permute-start | bytes 491528 | tf_op jit(solution)/shard_map/ppermute | solution.py:42
  25.6 3.1 %collective-permute-start.5 = (bf16[224,256]{1,0:T(8,128)(2,1)S(1)}, bf16[224,256]{1,0:T(8,128)(2,1)S(1)}, u32[]{:S(2)}, u32[]{:S(2)}) collective-permute-start(bf16[224,256]{1,0:T(8,128)(2,1)S(1)} %get-tuple-element.55), channel_id=1, source_target_pairs={{0,24},{8,0},{16,8},{24,16},{1,25},{9,1},{17,9},{25,17},{2,26},{10... | collective-permute-start | bytes 344072 | tf_op jit(solution)/shard_map/ppermute | solution.py:30
  34.2 2.8 %convolution_convert_fusion.1 = bf16[1280,1280]{1,0:T(8,128)(2,1)} fusion(bf16[64,1280]{1,0:T(8,128)(2,1)S(1)} %get-tuple-element.60, bf16[64,1280]{1,0:T(8,128)(2,1)S(1)} %add_convert_fusion.4), kind=kOutput, calls=%fused_computation.1 | convolution fusion | flops 211353600 | bytes 3604480 | tf_op jit(solution)/shard_map/sh,sd->hd/dot_general | solution.py:406
  36.9 2.2 %collective-permute-done.8 = bf16[64,1280]{1,0:T(8,128)(2,1)S(1)} collective-permute-done((bf16[64,1280]{1,0:T(8,128)(2,1)S(1)}, bf16[64,1280]{1,0:T(8,128)(2,1)S(1)}, u32[]{:S(2)}, u32[]{:S(2)}) %collective-permute-start.8) | collective-permute-done | bytes 163872 | tf_op jit(solution)/shard_map/ppermute | solution.py:38
  39.2 1.7 %collective-permute-start.10 = (bf16[64,1280]{1,0:T(8,128)(2,1)S(1)}, bf16[64,1280]{1,0:T(8,128)(2,1)S(1)}, u32[]{:S(2)}, u32[]{:S(2)}) collective-permute-start(bf16[64,1280]{1,0:T(8,128)(2,1)S(1)} %add_convert_fusion.2), channel_id=1, source_target_pairs={{0,96},{96,0},{32,64},{64,32},{1,97},{97,1},{33,65},{65,33},{2,98}... | collective-permute-start | bytes 491528 | tf_op jit(solution)/shard_map/ppermute | solution.py:42
  40.9 2.2 %combine_grad.1 = (f32[64,1024]{1,0:T(8,128)S(1)}, f32[2,1,1024]{2,1,0:T(1,128)S(1)}) custom-call(bf16[2,1024,1280]{2,1,0:T(8,128)(2,1)S(1)} %copy-done.1, bf16[64,1280]{1,0:T(8,128)(2,1)S(1)} %add_convert_fusion.3.sum_a, bf16[64,1280]{1,0:T(8,128)(2,1)S(1)} %collective-permute-done.9.sum_b, bf16[64,1024]{1,0:T(8,128)(2,1)S(1)} %bitcast.45), custom_call_target="tpu_custom_call" | custom-call | flops 350000000 | bytes 6000000 | tf_op jit(solution)/shard_map/combine_grad/pallas_call | solution.py:188
  45.9 1.9 %dispatch_grad.1 = (f32[64,1024]{1,0:T(8,128)S(1)}, bf16[64,1792]{1,0:T(8,128)(2,1)S(1)}, bf16[64,1792]{1,0:T(8,128)(2,1)S(1)}, bf16[64,1792]{1,0:T(8,128)(2,1)S(1)}, bf16[64,1792]{1,0:T(8,128)(2,1)S(1)}) custom-call(bf16[2,1024,1280]{2,1,0:T(8,128)(2,1)S(1)} %bitcast.42, bf16[64,1280]{1,0:T(8,128)(2,1)S(1)} %add_convert_fusion.1.gslot, ...), custom_call_target="tpu_custom_call" | custom-call | flops 350000000 | bytes 7000000 | tf_op jit(solution)/shard_map/dispatch_grad/pallas_call | solution.py:226
  47.7 3.1 %collective-permute-start.12 = (bf16[64,1792]{1,0:T(8,128)(2,1)S(1)}, bf16[64,1792]{1,0:T(8,128)(2,1)S(1)}, u32[]{:S(2)}, u32[]{:S(2)}) collective-permute-start(bf16[64,1792]{1,0:T(8,128)(2,1)S(1)} %get-tuple-element.71), channel_id=1, source_target_pairs={{0,24},{8,0},{16,8},{24,16},{1,25},{9,1},{17,9},{25,17},{2,26},{10... | collective-permute-start | bytes 688136 | tf_op jit(solution)/shard_map/ppermute | solution.py:30
  53.9 2.2 %collective-permute-done.15 = f32[2,1,1024]{2,1,0:T(1,128)S(1)} collective-permute-done((f32[2,1,1024]{2,1,0:T(1,128)S(1)}, f32[2,1,1024]{2,1,0:T(1,128)S(1)}, u32[]{:S(2)}, u32[]{:S(2)}) %collective-permute-start.15) | collective-permute-done | bytes 8224 | tf_op jit(solution)/shard_map/ppermute | solution.py:38
  56.1 2.8 %collective-permute-start.16 = (f32[2,1,1024]{2,1,0:T(1,128)S(1)}, f32[2,1,1024]{2,1,0:T(1,128)S(1)}, u32[]{:S(2)}, u32[]{:S(2)}) collective-permute-start(f32[2,1,1024]{2,1,0:T(1,128)S(1)} %add.66), channel_id=1, source_target_pairs={{0,6},{6,0},{2,4},{4,2},{1,7},{7,1},{3,5},{5,3},{8,14},{14,8},{10,... | collective-permute-start | bytes 24584 | tf_op jit(solution)/shard_map/ppermute | solution.py:42
  58.9 2.1 %collective-permute-done.16 = f32[2,1,1024]{2,1,0:T(1,128)S(1)} collective-permute-done((f32[2,1,1024]{2,1,0:T(1,128)S(1)}, f32[2,1,1024]{2,1,0:T(1,128)S(1)}, u32[]{:S(2)}, u32[]{:S(2)}) %collective-permute-start.16) | collective-permute-done | bytes 8224 | tf_op jit(solution)/shard_map/ppermute | solution.py:42
  61.1 2.0 %collective-permute-start.17 = (f32[2,1,1024]{2,1,0:T(1,128)S(1)}, f32[2,1,1024]{2,1,0:T(1,128)S(1)}, u32[]{:S(2)}, u32[]{:S(2)}) collective-permute-start(f32[2,1,1024]{2,1,0:T(1,128)S(1)} %add.67), channel_id=1, source_target_pairs={{0,8},{8,0},{16,24},{24,16},{1,9},{9,1},{17,25},{25,17},{2,10},{10... | collective-permute-start | bytes 24584 | tf_op jit(solution)/shard_map/ppermute | solution.py:38
  63.0 1.8 %collective-permute-done.17 = f32[2,1,1024]{2,1,0:T(1,128)S(1)} collective-permute-done((f32[2,1,1024]{2,1,0:T(1,128)S(1)}, f32[2,1,1024]{2,1,0:T(1,128)S(1)}, u32[]{:S(2)}, u32[]{:S(2)}) %collective-permute-start.17) | collective-permute-done | bytes 8224 | tf_op jit(solution)/shard_map/ppermute | solution.py:38
  64.8 2.5 %collective-permute-start.18 = (f32[2,1,1024]{2,1,0:T(1,128)S(1)}, f32[2,1,1024]{2,1,0:T(1,128)S(1)}, u32[]{:S(2)}, u32[]{:S(2)}) collective-permute-start(f32[2,1,1024]{2,1,0:T(1,128)S(1)} %add.68), channel_id=1, source_target_pairs={{0,24},{24,0},{8,16},{16,8},{1,25},{25,1},{9,17},{17,9},{2,26},{26... | collective-permute-start | bytes 24584 | tf_op jit(solution)/shard_map/ppermute | solution.py:42
  67.3 2.6 %collective-permute-done.18 = f32[2,1,1024]{2,1,0:T(1,128)S(1)} collective-permute-done((f32[2,1,1024]{2,1,0:T(1,128)S(1)}, f32[2,1,1024]{2,1,0:T(1,128)S(1)}, u32[]{:S(2)}, u32[]{:S(2)}) %collective-permute-start.18) | collective-permute-done | bytes 8224 | tf_op jit(solution)/shard_map/ppermute | solution.py:42
  70.7 3.1 %embed_grad.1 = bf16[32,1280]{1,0:T(8,128)(2,1)S(1)} custom-call(bf16[2,1024,1280]{2,1,0:T(8,128)(2,1)} %t11.3, bf16[2,1024,1280]{2,1,0:T(8,128)(2,1)} %t11.3, bf16[2,1024,1280]{2,1,0:T(8,128)(2,1)} %t11.3, bf16[2,1024,1280]{2,1,0:T(8,128)(2,1)} %t11.3, f32[64,1024]{1,0:T(8,128)S(1)} %get-tuple-element.77.partial_logits, bf16[64,1024]{1,0:T(8,128)(2,1)S(1)} %bitcast.47, ...), custom_call_target="tpu_custom_call" | custom-call | flops 170000000 | bytes 6000000 | tf_op jit(solution)/shard_map/embed_grad/pallas_call | solution.py:294
  75.0 4.0 %collective-permute-start.21 = (bf16[2,32,1280]{2,1,0:T(8,128)(2,1)}, bf16[2,32,1280]{2,1,0:T(8,128)(2,1)S(1)}, u32[]{:S(2)}, u32[]{:S(2)}) collective-permute-start(bf16[2,32,1280]{2,1,0:T(8,128)(2,1)} %get-tuple-element.82), channel_id=1, source_target_pairs={{0,4},{2,6},{4,0},{6,2},{1,5},{3,7},{5,1},{7,3},{8,12},{10,14},{12... | collective-permute-start | bytes 491528 | tf_op jit(solution)/shard_map/ppermute | solution.py:30
  79.2 3.7 %fusion = bf16[1,1280,1280]{2,1,0:T(8,128)(2,1)} fusion(bf16[64,1280]{1,0:T(8,128)(2,1)S(1)} %get-tuple-element.85.slot_in, bf16[64,1280]{1,0:T(8,128)(2,1)} %copy-done.5), kind=kOutput, calls=%fused_computation.2 | convolution fusion | flops 211353600 | bytes 3604480 | tf_op jit(solution)/shard_map/sd,sh->dh/dot_general | solution.py:435
  84.6 2.6 %collective-permute-done.21 = bf16[2,32,1280]{2,1,0:T(8,128)(2,1)S(1)} collective-permute-done((bf16[2,32,1280]{2,1,0:T(8,128)(2,1)}, bf16[2,32,1280]{2,1,0:T(8,128)(2,1)S(1)}, u32[]{:S(2)}, u32[]{:S(2)}) %collective-permute-start.21) | collective-permute-done | bytes 163872 | tf_op jit(solution)/shard_map/ppermute | solution.py:30
  (74 shorter events, 22.3 us)
Async XLA Ops:
  6.2 6.6 %collective-permute-start = (bf16[64,1408]{1,0:T(8,128)(2,1)S(1)}, bf16[64,1408]{1,0:T(8,128)(2,1)S(1)}, u32[]{:S(2)}, u32[]{:S(2)}) collective-permute-start(bf16[64,1408]{1,0:T(8,128)(2,1)S(1)} %get-tuple-element.48.a), channel_id=1, source_target_pairs={{0,32},{32,0},{64,96},{96,64},{1,33},{33,1},{65,97},{97,65},{2,34}... | collective-permute-start | bytes 540680 | tf_op jit(solution)/shard_map/ppermute | solution.py:38
  13.0 8.0 %collective-permute-start.1 = (bf16[64,1408]{1,0:T(8,128)(2,1)S(1)}, bf16[64,1408]{1,0:T(8,128)(2,1)S(1)}, u32[]{:S(2)}, u32[]{:S(2)}) collective-permute-start(bf16[64,1408]{1,0:T(8,128)(2,1)S(1)} %merge_pair.1.one), channel_id=1, source_target_pairs={{0,96},{96,0},{32,64},{64,32},{1,97},{97,1},{33,65},{65,33},{2,98}... | collective-permute-start | bytes 540680 | tf_op jit(solution)/shard_map/ppermute | solution.py:42
  17.0 5.3 %collective-permute-start.2 = (bf16[64,1280]{1,0:T(8,128)(2,1)S(1)}, bf16[64,1280]{1,0:T(8,128)(2,1)S(1)}, u32[]{:S(2)}, u32[]{:S(2)}) collective-permute-start(bf16[64,1280]{1,0:T(8,128)(2,1)S(1)} %bitcast.51), channel_id=1, source_target_pairs={{0,32},{32,0},{64,96},{96,64},{1,33},{33,1},{65,97},{97,65},{2,34}... | collective-permute-start | bytes 491528 | tf_op jit(solution)/shard_map/ppermute | solution.py:38
  17.0 15.1 %collective-permute-start.6 = (bf16[224,256]{1,0:T(8,128)(2,1)S(1)}, bf16[224,256]{1,0:T(8,128)(2,1)S(1)}, u32[]{:S(2)}, u32[]{:S(2)}) collective-permute-start(bf16[224,256]{1,0:T(8,128)(2,1)S(1)} %get-tuple-element.56), channel_id=1, source_target_pairs={{0,16},{8,24},{16,0},{24,8},{1,17},{9,25},{17,1},{25,9},{2,18},{10... | collective-permute-start | bytes 344072 | tf_op jit(solution)/shard_map/ppermute | solution.py:30
  20.3 11.8 %collective-permute-start.7 = (bf16[224,256]{1,0:T(8,128)(2,1)S(1)}, bf16[224,256]{1,0:T(8,128)(2,1)S(1)}, u32[]{:S(2)}, u32[]{:S(2)}) collective-permute-start(bf16[224,256]{1,0:T(8,128)(2,1)S(1)} %get-tuple-element.57), channel_id=1, source_target_pairs={{0,8},{8,16},{16,24},{24,0},{1,9},{9,17},{17,25},{25,1},{2,10},{10... | collective-permute-start | bytes 344072 | tf_op jit(solution)/shard_map/ppermute | solution.py:30
  22.4 6.6 %collective-permute-start.3 = (bf16[64,1280]{1,0:T(8,128)(2,1)S(1)}, bf16[64,1280]{1,0:T(8,128)(2,1)S(1)}, u32[]{:S(2)}, u32[]{:S(2)}) collective-permute-start(bf16[64,1280]{1,0:T(8,128)(2,1)S(1)} %add_convert_fusion.5), channel_id=1, source_target_pairs={{0,96},{96,0},{32,64},{64,32},{1,97},{97,1},{33,65},{65,33},{2,98}... | collective-permute-start | bytes 491528 | tf_op jit(solution)/shard_map/ppermute | solution.py:42
  25.5 5.4 %collective-permute-start.4 = (bf16[64,1280]{1,0:T(8,128)(2,1)S(1)}, bf16[64,1280]{1,0:T(8,128)(2,1)S(1)}, u32[]{:S(2)}, u32[]{:S(2)}) collective-permute-start(bf16[64,1280]{1,0:T(8,128)(2,1)S(1)} %fusion.18), channel_id=1, source_target_pairs={{0,32},{32,0},{64,96},{96,64},{1,33},{33,1},{65,97},{97,65},{2,34}... | collective-permute-start | bytes 491528 | tf_op jit(solution)/shard_map/ppermute | solution.py:38
  25.6 6.5 %collective-permute-start.5 = (bf16[224,256]{1,0:T(8,128)(2,1)S(1)}, bf16[224,256]{1,0:T(8,128)(2,1)S(1)}, u32[]{:S(2)}, u32[]{:S(2)}) collective-permute-start(bf16[224,256]{1,0:T(8,128)(2,1)S(1)} %get-tuple-element.55), channel_id=1, source_target_pairs={{0,24},{8,0},{16,8},{24,16},{1,25},{9,1},{17,9},{25,17},{2,26},{10... | collective-permute-start | bytes 344072 | tf_op jit(solution)/shard_map/ppermute | solution.py:30
  32.1 8.8 %collective-permute-start.9 = (bf16[64,1280]{1,0:T(8,128)(2,1)S(1)}, bf16[64,1280]{1,0:T(8,128)(2,1)S(1)}, u32[]{:S(2)}, u32[]{:S(2)}) collective-permute-start(bf16[64,1280]{1,0:T(8,128)(2,1)S(1)} %add_convert_fusion.3.sum_a), channel_id=1, source_target_pairs={{0,96},{96,0},{32,64},{64,32},{1,97},{97,1},{33,65},{65,33},{2,98}... | collective-permute-start | bytes 491528 | tf_op jit(solution)/shard_map/ppermute | solution.py:42
  33.8 5.3 %collective-permute-start.8 = (bf16[64,1280]{1,0:T(8,128)(2,1)S(1)}, bf16[64,1280]{1,0:T(8,128)(2,1)S(1)}, u32[]{:S(2)}, u32[]{:S(2)}) collective-permute-start(bf16[64,1280]{1,0:T(8,128)(2,1)S(1)} %fusion.15), channel_id=1, source_target_pairs={{0,32},{32,0},{64,96},{96,64},{1,33},{33,1},{65,97},{97,65},{2,34}... | collective-permute-start | bytes 491528 | tf_op jit(solution)/shard_map/ppermute | solution.py:38
  39.2 6.6 %collective-permute-start.10 = (bf16[64,1280]{1,0:T(8,128)(2,1)S(1)}, bf16[64,1280]{1,0:T(8,128)(2,1)S(1)}, u32[]{:S(2)}, u32[]{:S(2)}) collective-permute-start(bf16[64,1280]{1,0:T(8,128)(2,1)S(1)} %add_convert_fusion.2), channel_id=1, source_target_pairs={{0,96},{96,0},{32,64},{64,32},{1,97},{97,1},{33,65},{65,33},{2,98}... | collective-permute-start | bytes 491528 | tf_op jit(solution)/shard_map/ppermute | solution.py:42
  47.7 22.2 %collective-permute-start.12 = (bf16[64,1792]{1,0:T(8,128)(2,1)S(1)}, bf16[64,1792]{1,0:T(8,128)(2,1)S(1)}, u32[]{:S(2)}, u32[]{:S(2)}) collective-permute-start(bf16[64,1792]{1,0:T(8,128)(2,1)S(1)} %get-tuple-element.71), channel_id=1, source_target_pairs={{0,24},{8,0},{16,8},{24,16},{1,25},{9,1},{17,9},{25,17},{2,26},{10... | collective-permute-start | bytes 688136 | tf_op jit(solution)/shard_map/ppermute | solution.py:30
  50.8 19.1 %collective-permute-start.13 = (bf16[64,1792]{1,0:T(8,128)(2,1)S(1)}, bf16[64,1792]{1,0:T(8,128)(2,1)S(1)}, u32[]{:S(2)}, u32[]{:S(2)}) collective-permute-start(bf16[64,1792]{1,0:T(8,128)(2,1)S(1)} %get-tuple-element.72), channel_id=1, source_target_pairs={{0,16},{8,24},{16,0},{24,8},{1,17},{9,25},{17,1},{25,9},{2,18},{10... | collective-permute-start | bytes 688136 | tf_op jit(solution)/shard_map/ppermute | solution.py:30
  51.5 18.5 %collective-permute-start.14 = (bf16[64,1792]{1,0:T(8,128)(2,1)S(1)}, bf16[64,1792]{1,0:T(8,128)(2,1)S(1)}, u32[]{:S(2)}, u32[]{:S(2)}) collective-permute-start(bf16[64,1792]{1,0:T(8,128)(2,1)S(1)} %get-tuple-element.73), channel_id=1, source_target_pairs={{0,8},{8,16},{16,24},{24,0},{1,9},{9,17},{17,25},{25,1},{2,10},{10... | collective-permute-start | bytes 688136 | tf_op jit(solution)/shard_map/ppermute | solution.py:30
  52.4 3.7 %collective-permute-start.15 = (f32[2,1,1024]{2,1,0:T(1,128)S(1)}, f32[2,1,1024]{2,1,0:T(1,128)S(1)}, u32[]{:S(2)}, u32[]{:S(2)}) collective-permute-start(f32[2,1,1024]{2,1,0:T(1,128)S(1)} %add.65), channel_id=1, source_target_pairs={{0,2},{2,0},{4,6},{6,4},{1,3},{3,1},{5,7},{7,5},{8,10},{10,8},{12,... | collective-permute-start | bytes 24584 | tf_op jit(solution)/shard_map/ppermute | solution.py:38
  56.1 4.9 %collective-permute-start.16 = (f32[2,1,1024]{2,1,0:T(1,128)S(1)}, f32[2,1,1024]{2,1,0:T(1,128)S(1)}, u32[]{:S(2)}, u32[]{:S(2)}) collective-permute-start(f32[2,1,1024]{2,1,0:T(1,128)S(1)} %add.66), channel_id=1, source_target_pairs={{0,6},{6,0},{2,4},{4,2},{1,7},{7,1},{3,5},{5,3},{8,14},{14,8},{10,... | collective-permute-start | bytes 24584 | tf_op jit(solution)/shard_map/ppermute | solution.py:42
  61.1 3.7 %collective-permute-start.17 = (f32[2,1,1024]{2,1,0:T(1,128)S(1)}, f32[2,1,1024]{2,1,0:T(1,128)S(1)}, u32[]{:S(2)}, u32[]{:S(2)}) collective-permute-start(f32[2,1,1024]{2,1,0:T(1,128)S(1)} %add.67), channel_id=1, source_target_pairs={{0,8},{8,0},{16,24},{24,16},{1,9},{9,1},{17,25},{25,17},{2,10},{10... | collective-permute-start | bytes 24584 | tf_op jit(solution)/shard_map/ppermute | solution.py:38
  64.8 5.1 %collective-permute-start.18 = (f32[2,1,1024]{2,1,0:T(1,128)S(1)}, f32[2,1,1024]{2,1,0:T(1,128)S(1)}, u32[]{:S(2)}, u32[]{:S(2)}) collective-permute-start(f32[2,1,1024]{2,1,0:T(1,128)S(1)} %add.68), channel_id=1, source_target_pairs={{0,24},{24,0},{8,16},{16,8},{1,25},{25,1},{9,17},{17,9},{2,26},{26... | collective-permute-start | bytes 24584 | tf_op jit(solution)/shard_map/ppermute | solution.py:42
  70.6 3.2 %collective-permute-start.19 = (bf16[4,2,32,1280]{3,2,1,0:T(8,128)(2,1)S(1)}, bf16[4,2,32,1280]{3,2,1,0:T(8,128)(2,1)S(1)}, u32[]{:S(2)}, u32[]{:S(2)}) collective-permute-start(bf16[4,2,32,1280]{3,2,1,0:T(8,128)(2,1)S(1)} %get-tuple-element.79), channel_id=1, source_target_pairs={{0,1},{1,0},{2,3},{3,2},{4,5},{5,4},{6,7},{7,6},{8,9},{9,8},{10,11... | collective-permute-start | bytes 1966088 | tf_op jit(solution)/shard_map/ppermute | solution.py:34
  74.7 8.1 %collective-permute-start.20 = (bf16[2,32,1280]{2,1,0:T(8,128)(2,1)}, bf16[2,32,1280]{2,1,0:T(8,128)(2,1)}, u32[]{:S(2)}, u32[]{:S(2)}) collective-permute-start(bf16[2,32,1280]{2,1,0:T(8,128)(2,1)} %get-tuple-element.81), channel_id=1, source_target_pairs={{0,2},{2,4},{4,6},{6,0},{1,3},{3,5},{5,7},{7,1},{8,10},{10,12},{12... | collective-permute-start | bytes 491528 | tf_op jit(solution)/shard_map/ppermute | solution.py:30
  75.0 7.9 %collective-permute-start.23 = (bf16[32,1280]{1,0:T(8,128)(2,1)S(1)}, bf16[32,1280]{1,0:T(8,128)(2,1)S(1)}, u32[]{:S(2)}, u32[]{:S(2)}) collective-permute-start(bf16[32,1280]{1,0:T(8,128)(2,1)S(1)} %embed_grad.1), channel_id=1, source_target_pairs={{0,32},{32,0},{64,96},{96,64},{1,33},{33,1},{65,97},{97,65},{2,34}... | collective-permute-start | bytes 245768 | tf_op jit(solution)/shard_map/ppermute | solution.py:38
  75.0 12.2 %collective-permute-start.21 = (bf16[2,32,1280]{2,1,0:T(8,128)(2,1)}, bf16[2,32,1280]{2,1,0:T(8,128)(2,1)S(1)}, u32[]{:S(2)}, u32[]{:S(2)}) collective-permute-start(bf16[2,32,1280]{2,1,0:T(8,128)(2,1)} %get-tuple-element.82), channel_id=1, source_target_pairs={{0,4},{2,6},{4,0},{6,2},{1,5},{3,7},{5,1},{7,3},{8,12},{10,14},{12... | collective-permute-start | bytes 491528 | tf_op jit(solution)/shard_map/ppermute | solution.py:30
  79.0 8.3 %collective-permute-start.22 = (bf16[2,32,1280]{2,1,0:T(8,128)(2,1)}, bf16[2,32,1280]{2,1,0:T(8,128)(2,1)S(1)}, u32[]{:S(2)}, u32[]{:S(2)}) collective-permute-start(bf16[2,32,1280]{2,1,0:T(8,128)(2,1)} %get-tuple-element.83), channel_id=1, source_target_pairs={{0,6},{2,0},{4,2},{6,4},{1,7},{3,1},{5,3},{7,5},{8,14},{10,8},{12,... | collective-permute-start | bytes 491528 | tf_op jit(solution)/shard_map/ppermute | solution.py:30
  82.9 6.0 %collective-permute-start.24 = (bf16[32,1280]{1,0:T(8,128)(2,1)S(1)}, bf16[32,1280]{1,0:T(8,128)(2,1)S(1)}, u32[]{:S(2)}, u32[]{:S(2)}) collective-permute-start(bf16[32,1280]{1,0:T(8,128)(2,1)S(1)} %add_convert_fusion.6), channel_id=1, source_target_pairs={{0,96},{96,0},{32,64},{64,32},{1,97},{97,1},{33,65},{65,33},{2,98}... | collective-permute-start | bytes 245768 | tf_op jit(solution)/shard_map/ppermute | solution.py:42
  (10 other events, 109.1 us)

commit v9 on v8

--- a/solution.py
+++ b/solution.py
@@ -413,13 +413,17 @@
     row_dot = row_dot + swap_cores(row_dot)
     late, row_dot = lax.optimization_barrier((grad_slot_in, row_dot))
     row_dot = row_dot + near(row_dot, "x")
+    first_dot = row_dot
     row_dot = row_dot + far(row_dot, "x")
+    second_dot = row_dot
     row_dot = row_dot + near(row_dot, "y")
     row_dot = row_dot + far(row_dot, "y")
 
     partial_logits, *parts = dispatch_grad(
         tokens, late, slot_in, logits, lse, comb, grad_combine
     )
+    parts = list(lax.optimization_barrier((*parts, first_dot))[:4])
+    parts[3] = after(parts[3], second_dot)
     parts = sources(scatter_terms(parts, "y"))
 
     mine, other = patch_rows(parts, inputs, row_dot)
@@ -430,15 +434,17 @@
     embed_other = near(embed_part)
     sums = add_cores(after(mine, embed_part), other_core)
     terms = scatter_terms(sums, "x")
-    grad_tokens = sum(term.astype(F32) for term in terms).astype(BF16)
-    slot_late = after(slot_in, sums[0])
-    grad_w_in = jnp.einsum("sd,sh->dh", slot_late, grad_pre, preferred_element_type=F32)
-    grad_w_in = grad_w_in.astype(BF16)
-
     embed_part = add(after(embed_part, terms[1]), embed_other)
     embed_sum = add(embed_part, far(embed_part))
     z = lax.axis_index("seq")
     grad_embed = lax.dynamic_slice_in_dim(embed_sum, z * 320, 320, axis=1).T
+    slot_late = after(slot_in, embed_part)
+    grad_w_in = jnp.einsum("sd,sh->dh", slot_late, grad_pre, preferred_element_type=F32)
+    grad_w_in = grad_w_in.astype(BF16)
+
+    nearer = terms[0].astype(F32) + terms[1].astype(F32) + terms[3].astype(F32)
+    nearer, grad_w_in = lax.optimization_barrier((nearer, grad_w_in.astype(BF16)))
+    grad_tokens = (nearer + terms[2].astype(F32)).astype(BF16)
     return (
         grad_tokens,
         grad_embed,

time: 90.4 us -> 96.7 us (1.070)
  waiting for transfers between devices: 21.7 us -> 30.8 us
  starting transfers between devices: 38.4 us -> 35.3 us
  other arithmetic: 2.64 us -> 3.62 us
    ppermute x9, waiting for transfers between devices: 2.65 us -> 8.26 us  [shift(): return lax.ppermute(value, axis, [(i, (i + by) % 4) for i in range(4)])]
    ppermute x7, waiting for transfers between devices: 11.5 us -> 15.1 us  [near(): return lax.ppermute(value, axis, [(0, 1), (1, 0), (2, 3), (3, 2)])]
    ppermute x7, starting transfers between devices: 16.1 us -> 14 us  [far(): return lax.ppermute(value, axis, [(0, 3), (3, 0), (1, 2), (2, 1)])]
    ppermute x7, starting transfers between devices: 5.96 us -> 4.23 us  [near(): return lax.ppermute(value, axis, [(0, 1), (1, 0), (2, 3), (3, 2)])]
    add x0 -> x1, other arithmetic: none -> 1.06 us  [local(): nearer = terms[0].astype(F32) + terms[1].astype(F32) + terms[3].astype(F32)]
    convert_element_type x1, other arithmetic: 1.67 us -> 0.7 us  [local(): grad_tokens = (nearer + terms[2].astype(F32)).astype(BF16)]
  transfers between devices with their start and end apart: 25 -> 25, of which waited for: 12 -> 11; matrix products, arithmetic and copies ran while one was open for 14% -> 14% of each run, Pallas kernels for 6% -> 8%
where the time goes in v9:
time: 96.7 us; the launch traced here: 96.5 us
  starting transfers between devices  35.3 us (37%)
  waiting for transfers between devices  30.8 us (32%)
  Pallas kernels  14.7 us (15%)
  matrix products  11.1 us (11%)
  other arithmetic  3.62 us (4%)
    ppermute x9, starting transfers between devices, shift(): return lax.ppermute(value, axis, [(i, (i + by) % 4) for i in range(4)])  16.9 us
    ppermute x7, waiting for transfers between devices, near(): return lax.ppermute(value, axis, [(0, 1), (1, 0), (2, 3), (3, 2)])  15.1 us
    ppermute x7, starting transfers between devices, far(): return lax.ppermute(value, axis, [(0, 3), (3, 0), (1, 2), (2, 1)])  14 us
    ppermute x9, waiting for transfers between devices, shift(): return lax.ppermute(value, axis, [(i, (i + by) % 4) for i in range(4)])  8.26 us
    ppermute x7, waiting for transfers between devices, far(): return lax.ppermute(value, axis, [(0, 3), (3, 0), (1, 2), (2, 1)])  6.34 us
    pallas_call x1, Pallas kernels, local_softmax(): pl.pallas_call(softmax_kernel, grid=(2,), in_specs=[*patch_streams(), pl....  5.48 us
    ppermute x7, starting transfers between devices, near(): return lax.ppermute(value, axis, [(0, 1), (1, 0), (2, 3), (3, 2)])  4.23 us
    dot_general x1, matrix products, local(): jnp.einsum('sd,sh->dh', slot_late, grad_pre, preferred_element_type=F32)  3.68 us
  transfers between devices with their start and end apart: 25, of which 11 were waited for; matrix products, arithmetic and copies ran while one was open for 14% of the time, Pallas kernels for 8%

profile of v9, /device:TPU:0, one launch (start us, length us, event | category | flops | bytes accessed | tf_op | source)
XLA Modules:
  0.0 96.5 jit_solution(3990648259775097975)
XLA Ops:
  0.7 5.5 %local_softmax.1 = (f32[64,1024]{1,0:T(8,128)S(1)}, bf16[64,1408]{1,0:T(8,128)(2,1)S(1)}) custom-call(bf16[2,1024,1280]{2,1,0:T(8,128)(2,1)} %t11.3, bf16[2,1024,1280]{2,1,0:T(8,128)(2,1)} %t11.3, bf16[2,1024,1280]{2,1,0:T(8,128)(2,1)} %t11.3, bf16[2,1024,1280]{2,1,0:T(8,128)(2,1)} %t11.3, bf16[32,1280]{1,0:T(8,128)(2,1)} %bitcast.47), custom_call_target="tpu_custom_call" | custom-call | flops 700000000 | bytes 6000000 | tf_op jit(solution)/shard_map/local_softmax/pallas_call | solution.py:122
  6.2 2.1 %collective-permute-start = (bf16[64,1408]{1,0:T(8,128)(2,1)S(1)}, bf16[64,1408]{1,0:T(8,128)(2,1)S(1)}, u32[]{:S(2)}, u32[]{:S(2)}) collective-permute-start(bf16[64,1408]{1,0:T(8,128)(2,1)S(1)} %get-tuple-element.55.a), channel_id=1, source_target_pairs={{0,32},{32,0},{64,96},{96,64},{1,33},{33,1},{65,97},{97,65},{2,34}... | collective-permute-start | bytes 540680 | tf_op jit(solution)/shard_map/ppermute | solution.py:38
  9.2 3.6 %collective-permute-done.b = bf16[64,1408]{1,0:T(8,128)(2,1)S(1)} collective-permute-done((bf16[64,1408]{1,0:T(8,128)(2,1)S(1)}, bf16[64,1408]{1,0:T(8,128)(2,1)S(1)}, u32[]{:S(2)}, u32[]{:S(2)}) %collective-permute-start) | collective-permute-done | bytes 180256 | tf_op jit(solution)/shard_map/ppermute | solution.py:38
  13.0 3.9 %collective-permute-start.1 = (bf16[64,1408]{1,0:T(8,128)(2,1)S(1)}, bf16[64,1408]{1,0:T(8,128)(2,1)S(1)}, u32[]{:S(2)}, u32[]{:S(2)}) collective-permute-start(bf16[64,1408]{1,0:T(8,128)(2,1)S(1)} %merge_pair.1.one), channel_id=1, source_target_pairs={{0,96},{96,0},{32,64},{64,32},{1,97},{97,1},{33,65},{65,33},{2,98}... | collective-permute-start | bytes 540680 | tf_op jit(solution)/shard_map/ppermute | solution.py:42
  17.0 3.3 %collective-permute-start.6 = (bf16[224,256]{1,0:T(8,128)(2,1)S(1)}, bf16[224,256]{1,0:T(8,128)(2,1)S(1)}, u32[]{:S(2)}, u32[]{:S(2)}) collective-permute-start(bf16[224,256]{1,0:T(8,128)(2,1)S(1)} %get-tuple-element.63), channel_id=1, source_target_pairs={{0,16},{8,24},{16,0},{24,8},{1,17},{9,25},{17,1},{25,9},{2,18},{10... | collective-permute-start | bytes 344072 | tf_op jit(solution)/shard_map/ppermute | solution.py:30
  22.4 1.7 %collective-permute-start.3 = (bf16[64,1280]{1,0:T(8,128)(2,1)S(1)}, bf16[64,1280]{1,0:T(8,128)(2,1)S(1)}, u32[]{:S(2)}, u32[]{:S(2)}) collective-permute-start(bf16[64,1280]{1,0:T(8,128)(2,1)S(1)} %add_convert_fusion.5), channel_id=1, source_target_pairs={{0,96},{96,0},{32,64},{64,32},{1,97},{97,1},{33,65},{65,33},{2,98}... | collective-permute-start | bytes 491528 | tf_op jit(solution)/shard_map/ppermute | solution.py:42
  25.6 3.1 %collective-permute-start.5 = (bf16[224,256]{1,0:T(8,128)(2,1)S(1)}, bf16[224,256]{1,0:T(8,128)(2,1)S(1)}, u32[]{:S(2)}, u32[]{:S(2)}) collective-permute-start(bf16[224,256]{1,0:T(8,128)(2,1)S(1)} %get-tuple-element.62), channel_id=1, source_target_pairs={{0,24},{8,0},{16,8},{24,16},{1,25},{9,1},{17,9},{25,17},{2,26},{10... | collective-permute-start | bytes 344072 | tf_op jit(solution)/shard_map/ppermute | solution.py:30
  32.1 1.7 %collective-permute-start.9 = (bf16[64,1280]{1,0:T(8,128)(2,1)S(1)}, bf16[64,1280]{1,0:T(8,128)(2,1)S(1)}, u32[]{:S(2)}, u32[]{:S(2)}) collective-permute-start(bf16[64,1280]{1,0:T(8,128)(2,1)S(1)} %add_convert_fusion.3.sum_a), channel_id=1, source_target_pairs={{0,96},{96,0},{32,64},{64,32},{1,97},{97,1},{33,65},{65,33},{2,98}... | collective-permute-start | bytes 491528 | tf_op jit(solution)/shard_map/ppermute | solution.py:42
  34.2 2.8 %convolution_convert_fusion.1 = bf16[1280,1280]{1,0:T(8,128)(2,1)} fusion(bf16[64,1280]{1,0:T(8,128)(2,1)S(1)} %get-tuple-element.67, bf16[64,1280]{1,0:T(8,128)(2,1)S(1)} %add_convert_fusion.4), kind=kOutput, calls=%fused_computation.1 | convolution fusion | flops 211353600 | bytes 3604480 | tf_op jit(solution)/shard_map/sh,sd->hd/dot_general | solution.py:406
  36.9 2.2 %collective-permute-done.8 = bf16[64,1280]{1,0:T(8,128)(2,1)S(1)} collective-permute-done((bf16[64,1280]{1,0:T(8,128)(2,1)S(1)}, bf16[64,1280]{1,0:T(8,128)(2,1)S(1)}, u32[]{:S(2)}, u32[]{:S(2)}) %collective-permute-start.8) | collective-permute-done | bytes 163872 | tf_op jit(solution)/shard_map/ppermute | solution.py:38
  39.2 1.7 %collective-permute-start.10 = (bf16[64,1280]{1,0:T(8,128)(2,1)S(1)}, bf16[64,1280]{1,0:T(8,128)(2,1)S(1)}, u32[]{:S(2)}, u32[]{:S(2)}) collective-permute-start(bf16[64,1280]{1,0:T(8,128)(2,1)S(1)} %add_convert_fusion.2), channel_id=1, source_target_pairs={{0,96},{96,0},{32,64},{64,32},{1,97},{97,1},{33,65},{65,33},{2,98}... | collective-permute-start | bytes 491528 | tf_op jit(solution)/shard_map/ppermute | solution.py:42
  40.9 2.2 %combine_grad.1 = (f32[64,1024]{1,0:T(8,128)S(1)}, f32[2,1,1024]{2,1,0:T(1,128)S(1)}) custom-call(bf16[2,1024,1280]{2,1,0:T(8,128)(2,1)S(1)} %copy-done.1, bf16[64,1280]{1,0:T(8,128)(2,1)S(1)} %add_convert_fusion.3.sum_a, bf16[64,1280]{1,0:T(8,128)(2,1)S(1)} %collective-permute-done.9.sum_b, bf16[64,1024]{1,0:T(8,128)(2,1)S(1)} %bitcast.44), custom_call_target="tpu_custom_call" | custom-call | flops 350000000 | bytes 6000000 | tf_op jit(solution)/shard_map/combine_grad/pallas_call | solution.py:188
  47.4 2.2 %collective-permute-done.12 = f32[2,1,1024]{2,1,0:T(1,128)S(1)} collective-permute-done((f32[2,1,1024]{2,1,0:T(1,128)S(1)}, f32[2,1,1024]{2,1,0:T(1,128)S(1)}, u32[]{:S(2)}, u32[]{:S(2)}) %collective-permute-start.12) | collective-permute-done | bytes 8224 | tf_op jit(solution)/shard_map/ppermute | solution.py:38
  49.6 2.8 %collective-permute-start.13 = (f32[2,1,1024]{2,1,0:T(1,128)S(1)}, f32[2,1,1024]{2,1,0:T(1,128)S(1)}, u32[]{:S(2)}, u32[]{:S(2)}) collective-permute-start(f32[2,1,1024]{2,1,0:T(1,128)S(1)} %add.66), channel_id=1, source_target_pairs={{0,6},{6,0},{2,4},{4,2},{1,7},{7,1},{3,5},{5,3},{8,14},{14,8},{10,... | collective-permute-start | bytes 24584 | tf_op jit(solution)/shard_map/ppermute | solution.py:42
  52.4 1.9 %dispatch_grad.1 = (f32[64,1024]{1,0:T(8,128)S(1)}, bf16[64,1792]{1,0:T(8,128)(2,1)S(1)}, bf16[64,1792]{1,0:T(8,128)(2,1)S(1)}, bf16[64,1792]{1,0:T(8,128)(2,1)S(1)}, bf16[64,1792]{1,0:T(8,128)(2,1)S(1)}) custom-call(bf16[2,1024,1280]{2,1,0:T(8,128)(2,1)S(1)} %bitcast.41, bf16[64,1280]{1,0:T(8,128)(2,1)S(1)} %add_convert_fusion.1.gslot, ...), custom_call_target="tpu_custom_call" | custom-call | flops 350000000 | bytes 7000000 | tf_op jit(solution)/shard_map/dispatch_grad/pallas_call | solution.py:226
  54.3 3.3 %collective-permute-start.15 = (bf16[64,1792]{1,0:T(8,128)(2,1)S(1)}, bf16[64,1792]{1,0:T(8,128)(2,1)S(1)}, u32[]{:S(2)}, u32[]{:S(2)}) collective-permute-start(bf16[64,1792]{1,0:T(8,128)(2,1)S(1)} %get-tuple-element.85), channel_id=1, source_target_pairs={{0,16},{8,24},{16,0},{24,8},{1,17},{9,25},{17,1},{25,9},{2,18},{10... | collective-permute-start | bytes 688136 | tf_op jit(solution)/shard_map/ppermute | solution.py:30
  58.3 2.6 %collective-permute-start.14 = (bf16[64,1792]{1,0:T(8,128)(2,1)S(1)}, bf16[64,1792]{1,0:T(8,128)(2,1)S(1)}, u32[]{:S(2)}, u32[]{:S(2)}) collective-permute-start(bf16[64,1792]{1,0:T(8,128)(2,1)S(1)} %get-tuple-element.84), channel_id=1, source_target_pairs={{0,24},{8,0},{16,8},{24,16},{1,25},{9,1},{17,9},{25,17},{2,26},{10... | collective-permute-start | bytes 688136 | tf_op jit(solution)/shard_map/ppermute | solution.py:30
  60.9 5.3 %collective-permute-done.17 = f32[2,1,1024]{2,1,0:T(1,128)S(1)} collective-permute-done((f32[2,1,1024]{2,1,0:T(1,128)S(1)}, f32[2,1,1024]{2,1,0:T(1,128)S(1)}, u32[]{:S(2)}, u32[]{:S(2)}) %collective-permute-start.17) | collective-permute-done | bytes 8224 | tf_op jit(solution)/shard_map/ppermute | solution.py:38
  66.7 4.7 %collective-permute-done.18 = f32[2,1,1024]{2,1,0:T(1,128)S(1)} collective-permute-done((f32[2,1,1024]{2,1,0:T(1,128)S(1)}, f32[2,1,1024]{2,1,0:T(1,128)S(1)}, u32[]{:S(2)}, u32[]{:S(2)}) %collective-permute-start.18) | collective-permute-done | bytes 8224 | tf_op jit(solution)/shard_map/ppermute | solution.py:42
  72.2 3.1 %embed_grad.1 = bf16[32,1280]{1,0:T(8,128)(2,1)S(1)} custom-call(bf16[2,1024,1280]{2,1,0:T(8,128)(2,1)} %t11.3, bf16[2,1024,1280]{2,1,0:T(8,128)(2,1)} %t11.3, bf16[2,1024,1280]{2,1,0:T(8,128)(2,1)} %t11.3, bf16[2,1024,1280]{2,1,0:T(8,128)(2,1)} %t11.3, f32[64,1024]{1,0:T(8,128)S(1)} %get-tuple-element.89.partial_logits, bf16[64,1024]{1,0:T(8,128)(2,1)S(1)} %bitcast.46, ...), custom_call_target="tpu_custom_call" | custom-call | flops 170000000 | bytes 6000000 | tf_op jit(solution)/shard_map/embed_grad/pallas_call | solution.py:294
  76.6 3.0 %collective-permute-start.21 = (bf16[2,32,1280]{2,1,0:T(8,128)(2,1)}, bf16[2,32,1280]{2,1,0:T(8,128)(2,1)S(1)}, u32[]{:S(2)}, u32[]{:S(2)}) collective-permute-start(bf16[2,32,1280]{2,1,0:T(8,128)(2,1)} %get-tuple-element.94), channel_id=1, source_target_pairs={{0,6},{2,0},{4,2},{6,4},{1,7},{3,1},{5,3},{7,5},{8,14},{10,8},{12,... | collective-permute-start | bytes 491528 | tf_op jit(solution)/shard_map/ppermute | solution.py:30
  79.6 8.2 %collective-permute-done.20 = bf16[2,32,1280]{2,1,0:T(8,128)(2,1)} collective-permute-done((bf16[2,32,1280]{2,1,0:T(8,128)(2,1)}, bf16[2,32,1280]{2,1,0:T(8,128)(2,1)}, u32[]{:S(2)}, u32[]{:S(2)}) %collective-permute-start.20) | collective-permute-done | bytes 163872 | tf_op jit(solution)/shard_map/ppermute | solution.py:30
  88.7 1.7 %collective-permute-start.24 = (bf16[32,1280]{1,0:T(8,128)(2,1)S(1)}, bf16[32,1280]{1,0:T(8,128)(2,1)S(1)}, u32[]{:S(2)}, u32[]{:S(2)}) collective-permute-start(bf16[32,1280]{1,0:T(8,128)(2,1)S(1)} %add_convert_fusion.6), channel_id=1, source_target_pairs={{0,96},{96,0},{32,64},{64,32},{1,97},{97,1},{33,65},{65,33},{2,98}... | collective-permute-start | bytes 245768 | tf_op jit(solution)/shard_map/ppermute | solution.py:42
  91.5 3.7 %convolution_convert_fusion = bf16[1280,1280]{1,0:T(8,128)(2,1)} fusion(bf16[64,1280]{1,0:T(8,128)(2,1)S(1)} %get-tuple-element.96.slot_in, bf16[64,1280]{1,0:T(8,128)(2,1)} %copy-done.5), kind=kOutput, calls=%fused_computation | convolution fusion | flops 211353600 | bytes 3604480 | tf_op jit(solution)/shard_map/sd,sh->dh/dot_general | solution.py:442
  (73 shorter events, 19.4 us)
Async XLA Ops:
  6.2 6.6 %collective-permute-start = (bf16[64,1408]{1,0:T(8,128)(2,1)S(1)}, bf16[64,1408]{1,0:T(8,128)(2,1)S(1)}, u32[]{:S(2)}, u32[]{:S(2)}) collective-permute-start(bf16[64,1408]{1,0:T(8,128)(2,1)S(1)} %get-tuple-element.55.a), channel_id=1, source_target_pairs={{0,32},{32,0},{64,96},{96,64},{1,33},{33,1},{65,97},{97,65},{2,34}... | collective-permute-start | bytes 540680 | tf_op jit(solution)/shard_map/ppermute | solution.py:38
  13.0 8.0 %collective-permute-start.1 = (bf16[64,1408]{1,0:T(8,128)(2,1)S(1)}, bf16[64,1408]{1,0:T(8,128)(2,1)S(1)}, u32[]{:S(2)}, u32[]{:S(2)}) collective-permute-start(bf16[64,1408]{1,0:T(8,128)(2,1)S(1)} %merge_pair.1.one), channel_id=1, source_target_pairs={{0,96},{96,0},{32,64},{64,32},{1,97},{97,1},{33,65},{65,33},{2,98}... | collective-permute-start | bytes 540680 | tf_op jit(solution)/shard_map/ppermute | solution.py:42
  17.0 5.3 %collective-permute-start.2 = (bf16[64,1280]{1,0:T(8,128)(2,1)S(1)}, bf16[64,1280]{1,0:T(8,128)(2,1)S(1)}, u32[]{:S(2)}, u32[]{:S(2)}) collective-permute-start(bf16[64,1280]{1,0:T(8,128)(2,1)S(1)} %bitcast.51), channel_id=1, source_target_pairs={{0,32},{32,0},{64,96},{96,64},{1,33},{33,1},{65,97},{97,65},{2,34}... | collective-permute-start | bytes 491528 | tf_op jit(solution)/shard_map/ppermute | solution.py:38
  17.0 15.1 %collective-permute-start.6 = (bf16[224,256]{1,0:T(8,128)(2,1)S(1)}, bf16[224,256]{1,0:T(8,128)(2,1)S(1)}, u32[]{:S(2)}, u32[]{:S(2)}) collective-permute-start(bf16[224,256]{1,0:T(8,128)(2,1)S(1)} %get-tuple-element.63), channel_id=1, source_target_pairs={{0,16},{8,24},{16,0},{24,8},{1,17},{9,25},{17,1},{25,9},{2,18},{10... | collective-permute-start | bytes 344072 | tf_op jit(solution)/shard_map/ppermute | solution.py:30
  20.3 11.8 %collective-permute-start.7 = (bf16[224,256]{1,0:T(8,128)(2,1)S(1)}, bf16[224,256]{1,0:T(8,128)(2,1)S(1)}, u32[]{:S(2)}, u32[]{:S(2)}) collective-permute-start(bf16[224,256]{1,0:T(8,128)(2,1)S(1)} %get-tuple-element.64), channel_id=1, source_target_pairs={{0,8},{8,16},{16,24},{24,0},{1,9},{9,17},{17,25},{25,1},{2,10},{10... | collective-permute-start | bytes 344072 | tf_op jit(solution)/shard_map/ppermute | solution.py:30
  22.4 6.6 %collective-permute-start.3 = (bf16[64,1280]{1,0:T(8,128)(2,1)S(1)}, bf16[64,1280]{1,0:T(8,128)(2,1)S(1)}, u32[]{:S(2)}, u32[]{:S(2)}) collective-permute-start(bf16[64,1280]{1,0:T(8,128)(2,1)S(1)} %add_convert_fusion.5), channel_id=1, source_target_pairs={{0,96},{96,0},{32,64},{64,32},{1,97},{97,1},{33,65},{65,33},{2,98}... | collective-permute-start | bytes 491528 | tf_op jit(solution)/shard_map/ppermute | solution.py:42
  25.5 5.4 %collective-permute-start.4 = (bf16[64,1280]{1,0:T(8,128)(2,1)S(1)}, bf16[64,1280]{1,0:T(8,128)(2,1)S(1)}, u32[]{:S(2)}, u32[]{:S(2)}) collective-permute-start(bf16[64,1280]{1,0:T(8,128)(2,1)S(1)} %fusion.17), channel_id=1, source_target_pairs={{0,32},{32,0},{64,96},{96,64},{1,33},{33,1},{65,97},{97,65},{2,34}... | collective-permute-start | bytes 491528 | tf_op jit(solution)/shard_map/ppermute | solution.py:38
  25.6 6.5 %collective-permute-start.5 = (bf16[224,256]{1,0:T(8,128)(2,1)S(1)}, bf16[224,256]{1,0:T(8,128)(2,1)S(1)}, u32[]{:S(2)}, u32[]{:S(2)}) collective-permute-start(bf16[224,256]{1,0:T(8,128)(2,1)S(1)} %get-tuple-element.62), channel_id=1, source_target_pairs={{0,24},{8,0},{16,8},{24,16},{1,25},{9,1},{17,9},{25,17},{2,26},{10... | collective-permute-start | bytes 344072 | tf_op jit(solution)/shard_map/ppermute | solution.py:30
  32.1 8.8 %collective-permute-start.9 = (bf16[64,1280]{1,0:T(8,128)(2,1)S(1)}, bf16[64,1280]{1,0:T(8,128)(2,1)S(1)}, u32[]{:S(2)}, u32[]{:S(2)}) collective-permute-start(bf16[64,1280]{1,0:T(8,128)(2,1)S(1)} %add_convert_fusion.3.sum_a), channel_id=1, source_target_pairs={{0,96},{96,0},{32,64},{64,32},{1,97},{97,1},{33,65},{65,33},{2,98}... | collective-permute-start | bytes 491528 | tf_op jit(solution)/shard_map/ppermute | solution.py:42
  33.8 5.3 %collective-permute-start.8 = (bf16[64,1280]{1,0:T(8,128)(2,1)S(1)}, bf16[64,1280]{1,0:T(8,128)(2,1)S(1)}, u32[]{:S(2)}, u32[]{:S(2)}) collective-permute-start(bf16[64,1280]{1,0:T(8,128)(2,1)S(1)} %fusion.14), channel_id=1, source_target_pairs={{0,32},{32,0},{64,96},{96,64},{1,33},{33,1},{65,97},{97,65},{2,34}... | collective-permute-start | bytes 491528 | tf_op jit(solution)/shard_map/ppermute | solution.py:38
  39.2 6.6 %collective-permute-start.10 = (bf16[64,1280]{1,0:T(8,128)(2,1)S(1)}, bf16[64,1280]{1,0:T(8,128)(2,1)S(1)}, u32[]{:S(2)}, u32[]{:S(2)}) collective-permute-start(bf16[64,1280]{1,0:T(8,128)(2,1)S(1)} %add_convert_fusion.2), channel_id=1, source_target_pairs={{0,96},{96,0},{32,64},{64,32},{1,97},{97,1},{33,65},{65,33},{2,98}... | collective-permute-start | bytes 491528 | tf_op jit(solution)/shard_map/ppermute | solution.py:42
  45.8 3.7 %collective-permute-start.12 = (f32[2,1,1024]{2,1,0:T(1,128)S(1)}, f32[2,1,1024]{2,1,0:T(1,128)S(1)}, u32[]{:S(2)}, u32[]{:S(2)}) collective-permute-start(f32[2,1,1024]{2,1,0:T(1,128)S(1)} %add.65), channel_id=1, source_target_pairs={{0,2},{2,0},{4,6},{6,4},{1,3},{3,1},{5,7},{7,5},{8,10},{10,8},{12,... | collective-permute-start | bytes 24584 | tf_op jit(solution)/shard_map/ppermute | solution.py:38
  49.6 8.7 %collective-permute-start.13 = (f32[2,1,1024]{2,1,0:T(1,128)S(1)}, f32[2,1,1024]{2,1,0:T(1,128)S(1)}, u32[]{:S(2)}, u32[]{:S(2)}) collective-permute-start(f32[2,1,1024]{2,1,0:T(1,128)S(1)} %add.66), channel_id=1, source_target_pairs={{0,6},{6,0},{2,4},{4,2},{1,7},{7,1},{3,5},{5,3},{8,14},{14,8},{10,... | collective-permute-start | bytes 24584 | tf_op jit(solution)/shard_map/ppermute | solution.py:42
  54.3 17.1 %collective-permute-start.15 = (bf16[64,1792]{1,0:T(8,128)(2,1)S(1)}, bf16[64,1792]{1,0:T(8,128)(2,1)S(1)}, u32[]{:S(2)}, u32[]{:S(2)}) collective-permute-start(bf16[64,1792]{1,0:T(8,128)(2,1)S(1)} %get-tuple-element.85), channel_id=1, source_target_pairs={{0,16},{8,24},{16,0},{24,8},{1,17},{9,25},{17,1},{25,9},{2,18},{10... | collective-permute-start | bytes 688136 | tf_op jit(solution)/shard_map/ppermute | solution.py:30
  57.6 13.8 %collective-permute-start.16 = (bf16[64,1792]{1,0:T(8,128)(2,1)S(1)}, bf16[64,1792]{1,0:T(8,128)(2,1)S(1)}, u32[]{:S(2)}, u32[]{:S(2)}) collective-permute-start(bf16[64,1792]{1,0:T(8,128)(2,1)S(1)} %get-tuple-element.86), channel_id=1, source_target_pairs={{0,8},{8,16},{16,24},{24,0},{1,9},{9,17},{17,25},{25,1},{2,10},{10... | collective-permute-start | bytes 688136 | tf_op jit(solution)/shard_map/ppermute | solution.py:30
  58.3 13.1 %collective-permute-start.14 = (bf16[64,1792]{1,0:T(8,128)(2,1)S(1)}, bf16[64,1792]{1,0:T(8,128)(2,1)S(1)}, u32[]{:S(2)}, u32[]{:S(2)}) collective-permute-start(bf16[64,1792]{1,0:T(8,128)(2,1)S(1)} %get-tuple-element.84), channel_id=1, source_target_pairs={{0,24},{8,0},{16,8},{24,16},{1,25},{9,1},{17,9},{25,17},{2,26},{10... | collective-permute-start | bytes 688136 | tf_op jit(solution)/shard_map/ppermute | solution.py:30
  60.9 5.3 %collective-permute-start.17 = (f32[2,1,1024]{2,1,0:T(1,128)S(1)}, f32[2,1,1024]{2,1,0:T(1,128)S(1)}, u32[]{:S(2)}, u32[]{:S(2)}) collective-permute-start(f32[2,1,1024]{2,1,0:T(1,128)S(1)} %add.67), channel_id=1, source_target_pairs={{0,8},{8,0},{16,24},{24,16},{1,9},{9,1},{17,25},{25,17},{2,10},{10... | collective-permute-start | bytes 24584 | tf_op jit(solution)/shard_map/ppermute | solution.py:38
  66.2 5.1 %collective-permute-start.18 = (f32[2,1,1024]{2,1,0:T(1,128)S(1)}, f32[2,1,1024]{2,1,0:T(1,128)S(1)}, u32[]{:S(2)}, u32[]{:S(2)}) collective-permute-start(f32[2,1,1024]{2,1,0:T(1,128)S(1)} %add.68), channel_id=1, source_target_pairs={{0,24},{24,0},{8,16},{16,8},{1,25},{25,1},{9,17},{17,9},{2,26},{26... | collective-permute-start | bytes 24584 | tf_op jit(solution)/shard_map/ppermute | solution.py:42
  72.1 3.2 %collective-permute-start.19 = (bf16[4,2,32,1280]{3,2,1,0:T(8,128)(2,1)S(1)}, bf16[4,2,32,1280]{3,2,1,0:T(8,128)(2,1)S(1)}, u32[]{:S(2)}, u32[]{:S(2)}) collective-permute-start(bf16[4,2,32,1280]{3,2,1,0:T(8,128)(2,1)S(1)} %get-tuple-element.91), channel_id=1, source_target_pairs={{0,1},{1,0},{2,3},{3,2},{4,5},{5,4},{6,7},{7,6},{8,9},{9,8},{10,11... | collective-permute-start | bytes 1966088 | tf_op jit(solution)/shard_map/ppermute | solution.py:34
  76.2 11.6 %collective-permute-start.20 = (bf16[2,32,1280]{2,1,0:T(8,128)(2,1)}, bf16[2,32,1280]{2,1,0:T(8,128)(2,1)}, u32[]{:S(2)}, u32[]{:S(2)}) collective-permute-start(bf16[2,32,1280]{2,1,0:T(8,128)(2,1)} %get-tuple-element.93), channel_id=1, source_target_pairs={{0,2},{2,4},{4,6},{6,0},{1,3},{3,5},{5,7},{7,1},{8,10},{10,12},{12... | collective-permute-start | bytes 491528 | tf_op jit(solution)/shard_map/ppermute | solution.py:30
  76.4 11.4 %collective-permute-start.22 = (bf16[32,1280]{1,0:T(8,128)(2,1)S(1)}, bf16[32,1280]{1,0:T(8,128)(2,1)}, u32[]{:S(2)}, u32[]{:S(2)}) collective-permute-start(bf16[32,1280]{1,0:T(8,128)(2,1)S(1)} %embed_grad.1), channel_id=1, source_target_pairs={{0,32},{32,0},{64,96},{96,64},{1,33},{33,1},{65,97},{97,65},{2,34}... | collective-permute-start | bytes 245768 | tf_op jit(solution)/shard_map/ppermute | solution.py:38
  76.6 13.9 %collective-permute-start.21 = (bf16[2,32,1280]{2,1,0:T(8,128)(2,1)}, bf16[2,32,1280]{2,1,0:T(8,128)(2,1)S(1)}, u32[]{:S(2)}, u32[]{:S(2)}) collective-permute-start(bf16[2,32,1280]{2,1,0:T(8,128)(2,1)} %get-tuple-element.94), channel_id=1, source_target_pairs={{0,6},{2,0},{4,2},{6,4},{1,7},{3,1},{5,3},{7,5},{8,14},{10,8},{12,... | collective-permute-start | bytes 491528 | tf_op jit(solution)/shard_map/ppermute | solution.py:30
  79.6 15.6 %collective-permute-start.23 = (bf16[2,32,1280]{2,1,0:T(8,128)(2,1)}, bf16[2,32,1280]{2,1,0:T(8,128)(2,1)S(1)}, u32[]{:S(2)}, u32[]{:S(2)}) collective-permute-start(bf16[2,32,1280]{2,1,0:T(8,128)(2,1)} %get-tuple-element.98), channel_id=1, source_target_pairs={{0,4},{2,6},{4,0},{6,2},{1,5},{3,7},{5,1},{7,3},{8,12},{10,14},{12... | collective-permute-start | bytes 491528 | tf_op jit(solution)/shard_map/ppermute | solution.py:30
  88.7 7.1 %collective-permute-start.24 = (bf16[32,1280]{1,0:T(8,128)(2,1)S(1)}, bf16[32,1280]{1,0:T(8,128)(2,1)S(1)}, u32[]{:S(2)}, u32[]{:S(2)}) collective-permute-start(bf16[32,1280]{1,0:T(8,128)(2,1)S(1)} %add_convert_fusion.6), channel_id=1, source_target_pairs={{0,96},{96,0},{32,64},{64,32},{1,97},{97,1},{33,65},{65,33},{2,98}... | collective-permute-start | bytes 245768 | tf_op jit(solution)/shard_map/ppermute | solution.py:42
  (9 other events, 110.1 us)

commit v10 on v9

--- a/solution.py
+++ b/solution.py
@@ -72,46 +72,47 @@
     return lanes[:, 0:1] + lanes[:, 1:2] + lanes[:, 2:3]
 
 
-def softmax_kernel(t00, t01, t10, t11, embed, logits, part, peak, total, sums):
-    step = pl.program_id(0)
-
-    @pl.when(step == 0)
-    def _():
-        peak[...] = jnp.full_like(peak, -jnp.inf)
-        total[...] = jnp.zeros_like(total)
-        sums[...] = jnp.zeros_like(sums)
-
-    slots = embed[...]
-    blocks = [[t00[0], t01[0]], [t10[0], t11[0]]]
-    scores = [
-        jnp.concatenate(
-            [lax.dot_general(one, slots, NT, preferred_element_type=F32).T for one in pair],
-            axis=1,
-        )
-        for pair in blocks
+def start_patches(source, target, sems):
+    copies = [
+        [
+            pltpu.make_async_copy(
+                source.at[i, pl.ds(256 * n, 256)],
+                target.at[i, pl.ds(256 * n, 256)],
+                sems.at[4 * i + n],
+            )
+            for n in range(4)
+        ]
+        for i in range(2)
     ]
+    for i in range(2):
+        for n in range(4):
+            copies[i][n].start()
+    return lambda i, n: copies[i][n].wait()
+
+
+def softmax_kernel(tok, embed, logits, part, patches, slots, sems, embed_sem):
+    embed_copy = pltpu.make_async_copy(embed, slots, embed_sem)
+    embed_copy.start()
+    wait = start_patches(tok, patches, sems)
+    embed_copy.wait()
+    columns = slots[...]
+    scores = []
+    for i in range(2):
+        pieces = []
+        for n in range(4):
+            wait(i, n)
+            rows = patches[i, 256 * n : 256 * n + 256, :]
+            pieces.append(lax.dot_general(rows, columns, NT, preferred_element_type=F32).T)
+        scores.append(jnp.concatenate(pieces, axis=1))
     for i in range(2):
         half = slice(32 * i, 32 * i + 32)
         logits[half, :] = scores[i]
-        before = peak[half, :1]
-        top = jnp.maximum(before, jnp.max(scores[i], axis=1, keepdims=True))
-        scale = jnp.exp(before - top)
-        weight = jnp.exp(scores[i] - top)
-        new_total = total[half, :1] * scale + jnp.sum(weight, axis=1, keepdims=True)
-        weight = weight.astype(BF16)
-        new_sums = sums[half, :] * scale
-        for n in range(2):
-            new_sums = new_sums + jnp.dot(
-                weight[:, 256 * n : 256 * n + 256], blocks[i][n], preferred_element_type=F32
-            )
-        peak[half, :] = jnp.broadcast_to(top, (32, 128))
-        total[half, :] = jnp.broadcast_to(new_total, (32, 128))
-        sums[half, :] = new_sums
-
-        @pl.when(step == pl.num_programs(0) - 1)
-        def _():
-            part[half, :1280] = (new_sums / new_total).astype(BF16)
-            part[half, 1280:] = lse_lanes(top + jnp.log(new_total))
+        peak = jnp.max(scores[i], axis=1, keepdims=True)
+        weight = jnp.exp(scores[i] - peak)
+        total = jnp.sum(weight, axis=1, keepdims=True)
+        sums = jnp.dot(weight.astype(BF16), patches[i], preferred_element_type=F32)
+        part[half, :1280] = (sums / total).astype(BF16)
+        part[half, 1280:] = lse_lanes(peak + jnp.log(total))
 
 
 def in_hbm(value):
@@ -121,25 +122,18 @@
 def local_softmax(tokens, embed):
     return pl.pallas_call(
         softmax_kernel,
-        grid=(2,),
-        in_specs=[
-            *patch_streams(),
-            pl.BlockSpec((32, 1280), lambda t: (0, 0)),
-        ],
-        out_specs=[
-            pl.BlockSpec((64, 512), lambda t: (0, t)),
-            pl.BlockSpec((64, 1408), lambda t: (0, 0)),
-        ],
+        in_specs=[pl.BlockSpec(memory_space=pl.ANY)] * 2,
         out_shape=[shape((64, 1024), F32), shape((64, 1408), BF16)],
         scratch_shapes=[
-            pltpu.VMEM((64, 128), F32),
-            pltpu.VMEM((64, 128), F32),
-            pltpu.VMEM((64, 1280), F32),
+            pltpu.VMEM((2, 1024, 1280), BF16),
+            pltpu.VMEM((32, 1280), BF16),
+            pltpu.SemaphoreType.DMA((8,)),
+            pltpu.SemaphoreType.DMA,
         ],
         cost_estimate=pl.CostEstimate(flops=700_000_000, bytes_accessed=6_000_000, transcendentals=65536),
         compiler_params=LARGE,
         name="local_softmax",
-    )(*[in_hbm(tokens)] * 4, in_hbm(embed))
+    )(in_hbm(tokens), in_hbm(embed))
 
 
 def merge_kernel(one, two, sums, lse):
@@ -179,25 +173,16 @@
 
 def combine_grad_kernel(gout, sum_a, sum_b, comb, grad, row):
     slot_out = add(sum_a[...], sum_b[...])
-    value = lax.dot_general(gout[0], slot_out, NT, preferred_element_type=F32).T
-    grad[...] = value
-    row[0] = jnp.sum(comb[...].astype(F32) * value, axis=0, keepdims=True)
+    for i in range(2):
+        half = slice(32 * i, 32 * i + 32)
+        value = lax.dot_general(gout[i], slot_out[half, :], NT, preferred_element_type=F32).T
+        grad[half, :] = value
+        row[i] = jnp.sum(comb[half, :].astype(F32) * value, axis=0, keepdims=True)
 
 
 def combine_grad(grad_out, sum_a, sum_b, comb):
     return pl.pallas_call(
         combine_grad_kernel,
-        grid=(2, 2),
-        in_specs=[
-            pl.BlockSpec((1, 512, 1280), lambda i, t: (i, t, 0)),
-            pl.BlockSpec((32, 1280), lambda i, t: (i, 0)),
-            pl.BlockSpec((32, 1280), lambda i, t: (i, 0)),
-            pl.BlockSpec((32, 512), lambda i, t: (i, t)),
-        ],
-        out_specs=[
-            pl.BlockSpec((32, 512), lambda i, t: (i, t)),
-            pl.BlockSpec((1, 1, 512), lambda i, t: (i, 0, t)),
-        ],
         out_shape=[shape((64, 1024), F32), shape((2, 1, 1024), F32)],
         cost_estimate=pl.CostEstimate(flops=350_000_000, bytes_accessed=6_000_000, transcendentals=0),
         compiler_params=MEDIUM,
@@ -206,38 +191,26 @@
 
 
 def dispatch_grad_kernel(tok, gslot, slot_in, logits, lse, comb, gcomb, full, c0, c1, c2, c3, all_weight):
-    rows = gslot[...]
-    col_dot = jnp.sum(slot_in[...].astype(F32) * rows.astype(F32), axis=1, keepdims=True)
-    grad = lax.dot_general(tok[0], rows, NT, preferred_element_type=F32).T
-    weight = jnp.exp(logits[...] - lse[:, :1])
-    full[...] = weight * (grad - col_dot) + comb[...].astype(F32) * gcomb[...]
-    all_weight[...] = weight
-    for k, out in enumerate((c0, c1, c2, c3)):
-        piece = pl.ds(chunk("y", k, 256), 256)
-        out[:, :1280] = rows
-        out[:, 1280:1536] = full[:, piece].astype(BF16)
-        out[:, 1536:] = all_weight[:, piece].astype(BF16)
+    for i in range(2):
+        half = slice(32 * i, 32 * i + 32)
+        rows = gslot[half, :]
+        col_dot = jnp.sum(slot_in[half, :].astype(F32) * rows.astype(F32), axis=1, keepdims=True)
+        grad = lax.dot_general(tok[i], rows, NT, preferred_element_type=F32).T
+        weight = jnp.exp(logits[half, :] - lse[half, :1])
+        full[half, :] = weight * (grad - col_dot) + comb[half, :].astype(F32) * gcomb[half, :]
+        all_weight[half, :] = weight
+        for k, out in enumerate((c0, c1, c2, c3)):
+            piece = pl.ds(chunk("y", k, 256), 256)
+            out[half, :1280] = rows
+            out[half, 1280:1536] = full[half, piece].astype(BF16)
+            out[half, 1536:] = all_weight[half, piece].astype(BF16)
 
 
 def dispatch_grad(tokens, gslot, slot_in, logits, lse, comb, gcomb):
-    rows = pl.BlockSpec((32, 1280), lambda i: (i, 0))
-    wide = pl.BlockSpec((32, 1024), lambda i: (i, 0))
-    part = pl.BlockSpec((32, 1792), lambda i: (i, 0))
     return pl.pallas_call(
         dispatch_grad_kernel,
-        grid=(2,),
-        in_specs=[
-            pl.BlockSpec((1, 1024, 1280), lambda i: (i, 0, 0)),
-            rows,
-            rows,
-            wide,
-            pl.BlockSpec((32, 128), lambda i: (i, 0)),
-            wide,
-            wide,
-        ],
-        out_specs=[wide] + [part] * 4,
         out_shape=[shape((64, 1024), F32)] + [shape((64, 1792), BF16)] * 4,
-        scratch_shapes=[pltpu.VMEM((32, 1024), F32)],
+        scratch_shapes=[pltpu.VMEM((64, 1024), F32)],
         cost_estimate=pl.CostEstimate(flops=350_000_000, bytes_accessed=7_000_000, transcendentals=65536),
         compiler_params=MEDIUM,
         name="dispatch_grad",
@@ -261,47 +234,33 @@
     )(comb, embed)
 
 
-def embed_grad_kernel(t00, t01, t10, t11, partial_logits, comb, row_dot, out, sums):
+def embed_grad_kernel(tok, partial_logits, comb, row_dot, out, patches, sems):
+    wait = start_patches(tok, patches, sems)
     value = 0.0
-    for i, pair in enumerate(((t00, t01), (t10, t11))):
+    for i in range(2):
         half = slice(32 * i, 32 * i + 32)
         grad = partial_logits[half, :] - comb[half, :].astype(F32) * row_dot[i]
         grad = grad.astype(BF16)
-        for n in range(2):
+        for n in range(4):
+            wait(i, n)
+            span = slice(256 * n, 256 * n + 256)
             value = value + jnp.dot(
-                grad[:, 256 * n : 256 * n + 256], pair[n][0], preferred_element_type=F32
+                grad[:, span], patches[i, span, :], preferred_element_type=F32
             )
-
-    @pl.when(pl.program_id(0) == 0)
-    def _():
-        sums[...] = value
-
-    @pl.when(pl.program_id(0) == 1)
-    def _():
-        out[...] = (sums[...] + value).astype(BF16)
-
-
-def patch_streams():
-    return [
-        pl.BlockSpec((1, 256, 1280), lambda t, i=i, n=n: (i, 2 * t + n, 0))
-        for i in range(2)
-        for n in range(2)
-    ]
+    out[...] = value.astype(BF16)
 
 
 def embed_grad(tokens, partial_logits, comb, row_dot):
-    wide = pl.BlockSpec((64, 512), lambda t: (0, t))
     return pl.pallas_call(
         embed_grad_kernel,
-        grid=(2,),
-        in_specs=[*patch_streams(), wide, wide, pl.BlockSpec((2, 1, 512), lambda t: (0, 0, t))],
-        out_specs=pl.BlockSpec((32, 1280), lambda t: (0, 0)),
+        in_specs=[pl.BlockSpec(memory_space=pl.ANY)]
+        + [pl.BlockSpec(memory_space=pltpu.VMEM)] * 3,
         out_shape=shape((32, 1280), BF16),
-        scratch_shapes=[pltpu.VMEM((32, 1280), F32)],
+        scratch_shapes=[pltpu.VMEM((2, 1024, 1280), BF16), pltpu.SemaphoreType.DMA((8,))],
         cost_estimate=pl.CostEstimate(flops=170_000_000, bytes_accessed=6_000_000, transcendentals=0),
         compiler_params=MEDIUM,
         name="embed_grad",
-    )(*[in_hbm(tokens)] * 4, partial_logits, comb, row_dot)
+    )(in_hbm(tokens), partial_logits, comb, row_dot)
 
 
 def rows_kernel(*refs):
@@ -413,17 +372,13 @@
     row_dot = row_dot + swap_cores(row_dot)
     late, row_dot = lax.optimization_barrier((grad_slot_in, row_dot))
     row_dot = row_dot + near(row_dot, "x")
-    first_dot = row_dot
     row_dot = row_dot + far(row_dot, "x")
-    second_dot = row_dot
     row_dot = row_dot + near(row_dot, "y")
     row_dot = row_dot + far(row_dot, "y")
 
     partial_logits, *parts = dispatch_grad(
         tokens, late, slot_in, logits, lse, comb, grad_combine
     )
-    parts = list(lax.optimization_barrier((*parts, first_dot))[:4])
-    parts[3] = after(parts[3], second_dot)
     parts = sources(scatter_terms(parts, "y"))
 
     mine, other = patch_rows(parts, inputs, row_dot)
@@ -431,10 +386,12 @@
 
     partial_logits, mine = lax.optimization_barrier((partial_logits, mine))
     embed_part = embed_grad(tokens, partial_logits, comb, row_dot)
+    sums = add_cores(after(mine, embed_part), other_core)
+    embed_part = after(embed_part, sums[0])
     embed_other = near(embed_part)
-    sums = add_cores(after(mine, embed_part), other_core)
     terms = scatter_terms(sums, "x")
-    embed_part = add(after(embed_part, terms[1]), embed_other)
+    grad_tokens = sum(term.astype(F32) for term in terms).astype(BF16)
+    embed_part = add(embed_part, embed_other)
     embed_sum = add(embed_part, far(embed_part))
     z = lax.axis_index("seq")
     grad_embed = lax.dynamic_slice_in_dim(embed_sum, z * 320, 320, axis=1).T
@@ -442,9 +399,6 @@
     grad_w_in = jnp.einsum("sd,sh->dh", slot_late, grad_pre, preferred_element_type=F32)
     grad_w_in = grad_w_in.astype(BF16)
 
-    nearer = terms[0].astype(F32) + terms[1].astype(F32) + terms[3].astype(F32)
-    nearer, grad_w_in = lax.optimization_barrier((nearer, grad_w_in.astype(BF16)))
-    grad_tokens = (nearer + terms[2].astype(F32)).astype(BF16)
     return (
         grad_tokens,
         grad_embed,

time: 96.7 us -> 90 us (0.931)
  waiting for transfers between devices: 30.8 us -> 19.9 us
  starting transfers between devices: 35.3 us -> 38.4 us
  other arithmetic: 3.62 us -> 2.61 us
    ppermute x9, waiting for transfers between devices: 8.26 us -> 0.27 us  [shift(): return lax.ppermute(value, axis, [(i, (i + by) % 4) for i in range(4)])]
    ppermute x7, waiting for transfers between devices: 15.1 us -> 11.1 us  [near(): return lax.ppermute(value, axis, [(0, 1), (1, 0), (2, 3), (3, 2)])]
    ppermute x7, starting transfers between devices: 14 us -> 15.9 us  [far(): return lax.ppermute(value, axis, [(0, 3), (3, 0), (1, 2), (2, 1)])]
    ppermute x7, starting transfers between devices: 4.23 us -> 5.94 us  [near(): return lax.ppermute(value, axis, [(0, 1), (1, 0), (2, 3), (3, 2)])]
    add x1 -> x0, other arithmetic: 1.06 us -> none  [local(): nearer = terms[0].astype(F32) + terms[1].astype(F32) + terms[3].astype(F32)]
    ppermute x7, waiting for transfers between devices: 6.34 us -> 7.39 us  [far(): return lax.ppermute(value, axis, [(0, 3), (3, 0), (1, 2), (2, 1)])]
  transfers between devices with their start and end apart: 25 -> 25, of which waited for: 11 -> 14; matrix products, arithmetic and copies ran while one was open for 14% -> 15% of each run, Pallas kernels for 8% -> 5%
where the time goes in v10:
time: 90 us; the launch traced here: 89.2 us
  starting transfers between devices  38.4 us (43%)
  waiting for transfers between devices  19.9 us (22%)
  Pallas kernels  15.3 us (17%)
  matrix products  12 us (13%)
  other arithmetic  2.61 us (3%)
  between operations  0.95 us (1%)
    ppermute x9, starting transfers between devices, shift(): return lax.ppermute(value, axis, [(i, (i + by) % 4) for i in range(4)])  16.4 us
    ppermute x7, starting transfers between devices, far(): return lax.ppermute(value, axis, [(0, 3), (3, 0), (1, 2), (2, 1)])  15.9 us
    ppermute x7, waiting for transfers between devices, near(): return lax.ppermute(value, axis, [(0, 1), (1, 0), (2, 3), (3, 2)])  11.1 us
    ppermute x7, waiting for transfers between devices, far(): return lax.ppermute(value, axis, [(0, 3), (3, 0), (1, 2), (2, 1)])  7.39 us
    pallas_call x1, Pallas kernels, local_softmax(): pl.pallas_call(softmax_kernel, in_specs=[pl.BlockSpec(memory_space=pl.ANY...  7.23 us
    ppermute x7, starting transfers between devices, near(): return lax.ppermute(value, axis, [(0, 1), (1, 0), (2, 3), (3, 2)])  5.94 us
    dot_general x1, matrix products, local(): jnp.einsum('sd,sh->dh', slot_late, grad_pre, preferred_element_type=F32)  3.67 us
    pallas_call x1, Pallas kernels, embed_grad(): pl.pallas_call(embed_grad_kernel, in_specs=[pl.BlockSpec(memory_space=pl....  2.78 us
  transfers between devices with their start and end apart: 25, of which 14 were waited for; matrix products, arithmetic and copies ran while one was open for 15% of the time, Pallas kernels for 5%

profile of v10, /device:TPU:0, one launch (start us, length us, event | category | flops | bytes accessed | tf_op | source)
XLA Modules:
  0.0 89.2 jit_solution(10686930900154773924)
XLA Ops:
  0.7 7.2 %local_softmax.1 = (f32[64,1024]{1,0:T(8,128)S(1)}, bf16[64,1408]{1,0:T(8,128)(2,1)S(1)}) custom-call(bf16[2,1024,1280]{2,1,0:T(8,128)(2,1)} %tok.5, bf16[32,1280]{1,0:T(8,128)(2,1)} %bitcast.48), custom_call_target="tpu_custom_call" | custom-call | flops 700000000 | bytes 6000000 | tf_op jit(solution)/shard_map/local_softmax/pallas_call | solution.py:123
  7.9 2.1 %collective-permute-start = (bf16[64,1408]{1,0:T(8,128)(2,1)S(1)}, bf16[64,1408]{1,0:T(8,128)(2,1)S(1)}, u32[]{:S(2)}, u32[]{:S(2)}) collective-permute-start(bf16[64,1408]{1,0:T(8,128)(2,1)S(1)} %get-tuple-element.48.a), channel_id=1, source_target_pairs={{0,32},{32,0},{64,96},{96,64},{1,33},{33,1},{65,97},{97,65},{2,34}... | collective-permute-start | bytes 540680 | tf_op jit(solution)/shard_map/ppermute | solution.py:38
  10.0 1.9 %convolution_convert_fusion.2 = bf16[2,32,1280]{2,1,0:T(8,128)(2,1)S(1)} fusion(bf16[2,32,1024]{2,1,0:T(8,128)(2,1)} %bitcast.43, bf16[2,1024,1280]{2,1,0:T(8,128)(2,1)S(1)} %copy-done.1), kind=kOutput, calls=%fused_computation.15 | convolution fusion | flops 167854080 | bytes 5537792 | tf_op jit(solution)/shard_map/ijt,itd->ijd/dot_general | solution.py:334
  11.9 2.7 %collective-permute-done.b = bf16[64,1408]{1,0:T(8,128)(2,1)S(1)} collective-permute-done((bf16[64,1408]{1,0:T(8,128)(2,1)S(1)}, bf16[64,1408]{1,0:T(8,128)(2,1)S(1)}, u32[]{:S(2)}, u32[]{:S(2)}) %collective-permute-start) | collective-permute-done | bytes 180256 | tf_op jit(solution)/shard_map/ppermute | solution.py:38
  14.8 3.9 %collective-permute-start.1 = (bf16[64,1408]{1,0:T(8,128)(2,1)S(1)}, bf16[64,1408]{1,0:T(8,128)(2,1)S(1)}, u32[]{:S(2)}, u32[]{:S(2)}) collective-permute-start(bf16[64,1408]{1,0:T(8,128)(2,1)S(1)} %merge_pair.1.one), channel_id=1, source_target_pairs={{0,96},{96,0},{32,64},{64,32},{1,97},{97,1},{33,65},{65,33},{2,98}... | collective-permute-start | bytes 540680 | tf_op jit(solution)/shard_map/ppermute | solution.py:42
  18.8 3.3 %collective-permute-start.6 = (bf16[224,256]{1,0:T(8,128)(2,1)S(1)}, bf16[224,256]{1,0:T(8,128)(2,1)S(1)}, u32[]{:S(2)}, u32[]{:S(2)}) collective-permute-start(bf16[224,256]{1,0:T(8,128)(2,1)S(1)} %get-tuple-element.56), channel_id=1, source_target_pairs={{0,16},{8,24},{16,0},{24,8},{1,17},{9,25},{17,1},{25,9},{2,18},{10... | collective-permute-start | bytes 344072 | tf_op jit(solution)/shard_map/ppermute | solution.py:30
  24.1 1.7 %collective-permute-start.3 = (bf16[64,1280]{1,0:T(8,128)(2,1)S(1)}, bf16[64,1280]{1,0:T(8,128)(2,1)S(1)}, u32[]{:S(2)}, u32[]{:S(2)}) collective-permute-start(bf16[64,1280]{1,0:T(8,128)(2,1)S(1)} %add_convert_fusion.5), channel_id=1, source_target_pairs={{0,96},{96,0},{32,64},{64,32},{1,97},{97,1},{33,65},{65,33},{2,98}... | collective-permute-start | bytes 491528 | tf_op jit(solution)/shard_map/ppermute | solution.py:42
  27.3 3.1 %collective-permute-start.5 = (bf16[224,256]{1,0:T(8,128)(2,1)S(1)}, bf16[224,256]{1,0:T(8,128)(2,1)S(1)}, u32[]{:S(2)}, u32[]{:S(2)}) collective-permute-start(bf16[224,256]{1,0:T(8,128)(2,1)S(1)} %get-tuple-element.55), channel_id=1, source_target_pairs={{0,24},{8,0},{16,8},{24,16},{1,25},{9,1},{17,9},{25,17},{2,26},{10... | collective-permute-start | bytes 344072 | tf_op jit(solution)/shard_map/ppermute | solution.py:30
  35.9 2.8 %convolution_convert_fusion.1 = bf16[1280,1280]{1,0:T(8,128)(2,1)} fusion(bf16[64,1280]{1,0:T(8,128)(2,1)S(1)} %get-tuple-element.60, bf16[64,1280]{1,0:T(8,128)(2,1)S(1)} %add_convert_fusion.4), kind=kOutput, calls=%fused_computation.1 | convolution fusion | flops 211353600 | bytes 3604480 | tf_op jit(solution)/shard_map/sh,sd->hd/dot_general | solution.py:365
  38.6 2.2 %collective-permute-done.8 = bf16[64,1280]{1,0:T(8,128)(2,1)S(1)} collective-permute-done((bf16[64,1280]{1,0:T(8,128)(2,1)S(1)}, bf16[64,1280]{1,0:T(8,128)(2,1)S(1)}, u32[]{:S(2)}, u32[]{:S(2)}) %collective-permute-start.8) | collective-permute-done | bytes 163872 | tf_op jit(solution)/shard_map/ppermute | solution.py:38
  40.9 1.7 %collective-permute-start.10 = (bf16[64,1280]{1,0:T(8,128)(2,1)S(1)}, bf16[64,1280]{1,0:T(8,128)(2,1)S(1)}, u32[]{:S(2)}, u32[]{:S(2)}) collective-permute-start(bf16[64,1280]{1,0:T(8,128)(2,1)S(1)} %add_convert_fusion.2), channel_id=1, source_target_pairs={{0,96},{96,0},{32,64},{64,32},{1,97},{97,1},{33,65},{65,33},{2,98}... | collective-permute-start | bytes 491528 | tf_op jit(solution)/shard_map/ppermute | solution.py:42
  45.5 2.0 %collective-permute-done.10 = bf16[64,1280]{1,0:T(8,128)(2,1)S(1)} collective-permute-done((bf16[64,1280]{1,0:T(8,128)(2,1)S(1)}, bf16[64,1280]{1,0:T(8,128)(2,1)S(1)}, u32[]{:S(2)}, u32[]{:S(2)}) %collective-permute-start.10) | collective-permute-done | bytes 163872 | tf_op jit(solution)/shard_map/ppermute | solution.py:42
  49.3 3.3 %collective-permute-start.12 = (bf16[64,1792]{1,0:T(8,128)(2,1)S(1)}, bf16[64,1792]{1,0:T(8,128)(2,1)S(1)}, u32[]{:S(2)}, u32[]{:S(2)}) collective-permute-start(bf16[64,1792]{1,0:T(8,128)(2,1)S(1)} %get-tuple-element.71), channel_id=1, source_target_pairs={{0,24},{8,0},{16,8},{24,16},{1,25},{9,1},{17,9},{25,17},{2,26},{10... | collective-permute-start | bytes 688136 | tf_op jit(solution)/shard_map/ppermute | solution.py:30
  55.6 2.2 %collective-permute-done.15 = f32[2,1,1024]{2,1,0:T(1,128)S(1)} collective-permute-done((f32[2,1,1024]{2,1,0:T(1,128)S(1)}, f32[2,1,1024]{2,1,0:T(1,128)S(1)}, u32[]{:S(2)}, u32[]{:S(2)}) %collective-permute-start.15) | collective-permute-done | bytes 8224 | tf_op jit(solution)/shard_map/ppermute | solution.py:38
  57.8 2.8 %collective-permute-start.16 = (f32[2,1,1024]{2,1,0:T(1,128)S(1)}, f32[2,1,1024]{2,1,0:T(1,128)S(1)}, u32[]{:S(2)}, u32[]{:S(2)}) collective-permute-start(f32[2,1,1024]{2,1,0:T(1,128)S(1)} %add.66), channel_id=1, source_target_pairs={{0,6},{6,0},{2,4},{4,2},{1,7},{7,1},{3,5},{5,3},{8,14},{14,8},{10,... | collective-permute-start | bytes 24584 | tf_op jit(solution)/shard_map/ppermute | solution.py:42
  60.6 2.1 %collective-permute-done.16 = f32[2,1,1024]{2,1,0:T(1,128)S(1)} collective-permute-done((f32[2,1,1024]{2,1,0:T(1,128)S(1)}, f32[2,1,1024]{2,1,0:T(1,128)S(1)}, u32[]{:S(2)}, u32[]{:S(2)}) %collective-permute-start.16) | collective-permute-done | bytes 8224 | tf_op jit(solution)/shard_map/ppermute | solution.py:42
  62.7 2.0 %collective-permute-start.17 = (f32[2,1,1024]{2,1,0:T(1,128)S(1)}, f32[2,1,1024]{2,1,0:T(1,128)S(1)}, u32[]{:S(2)}, u32[]{:S(2)}) collective-permute-start(f32[2,1,1024]{2,1,0:T(1,128)S(1)} %add.67), channel_id=1, source_target_pairs={{0,8},{8,0},{16,24},{24,16},{1,9},{9,1},{17,25},{25,17},{2,10},{10... | collective-permute-start | bytes 24584 | tf_op jit(solution)/shard_map/ppermute | solution.py:38
  64.7 1.8 %collective-permute-done.17 = f32[2,1,1024]{2,1,0:T(1,128)S(1)} collective-permute-done((f32[2,1,1024]{2,1,0:T(1,128)S(1)}, f32[2,1,1024]{2,1,0:T(1,128)S(1)}, u32[]{:S(2)}, u32[]{:S(2)}) %collective-permute-start.17) | collective-permute-done | bytes 8224 | tf_op jit(solution)/shard_map/ppermute | solution.py:38
  66.5 2.3 %collective-permute-start.18 = (f32[2,1,1024]{2,1,0:T(1,128)S(1)}, f32[2,1,1024]{2,1,0:T(1,128)S(1)}, u32[]{:S(2)}, u32[]{:S(2)}) collective-permute-start(f32[2,1,1024]{2,1,0:T(1,128)S(1)} %add.68), channel_id=1, source_target_pairs={{0,24},{24,0},{8,16},{16,8},{1,25},{25,1},{9,17},{17,9},{2,26},{26... | collective-permute-start | bytes 24584 | tf_op jit(solution)/shard_map/ppermute | solution.py:42
  68.8 2.6 %collective-permute-done.18 = f32[2,1,1024]{2,1,0:T(1,128)S(1)} collective-permute-done((f32[2,1,1024]{2,1,0:T(1,128)S(1)}, f32[2,1,1024]{2,1,0:T(1,128)S(1)}, u32[]{:S(2)}, u32[]{:S(2)}) %collective-permute-start.18) | collective-permute-done | bytes 8224 | tf_op jit(solution)/shard_map/ppermute | solution.py:42
  72.2 2.8 %embed_grad.1 = bf16[32,1280]{1,0:T(8,128)(2,1)S(1)} custom-call(bf16[2,1024,1280]{2,1,0:T(8,128)(2,1)} %tok.5, f32[64,1024]{1,0:T(8,128)S(1)} %get-tuple-element.77.partial_logits, bf16[64,1024]{1,0:T(8,128)(2,1)S(1)} %bitcast.47, f32[2,1,1024]{2,1,0:T(1,128)S(1)} %add.69.refs_8_.row_dot), custom_call_target="tpu_custom_call" | custom-call | flops 170000000 | bytes 6000000 | tf_op jit(solution)/shard_map/embed_grad/pallas_call | solution.py:254
  76.2 3.9 %collective-permute-start.21 = (bf16[2,32,1280]{2,1,0:T(8,128)(2,1)}, bf16[2,32,1280]{2,1,0:T(8,128)(2,1)S(1)}, u32[]{:S(2)}, u32[]{:S(2)}) collective-permute-start(bf16[2,32,1280]{2,1,0:T(8,128)(2,1)} %get-tuple-element.82), channel_id=1, source_target_pairs={{0,4},{2,6},{4,0},{6,2},{1,5},{3,7},{5,1},{7,3},{8,12},{10,14},{12... | collective-permute-start | bytes 491528 | tf_op jit(solution)/shard_map/ppermute | solution.py:30
  81.8 1.7 %collective-permute-start.24 = (bf16[32,1280]{1,0:T(8,128)(2,1)S(1)}, bf16[32,1280]{1,0:T(8,128)(2,1)S(1)}, u32[]{:S(2)}, u32[]{:S(2)}) collective-permute-start(bf16[32,1280]{1,0:T(8,128)(2,1)S(1)} %add_convert_fusion.6), channel_id=1, source_target_pairs={{0,96},{96,0},{32,64},{64,32},{1,97},{97,1},{33,65},{65,33},{2,98}... | collective-permute-start | bytes 245768 | tf_op jit(solution)/shard_map/ppermute | solution.py:42
  83.5 3.7 %fusion = bf16[1,1280,1280]{2,1,0:T(8,128)(2,1)} fusion(bf16[64,1280]{1,0:T(8,128)(2,1)S(1)} %get-tuple-element.85.slot_in, bf16[64,1280]{1,0:T(8,128)(2,1)} %copy-done.5), kind=kOutput, calls=%fused_computation.2 | convolution fusion | flops 211353600 | bytes 3604480 | tf_op jit(solution)/shard_map/sd,sh->dh/dot_general | solution.py:399
  (74 shorter events, 22.5 us)
Async XLA Ops:
  7.9 6.6 %collective-permute-start = (bf16[64,1408]{1,0:T(8,128)(2,1)S(1)}, bf16[64,1408]{1,0:T(8,128)(2,1)S(1)}, u32[]{:S(2)}, u32[]{:S(2)}) collective-permute-start(bf16[64,1408]{1,0:T(8,128)(2,1)S(1)} %get-tuple-element.48.a), channel_id=1, source_target_pairs={{0,32},{32,0},{64,96},{96,64},{1,33},{33,1},{65,97},{97,65},{2,34}... | collective-permute-start | bytes 540680 | tf_op jit(solution)/shard_map/ppermute | solution.py:38
  14.8 7.9 %collective-permute-start.1 = (bf16[64,1408]{1,0:T(8,128)(2,1)S(1)}, bf16[64,1408]{1,0:T(8,128)(2,1)S(1)}, u32[]{:S(2)}, u32[]{:S(2)}) collective-permute-start(bf16[64,1408]{1,0:T(8,128)(2,1)S(1)} %merge_pair.1.one), channel_id=1, source_target_pairs={{0,96},{96,0},{32,64},{64,32},{1,97},{97,1},{33,65},{65,33},{2,98}... | collective-permute-start | bytes 540680 | tf_op jit(solution)/shard_map/ppermute | solution.py:42
  18.7 5.3 %collective-permute-start.2 = (bf16[64,1280]{1,0:T(8,128)(2,1)S(1)}, bf16[64,1280]{1,0:T(8,128)(2,1)S(1)}, u32[]{:S(2)}, u32[]{:S(2)}) collective-permute-start(bf16[64,1280]{1,0:T(8,128)(2,1)S(1)} %bitcast.51), channel_id=1, source_target_pairs={{0,32},{32,0},{64,96},{96,64},{1,33},{33,1},{65,97},{97,65},{2,34}... | collective-permute-start | bytes 491528 | tf_op jit(solution)/shard_map/ppermute | solution.py:38
  18.8 15.0 %collective-permute-start.6 = (bf16[224,256]{1,0:T(8,128)(2,1)S(1)}, bf16[224,256]{1,0:T(8,128)(2,1)S(1)}, u32[]{:S(2)}, u32[]{:S(2)}) collective-permute-start(bf16[224,256]{1,0:T(8,128)(2,1)S(1)} %get-tuple-element.56), channel_id=1, source_target_pairs={{0,16},{8,24},{16,0},{24,8},{1,17},{9,25},{17,1},{25,9},{2,18},{10... | collective-permute-start | bytes 344072 | tf_op jit(solution)/shard_map/ppermute | solution.py:30
  22.1 11.8 %collective-permute-start.7 = (bf16[224,256]{1,0:T(8,128)(2,1)S(1)}, bf16[224,256]{1,0:T(8,128)(2,1)S(1)}, u32[]{:S(2)}, u32[]{:S(2)}) collective-permute-start(bf16[224,256]{1,0:T(8,128)(2,1)S(1)} %get-tuple-element.57), channel_id=1, source_target_pairs={{0,8},{8,16},{16,24},{24,0},{1,9},{9,17},{17,25},{25,1},{2,10},{10... | collective-permute-start | bytes 344072 | tf_op jit(solution)/shard_map/ppermute | solution.py:30
  24.1 6.6 %collective-permute-start.3 = (bf16[64,1280]{1,0:T(8,128)(2,1)S(1)}, bf16[64,1280]{1,0:T(8,128)(2,1)S(1)}, u32[]{:S(2)}, u32[]{:S(2)}) collective-permute-start(bf16[64,1280]{1,0:T(8,128)(2,1)S(1)} %add_convert_fusion.5), channel_id=1, source_target_pairs={{0,96},{96,0},{32,64},{64,32},{1,97},{97,1},{33,65},{65,33},{2,98}... | collective-permute-start | bytes 491528 | tf_op jit(solution)/shard_map/ppermute | solution.py:42
  27.2 5.4 %collective-permute-start.4 = (bf16[64,1280]{1,0:T(8,128)(2,1)S(1)}, bf16[64,1280]{1,0:T(8,128)(2,1)S(1)}, u32[]{:S(2)}, u32[]{:S(2)}) collective-permute-start(bf16[64,1280]{1,0:T(8,128)(2,1)S(1)} %fusion.18), channel_id=1, source_target_pairs={{0,32},{32,0},{64,96},{96,64},{1,33},{33,1},{65,97},{97,65},{2,34}... | collective-permute-start | bytes 491528 | tf_op jit(solution)/shard_map/ppermute | solution.py:38
  27.3 6.5 %collective-permute-start.5 = (bf16[224,256]{1,0:T(8,128)(2,1)S(1)}, bf16[224,256]{1,0:T(8,128)(2,1)S(1)}, u32[]{:S(2)}, u32[]{:S(2)}) collective-permute-start(bf16[224,256]{1,0:T(8,128)(2,1)S(1)} %get-tuple-element.55), channel_id=1, source_target_pairs={{0,24},{8,0},{16,8},{24,16},{1,25},{9,1},{17,9},{25,17},{2,26},{10... | collective-permute-start | bytes 344072 | tf_op jit(solution)/shard_map/ppermute | solution.py:30
  33.9 8.8 %collective-permute-start.9 = (bf16[64,1280]{1,0:T(8,128)(2,1)S(1)}, bf16[64,1280]{1,0:T(8,128)(2,1)S(1)}, u32[]{:S(2)}, u32[]{:S(2)}) collective-permute-start(bf16[64,1280]{1,0:T(8,128)(2,1)S(1)} %add_convert_fusion.3.sum_a), channel_id=1, source_target_pairs={{0,96},{96,0},{32,64},{64,32},{1,97},{97,1},{33,65},{65,33},{2,98}... | collective-permute-start | bytes 491528 | tf_op jit(solution)/shard_map/ppermute | solution.py:42
  35.6 5.3 %collective-permute-start.8 = (bf16[64,1280]{1,0:T(8,128)(2,1)S(1)}, bf16[64,1280]{1,0:T(8,128)(2,1)S(1)}, u32[]{:S(2)}, u32[]{:S(2)}) collective-permute-start(bf16[64,1280]{1,0:T(8,128)(2,1)S(1)} %fusion.15), channel_id=1, source_target_pairs={{0,32},{32,0},{64,96},{96,64},{1,33},{33,1},{65,97},{97,65},{2,34}... | collective-permute-start | bytes 491528 | tf_op jit(solution)/shard_map/ppermute | solution.py:38
  40.9 6.6 %collective-permute-start.10 = (bf16[64,1280]{1,0:T(8,128)(2,1)S(1)}, bf16[64,1280]{1,0:T(8,128)(2,1)S(1)}, u32[]{:S(2)}, u32[]{:S(2)}) collective-permute-start(bf16[64,1280]{1,0:T(8,128)(2,1)S(1)} %add_convert_fusion.2), channel_id=1, source_target_pairs={{0,96},{96,0},{32,64},{64,32},{1,97},{97,1},{33,65},{65,33},{2,98}... | collective-permute-start | bytes 491528 | tf_op jit(solution)/shard_map/ppermute | solution.py:42
  49.3 22.2 %collective-permute-start.12 = (bf16[64,1792]{1,0:T(8,128)(2,1)S(1)}, bf16[64,1792]{1,0:T(8,128)(2,1)S(1)}, u32[]{:S(2)}, u32[]{:S(2)}) collective-permute-start(bf16[64,1792]{1,0:T(8,128)(2,1)S(1)} %get-tuple-element.71), channel_id=1, source_target_pairs={{0,24},{8,0},{16,8},{24,16},{1,25},{9,1},{17,9},{25,17},{2,26},{10... | collective-permute-start | bytes 688136 | tf_op jit(solution)/shard_map/ppermute | solution.py:30
  52.5 18.9 %collective-permute-start.13 = (bf16[64,1792]{1,0:T(8,128)(2,1)S(1)}, bf16[64,1792]{1,0:T(8,128)(2,1)S(1)}, u32[]{:S(2)}, u32[]{:S(2)}) collective-permute-start(bf16[64,1792]{1,0:T(8,128)(2,1)S(1)} %get-tuple-element.72), channel_id=1, source_target_pairs={{0,16},{8,24},{16,0},{24,8},{1,17},{9,25},{17,1},{25,9},{2,18},{10... | collective-permute-start | bytes 688136 | tf_op jit(solution)/shard_map/ppermute | solution.py:30
  53.1 18.3 %collective-permute-start.14 = (bf16[64,1792]{1,0:T(8,128)(2,1)S(1)}, bf16[64,1792]{1,0:T(8,128)(2,1)S(1)}, u32[]{:S(2)}, u32[]{:S(2)}) collective-permute-start(bf16[64,1792]{1,0:T(8,128)(2,1)S(1)} %get-tuple-element.73), channel_id=1, source_target_pairs={{0,8},{8,16},{16,24},{24,0},{1,9},{9,17},{17,25},{25,1},{2,10},{10... | collective-permute-start | bytes 688136 | tf_op jit(solution)/shard_map/ppermute | solution.py:30
  54.1 3.7 %collective-permute-start.15 = (f32[2,1,1024]{2,1,0:T(1,128)S(1)}, f32[2,1,1024]{2,1,0:T(1,128)S(1)}, u32[]{:S(2)}, u32[]{:S(2)}) collective-permute-start(f32[2,1,1024]{2,1,0:T(1,128)S(1)} %add.65), channel_id=1, source_target_pairs={{0,2},{2,0},{4,6},{6,4},{1,3},{3,1},{5,7},{7,5},{8,10},{10,8},{12,... | collective-permute-start | bytes 24584 | tf_op jit(solution)/shard_map/ppermute | solution.py:38
  57.8 4.9 %collective-permute-start.16 = (f32[2,1,1024]{2,1,0:T(1,128)S(1)}, f32[2,1,1024]{2,1,0:T(1,128)S(1)}, u32[]{:S(2)}, u32[]{:S(2)}) collective-permute-start(f32[2,1,1024]{2,1,0:T(1,128)S(1)} %add.66), channel_id=1, source_target_pairs={{0,6},{6,0},{2,4},{4,2},{1,7},{7,1},{3,5},{5,3},{8,14},{14,8},{10,... | collective-permute-start | bytes 24584 | tf_op jit(solution)/shard_map/ppermute | solution.py:42
  62.7 3.7 %collective-permute-start.17 = (f32[2,1,1024]{2,1,0:T(1,128)S(1)}, f32[2,1,1024]{2,1,0:T(1,128)S(1)}, u32[]{:S(2)}, u32[]{:S(2)}) collective-permute-start(f32[2,1,1024]{2,1,0:T(1,128)S(1)} %add.67), channel_id=1, source_target_pairs={{0,8},{8,0},{16,24},{24,16},{1,9},{9,1},{17,25},{25,17},{2,10},{10... | collective-permute-start | bytes 24584 | tf_op jit(solution)/shard_map/ppermute | solution.py:38
  66.5 4.9 %collective-permute-start.18 = (f32[2,1,1024]{2,1,0:T(1,128)S(1)}, f32[2,1,1024]{2,1,0:T(1,128)S(1)}, u32[]{:S(2)}, u32[]{:S(2)}) collective-permute-start(f32[2,1,1024]{2,1,0:T(1,128)S(1)} %add.68), channel_id=1, source_target_pairs={{0,24},{24,0},{8,16},{16,8},{1,25},{25,1},{9,17},{17,9},{2,26},{26... | collective-permute-start | bytes 24584 | tf_op jit(solution)/shard_map/ppermute | solution.py:42
  72.1 2.9 %collective-permute-start.19 = (bf16[4,2,32,1280]{3,2,1,0:T(8,128)(2,1)S(1)}, bf16[4,2,32,1280]{3,2,1,0:T(8,128)(2,1)S(1)}, u32[]{:S(2)}, u32[]{:S(2)}) collective-permute-start(bf16[4,2,32,1280]{3,2,1,0:T(8,128)(2,1)S(1)} %get-tuple-element.79), channel_id=1, source_target_pairs={{0,1},{1,0},{2,3},{3,2},{4,5},{5,4},{6,7},{7,6},{8,9},{9,8},{10,11... | collective-permute-start | bytes 1966088 | tf_op jit(solution)/shard_map/ppermute | solution.py:34
  75.9 4.9 %collective-permute-start.23 = (bf16[32,1280]{1,0:T(8,128)(2,1)S(1)}, bf16[32,1280]{1,0:T(8,128)(2,1)}, u32[]{:S(2)}, u32[]{:S(2)}) collective-permute-start(bf16[32,1280]{1,0:T(8,128)(2,1)S(1)} %embed_grad.1), channel_id=1, source_target_pairs={{0,32},{32,0},{64,96},{96,64},{1,33},{33,1},{65,97},{97,65},{2,34}... | collective-permute-start | bytes 245768 | tf_op jit(solution)/shard_map/ppermute | solution.py:38
  75.9 12.3 %collective-permute-start.20 = (bf16[2,32,1280]{2,1,0:T(8,128)(2,1)}, bf16[2,32,1280]{2,1,0:T(8,128)(2,1)S(1)}, u32[]{:S(2)}, u32[]{:S(2)}) collective-permute-start(bf16[2,32,1280]{2,1,0:T(8,128)(2,1)} %get-tuple-element.81), channel_id=1, source_target_pairs={{0,2},{2,4},{4,6},{6,0},{1,3},{3,5},{5,7},{7,1},{8,10},{10,12},{12... | collective-permute-start | bytes 491528 | tf_op jit(solution)/shard_map/ppermute | solution.py:30
  76.2 12.2 %collective-permute-start.21 = (bf16[2,32,1280]{2,1,0:T(8,128)(2,1)}, bf16[2,32,1280]{2,1,0:T(8,128)(2,1)S(1)}, u32[]{:S(2)}, u32[]{:S(2)}) collective-permute-start(bf16[2,32,1280]{2,1,0:T(8,128)(2,1)} %get-tuple-element.82), channel_id=1, source_target_pairs={{0,4},{2,6},{4,0},{6,2},{1,5},{3,7},{5,1},{7,3},{8,12},{10,14},{12... | collective-permute-start | bytes 491528 | tf_op jit(solution)/shard_map/ppermute | solution.py:30
  80.2 8.3 %collective-permute-start.22 = (bf16[2,32,1280]{2,1,0:T(8,128)(2,1)}, bf16[2,32,1280]{2,1,0:T(8,128)(2,1)S(1)}, u32[]{:S(2)}, u32[]{:S(2)}) collective-permute-start(bf16[2,32,1280]{2,1,0:T(8,128)(2,1)} %get-tuple-element.83), channel_id=1, source_target_pairs={{0,6},{2,0},{4,2},{6,4},{1,7},{3,1},{5,3},{7,5},{8,14},{10,8},{12,... | collective-permute-start | bytes 491528 | tf_op jit(solution)/shard_map/ppermute | solution.py:30
  81.8 5.7 %collective-permute-start.24 = (bf16[32,1280]{1,0:T(8,128)(2,1)S(1)}, bf16[32,1280]{1,0:T(8,128)(2,1)S(1)}, u32[]{:S(2)}, u32[]{:S(2)}) collective-permute-start(bf16[32,1280]{1,0:T(8,128)(2,1)S(1)} %add_convert_fusion.6), channel_id=1, source_target_pairs={{0,96},{96,0},{32,64},{64,32},{1,97},{97,1},{33,65},{65,33},{2,98}... | collective-permute-start | bytes 245768 | tf_op jit(solution)/shard_map/ppermute | solution.py:42
  (10 other events, 115.3 us)

commit v11 on v10

--- a/solution.py
+++ b/solution.py
@@ -90,27 +90,29 @@
     return lambda i, n: copies[i][n].wait()
 
 
-def softmax_kernel(tok, embed, logits, part, patches, slots, sems, embed_sem):
-    embed_copy = pltpu.make_async_copy(embed, slots, embed_sem)
-    embed_copy.start()
-    wait = start_patches(tok, patches, sems)
-    embed_copy.wait()
-    columns = slots[...]
-    scores = []
-    for i in range(2):
-        pieces = []
-        for n in range(4):
-            wait(i, n)
-            rows = patches[i, 256 * n : 256 * n + 256, :]
-            pieces.append(lax.dot_general(rows, columns, NT, preferred_element_type=F32).T)
-        scores.append(jnp.concatenate(pieces, axis=1))
+def softmax_kernel(*refs):
+    embed, logits, part = refs[8:]
+    columns = embed[...]
+    blocks = [[one[0] for one in refs[4 * i : 4 * i + 4]] for i in range(2)]
+    scores = [
+        jnp.concatenate(
+            [lax.dot_general(one, columns, NT, preferred_element_type=F32).T for one in four],
+            axis=1,
+        )
+        for four in blocks
+    ]
     for i in range(2):
         half = slice(32 * i, 32 * i + 32)
         logits[half, :] = scores[i]
         peak = jnp.max(scores[i], axis=1, keepdims=True)
         weight = jnp.exp(scores[i] - peak)
         total = jnp.sum(weight, axis=1, keepdims=True)
-        sums = jnp.dot(weight.astype(BF16), patches[i], preferred_element_type=F32)
+        weight = weight.astype(BF16)
+        sums = 0.0
+        for n in range(4):
+            sums = sums + jnp.dot(
+                weight[:, 256 * n : 256 * n + 256], blocks[i][n], preferred_element_type=F32
+            )
         part[half, :1280] = (sums / total).astype(BF16)
         part[half, 1280:] = lse_lanes(peak + jnp.log(total))
 
@@ -122,18 +124,22 @@
 def local_softmax(tokens, embed):
     return pl.pallas_call(
         softmax_kernel,
-        in_specs=[pl.BlockSpec(memory_space=pl.ANY)] * 2,
+        grid=(1,),
+        in_specs=[
+            pl.BlockSpec((1, 256, 1280), lambda t, i=i, n=n: (i, n, 0))
+            for i in range(2)
+            for n in range(4)
+        ]
+        + [pl.BlockSpec((32, 1280), lambda t: (0, 0))],
+        out_specs=[
+            pl.BlockSpec((64, 1024), lambda t: (0, 0)),
+            pl.BlockSpec((64, 1408), lambda t: (0, 0)),
+        ],
         out_shape=[shape((64, 1024), F32), shape((64, 1408), BF16)],
-        scratch_shapes=[
-            pltpu.VMEM((2, 1024, 1280), BF16),
-            pltpu.VMEM((32, 1280), BF16),
-            pltpu.SemaphoreType.DMA((8,)),
-            pltpu.SemaphoreType.DMA,
-        ],
         cost_estimate=pl.CostEstimate(flops=700_000_000, bytes_accessed=6_000_000, transcendentals=65536),
         compiler_params=LARGE,
         name="local_softmax",
-    )(in_hbm(tokens), in_hbm(embed))
+    )(*[in_hbm(tokens)] * 8, in_hbm(embed))
 
 
 def merge_kernel(one, two, sums, lse):

time: 90 us -> 87.7 us (0.974)
  Pallas kernels: 15.3 us -> 13.2 us
  waiting for transfers between devices: 19.9 us -> 20.8 us
  matrix products: 12 us -> 11.1 us
    pallas_call x1, Pallas kernels: 7.23 us -> 5.11 us  [local_softmax(): pl.pallas_call(softmax_kernel, grid=(1,), in_specs=[pl.BlockSpec((1, 256,...]
    dot_general x1, matrix products: 1.88 us -> 0.97 us  [local(): jnp.einsum('ijt,itd->ijd', comb_late.reshape(2, 32, 1024), grad_out, pref...]
where the time goes in v11:
time: 87.7 us; the launch traced here: 86.9 us
  starting transfers between devices  38.3 us (44%)
  waiting for transfers between devices  20.8 us (24%)
  Pallas kernels  13.2 us (15%)
  matrix products  11.1 us (13%)
  other arithmetic  2.61 us (3%)
  between operations  0.95 us (1%)
    ppermute x9, starting transfers between devices, shift(): return lax.ppermute(value, axis, [(i, (i + by) % 4) for i in range(4)])  16.2 us
    ppermute x7, starting transfers between devices, far(): return lax.ppermute(value, axis, [(0, 3), (3, 0), (1, 2), (2, 1)])  15.9 us
    ppermute x7, waiting for transfers between devices, near(): return lax.ppermute(value, axis, [(0, 1), (1, 0), (2, 3), (3, 2)])  12 us
    ppermute x7, waiting for transfers between devices, far(): return lax.ppermute(value, axis, [(0, 3), (3, 0), (1, 2), (2, 1)])  7.38 us
    ppermute x7, starting transfers between devices, near(): return lax.ppermute(value, axis, [(0, 1), (1, 0), (2, 3), (3, 2)])  5.95 us
    pallas_call x1, Pallas kernels, local_softmax(): pl.pallas_call(softmax_kernel, grid=(1,), in_specs=[pl.BlockSpec((1, 256,...  5.11 us
    dot_general x1, matrix products, local(): jnp.einsum('sd,sh->dh', slot_late, grad_pre, preferred_element_type=F32)  3.68 us
    pallas_call x1, Pallas kernels, embed_grad(): pl.pallas_call(embed_grad_kernel, in_specs=[pl.BlockSpec(memory_space=pl....  2.78 us
  transfers between devices with their start and end apart: 25, of which 14 were waited for; matrix products, arithmetic and copies ran while one was open for 15% of the time, Pallas kernels for 5%

profile of v11, /device:TPU:0, one launch (start us, length us, event | category | flops | bytes accessed | tf_op | source)
XLA Modules:
  0.0 86.9 jit_solution(13144912502655521078)
XLA Ops:
  0.7 5.1 %local_softmax.1 = (f32[64,1024]{1,0:T(8,128)S(1)}, bf16[64,1408]{1,0:T(8,128)(2,1)S(1)}) custom-call(bf16[2,1024,1280]{2,1,0:T(8,128)(2,1)} %tok.3, bf16[2,1024,1280]{2,1,0:T(8,128)(2,1)} %tok.3, bf16[2,1024,1280]{2,1,0:T(8,128)(2,1)} %tok.3, bf16[2,1024,1280]{2,1,0:T(8,128)(2,1)} %tok.3, bf16[2,1024,1280]{2,1,0:T(8,128)(2,1)} %tok.3, ...), custom_call_target="tpu_custom_call" | custom-call | flops 700000000 | bytes 6000000 | tf_op jit(solution)/shard_map/local_softmax/pallas_call | solution.py:125
  5.8 2.1 %collective-permute-start = (bf16[64,1408]{1,0:T(8,128)(2,1)S(1)}, bf16[64,1408]{1,0:T(8,128)(2,1)S(1)}, u32[]{:S(2)}, u32[]{:S(2)}) collective-permute-start(bf16[64,1408]{1,0:T(8,128)(2,1)S(1)} %get-tuple-element.48.a), channel_id=1, source_target_pairs={{0,32},{32,0},{64,96},{96,64},{1,33},{33,1},{65,97},{97,65},{2,34}... | collective-permute-start | bytes 540680 | tf_op jit(solution)/shard_map/ppermute | solution.py:38
  8.9 3.6 %collective-permute-done.b = bf16[64,1408]{1,0:T(8,128)(2,1)S(1)} collective-permute-done((bf16[64,1408]{1,0:T(8,128)(2,1)S(1)}, bf16[64,1408]{1,0:T(8,128)(2,1)S(1)}, u32[]{:S(2)}, u32[]{:S(2)}) %collective-permute-start) | collective-permute-done | bytes 180256 | tf_op jit(solution)/shard_map/ppermute | solution.py:38
  12.7 3.9 %collective-permute-start.1 = (bf16[64,1408]{1,0:T(8,128)(2,1)S(1)}, bf16[64,1408]{1,0:T(8,128)(2,1)S(1)}, u32[]{:S(2)}, u32[]{:S(2)}) collective-permute-start(bf16[64,1408]{1,0:T(8,128)(2,1)S(1)} %merge_pair.1.one), channel_id=1, source_target_pairs={{0,96},{96,0},{32,64},{64,32},{1,97},{97,1},{33,65},{65,33},{2,98}... | collective-permute-start | bytes 540680 | tf_op jit(solution)/shard_map/ppermute | solution.py:42
  16.6 3.3 %collective-permute-start.6 = (bf16[224,256]{1,0:T(8,128)(2,1)S(1)}, bf16[224,256]{1,0:T(8,128)(2,1)S(1)}, u32[]{:S(2)}, u32[]{:S(2)}) collective-permute-start(bf16[224,256]{1,0:T(8,128)(2,1)S(1)} %get-tuple-element.56), channel_id=1, source_target_pairs={{0,16},{8,24},{16,0},{24,8},{1,17},{9,25},{17,1},{25,9},{2,18},{10... | collective-permute-start | bytes 344072 | tf_op jit(solution)/shard_map/ppermute | solution.py:30
  22.0 1.7 %collective-permute-start.3 = (bf16[64,1280]{1,0:T(8,128)(2,1)S(1)}, bf16[64,1280]{1,0:T(8,128)(2,1)S(1)}, u32[]{:S(2)}, u32[]{:S(2)}) collective-permute-start(bf16[64,1280]{1,0:T(8,128)(2,1)S(1)} %add_convert_fusion.5), channel_id=1, source_target_pairs={{0,96},{96,0},{32,64},{64,32},{1,97},{97,1},{33,65},{65,33},{2,98}... | collective-permute-start | bytes 491528 | tf_op jit(solution)/shard_map/ppermute | solution.py:42
  25.2 3.1 %collective-permute-start.5 = (bf16[224,256]{1,0:T(8,128)(2,1)S(1)}, bf16[224,256]{1,0:T(8,128)(2,1)S(1)}, u32[]{:S(2)}, u32[]{:S(2)}) collective-permute-start(bf16[224,256]{1,0:T(8,128)(2,1)S(1)} %get-tuple-element.55), channel_id=1, source_target_pairs={{0,24},{8,0},{16,8},{24,16},{1,25},{9,1},{17,9},{25,17},{2,26},{10... | collective-permute-start | bytes 344072 | tf_op jit(solution)/shard_map/ppermute | solution.py:30
  31.8 1.7 %collective-permute-start.9 = (bf16[64,1280]{1,0:T(8,128)(2,1)S(1)}, bf16[64,1280]{1,0:T(8,128)(2,1)S(1)}, u32[]{:S(2)}, u32[]{:S(2)}) collective-permute-start(bf16[64,1280]{1,0:T(8,128)(2,1)S(1)} %add_convert_fusion.3.sum_a), channel_id=1, source_target_pairs={{0,96},{96,0},{32,64},{64,32},{1,97},{97,1},{33,65},{65,33},{2,98}... | collective-permute-start | bytes 491528 | tf_op jit(solution)/shard_map/ppermute | solution.py:42
  33.8 2.8 %convolution_convert_fusion.1 = bf16[1280,1280]{1,0:T(8,128)(2,1)} fusion(bf16[64,1280]{1,0:T(8,128)(2,1)S(1)} %get-tuple-element.60, bf16[64,1280]{1,0:T(8,128)(2,1)S(1)} %add_convert_fusion.4), kind=kOutput, calls=%fused_computation.1 | convolution fusion | flops 211353600 | bytes 3604480 | tf_op jit(solution)/shard_map/sh,sd->hd/dot_general | solution.py:371
  36.5 2.2 %collective-permute-done.8 = bf16[64,1280]{1,0:T(8,128)(2,1)S(1)} collective-permute-done((bf16[64,1280]{1,0:T(8,128)(2,1)S(1)}, bf16[64,1280]{1,0:T(8,128)(2,1)S(1)}, u32[]{:S(2)}, u32[]{:S(2)}) %collective-permute-start.8) | collective-permute-done | bytes 163872 | tf_op jit(solution)/shard_map/ppermute | solution.py:38
  38.8 1.7 %collective-permute-start.10 = (bf16[64,1280]{1,0:T(8,128)(2,1)S(1)}, bf16[64,1280]{1,0:T(8,128)(2,1)S(1)}, u32[]{:S(2)}, u32[]{:S(2)}) collective-permute-start(bf16[64,1280]{1,0:T(8,128)(2,1)S(1)} %add_convert_fusion.2), channel_id=1, source_target_pairs={{0,96},{96,0},{32,64},{64,32},{1,97},{97,1},{33,65},{65,33},{2,98}... | collective-permute-start | bytes 491528 | tf_op jit(solution)/shard_map/ppermute | solution.py:42
  43.4 2.0 %collective-permute-done.10 = bf16[64,1280]{1,0:T(8,128)(2,1)S(1)} collective-permute-done((bf16[64,1280]{1,0:T(8,128)(2,1)S(1)}, bf16[64,1280]{1,0:T(8,128)(2,1)S(1)}, u32[]{:S(2)}, u32[]{:S(2)}) %collective-permute-start.10) | collective-permute-done | bytes 163872 | tf_op jit(solution)/shard_map/ppermute | solution.py:42
  47.1 3.1 %collective-permute-start.12 = (bf16[64,1792]{1,0:T(8,128)(2,1)S(1)}, bf16[64,1792]{1,0:T(8,128)(2,1)S(1)}, u32[]{:S(2)}, u32[]{:S(2)}) collective-permute-start(bf16[64,1792]{1,0:T(8,128)(2,1)S(1)} %get-tuple-element.71), channel_id=1, source_target_pairs={{0,24},{8,0},{16,8},{24,16},{1,25},{9,1},{17,9},{25,17},{2,26},{10... | collective-permute-start | bytes 688136 | tf_op jit(solution)/shard_map/ppermute | solution.py:30
  53.3 2.2 %collective-permute-done.15 = f32[2,1,1024]{2,1,0:T(1,128)S(1)} collective-permute-done((f32[2,1,1024]{2,1,0:T(1,128)S(1)}, f32[2,1,1024]{2,1,0:T(1,128)S(1)}, u32[]{:S(2)}, u32[]{:S(2)}) %collective-permute-start.15) | collective-permute-done | bytes 8224 | tf_op jit(solution)/shard_map/ppermute | solution.py:38
  55.5 2.8 %collective-permute-start.16 = (f32[2,1,1024]{2,1,0:T(1,128)S(1)}, f32[2,1,1024]{2,1,0:T(1,128)S(1)}, u32[]{:S(2)}, u32[]{:S(2)}) collective-permute-start(f32[2,1,1024]{2,1,0:T(1,128)S(1)} %add.66), channel_id=1, source_target_pairs={{0,6},{6,0},{2,4},{4,2},{1,7},{7,1},{3,5},{5,3},{8,14},{14,8},{10,... | collective-permute-start | bytes 24584 | tf_op jit(solution)/shard_map/ppermute | solution.py:42
  58.3 2.1 %collective-permute-done.16 = f32[2,1,1024]{2,1,0:T(1,128)S(1)} collective-permute-done((f32[2,1,1024]{2,1,0:T(1,128)S(1)}, f32[2,1,1024]{2,1,0:T(1,128)S(1)}, u32[]{:S(2)}, u32[]{:S(2)}) %collective-permute-start.16) | collective-permute-done | bytes 8224 | tf_op jit(solution)/shard_map/ppermute | solution.py:42
  60.4 2.0 %collective-permute-start.17 = (f32[2,1,1024]{2,1,0:T(1,128)S(1)}, f32[2,1,1024]{2,1,0:T(1,128)S(1)}, u32[]{:S(2)}, u32[]{:S(2)}) collective-permute-start(f32[2,1,1024]{2,1,0:T(1,128)S(1)} %add.67), channel_id=1, source_target_pairs={{0,8},{8,0},{16,24},{24,16},{1,9},{9,1},{17,25},{25,17},{2,10},{10... | collective-permute-start | bytes 24584 | tf_op jit(solution)/shard_map/ppermute | solution.py:38
  62.4 1.8 %collective-permute-done.17 = f32[2,1,1024]{2,1,0:T(1,128)S(1)} collective-permute-done((f32[2,1,1024]{2,1,0:T(1,128)S(1)}, f32[2,1,1024]{2,1,0:T(1,128)S(1)}, u32[]{:S(2)}, u32[]{:S(2)}) %collective-permute-start.17) | collective-permute-done | bytes 8224 | tf_op jit(solution)/shard_map/ppermute | solution.py:38
  64.2 2.3 %collective-permute-start.18 = (f32[2,1,1024]{2,1,0:T(1,128)S(1)}, f32[2,1,1024]{2,1,0:T(1,128)S(1)}, u32[]{:S(2)}, u32[]{:S(2)}) collective-permute-start(f32[2,1,1024]{2,1,0:T(1,128)S(1)} %add.68), channel_id=1, source_target_pairs={{0,24},{24,0},{8,16},{16,8},{1,25},{25,1},{9,17},{17,9},{2,26},{26... | collective-permute-start | bytes 24584 | tf_op jit(solution)/shard_map/ppermute | solution.py:42
  66.5 2.6 %collective-permute-done.18 = f32[2,1,1024]{2,1,0:T(1,128)S(1)} collective-permute-done((f32[2,1,1024]{2,1,0:T(1,128)S(1)}, f32[2,1,1024]{2,1,0:T(1,128)S(1)}, u32[]{:S(2)}, u32[]{:S(2)}) %collective-permute-start.18) | collective-permute-done | bytes 8224 | tf_op jit(solution)/shard_map/ppermute | solution.py:42
  69.9 2.8 %embed_grad.1 = bf16[32,1280]{1,0:T(8,128)(2,1)S(1)} custom-call(bf16[2,1024,1280]{2,1,0:T(8,128)(2,1)} %tok.3, f32[64,1024]{1,0:T(8,128)S(1)} %get-tuple-element.77.partial_logits, bf16[64,1024]{1,0:T(8,128)(2,1)S(1)} %bitcast.47, f32[2,1,1024]{2,1,0:T(1,128)S(1)} %add.69.refs_8_.row_dot), custom_call_target="tpu_custom_call" | custom-call | flops 170000000 | bytes 6000000 | tf_op jit(solution)/shard_map/embed_grad/pallas_call | solution.py:260
  73.9 4.0 %collective-permute-start.21 = (bf16[2,32,1280]{2,1,0:T(8,128)(2,1)}, bf16[2,32,1280]{2,1,0:T(8,128)(2,1)S(1)}, u32[]{:S(2)}, u32[]{:S(2)}) collective-permute-start(bf16[2,32,1280]{2,1,0:T(8,128)(2,1)} %get-tuple-element.82), channel_id=1, source_target_pairs={{0,4},{2,6},{4,0},{6,2},{1,5},{3,7},{5,1},{7,3},{8,12},{10,14},{12... | collective-permute-start | bytes 491528 | tf_op jit(solution)/shard_map/ppermute | solution.py:30
  79.5 1.7 %collective-permute-start.24 = (bf16[32,1280]{1,0:T(8,128)(2,1)S(1)}, bf16[32,1280]{1,0:T(8,128)(2,1)S(1)}, u32[]{:S(2)}, u32[]{:S(2)}) collective-permute-start(bf16[32,1280]{1,0:T(8,128)(2,1)S(1)} %add_convert_fusion.6), channel_id=1, source_target_pairs={{0,96},{96,0},{32,64},{64,32},{1,97},{97,1},{33,65},{65,33},{2,98}... | collective-permute-start | bytes 245768 | tf_op jit(solution)/shard_map/ppermute | solution.py:42
  81.2 3.7 %fusion = bf16[1,1280,1280]{2,1,0:T(8,128)(2,1)} fusion(bf16[64,1280]{1,0:T(8,128)(2,1)S(1)} %get-tuple-element.85.slot_in, bf16[64,1280]{1,0:T(8,128)(2,1)} %copy-done.5), kind=kOutput, calls=%fused_computation.2 | convolution fusion | flops 211353600 | bytes 3604480 | tf_op jit(solution)/shard_map/sd,sh->dh/dot_general | solution.py:405
  (74 shorter events, 21.8 us)
Async XLA Ops:
  5.8 6.6 %collective-permute-start = (bf16[64,1408]{1,0:T(8,128)(2,1)S(1)}, bf16[64,1408]{1,0:T(8,128)(2,1)S(1)}, u32[]{:S(2)}, u32[]{:S(2)}) collective-permute-start(bf16[64,1408]{1,0:T(8,128)(2,1)S(1)} %get-tuple-element.48.a), channel_id=1, source_target_pairs={{0,32},{32,0},{64,96},{96,64},{1,33},{33,1},{65,97},{97,65},{2,34}... | collective-permute-start | bytes 540680 | tf_op jit(solution)/shard_map/ppermute | solution.py:38
  12.7 7.9 %collective-permute-start.1 = (bf16[64,1408]{1,0:T(8,128)(2,1)S(1)}, bf16[64,1408]{1,0:T(8,128)(2,1)S(1)}, u32[]{:S(2)}, u32[]{:S(2)}) collective-permute-start(bf16[64,1408]{1,0:T(8,128)(2,1)S(1)} %merge_pair.1.one), channel_id=1, source_target_pairs={{0,96},{96,0},{32,64},{64,32},{1,97},{97,1},{33,65},{65,33},{2,98}... | collective-permute-start | bytes 540680 | tf_op jit(solution)/shard_map/ppermute | solution.py:42
  16.6 5.3 %collective-permute-start.2 = (bf16[64,1280]{1,0:T(8,128)(2,1)S(1)}, bf16[64,1280]{1,0:T(8,128)(2,1)S(1)}, u32[]{:S(2)}, u32[]{:S(2)}) collective-permute-start(bf16[64,1280]{1,0:T(8,128)(2,1)S(1)} %bitcast.51), channel_id=1, source_target_pairs={{0,32},{32,0},{64,96},{96,64},{1,33},{33,1},{65,97},{97,65},{2,34}... | collective-permute-start | bytes 491528 | tf_op jit(solution)/shard_map/ppermute | solution.py:38
  16.6 15.1 %collective-permute-start.6 = (bf16[224,256]{1,0:T(8,128)(2,1)S(1)}, bf16[224,256]{1,0:T(8,128)(2,1)S(1)}, u32[]{:S(2)}, u32[]{:S(2)}) collective-permute-start(bf16[224,256]{1,0:T(8,128)(2,1)S(1)} %get-tuple-element.56), channel_id=1, source_target_pairs={{0,16},{8,24},{16,0},{24,8},{1,17},{9,25},{17,1},{25,9},{2,18},{10... | collective-permute-start | bytes 344072 | tf_op jit(solution)/shard_map/ppermute | solution.py:30
  19.9 11.8 %collective-permute-start.7 = (bf16[224,256]{1,0:T(8,128)(2,1)S(1)}, bf16[224,256]{1,0:T(8,128)(2,1)S(1)}, u32[]{:S(2)}, u32[]{:S(2)}) collective-permute-start(bf16[224,256]{1,0:T(8,128)(2,1)S(1)} %get-tuple-element.57), channel_id=1, source_target_pairs={{0,8},{8,16},{16,24},{24,0},{1,9},{9,17},{17,25},{25,1},{2,10},{10... | collective-permute-start | bytes 344072 | tf_op jit(solution)/shard_map/ppermute | solution.py:30
  22.0 6.6 %collective-permute-start.3 = (bf16[64,1280]{1,0:T(8,128)(2,1)S(1)}, bf16[64,1280]{1,0:T(8,128)(2,1)S(1)}, u32[]{:S(2)}, u32[]{:S(2)}) collective-permute-start(bf16[64,1280]{1,0:T(8,128)(2,1)S(1)} %add_convert_fusion.5), channel_id=1, source_target_pairs={{0,96},{96,0},{32,64},{64,32},{1,97},{97,1},{33,65},{65,33},{2,98}... | collective-permute-start | bytes 491528 | tf_op jit(solution)/shard_map/ppermute | solution.py:42
  25.1 5.4 %collective-permute-start.4 = (bf16[64,1280]{1,0:T(8,128)(2,1)S(1)}, bf16[64,1280]{1,0:T(8,128)(2,1)S(1)}, u32[]{:S(2)}, u32[]{:S(2)}) collective-permute-start(bf16[64,1280]{1,0:T(8,128)(2,1)S(1)} %fusion.18), channel_id=1, source_target_pairs={{0,32},{32,0},{64,96},{96,64},{1,33},{33,1},{65,97},{97,65},{2,34}... | collective-permute-start | bytes 491528 | tf_op jit(solution)/shard_map/ppermute | solution.py:38
  25.2 6.5 %collective-permute-start.5 = (bf16[224,256]{1,0:T(8,128)(2,1)S(1)}, bf16[224,256]{1,0:T(8,128)(2,1)S(1)}, u32[]{:S(2)}, u32[]{:S(2)}) collective-permute-start(bf16[224,256]{1,0:T(8,128)(2,1)S(1)} %get-tuple-element.55), channel_id=1, source_target_pairs={{0,24},{8,0},{16,8},{24,16},{1,25},{9,1},{17,9},{25,17},{2,26},{10... | collective-permute-start | bytes 344072 | tf_op jit(solution)/shard_map/ppermute | solution.py:30
  31.8 8.8 %collective-permute-start.9 = (bf16[64,1280]{1,0:T(8,128)(2,1)S(1)}, bf16[64,1280]{1,0:T(8,128)(2,1)S(1)}, u32[]{:S(2)}, u32[]{:S(2)}) collective-permute-start(bf16[64,1280]{1,0:T(8,128)(2,1)S(1)} %add_convert_fusion.3.sum_a), channel_id=1, source_target_pairs={{0,96},{96,0},{32,64},{64,32},{1,97},{97,1},{33,65},{65,33},{2,98}... | collective-permute-start | bytes 491528 | tf_op jit(solution)/shard_map/ppermute | solution.py:42
  33.4 5.3 %collective-permute-start.8 = (bf16[64,1280]{1,0:T(8,128)(2,1)S(1)}, bf16[64,1280]{1,0:T(8,128)(2,1)S(1)}, u32[]{:S(2)}, u32[]{:S(2)}) collective-permute-start(bf16[64,1280]{1,0:T(8,128)(2,1)S(1)} %fusion.15), channel_id=1, source_target_pairs={{0,32},{32,0},{64,96},{96,64},{1,33},{33,1},{65,97},{97,65},{2,34}... | collective-permute-start | bytes 491528 | tf_op jit(solution)/shard_map/ppermute | solution.py:38
  38.8 6.6 %collective-permute-start.10 = (bf16[64,1280]{1,0:T(8,128)(2,1)S(1)}, bf16[64,1280]{1,0:T(8,128)(2,1)S(1)}, u32[]{:S(2)}, u32[]{:S(2)}) collective-permute-start(bf16[64,1280]{1,0:T(8,128)(2,1)S(1)} %add_convert_fusion.2), channel_id=1, source_target_pairs={{0,96},{96,0},{32,64},{64,32},{1,97},{97,1},{33,65},{65,33},{2,98}... | collective-permute-start | bytes 491528 | tf_op jit(solution)/shard_map/ppermute | solution.py:42
  47.1 22.0 %collective-permute-start.12 = (bf16[64,1792]{1,0:T(8,128)(2,1)S(1)}, bf16[64,1792]{1,0:T(8,128)(2,1)S(1)}, u32[]{:S(2)}, u32[]{:S(2)}) collective-permute-start(bf16[64,1792]{1,0:T(8,128)(2,1)S(1)} %get-tuple-element.71), channel_id=1, source_target_pairs={{0,24},{8,0},{16,8},{24,16},{1,25},{9,1},{17,9},{25,17},{2,26},{10... | collective-permute-start | bytes 688136 | tf_op jit(solution)/shard_map/ppermute | solution.py:30
  50.2 18.9 %collective-permute-start.13 = (bf16[64,1792]{1,0:T(8,128)(2,1)S(1)}, bf16[64,1792]{1,0:T(8,128)(2,1)S(1)}, u32[]{:S(2)}, u32[]{:S(2)}) collective-permute-start(bf16[64,1792]{1,0:T(8,128)(2,1)S(1)} %get-tuple-element.72), channel_id=1, source_target_pairs={{0,16},{8,24},{16,0},{24,8},{1,17},{9,25},{17,1},{25,9},{2,18},{10... | collective-permute-start | bytes 688136 | tf_op jit(solution)/shard_map/ppermute | solution.py:30
  50.8 18.3 %collective-permute-start.14 = (bf16[64,1792]{1,0:T(8,128)(2,1)S(1)}, bf16[64,1792]{1,0:T(8,128)(2,1)S(1)}, u32[]{:S(2)}, u32[]{:S(2)}) collective-permute-start(bf16[64,1792]{1,0:T(8,128)(2,1)S(1)} %get-tuple-element.73), channel_id=1, source_target_pairs={{0,8},{8,16},{16,24},{24,0},{1,9},{9,17},{17,25},{25,1},{2,10},{10... | collective-permute-start | bytes 688136 | tf_op jit(solution)/shard_map/ppermute | solution.py:30
  51.8 3.7 %collective-permute-start.15 = (f32[2,1,1024]{2,1,0:T(1,128)S(1)}, f32[2,1,1024]{2,1,0:T(1,128)S(1)}, u32[]{:S(2)}, u32[]{:S(2)}) collective-permute-start(f32[2,1,1024]{2,1,0:T(1,128)S(1)} %add.65), channel_id=1, source_target_pairs={{0,2},{2,0},{4,6},{6,4},{1,3},{3,1},{5,7},{7,5},{8,10},{10,8},{12,... | collective-permute-start | bytes 24584 | tf_op jit(solution)/shard_map/ppermute | solution.py:38
  55.5 4.9 %collective-permute-start.16 = (f32[2,1,1024]{2,1,0:T(1,128)S(1)}, f32[2,1,1024]{2,1,0:T(1,128)S(1)}, u32[]{:S(2)}, u32[]{:S(2)}) collective-permute-start(f32[2,1,1024]{2,1,0:T(1,128)S(1)} %add.66), channel_id=1, source_target_pairs={{0,6},{6,0},{2,4},{4,2},{1,7},{7,1},{3,5},{5,3},{8,14},{14,8},{10,... | collective-permute-start | bytes 24584 | tf_op jit(solution)/shard_map/ppermute | solution.py:42
  60.4 3.7 %collective-permute-start.17 = (f32[2,1,1024]{2,1,0:T(1,128)S(1)}, f32[2,1,1024]{2,1,0:T(1,128)S(1)}, u32[]{:S(2)}, u32[]{:S(2)}) collective-permute-start(f32[2,1,1024]{2,1,0:T(1,128)S(1)} %add.67), channel_id=1, source_target_pairs={{0,8},{8,0},{16,24},{24,16},{1,9},{9,1},{17,25},{25,17},{2,10},{10... | collective-permute-start | bytes 24584 | tf_op jit(solution)/shard_map/ppermute | solution.py:38
  64.2 4.9 %collective-permute-start.18 = (f32[2,1,1024]{2,1,0:T(1,128)S(1)}, f32[2,1,1024]{2,1,0:T(1,128)S(1)}, u32[]{:S(2)}, u32[]{:S(2)}) collective-permute-start(f32[2,1,1024]{2,1,0:T(1,128)S(1)} %add.68), channel_id=1, source_target_pairs={{0,24},{24,0},{8,16},{16,8},{1,25},{25,1},{9,17},{17,9},{2,26},{26... | collective-permute-start | bytes 24584 | tf_op jit(solution)/shard_map/ppermute | solution.py:42
  69.8 2.9 %collective-permute-start.19 = (bf16[4,2,32,1280]{3,2,1,0:T(8,128)(2,1)S(1)}, bf16[4,2,32,1280]{3,2,1,0:T(8,128)(2,1)S(1)}, u32[]{:S(2)}, u32[]{:S(2)}) collective-permute-start(bf16[4,2,32,1280]{3,2,1,0:T(8,128)(2,1)S(1)} %get-tuple-element.79), channel_id=1, source_target_pairs={{0,1},{1,0},{2,3},{3,2},{4,5},{5,4},{6,7},{7,6},{8,9},{9,8},{10,11... | collective-permute-start | bytes 1966088 | tf_op jit(solution)/shard_map/ppermute | solution.py:34
  73.6 4.9 %collective-permute-start.23 = (bf16[32,1280]{1,0:T(8,128)(2,1)S(1)}, bf16[32,1280]{1,0:T(8,128)(2,1)}, u32[]{:S(2)}, u32[]{:S(2)}) collective-permute-start(bf16[32,1280]{1,0:T(8,128)(2,1)S(1)} %embed_grad.1), channel_id=1, source_target_pairs={{0,32},{32,0},{64,96},{96,64},{1,33},{33,1},{65,97},{97,65},{2,34}... | collective-permute-start | bytes 245768 | tf_op jit(solution)/shard_map/ppermute | solution.py:38
  73.6 12.3 %collective-permute-start.20 = (bf16[2,32,1280]{2,1,0:T(8,128)(2,1)}, bf16[2,32,1280]{2,1,0:T(8,128)(2,1)S(1)}, u32[]{:S(2)}, u32[]{:S(2)}) collective-permute-start(bf16[2,32,1280]{2,1,0:T(8,128)(2,1)} %get-tuple-element.81), channel_id=1, source_target_pairs={{0,2},{2,4},{4,6},{6,0},{1,3},{3,5},{5,7},{7,1},{8,10},{10,12},{12... | collective-permute-start | bytes 491528 | tf_op jit(solution)/shard_map/ppermute | solution.py:30
  73.9 12.2 %collective-permute-start.21 = (bf16[2,32,1280]{2,1,0:T(8,128)(2,1)}, bf16[2,32,1280]{2,1,0:T(8,128)(2,1)S(1)}, u32[]{:S(2)}, u32[]{:S(2)}) collective-permute-start(bf16[2,32,1280]{2,1,0:T(8,128)(2,1)} %get-tuple-element.82), channel_id=1, source_target_pairs={{0,4},{2,6},{4,0},{6,2},{1,5},{3,7},{5,1},{7,3},{8,12},{10,14},{12... | collective-permute-start | bytes 491528 | tf_op jit(solution)/shard_map/ppermute | solution.py:30
  77.9 8.3 %collective-permute-start.22 = (bf16[2,32,1280]{2,1,0:T(8,128)(2,1)}, bf16[2,32,1280]{2,1,0:T(8,128)(2,1)S(1)}, u32[]{:S(2)}, u32[]{:S(2)}) collective-permute-start(bf16[2,32,1280]{2,1,0:T(8,128)(2,1)} %get-tuple-element.83), channel_id=1, source_target_pairs={{0,6},{2,0},{4,2},{6,4},{1,7},{3,1},{5,3},{7,5},{8,14},{10,8},{12,... | collective-permute-start | bytes 491528 | tf_op jit(solution)/shard_map/ppermute | solution.py:30
  79.5 5.7 %collective-permute-start.24 = (bf16[32,1280]{1,0:T(8,128)(2,1)S(1)}, bf16[32,1280]{1,0:T(8,128)(2,1)S(1)}, u32[]{:S(2)}, u32[]{:S(2)}) collective-permute-start(bf16[32,1280]{1,0:T(8,128)(2,1)S(1)} %add_convert_fusion.6), channel_id=1, source_target_pairs={{0,96},{96,0},{32,64},{64,32},{1,97},{97,1},{33,65},{65,33},{2,98}... | collective-permute-start | bytes 245768 | tf_op jit(solution)/shard_map/ppermute | solution.py:42
  (10 other events, 108.3 us)

commit v12 on v11

--- a/solution.py
+++ b/solution.py
@@ -343,13 +343,12 @@
     out_part = out_part.astype(BF16).reshape(64, 1280)
     part_other = near(part)
     part, out_part = lax.optimization_barrier((part, out_part))
-    out_other = near(out_part)
+    out_other = far(out_part)
     part = merge_pair(part, part_other)
-    comb_late = after(comb_late, part)
+    out_part = add(after(out_part, part), out_other)
+    grad_slot_out = add(out_part, near(out_part))
     slot_in, lse = merge_last(part, far(part))
-    inputs = list(input_blocks(comb_late, embed))
-    out_part = add(after(out_part, slot_in), out_other)
-    grad_slot_out = add(out_part, far(out_part))
+    inputs = list(input_blocks(after(comb_late, out_part), embed))
 
     pre_act = jnp.dot(slot_in, w_in, preferred_element_type=F32)
     act, slope = gelu_parts(pre_act)

time: 87.7 us -> 87.9 us (level)
    ppermute x7, waiting for transfers between devices: 7.38 us -> 12.9 us  [far(): return lax.ppermute(value, axis, [(0, 3), (3, 0), (1, 2), (2, 1)])]
    ppermute x7, waiting for transfers between devices: 12 us -> 6.78 us  [near(): return lax.ppermute(value, axis, [(0, 1), (1, 0), (2, 3), (3, 2)])]
    ppermute x7, starting transfers between devices: 5.95 us -> 8.48 us  [near(): return lax.ppermute(value, axis, [(0, 1), (1, 0), (2, 3), (3, 2)])]
    ppermute x7, starting transfers between devices: 15.9 us -> 13.8 us  [far(): return lax.ppermute(value, axis, [(0, 3), (3, 0), (1, 2), (2, 1)])]
  transfers between devices with their start and end apart: 25 -> 25, of which waited for: 14 -> 13; matrix products, arithmetic and copies ran while one was open for 15% -> 15% of each run, Pallas kernels for 5% -> 6%
where the time goes in v12:
time: 87.9 us; the launch traced here: 87.1 us
  starting transfers between devices  38.2 us (43%)
  waiting for transfers between devices  21.1 us (24%)
  Pallas kernels  13.2 us (15%)
  matrix products  11.1 us (13%)
  other arithmetic  2.61 us (3%)
  between operations  0.95 us (1%)
    ppermute x9, starting transfers between devices, shift(): return lax.ppermute(value, axis, [(i, (i + by) % 4) for i in range(4)])  15.7 us
    ppermute x7, starting transfers between devices, far(): return lax.ppermute(value, axis, [(0, 3), (3, 0), (1, 2), (2, 1)])  13.8 us
    ppermute x7, waiting for transfers between devices, far(): return lax.ppermute(value, axis, [(0, 3), (3, 0), (1, 2), (2, 1)])  12.9 us
    ppermute x7, starting transfers between devices, near(): return lax.ppermute(value, axis, [(0, 1), (1, 0), (2, 3), (3, 2)])  8.48 us
    ppermute x7, waiting for transfers between devices, near(): return lax.ppermute(value, axis, [(0, 1), (1, 0), (2, 3), (3, 2)])  6.78 us
    pallas_call x1, Pallas kernels, local_softmax(): pl.pallas_call(softmax_kernel, grid=(1,), in_specs=[pl.BlockSpec((1, 256,...  5.11 us
    dot_general x1, matrix products, local(): jnp.einsum('sd,sh->dh', slot_late, grad_pre, preferred_element_type=F32)  3.67 us
    pallas_call x1, Pallas kernels, embed_grad(): pl.pallas_call(embed_grad_kernel, in_specs=[pl.BlockSpec(memory_space=pl....  2.78 us
  transfers between devices with their start and end apart: 25, of which 13 were waited for; matrix products, arithmetic and copies ran while one was open for 15% of the time, Pallas kernels for 6%

profile of v12, /device:TPU:0, one launch (start us, length us, event | category | flops | bytes accessed | tf_op | source)
XLA Modules:
  0.0 87.1 jit_solution(9656247425936140939)
XLA Ops:
  0.7 5.1 %local_softmax.1 = (f32[64,1024]{1,0:T(8,128)S(1)}, bf16[64,1408]{1,0:T(8,128)(2,1)S(1)}) custom-call(bf16[2,1024,1280]{2,1,0:T(8,128)(2,1)} %tok.3, bf16[2,1024,1280]{2,1,0:T(8,128)(2,1)} %tok.3, bf16[2,1024,1280]{2,1,0:T(8,128)(2,1)} %tok.3, bf16[2,1024,1280]{2,1,0:T(8,128)(2,1)} %tok.3, bf16[2,1024,1280]{2,1,0:T(8,128)(2,1)} %tok.3, ...), custom_call_target="tpu_custom_call" | custom-call | flops 700000000 | bytes 6000000 | tf_op jit(solution)/shard_map/local_softmax/pallas_call | solution.py:125
  5.8 2.1 %collective-permute-start = (bf16[64,1408]{1,0:T(8,128)(2,1)S(1)}, bf16[64,1408]{1,0:T(8,128)(2,1)S(1)}, u32[]{:S(2)}, u32[]{:S(2)}) collective-permute-start(bf16[64,1408]{1,0:T(8,128)(2,1)S(1)} %get-tuple-element.48.a), channel_id=1, source_target_pairs={{0,32},{32,0},{64,96},{96,64},{1,33},{33,1},{65,97},{97,65},{2,34}... | collective-permute-start | bytes 540680 | tf_op jit(solution)/shard_map/ppermute | solution.py:38
  8.9 2.6 %collective-permute-start.1 = (bf16[64,1280]{1,0:T(8,128)(2,1)S(1)}, bf16[64,1280]{1,0:T(8,128)(2,1)S(1)}, u32[]{:S(2)}, u32[]{:S(2)}) collective-permute-start(bf16[64,1280]{1,0:T(8,128)(2,1)S(1)} %bitcast.51), channel_id=1, source_target_pairs={{0,96},{96,0},{32,64},{64,32},{1,97},{97,1},{33,65},{65,33},{2,98}... | collective-permute-start | bytes 491528 | tf_op jit(solution)/shard_map/ppermute | solution.py:42
  12.7 3.2 %collective-permute-done.1 = bf16[64,1280]{1,0:T(8,128)(2,1)S(1)} collective-permute-done((bf16[64,1280]{1,0:T(8,128)(2,1)S(1)}, bf16[64,1280]{1,0:T(8,128)(2,1)S(1)}, u32[]{:S(2)}, u32[]{:S(2)}) %collective-permute-start.1) | collective-permute-done | bytes 163872 | tf_op jit(solution)/shard_map/ppermute | solution.py:42
  16.5 2.3 %collective-permute-start.3 = (bf16[64,1408]{1,0:T(8,128)(2,1)S(1)}, bf16[64,1408]{1,0:T(8,128)(2,1)S(1)}, u32[]{:S(2)}, u32[]{:S(2)}) collective-permute-start(bf16[64,1408]{1,0:T(8,128)(2,1)S(1)} %merge_pair.1.one), channel_id=1, source_target_pairs={{0,96},{96,0},{32,64},{64,32},{1,97},{97,1},{33,65},{65,33},{2,98}... | collective-permute-start | bytes 540680 | tf_op jit(solution)/shard_map/ppermute | solution.py:42
  18.9 3.3 %collective-permute-start.6 = (bf16[224,256]{1,0:T(8,128)(2,1)S(1)}, bf16[224,256]{1,0:T(8,128)(2,1)S(1)}, u32[]{:S(2)}, u32[]{:S(2)}) collective-permute-start(bf16[224,256]{1,0:T(8,128)(2,1)S(1)} %get-tuple-element.56), channel_id=1, source_target_pairs={{0,16},{8,24},{16,0},{24,8},{1,17},{9,25},{17,1},{25,9},{2,18},{10... | collective-permute-start | bytes 344072 | tf_op jit(solution)/shard_map/ppermute | solution.py:30
  25.7 2.6 %collective-permute-start.5 = (bf16[224,256]{1,0:T(8,128)(2,1)S(1)}, bf16[224,256]{1,0:T(8,128)(2,1)S(1)}, u32[]{:S(2)}, u32[]{:S(2)}) collective-permute-start(bf16[224,256]{1,0:T(8,128)(2,1)S(1)} %get-tuple-element.55), channel_id=1, source_target_pairs={{0,24},{8,0},{16,8},{24,16},{1,25},{9,1},{17,9},{25,17},{2,26},{10... | collective-permute-start | bytes 344072 | tf_op jit(solution)/shard_map/ppermute | solution.py:30
  30.6 2.6 %collective-permute-start.9 = (bf16[64,1280]{1,0:T(8,128)(2,1)S(1)}, bf16[64,1280]{1,0:T(8,128)(2,1)S(1)}, u32[]{:S(2)}, u32[]{:S(2)}) collective-permute-start(bf16[64,1280]{1,0:T(8,128)(2,1)S(1)} %add_convert_fusion.3.sum_a), channel_id=1, source_target_pairs={{0,96},{96,0},{32,64},{64,32},{1,97},{97,1},{33,65},{65,33},{2,98}... | collective-permute-start | bytes 491528 | tf_op jit(solution)/shard_map/ppermute | solution.py:42
  34.2 2.8 %convolution_convert_fusion.1 = bf16[1280,1280]{1,0:T(8,128)(2,1)} fusion(bf16[64,1280]{1,0:T(8,128)(2,1)S(1)} %get-tuple-element.60, bf16[64,1280]{1,0:T(8,128)(2,1)S(1)} %add_convert_fusion.4), kind=kOutput, calls=%fused_computation.1 | convolution fusion | flops 211353600 | bytes 3604480 | tf_op jit(solution)/shard_map/sh,sd->hd/dot_general | solution.py:370
  37.0 1.5 %collective-permute-done.8 = bf16[64,1280]{1,0:T(8,128)(2,1)S(1)} collective-permute-done((bf16[64,1280]{1,0:T(8,128)(2,1)S(1)}, bf16[64,1280]{1,0:T(8,128)(2,1)S(1)}, u32[]{:S(2)}, u32[]{:S(2)}) %collective-permute-start.8) | collective-permute-done | bytes 163872 | tf_op jit(solution)/shard_map/ppermute | solution.py:38
  39.4 1.6 %combine_grad.1 = (f32[64,1024]{1,0:T(8,128)S(1)}, f32[2,1,1024]{2,1,0:T(1,128)S(1)}) custom-call(bf16[2,1024,1280]{2,1,0:T(8,128)(2,1)S(1)} %copy-done.1, bf16[64,1280]{1,0:T(8,128)(2,1)S(1)} %add_convert_fusion.3.sum_a, bf16[64,1280]{1,0:T(8,128)(2,1)S(1)} %collective-permute-done.9.sum_b, bf16[64,1024]{1,0:T(8,128)(2,1)S(1)} %bitcast.45), custom_call_target="tpu_custom_call" | custom-call | flops 350000000 | bytes 6000000 | tf_op jit(solution)/shard_map/combine_grad/pallas_call | solution.py:190
  42.2 3.0 %collective-permute-done.10 = bf16[64,1280]{1,0:T(8,128)(2,1)S(1)} collective-permute-done((bf16[64,1280]{1,0:T(8,128)(2,1)S(1)}, bf16[64,1280]{1,0:T(8,128)(2,1)S(1)}, u32[]{:S(2)}, u32[]{:S(2)}) %collective-permute-start.10) | collective-permute-done | bytes 163872 | tf_op jit(solution)/shard_map/ppermute | solution.py:42
  45.3 1.6 %dispatch_grad.1 = (f32[64,1024]{1,0:T(8,128)S(1)}, bf16[64,1792]{1,0:T(8,128)(2,1)S(1)}, bf16[64,1792]{1,0:T(8,128)(2,1)S(1)}, bf16[64,1792]{1,0:T(8,128)(2,1)S(1)}, bf16[64,1792]{1,0:T(8,128)(2,1)S(1)}) custom-call(bf16[2,1024,1280]{2,1,0:T(8,128)(2,1)S(1)} %bitcast.42, bf16[64,1280]{1,0:T(8,128)(2,1)S(1)} %add_convert_fusion.1.gslot, ...), custom_call_target="tpu_custom_call" | custom-call | flops 350000000 | bytes 7000000 | tf_op jit(solution)/shard_map/dispatch_grad/pallas_call | solution.py:216
  46.9 3.6 %collective-permute-start.12 = (bf16[64,1792]{1,0:T(8,128)(2,1)S(1)}, bf16[64,1792]{1,0:T(8,128)(2,1)S(1)}, u32[]{:S(2)}, u32[]{:S(2)}) collective-permute-start(bf16[64,1792]{1,0:T(8,128)(2,1)S(1)} %get-tuple-element.71), channel_id=1, source_target_pairs={{0,24},{8,0},{16,8},{24,16},{1,25},{9,1},{17,9},{25,17},{2,26},{10... | collective-permute-start | bytes 688136 | tf_op jit(solution)/shard_map/ppermute | solution.py:30
  53.1 2.2 %collective-permute-done.15 = f32[2,1,1024]{2,1,0:T(1,128)S(1)} collective-permute-done((f32[2,1,1024]{2,1,0:T(1,128)S(1)}, f32[2,1,1024]{2,1,0:T(1,128)S(1)}, u32[]{:S(2)}, u32[]{:S(2)}) %collective-permute-start.15) | collective-permute-done | bytes 8224 | tf_op jit(solution)/shard_map/ppermute | solution.py:38
  55.3 2.8 %collective-permute-start.16 = (f32[2,1,1024]{2,1,0:T(1,128)S(1)}, f32[2,1,1024]{2,1,0:T(1,128)S(1)}, u32[]{:S(2)}, u32[]{:S(2)}) collective-permute-start(f32[2,1,1024]{2,1,0:T(1,128)S(1)} %add.66), channel_id=1, source_target_pairs={{0,6},{6,0},{2,4},{4,2},{1,7},{7,1},{3,5},{5,3},{8,14},{14,8},{10,... | collective-permute-start | bytes 24584 | tf_op jit(solution)/shard_map/ppermute | solution.py:42
  58.1 2.1 %collective-permute-done.16 = f32[2,1,1024]{2,1,0:T(1,128)S(1)} collective-permute-done((f32[2,1,1024]{2,1,0:T(1,128)S(1)}, f32[2,1,1024]{2,1,0:T(1,128)S(1)}, u32[]{:S(2)}, u32[]{:S(2)}) %collective-permute-start.16) | collective-permute-done | bytes 8224 | tf_op jit(solution)/shard_map/ppermute | solution.py:42
  60.3 2.4 %collective-permute-start.17 = (f32[2,1,1024]{2,1,0:T(1,128)S(1)}, f32[2,1,1024]{2,1,0:T(1,128)S(1)}, u32[]{:S(2)}, u32[]{:S(2)}) collective-permute-start(f32[2,1,1024]{2,1,0:T(1,128)S(1)} %add.67), channel_id=1, source_target_pairs={{0,8},{8,0},{16,24},{24,16},{1,9},{9,1},{17,25},{25,17},{2,10},{10... | collective-permute-start | bytes 24584 | tf_op jit(solution)/shard_map/ppermute | solution.py:38
  62.7 1.6 %collective-permute-done.17 = f32[2,1,1024]{2,1,0:T(1,128)S(1)} collective-permute-done((f32[2,1,1024]{2,1,0:T(1,128)S(1)}, f32[2,1,1024]{2,1,0:T(1,128)S(1)}, u32[]{:S(2)}, u32[]{:S(2)}) %collective-permute-start.17) | collective-permute-done | bytes 8224 | tf_op jit(solution)/shard_map/ppermute | solution.py:38
  64.3 1.9 %collective-permute-start.18 = (f32[2,1,1024]{2,1,0:T(1,128)S(1)}, f32[2,1,1024]{2,1,0:T(1,128)S(1)}, u32[]{:S(2)}, u32[]{:S(2)}) collective-permute-start(f32[2,1,1024]{2,1,0:T(1,128)S(1)} %add.68), channel_id=1, source_target_pairs={{0,24},{24,0},{8,16},{16,8},{1,25},{25,1},{9,17},{17,9},{2,26},{26... | collective-permute-start | bytes 24584 | tf_op jit(solution)/shard_map/ppermute | solution.py:42
  66.2 3.1 %collective-permute-done.18 = f32[2,1,1024]{2,1,0:T(1,128)S(1)} collective-permute-done((f32[2,1,1024]{2,1,0:T(1,128)S(1)}, f32[2,1,1024]{2,1,0:T(1,128)S(1)}, u32[]{:S(2)}, u32[]{:S(2)}) %collective-permute-start.18) | collective-permute-done | bytes 8224 | tf_op jit(solution)/shard_map/ppermute | solution.py:42
  70.1 2.8 %embed_grad.1 = bf16[32,1280]{1,0:T(8,128)(2,1)S(1)} custom-call(bf16[2,1024,1280]{2,1,0:T(8,128)(2,1)} %tok.3, f32[64,1024]{1,0:T(8,128)S(1)} %get-tuple-element.77.partial_logits, bf16[64,1024]{1,0:T(8,128)(2,1)S(1)} %bitcast.47, f32[2,1,1024]{2,1,0:T(1,128)S(1)} %add.69.refs_8_.row_dot), custom_call_target="tpu_custom_call" | custom-call | flops 170000000 | bytes 6000000 | tf_op jit(solution)/shard_map/embed_grad/pallas_call | solution.py:260
  74.1 3.9 %collective-permute-start.21 = (bf16[2,32,1280]{2,1,0:T(8,128)(2,1)}, bf16[2,32,1280]{2,1,0:T(8,128)(2,1)S(1)}, u32[]{:S(2)}, u32[]{:S(2)}) collective-permute-start(bf16[2,32,1280]{2,1,0:T(8,128)(2,1)} %get-tuple-element.82), channel_id=1, source_target_pairs={{0,4},{2,6},{4,0},{6,2},{1,5},{3,7},{5,1},{7,3},{8,12},{10,14},{12... | collective-permute-start | bytes 491528 | tf_op jit(solution)/shard_map/ppermute | solution.py:30
  80.4 3.7 %fusion = bf16[1,1280,1280]{2,1,0:T(8,128)(2,1)} fusion(bf16[64,1280]{1,0:T(8,128)(2,1)S(1)} %get-tuple-element.85.slot_in, bf16[64,1280]{1,0:T(8,128)(2,1)} %copy-done.5), kind=kOutput, calls=%fused_computation.2 | convolution fusion | flops 211353600 | bytes 3604480 | tf_op jit(solution)/shard_map/sd,sh->dh/dot_general | solution.py:404
  (74 shorter events, 21.9 us)
Async XLA Ops:
  5.8 6.6 %collective-permute-start = (bf16[64,1408]{1,0:T(8,128)(2,1)S(1)}, bf16[64,1408]{1,0:T(8,128)(2,1)S(1)}, u32[]{:S(2)}, u32[]{:S(2)}) collective-permute-start(bf16[64,1408]{1,0:T(8,128)(2,1)S(1)} %get-tuple-element.48.a), channel_id=1, source_target_pairs={{0,32},{32,0},{64,96},{96,64},{1,33},{33,1},{65,97},{97,65},{2,34}... | collective-permute-start | bytes 540680 | tf_op jit(solution)/shard_map/ppermute | solution.py:38
  8.9 6.9 %collective-permute-start.1 = (bf16[64,1280]{1,0:T(8,128)(2,1)S(1)}, bf16[64,1280]{1,0:T(8,128)(2,1)S(1)}, u32[]{:S(2)}, u32[]{:S(2)}) collective-permute-start(bf16[64,1280]{1,0:T(8,128)(2,1)S(1)} %bitcast.51), channel_id=1, source_target_pairs={{0,96},{96,0},{32,64},{64,32},{1,97},{97,1},{33,65},{65,33},{2,98}... | collective-permute-start | bytes 491528 | tf_op jit(solution)/shard_map/ppermute | solution.py:42
  15.9 7.0 %collective-permute-start.2 = (bf16[64,1280]{1,0:T(8,128)(2,1)S(1)}, bf16[64,1280]{1,0:T(8,128)(2,1)S(1)}, u32[]{:S(2)}, u32[]{:S(2)}) collective-permute-start(bf16[64,1280]{1,0:T(8,128)(2,1)S(1)} %add_convert_fusion.5), channel_id=1, source_target_pairs={{0,32},{32,0},{64,96},{96,64},{1,33},{33,1},{65,97},{97,65},{2,34}... | collective-permute-start | bytes 491528 | tf_op jit(solution)/shard_map/ppermute | solution.py:38
  16.5 6.7 %collective-permute-start.3 = (bf16[64,1408]{1,0:T(8,128)(2,1)S(1)}, bf16[64,1408]{1,0:T(8,128)(2,1)S(1)}, u32[]{:S(2)}, u32[]{:S(2)}) collective-permute-start(bf16[64,1408]{1,0:T(8,128)(2,1)S(1)} %merge_pair.1.one), channel_id=1, source_target_pairs={{0,96},{96,0},{32,64},{64,32},{1,97},{97,1},{33,65},{65,33},{2,98}... | collective-permute-start | bytes 540680 | tf_op jit(solution)/shard_map/ppermute | solution.py:42
  18.9 11.7 %collective-permute-start.6 = (bf16[224,256]{1,0:T(8,128)(2,1)S(1)}, bf16[224,256]{1,0:T(8,128)(2,1)S(1)}, u32[]{:S(2)}, u32[]{:S(2)}) collective-permute-start(bf16[224,256]{1,0:T(8,128)(2,1)S(1)} %get-tuple-element.56), channel_id=1, source_target_pairs={{0,16},{8,24},{16,0},{24,8},{1,17},{9,25},{17,1},{25,9},{2,18},{10... | collective-permute-start | bytes 344072 | tf_op jit(solution)/shard_map/ppermute | solution.py:30
  22.2 8.4 %collective-permute-start.7 = (bf16[224,256]{1,0:T(8,128)(2,1)S(1)}, bf16[224,256]{1,0:T(8,128)(2,1)S(1)}, u32[]{:S(2)}, u32[]{:S(2)}) collective-permute-start(bf16[224,256]{1,0:T(8,128)(2,1)S(1)} %get-tuple-element.57), channel_id=1, source_target_pairs={{0,8},{8,16},{16,24},{24,0},{1,9},{9,17},{17,25},{25,1},{2,10},{10... | collective-permute-start | bytes 344072 | tf_op jit(solution)/shard_map/ppermute | solution.py:30
  24.9 5.6 %collective-permute-start.4 = (bf16[64,1280]{1,0:T(8,128)(2,1)S(1)}, bf16[64,1280]{1,0:T(8,128)(2,1)S(1)}, u32[]{:S(2)}, u32[]{:S(2)}) collective-permute-start(bf16[64,1280]{1,0:T(8,128)(2,1)S(1)} %fusion.18), channel_id=1, source_target_pairs={{0,32},{32,0},{64,96},{96,64},{1,33},{33,1},{65,97},{97,65},{2,34}... | collective-permute-start | bytes 491528 | tf_op jit(solution)/shard_map/ppermute | solution.py:38
  25.7 4.9 %collective-permute-start.5 = (bf16[224,256]{1,0:T(8,128)(2,1)S(1)}, bf16[224,256]{1,0:T(8,128)(2,1)S(1)}, u32[]{:S(2)}, u32[]{:S(2)}) collective-permute-start(bf16[224,256]{1,0:T(8,128)(2,1)S(1)} %get-tuple-element.55), channel_id=1, source_target_pairs={{0,24},{8,0},{16,8},{24,16},{1,25},{9,1},{17,9},{25,17},{2,26},{10... | collective-permute-start | bytes 344072 | tf_op jit(solution)/shard_map/ppermute | solution.py:30
  30.6 8.8 %collective-permute-start.9 = (bf16[64,1280]{1,0:T(8,128)(2,1)S(1)}, bf16[64,1280]{1,0:T(8,128)(2,1)S(1)}, u32[]{:S(2)}, u32[]{:S(2)}) collective-permute-start(bf16[64,1280]{1,0:T(8,128)(2,1)S(1)} %add_convert_fusion.3.sum_a), channel_id=1, source_target_pairs={{0,96},{96,0},{32,64},{64,32},{1,97},{97,1},{33,65},{65,33},{2,98}... | collective-permute-start | bytes 491528 | tf_op jit(solution)/shard_map/ppermute | solution.py:42
  33.2 5.3 %collective-permute-start.8 = (bf16[64,1280]{1,0:T(8,128)(2,1)S(1)}, bf16[64,1280]{1,0:T(8,128)(2,1)S(1)}, u32[]{:S(2)}, u32[]{:S(2)}) collective-permute-start(bf16[64,1280]{1,0:T(8,128)(2,1)S(1)} %fusion.15), channel_id=1, source_target_pairs={{0,32},{32,0},{64,96},{96,64},{1,33},{33,1},{65,97},{97,65},{2,34}... | collective-permute-start | bytes 491528 | tf_op jit(solution)/shard_map/ppermute | solution.py:38
  38.6 6.6 %collective-permute-start.10 = (bf16[64,1280]{1,0:T(8,128)(2,1)S(1)}, bf16[64,1280]{1,0:T(8,128)(2,1)S(1)}, u32[]{:S(2)}, u32[]{:S(2)}) collective-permute-start(bf16[64,1280]{1,0:T(8,128)(2,1)S(1)} %add_convert_fusion.2), channel_id=1, source_target_pairs={{0,96},{96,0},{32,64},{64,32},{1,97},{97,1},{33,65},{65,33},{2,98}... | collective-permute-start | bytes 491528 | tf_op jit(solution)/shard_map/ppermute | solution.py:42
  46.9 22.4 %collective-permute-start.12 = (bf16[64,1792]{1,0:T(8,128)(2,1)S(1)}, bf16[64,1792]{1,0:T(8,128)(2,1)S(1)}, u32[]{:S(2)}, u32[]{:S(2)}) collective-permute-start(bf16[64,1792]{1,0:T(8,128)(2,1)S(1)} %get-tuple-element.71), channel_id=1, source_target_pairs={{0,24},{8,0},{16,8},{24,16},{1,25},{9,1},{17,9},{25,17},{2,26},{10... | collective-permute-start | bytes 688136 | tf_op jit(solution)/shard_map/ppermute | solution.py:30
  50.5 18.8 %collective-permute-start.13 = (bf16[64,1792]{1,0:T(8,128)(2,1)S(1)}, bf16[64,1792]{1,0:T(8,128)(2,1)S(1)}, u32[]{:S(2)}, u32[]{:S(2)}) collective-permute-start(bf16[64,1792]{1,0:T(8,128)(2,1)S(1)} %get-tuple-element.72), channel_id=1, source_target_pairs={{0,16},{8,24},{16,0},{24,8},{1,17},{9,25},{17,1},{25,9},{2,18},{10... | collective-permute-start | bytes 688136 | tf_op jit(solution)/shard_map/ppermute | solution.py:30
  50.5 18.8 %collective-permute-start.14 = (bf16[64,1792]{1,0:T(8,128)(2,1)S(1)}, bf16[64,1792]{1,0:T(8,128)(2,1)S(1)}, u32[]{:S(2)}, u32[]{:S(2)}) collective-permute-start(bf16[64,1792]{1,0:T(8,128)(2,1)S(1)} %get-tuple-element.73), channel_id=1, source_target_pairs={{0,8},{8,16},{16,24},{24,0},{1,9},{9,17},{17,25},{25,1},{2,10},{10... | collective-permute-start | bytes 688136 | tf_op jit(solution)/shard_map/ppermute | solution.py:30
  51.6 3.7 %collective-permute-start.15 = (f32[2,1,1024]{2,1,0:T(1,128)S(1)}, f32[2,1,1024]{2,1,0:T(1,128)S(1)}, u32[]{:S(2)}, u32[]{:S(2)}) collective-permute-start(f32[2,1,1024]{2,1,0:T(1,128)S(1)} %add.65), channel_id=1, source_target_pairs={{0,2},{2,0},{4,6},{6,4},{1,3},{3,1},{5,7},{7,5},{8,10},{10,8},{12,... | collective-permute-start | bytes 24584 | tf_op jit(solution)/shard_map/ppermute | solution.py:38
  55.3 4.9 %collective-permute-start.16 = (f32[2,1,1024]{2,1,0:T(1,128)S(1)}, f32[2,1,1024]{2,1,0:T(1,128)S(1)}, u32[]{:S(2)}, u32[]{:S(2)}) collective-permute-start(f32[2,1,1024]{2,1,0:T(1,128)S(1)} %add.66), channel_id=1, source_target_pairs={{0,6},{6,0},{2,4},{4,2},{1,7},{7,1},{3,5},{5,3},{8,14},{14,8},{10,... | collective-permute-start | bytes 24584 | tf_op jit(solution)/shard_map/ppermute | solution.py:42
  60.3 4.1 %collective-permute-start.17 = (f32[2,1,1024]{2,1,0:T(1,128)S(1)}, f32[2,1,1024]{2,1,0:T(1,128)S(1)}, u32[]{:S(2)}, u32[]{:S(2)}) collective-permute-start(f32[2,1,1024]{2,1,0:T(1,128)S(1)} %add.67), channel_id=1, source_target_pairs={{0,8},{8,0},{16,24},{24,16},{1,9},{9,1},{17,25},{25,17},{2,10},{10... | collective-permute-start | bytes 24584 | tf_op jit(solution)/shard_map/ppermute | solution.py:38
  64.3 4.9 %collective-permute-start.18 = (f32[2,1,1024]{2,1,0:T(1,128)S(1)}, f32[2,1,1024]{2,1,0:T(1,128)S(1)}, u32[]{:S(2)}, u32[]{:S(2)}) collective-permute-start(f32[2,1,1024]{2,1,0:T(1,128)S(1)} %add.68), channel_id=1, source_target_pairs={{0,24},{24,0},{8,16},{16,8},{1,25},{25,1},{9,17},{17,9},{2,26},{26... | collective-permute-start | bytes 24584 | tf_op jit(solution)/shard_map/ppermute | solution.py:42
  70.0 2.9 %collective-permute-start.19 = (bf16[4,2,32,1280]{3,2,1,0:T(8,128)(2,1)S(1)}, bf16[4,2,32,1280]{3,2,1,0:T(8,128)(2,1)S(1)}, u32[]{:S(2)}, u32[]{:S(2)}) collective-permute-start(bf16[4,2,32,1280]{3,2,1,0:T(8,128)(2,1)S(1)} %get-tuple-element.79), channel_id=1, source_target_pairs={{0,1},{1,0},{2,3},{3,2},{4,5},{5,4},{6,7},{7,6},{8,9},{9,8},{10,11... | collective-permute-start | bytes 1966088 | tf_op jit(solution)/shard_map/ppermute | solution.py:34
  73.8 4.9 %collective-permute-start.23 = (bf16[32,1280]{1,0:T(8,128)(2,1)S(1)}, bf16[32,1280]{1,0:T(8,128)(2,1)}, u32[]{:S(2)}, u32[]{:S(2)}) collective-permute-start(bf16[32,1280]{1,0:T(8,128)(2,1)S(1)} %embed_grad.1), channel_id=1, source_target_pairs={{0,32},{32,0},{64,96},{96,64},{1,33},{33,1},{65,97},{97,65},{2,34}... | collective-permute-start | bytes 245768 | tf_op jit(solution)/shard_map/ppermute | solution.py:38
  73.8 12.3 %collective-permute-start.20 = (bf16[2,32,1280]{2,1,0:T(8,128)(2,1)}, bf16[2,32,1280]{2,1,0:T(8,128)(2,1)S(1)}, u32[]{:S(2)}, u32[]{:S(2)}) collective-permute-start(bf16[2,32,1280]{2,1,0:T(8,128)(2,1)} %get-tuple-element.81), channel_id=1, source_target_pairs={{0,2},{2,4},{4,6},{6,0},{1,3},{3,5},{5,7},{7,1},{8,10},{10,12},{12... | collective-permute-start | bytes 491528 | tf_op jit(solution)/shard_map/ppermute | solution.py:30
  74.1 12.2 %collective-permute-start.21 = (bf16[2,32,1280]{2,1,0:T(8,128)(2,1)}, bf16[2,32,1280]{2,1,0:T(8,128)(2,1)S(1)}, u32[]{:S(2)}, u32[]{:S(2)}) collective-permute-start(bf16[2,32,1280]{2,1,0:T(8,128)(2,1)} %get-tuple-element.82), channel_id=1, source_target_pairs={{0,4},{2,6},{4,0},{6,2},{1,5},{3,7},{5,1},{7,3},{8,12},{10,14},{12... | collective-permute-start | bytes 491528 | tf_op jit(solution)/shard_map/ppermute | solution.py:30
  78.0 8.3 %collective-permute-start.22 = (bf16[2,32,1280]{2,1,0:T(8,128)(2,1)}, bf16[2,32,1280]{2,1,0:T(8,128)(2,1)S(1)}, u32[]{:S(2)}, u32[]{:S(2)}) collective-permute-start(bf16[2,32,1280]{2,1,0:T(8,128)(2,1)} %get-tuple-element.83), channel_id=1, source_target_pairs={{0,6},{2,0},{4,2},{6,4},{1,7},{3,1},{5,3},{7,5},{8,14},{10,8},{12,... | collective-permute-start | bytes 491528 | tf_op jit(solution)/shard_map/ppermute | solution.py:30
  79.6 5.7 %collective-permute-start.24 = (bf16[32,1280]{1,0:T(8,128)(2,1)S(1)}, bf16[32,1280]{1,0:T(8,128)(2,1)S(1)}, u32[]{:S(2)}, u32[]{:S(2)}) collective-permute-start(bf16[32,1280]{1,0:T(8,128)(2,1)S(1)} %add_convert_fusion.6), channel_id=1, source_target_pairs={{0,96},{96,0},{32,64},{64,32},{1,97},{97,1},{33,65},{65,33},{2,98}... | collective-permute-start | bytes 245768 | tf_op jit(solution)/shard_map/ppermute | solution.py:42
  (10 other events, 109.1 us)

commit v13 on v12

--- a/solution.py
+++ b/solution.py
@@ -346,7 +346,7 @@
     out_other = far(out_part)
     part = merge_pair(part, part_other)
     out_part = add(after(out_part, part), out_other)
-    grad_slot_out = add(out_part, near(out_part))
+    out_other = near(out_part)
     slot_in, lse = merge_last(part, far(part))
     inputs = list(input_blocks(after(comb_late, out_part), embed))
 
@@ -354,7 +354,7 @@
     act, slope = gelu_parts(pre_act)
     act = act.astype(BF16)
     out_sum = jnp.dot(act, w_out, preferred_element_type=F32).astype(BF16)
-    grad_slot_out = after(grad_slot_out, out_sum)
+    grad_slot_out = add(after(out_part, out_sum), out_other)
     inputs[3] = after(inputs[3], out_sum)
     inputs = sources(scatter_terms(inputs, "y"))
     out_sum = add(out_sum, near(out_sum))

time: 87.9 us -> 85.9 us (0.977)
  waiting for transfers between devices: 21.1 us -> 16.4 us
  starting transfers between devices: 38.2 us -> 40.9 us
    ppermute x7, waiting for transfers between devices: 12.9 us -> 7.86 us  [far(): return lax.ppermute(value, axis, [(0, 3), (3, 0), (1, 2), (2, 1)])]
    ppermute x7, starting transfers between devices: 13.8 us -> 16.2 us  [far(): return lax.ppermute(value, axis, [(0, 3), (3, 0), (1, 2), (2, 1)])]
  transfers between devices with their start and end apart: 25 -> 25, of which waited for: 13 -> 11; matrix products, arithmetic and copies ran while one was open for 15% -> 15% of each run, Pallas kernels for 6% -> 6%
where the time goes in v13:
time: 85.9 us; the launch traced here: 85.1 us
  starting transfers between devices  40.9 us (48%)
  waiting for transfers between devices  16.4 us (19%)
  Pallas kernels  13.1 us (15%)
  matrix products  11.1 us (13%)
  other arithmetic  2.61 us (3%)
  between operations  0.97 us (1%)
    ppermute x7, starting transfers between devices, far(): return lax.ppermute(value, axis, [(0, 3), (3, 0), (1, 2), (2, 1)])  16.2 us
    ppermute x9, starting transfers between devices, shift(): return lax.ppermute(value, axis, [(i, (i + by) % 4) for i in range(4)])  15.6 us
    ppermute x7, starting transfers between devices, near(): return lax.ppermute(value, axis, [(0, 1), (1, 0), (2, 3), (3, 2)])  8.89 us
    ppermute x7, waiting for transfers between devices, far(): return lax.ppermute(value, axis, [(0, 3), (3, 0), (1, 2), (2, 1)])  7.86 us
    ppermute x7, waiting for transfers between devices, near(): return lax.ppermute(value, axis, [(0, 1), (1, 0), (2, 3), (3, 2)])  7.09 us
    pallas_call x1, Pallas kernels, local_softmax(): pl.pallas_call(softmax_kernel, grid=(1,), in_specs=[pl.BlockSpec((1, 256,...  5.11 us
    dot_general x1, matrix products, local(): jnp.einsum('sd,sh->dh', slot_late, grad_pre, preferred_element_type=F32)  3.67 us
    pallas_call x1, Pallas kernels, embed_grad(): pl.pallas_call(embed_grad_kernel, in_specs=[pl.BlockSpec(memory_space=pl....  2.78 us
  transfers between devices with their start and end apart: 25, of which 11 were waited for; matrix products, arithmetic and copies ran while one was open for 15% of the time, Pallas kernels for 6%

profile of v13, /device:TPU:0, one launch (start us, length us, event | category | flops | bytes accessed | tf_op | source)
XLA Modules:
  0.0 85.1 jit_solution(9282050468811800123)
XLA Ops:
  0.7 5.1 %local_softmax.1 = (f32[64,1024]{1,0:T(8,128)S(1)}, bf16[64,1408]{1,0:T(8,128)(2,1)S(1)}) custom-call(bf16[2,1024,1280]{2,1,0:T(8,128)(2,1)} %tok.3, bf16[2,1024,1280]{2,1,0:T(8,128)(2,1)} %tok.3, bf16[2,1024,1280]{2,1,0:T(8,128)(2,1)} %tok.3, bf16[2,1024,1280]{2,1,0:T(8,128)(2,1)} %tok.3, bf16[2,1024,1280]{2,1,0:T(8,128)(2,1)} %tok.3, ...), custom_call_target="tpu_custom_call" | custom-call | flops 700000000 | bytes 6000000 | tf_op jit(solution)/shard_map/local_softmax/pallas_call | solution.py:125
  5.8 2.1 %collective-permute-start = (bf16[64,1408]{1,0:T(8,128)(2,1)S(1)}, bf16[64,1408]{1,0:T(8,128)(2,1)S(1)}, u32[]{:S(2)}, u32[]{:S(2)}) collective-permute-start(bf16[64,1408]{1,0:T(8,128)(2,1)S(1)} %get-tuple-element.48.a), channel_id=1, source_target_pairs={{0,32},{32,0},{64,96},{96,64},{1,33},{33,1},{65,97},{97,65},{2,34}... | collective-permute-start | bytes 540680 | tf_op jit(solution)/shard_map/ppermute | solution.py:38
  8.9 2.6 %collective-permute-start.1 = (bf16[64,1280]{1,0:T(8,128)(2,1)S(1)}, bf16[64,1280]{1,0:T(8,128)(2,1)S(1)}, u32[]{:S(2)}, u32[]{:S(2)}) collective-permute-start(bf16[64,1280]{1,0:T(8,128)(2,1)S(1)} %bitcast.51), channel_id=1, source_target_pairs={{0,96},{96,0},{32,64},{64,32},{1,97},{97,1},{33,65},{65,33},{2,98}... | collective-permute-start | bytes 491528 | tf_op jit(solution)/shard_map/ppermute | solution.py:42
  12.7 3.9 %collective-permute-start.2 = (bf16[64,1408]{1,0:T(8,128)(2,1)S(1)}, bf16[64,1408]{1,0:T(8,128)(2,1)S(1)}, u32[]{:S(2)}, u32[]{:S(2)}) collective-permute-start(bf16[64,1408]{1,0:T(8,128)(2,1)S(1)} %merge_pair.1.one), channel_id=1, source_target_pairs={{0,96},{96,0},{32,64},{64,32},{1,97},{97,1},{33,65},{65,33},{2,98}... | collective-permute-start | bytes 540680 | tf_op jit(solution)/shard_map/ppermute | solution.py:42
  16.8 3.3 %collective-permute-start.6 = (bf16[224,256]{1,0:T(8,128)(2,1)S(1)}, bf16[224,256]{1,0:T(8,128)(2,1)S(1)}, u32[]{:S(2)}, u32[]{:S(2)}) collective-permute-start(bf16[224,256]{1,0:T(8,128)(2,1)S(1)} %get-tuple-element.56), channel_id=1, source_target_pairs={{0,16},{8,24},{16,0},{24,8},{1,17},{9,25},{17,1},{25,9},{2,18},{10... | collective-permute-start | bytes 344072 | tf_op jit(solution)/shard_map/ppermute | solution.py:30
  22.4 2.1 %collective-permute-start.4 = (bf16[64,1280]{1,0:T(8,128)(2,1)S(1)}, bf16[64,1280]{1,0:T(8,128)(2,1)S(1)}, u32[]{:S(2)}, u32[]{:S(2)}) collective-permute-start(bf16[64,1280]{1,0:T(8,128)(2,1)S(1)} %fusion.18), channel_id=1, source_target_pairs={{0,32},{32,0},{64,96},{96,64},{1,33},{33,1},{65,97},{97,65},{2,34}... | collective-permute-start | bytes 491528 | tf_op jit(solution)/shard_map/ppermute | solution.py:38
  24.5 2.6 %collective-permute-start.5 = (bf16[224,256]{1,0:T(8,128)(2,1)S(1)}, bf16[224,256]{1,0:T(8,128)(2,1)S(1)}, u32[]{:S(2)}, u32[]{:S(2)}) collective-permute-start(bf16[224,256]{1,0:T(8,128)(2,1)S(1)} %get-tuple-element.55), channel_id=1, source_target_pairs={{0,24},{8,0},{16,8},{24,16},{1,25},{9,1},{17,9},{25,17},{2,26},{10... | collective-permute-start | bytes 344072 | tf_op jit(solution)/shard_map/ppermute | solution.py:30
  29.5 1.8 %collective-permute-start.9 = (bf16[64,1280]{1,0:T(8,128)(2,1)S(1)}, bf16[64,1280]{1,0:T(8,128)(2,1)S(1)}, u32[]{:S(2)}, u32[]{:S(2)}) collective-permute-start(bf16[64,1280]{1,0:T(8,128)(2,1)S(1)} %add_convert_fusion.3.sum_a), channel_id=1, source_target_pairs={{0,96},{96,0},{32,64},{64,32},{1,97},{97,1},{33,65},{65,33},{2,98}... | collective-permute-start | bytes 491528 | tf_op jit(solution)/shard_map/ppermute | solution.py:42
  32.0 2.8 %convolution_convert_fusion.1 = bf16[1280,1280]{1,0:T(8,128)(2,1)} fusion(bf16[64,1280]{1,0:T(8,128)(2,1)S(1)} %get-tuple-element.60, bf16[64,1280]{1,0:T(8,128)(2,1)S(1)} %add_convert_fusion.4), kind=kOutput, calls=%fused_computation.1 | convolution fusion | flops 211353600 | bytes 3604480 | tf_op jit(solution)/shard_map/sh,sd->hd/dot_general | solution.py:370
  34.8 1.9 %collective-permute-done.8 = bf16[64,1280]{1,0:T(8,128)(2,1)S(1)} collective-permute-done((bf16[64,1280]{1,0:T(8,128)(2,1)S(1)}, bf16[64,1280]{1,0:T(8,128)(2,1)S(1)}, u32[]{:S(2)}, u32[]{:S(2)}) %collective-permute-start.8) | collective-permute-done | bytes 163872 | tf_op jit(solution)/shard_map/ppermute | solution.py:38
  41.1 2.2 %collective-permute-done.10 = bf16[64,1280]{1,0:T(8,128)(2,1)S(1)} collective-permute-done((bf16[64,1280]{1,0:T(8,128)(2,1)S(1)}, bf16[64,1280]{1,0:T(8,128)(2,1)S(1)}, u32[]{:S(2)}, u32[]{:S(2)}) %collective-permute-start.10) | collective-permute-done | bytes 163872 | tf_op jit(solution)/shard_map/ppermute | solution.py:42
  43.4 1.6 %dispatch_grad.1 = (f32[64,1024]{1,0:T(8,128)S(1)}, bf16[64,1792]{1,0:T(8,128)(2,1)S(1)}, bf16[64,1792]{1,0:T(8,128)(2,1)S(1)}, bf16[64,1792]{1,0:T(8,128)(2,1)S(1)}, bf16[64,1792]{1,0:T(8,128)(2,1)S(1)}) custom-call(bf16[2,1024,1280]{2,1,0:T(8,128)(2,1)S(1)} %bitcast.42, bf16[64,1280]{1,0:T(8,128)(2,1)S(1)} %add_convert_fusion.1.gslot, ...), custom_call_target="tpu_custom_call" | custom-call | flops 350000000 | bytes 7000000 | tf_op jit(solution)/shard_map/dispatch_grad/pallas_call | solution.py:216
  45.0 3.5 %collective-permute-start.12 = (bf16[64,1792]{1,0:T(8,128)(2,1)S(1)}, bf16[64,1792]{1,0:T(8,128)(2,1)S(1)}, u32[]{:S(2)}, u32[]{:S(2)}) collective-permute-start(bf16[64,1792]{1,0:T(8,128)(2,1)S(1)} %get-tuple-element.71), channel_id=1, source_target_pairs={{0,24},{8,0},{16,8},{24,16},{1,25},{9,1},{17,9},{25,17},{2,26},{10... | collective-permute-start | bytes 688136 | tf_op jit(solution)/shard_map/ppermute | solution.py:30
  51.2 2.2 %collective-permute-done.15 = f32[2,1,1024]{2,1,0:T(1,128)S(1)} collective-permute-done((f32[2,1,1024]{2,1,0:T(1,128)S(1)}, f32[2,1,1024]{2,1,0:T(1,128)S(1)}, u32[]{:S(2)}, u32[]{:S(2)}) %collective-permute-start.15) | collective-permute-done | bytes 8224 | tf_op jit(solution)/shard_map/ppermute | solution.py:38
  53.3 2.8 %collective-permute-start.16 = (f32[2,1,1024]{2,1,0:T(1,128)S(1)}, f32[2,1,1024]{2,1,0:T(1,128)S(1)}, u32[]{:S(2)}, u32[]{:S(2)}) collective-permute-start(f32[2,1,1024]{2,1,0:T(1,128)S(1)} %add.66), channel_id=1, source_target_pairs={{0,6},{6,0},{2,4},{4,2},{1,7},{7,1},{3,5},{5,3},{8,14},{14,8},{10,... | collective-permute-start | bytes 24584 | tf_op jit(solution)/shard_map/ppermute | solution.py:42
  56.2 2.1 %collective-permute-done.16 = f32[2,1,1024]{2,1,0:T(1,128)S(1)} collective-permute-done((f32[2,1,1024]{2,1,0:T(1,128)S(1)}, f32[2,1,1024]{2,1,0:T(1,128)S(1)}, u32[]{:S(2)}, u32[]{:S(2)}) %collective-permute-start.16) | collective-permute-done | bytes 8224 | tf_op jit(solution)/shard_map/ppermute | solution.py:42
  58.3 2.4 %collective-permute-start.17 = (f32[2,1,1024]{2,1,0:T(1,128)S(1)}, f32[2,1,1024]{2,1,0:T(1,128)S(1)}, u32[]{:S(2)}, u32[]{:S(2)}) collective-permute-start(f32[2,1,1024]{2,1,0:T(1,128)S(1)} %add.67), channel_id=1, source_target_pairs={{0,8},{8,0},{16,24},{24,16},{1,9},{9,1},{17,25},{25,17},{2,10},{10... | collective-permute-start | bytes 24584 | tf_op jit(solution)/shard_map/ppermute | solution.py:38
  60.7 1.6 %collective-permute-done.17 = f32[2,1,1024]{2,1,0:T(1,128)S(1)} collective-permute-done((f32[2,1,1024]{2,1,0:T(1,128)S(1)}, f32[2,1,1024]{2,1,0:T(1,128)S(1)}, u32[]{:S(2)}, u32[]{:S(2)}) %collective-permute-start.17) | collective-permute-done | bytes 8224 | tf_op jit(solution)/shard_map/ppermute | solution.py:38
  62.4 1.9 %collective-permute-start.18 = (f32[2,1,1024]{2,1,0:T(1,128)S(1)}, f32[2,1,1024]{2,1,0:T(1,128)S(1)}, u32[]{:S(2)}, u32[]{:S(2)}) collective-permute-start(f32[2,1,1024]{2,1,0:T(1,128)S(1)} %add.68), channel_id=1, source_target_pairs={{0,24},{24,0},{8,16},{16,8},{1,25},{25,1},{9,17},{17,9},{2,26},{26... | collective-permute-start | bytes 24584 | tf_op jit(solution)/shard_map/ppermute | solution.py:42
  64.2 3.1 %collective-permute-done.18 = f32[2,1,1024]{2,1,0:T(1,128)S(1)} collective-permute-done((f32[2,1,1024]{2,1,0:T(1,128)S(1)}, f32[2,1,1024]{2,1,0:T(1,128)S(1)}, u32[]{:S(2)}, u32[]{:S(2)}) %collective-permute-start.18) | collective-permute-done | bytes 8224 | tf_op jit(solution)/shard_map/ppermute | solution.py:42
  68.1 2.8 %embed_grad.1 = bf16[32,1280]{1,0:T(8,128)(2,1)S(1)} custom-call(bf16[2,1024,1280]{2,1,0:T(8,128)(2,1)} %tok.3, f32[64,1024]{1,0:T(8,128)S(1)} %get-tuple-element.77.partial_logits, bf16[64,1024]{1,0:T(8,128)(2,1)S(1)} %bitcast.47, f32[2,1,1024]{2,1,0:T(1,128)S(1)} %add.69.refs_8_.row_dot), custom_call_target="tpu_custom_call" | custom-call | flops 170000000 | bytes 6000000 | tf_op jit(solution)/shard_map/embed_grad/pallas_call | solution.py:260
  72.1 3.9 %collective-permute-start.21 = (bf16[2,32,1280]{2,1,0:T(8,128)(2,1)}, bf16[2,32,1280]{2,1,0:T(8,128)(2,1)S(1)}, u32[]{:S(2)}, u32[]{:S(2)}) collective-permute-start(bf16[2,32,1280]{2,1,0:T(8,128)(2,1)} %get-tuple-element.82), channel_id=1, source_target_pairs={{0,4},{2,6},{4,0},{6,2},{1,5},{3,7},{5,1},{7,3},{8,12},{10,14},{12... | collective-permute-start | bytes 491528 | tf_op jit(solution)/shard_map/ppermute | solution.py:30
  77.7 1.6 %collective-permute-start.24 = (bf16[32,1280]{1,0:T(8,128)(2,1)S(1)}, bf16[32,1280]{1,0:T(8,128)(2,1)S(1)}, u32[]{:S(2)}, u32[]{:S(2)}) collective-permute-start(bf16[32,1280]{1,0:T(8,128)(2,1)S(1)} %add_convert_fusion.6), channel_id=1, source_target_pairs={{0,96},{96,0},{32,64},{64,32},{1,97},{97,1},{33,65},{65,33},{2,98}... | collective-permute-start | bytes 245768 | tf_op jit(solution)/shard_map/ppermute | solution.py:42
  79.3 3.7 %fusion = bf16[1,1280,1280]{2,1,0:T(8,128)(2,1)} fusion(bf16[64,1280]{1,0:T(8,128)(2,1)S(1)} %get-tuple-element.85.slot_in, bf16[64,1280]{1,0:T(8,128)(2,1)} %copy-done.5), kind=kOutput, calls=%fused_computation.2 | convolution fusion | flops 211353600 | bytes 3604480 | tf_op jit(solution)/shard_map/sd,sh->dh/dot_general | solution.py:404
  (74 shorter events, 20.6 us)
Async XLA Ops:
  5.8 6.6 %collective-permute-start = (bf16[64,1408]{1,0:T(8,128)(2,1)S(1)}, bf16[64,1408]{1,0:T(8,128)(2,1)S(1)}, u32[]{:S(2)}, u32[]{:S(2)}) collective-permute-start(bf16[64,1408]{1,0:T(8,128)(2,1)S(1)} %get-tuple-element.48.a), channel_id=1, source_target_pairs={{0,32},{32,0},{64,96},{96,64},{1,33},{33,1},{65,97},{97,65},{2,34}... | collective-permute-start | bytes 540680 | tf_op jit(solution)/shard_map/ppermute | solution.py:38
  8.9 7.7 %collective-permute-start.1 = (bf16[64,1280]{1,0:T(8,128)(2,1)S(1)}, bf16[64,1280]{1,0:T(8,128)(2,1)S(1)}, u32[]{:S(2)}, u32[]{:S(2)}) collective-permute-start(bf16[64,1280]{1,0:T(8,128)(2,1)S(1)} %bitcast.51), channel_id=1, source_target_pairs={{0,96},{96,0},{32,64},{64,32},{1,97},{97,1},{33,65},{65,33},{2,98}... | collective-permute-start | bytes 491528 | tf_op jit(solution)/shard_map/ppermute | solution.py:42
  12.7 8.1 %collective-permute-start.2 = (bf16[64,1408]{1,0:T(8,128)(2,1)S(1)}, bf16[64,1408]{1,0:T(8,128)(2,1)S(1)}, u32[]{:S(2)}, u32[]{:S(2)}) collective-permute-start(bf16[64,1408]{1,0:T(8,128)(2,1)S(1)} %merge_pair.1.one), channel_id=1, source_target_pairs={{0,96},{96,0},{32,64},{64,32},{1,97},{97,1},{33,65},{65,33},{2,98}... | collective-permute-start | bytes 540680 | tf_op jit(solution)/shard_map/ppermute | solution.py:42
  16.6 10.4 %collective-permute-start.3 = (bf16[64,1280]{1,0:T(8,128)(2,1)S(1)}, bf16[64,1280]{1,0:T(8,128)(2,1)S(1)}, u32[]{:S(2)}, u32[]{:S(2)}) collective-permute-start(bf16[64,1280]{1,0:T(8,128)(2,1)S(1)} %add_convert_fusion.5), channel_id=1, source_target_pairs={{0,32},{32,0},{64,96},{96,64},{1,33},{33,1},{65,97},{97,65},{2,34}... | collective-permute-start | bytes 491528 | tf_op jit(solution)/shard_map/ppermute | solution.py:38
  16.8 12.7 %collective-permute-start.6 = (bf16[224,256]{1,0:T(8,128)(2,1)S(1)}, bf16[224,256]{1,0:T(8,128)(2,1)S(1)}, u32[]{:S(2)}, u32[]{:S(2)}) collective-permute-start(bf16[224,256]{1,0:T(8,128)(2,1)S(1)} %get-tuple-element.56), channel_id=1, source_target_pairs={{0,16},{8,24},{16,0},{24,8},{1,17},{9,25},{17,1},{25,9},{2,18},{10... | collective-permute-start | bytes 344072 | tf_op jit(solution)/shard_map/ppermute | solution.py:30
  20.1 9.4 %collective-permute-start.7 = (bf16[224,256]{1,0:T(8,128)(2,1)S(1)}, bf16[224,256]{1,0:T(8,128)(2,1)S(1)}, u32[]{:S(2)}, u32[]{:S(2)}) collective-permute-start(bf16[224,256]{1,0:T(8,128)(2,1)S(1)} %get-tuple-element.57), channel_id=1, source_target_pairs={{0,8},{8,16},{16,24},{24,0},{1,9},{9,17},{17,25},{25,1},{2,10},{10... | collective-permute-start | bytes 344072 | tf_op jit(solution)/shard_map/ppermute | solution.py:30
  22.4 7.0 %collective-permute-start.4 = (bf16[64,1280]{1,0:T(8,128)(2,1)S(1)}, bf16[64,1280]{1,0:T(8,128)(2,1)S(1)}, u32[]{:S(2)}, u32[]{:S(2)}) collective-permute-start(bf16[64,1280]{1,0:T(8,128)(2,1)S(1)} %fusion.18), channel_id=1, source_target_pairs={{0,32},{32,0},{64,96},{96,64},{1,33},{33,1},{65,97},{97,65},{2,34}... | collective-permute-start | bytes 491528 | tf_op jit(solution)/shard_map/ppermute | solution.py:38
  24.5 5.0 %collective-permute-start.5 = (bf16[224,256]{1,0:T(8,128)(2,1)S(1)}, bf16[224,256]{1,0:T(8,128)(2,1)S(1)}, u32[]{:S(2)}, u32[]{:S(2)}) collective-permute-start(bf16[224,256]{1,0:T(8,128)(2,1)S(1)} %get-tuple-element.55), channel_id=1, source_target_pairs={{0,24},{8,0},{16,8},{24,16},{1,25},{9,1},{17,9},{25,17},{2,26},{10... | collective-permute-start | bytes 344072 | tf_op jit(solution)/shard_map/ppermute | solution.py:30
  29.5 8.8 %collective-permute-start.9 = (bf16[64,1280]{1,0:T(8,128)(2,1)S(1)}, bf16[64,1280]{1,0:T(8,128)(2,1)S(1)}, u32[]{:S(2)}, u32[]{:S(2)}) collective-permute-start(bf16[64,1280]{1,0:T(8,128)(2,1)S(1)} %add_convert_fusion.3.sum_a), channel_id=1, source_target_pairs={{0,96},{96,0},{32,64},{64,32},{1,97},{97,1},{33,65},{65,33},{2,98}... | collective-permute-start | bytes 491528 | tf_op jit(solution)/shard_map/ppermute | solution.py:42
  31.3 5.3 %collective-permute-start.8 = (bf16[64,1280]{1,0:T(8,128)(2,1)S(1)}, bf16[64,1280]{1,0:T(8,128)(2,1)S(1)}, u32[]{:S(2)}, u32[]{:S(2)}) collective-permute-start(bf16[64,1280]{1,0:T(8,128)(2,1)S(1)} %fusion.15), channel_id=1, source_target_pairs={{0,32},{32,0},{64,96},{96,64},{1,33},{33,1},{65,97},{97,65},{2,34}... | collective-permute-start | bytes 491528 | tf_op jit(solution)/shard_map/ppermute | solution.py:38
  36.7 6.6 %collective-permute-start.10 = (bf16[64,1280]{1,0:T(8,128)(2,1)S(1)}, bf16[64,1280]{1,0:T(8,128)(2,1)S(1)}, u32[]{:S(2)}, u32[]{:S(2)}) collective-permute-start(bf16[64,1280]{1,0:T(8,128)(2,1)S(1)} %add_convert_fusion.2), channel_id=1, source_target_pairs={{0,96},{96,0},{32,64},{64,32},{1,97},{97,1},{33,65},{65,33},{2,98}... | collective-permute-start | bytes 491528 | tf_op jit(solution)/shard_map/ppermute | solution.py:42
  45.0 22.3 %collective-permute-start.12 = (bf16[64,1792]{1,0:T(8,128)(2,1)S(1)}, bf16[64,1792]{1,0:T(8,128)(2,1)S(1)}, u32[]{:S(2)}, u32[]{:S(2)}) collective-permute-start(bf16[64,1792]{1,0:T(8,128)(2,1)S(1)} %get-tuple-element.71), channel_id=1, source_target_pairs={{0,24},{8,0},{16,8},{24,16},{1,25},{9,1},{17,9},{25,17},{2,26},{10... | collective-permute-start | bytes 688136 | tf_op jit(solution)/shard_map/ppermute | solution.py:30
  48.5 18.8 %collective-permute-start.13 = (bf16[64,1792]{1,0:T(8,128)(2,1)S(1)}, bf16[64,1792]{1,0:T(8,128)(2,1)S(1)}, u32[]{:S(2)}, u32[]{:S(2)}) collective-permute-start(bf16[64,1792]{1,0:T(8,128)(2,1)S(1)} %get-tuple-element.72), channel_id=1, source_target_pairs={{0,16},{8,24},{16,0},{24,8},{1,17},{9,25},{17,1},{25,9},{2,18},{10... | collective-permute-start | bytes 688136 | tf_op jit(solution)/shard_map/ppermute | solution.py:30
  48.6 18.8 %collective-permute-start.14 = (bf16[64,1792]{1,0:T(8,128)(2,1)S(1)}, bf16[64,1792]{1,0:T(8,128)(2,1)S(1)}, u32[]{:S(2)}, u32[]{:S(2)}) collective-permute-start(bf16[64,1792]{1,0:T(8,128)(2,1)S(1)} %get-tuple-element.73), channel_id=1, source_target_pairs={{0,8},{8,16},{16,24},{24,0},{1,9},{9,17},{17,25},{25,1},{2,10},{10... | collective-permute-start | bytes 688136 | tf_op jit(solution)/shard_map/ppermute | solution.py:30
  49.7 3.7 %collective-permute-start.15 = (f32[2,1,1024]{2,1,0:T(1,128)S(1)}, f32[2,1,1024]{2,1,0:T(1,128)S(1)}, u32[]{:S(2)}, u32[]{:S(2)}) collective-permute-start(f32[2,1,1024]{2,1,0:T(1,128)S(1)} %add.65), channel_id=1, source_target_pairs={{0,2},{2,0},{4,6},{6,4},{1,3},{3,1},{5,7},{7,5},{8,10},{10,8},{12,... | collective-permute-start | bytes 24584 | tf_op jit(solution)/shard_map/ppermute | solution.py:38
  53.3 4.9 %collective-permute-start.16 = (f32[2,1,1024]{2,1,0:T(1,128)S(1)}, f32[2,1,1024]{2,1,0:T(1,128)S(1)}, u32[]{:S(2)}, u32[]{:S(2)}) collective-permute-start(f32[2,1,1024]{2,1,0:T(1,128)S(1)} %add.66), channel_id=1, source_target_pairs={{0,6},{6,0},{2,4},{4,2},{1,7},{7,1},{3,5},{5,3},{8,14},{14,8},{10,... | collective-permute-start | bytes 24584 | tf_op jit(solution)/shard_map/ppermute | solution.py:42
  58.3 4.1 %collective-permute-start.17 = (f32[2,1,1024]{2,1,0:T(1,128)S(1)}, f32[2,1,1024]{2,1,0:T(1,128)S(1)}, u32[]{:S(2)}, u32[]{:S(2)}) collective-permute-start(f32[2,1,1024]{2,1,0:T(1,128)S(1)} %add.67), channel_id=1, source_target_pairs={{0,8},{8,0},{16,24},{24,16},{1,9},{9,1},{17,25},{25,17},{2,10},{10... | collective-permute-start | bytes 24584 | tf_op jit(solution)/shard_map/ppermute | solution.py:38
  62.4 4.9 %collective-permute-start.18 = (f32[2,1,1024]{2,1,0:T(1,128)S(1)}, f32[2,1,1024]{2,1,0:T(1,128)S(1)}, u32[]{:S(2)}, u32[]{:S(2)}) collective-permute-start(f32[2,1,1024]{2,1,0:T(1,128)S(1)} %add.68), channel_id=1, source_target_pairs={{0,24},{24,0},{8,16},{16,8},{1,25},{25,1},{9,17},{17,9},{2,26},{26... | collective-permute-start | bytes 24584 | tf_op jit(solution)/shard_map/ppermute | solution.py:42
  68.0 2.9 %collective-permute-start.19 = (bf16[4,2,32,1280]{3,2,1,0:T(8,128)(2,1)S(1)}, bf16[4,2,32,1280]{3,2,1,0:T(8,128)(2,1)S(1)}, u32[]{:S(2)}, u32[]{:S(2)}) collective-permute-start(bf16[4,2,32,1280]{3,2,1,0:T(8,128)(2,1)S(1)} %get-tuple-element.79), channel_id=1, source_target_pairs={{0,1},{1,0},{2,3},{3,2},{4,5},{5,4},{6,7},{7,6},{8,9},{9,8},{10,11... | collective-permute-start | bytes 1966088 | tf_op jit(solution)/shard_map/ppermute | solution.py:34
  71.8 4.9 %collective-permute-start.23 = (bf16[32,1280]{1,0:T(8,128)(2,1)S(1)}, bf16[32,1280]{1,0:T(8,128)(2,1)}, u32[]{:S(2)}, u32[]{:S(2)}) collective-permute-start(bf16[32,1280]{1,0:T(8,128)(2,1)S(1)} %embed_grad.1), channel_id=1, source_target_pairs={{0,32},{32,0},{64,96},{96,64},{1,33},{33,1},{65,97},{97,65},{2,34}... | collective-permute-start | bytes 245768 | tf_op jit(solution)/shard_map/ppermute | solution.py:38
  71.8 12.3 %collective-permute-start.20 = (bf16[2,32,1280]{2,1,0:T(8,128)(2,1)}, bf16[2,32,1280]{2,1,0:T(8,128)(2,1)S(1)}, u32[]{:S(2)}, u32[]{:S(2)}) collective-permute-start(bf16[2,32,1280]{2,1,0:T(8,128)(2,1)} %get-tuple-element.81), channel_id=1, source_target_pairs={{0,2},{2,4},{4,6},{6,0},{1,3},{3,5},{5,7},{7,1},{8,10},{10,12},{12... | collective-permute-start | bytes 491528 | tf_op jit(solution)/shard_map/ppermute | solution.py:30
  72.1 12.2 %collective-permute-start.21 = (bf16[2,32,1280]{2,1,0:T(8,128)(2,1)}, bf16[2,32,1280]{2,1,0:T(8,128)(2,1)S(1)}, u32[]{:S(2)}, u32[]{:S(2)}) collective-permute-start(bf16[2,32,1280]{2,1,0:T(8,128)(2,1)} %get-tuple-element.82), channel_id=1, source_target_pairs={{0,4},{2,6},{4,0},{6,2},{1,5},{3,7},{5,1},{7,3},{8,12},{10,14},{12... | collective-permute-start | bytes 491528 | tf_op jit(solution)/shard_map/ppermute | solution.py:30
  76.1 8.3 %collective-permute-start.22 = (bf16[2,32,1280]{2,1,0:T(8,128)(2,1)}, bf16[2,32,1280]{2,1,0:T(8,128)(2,1)S(1)}, u32[]{:S(2)}, u32[]{:S(2)}) collective-permute-start(bf16[2,32,1280]{2,1,0:T(8,128)(2,1)} %get-tuple-element.83), channel_id=1, source_target_pairs={{0,6},{2,0},{4,2},{6,4},{1,7},{3,1},{5,3},{7,5},{8,14},{10,8},{12,... | collective-permute-start | bytes 491528 | tf_op jit(solution)/shard_map/ppermute | solution.py:30
  77.7 5.7 %collective-permute-start.24 = (bf16[32,1280]{1,0:T(8,128)(2,1)S(1)}, bf16[32,1280]{1,0:T(8,128)(2,1)S(1)}, u32[]{:S(2)}, u32[]{:S(2)}) collective-permute-start(bf16[32,1280]{1,0:T(8,128)(2,1)S(1)} %add_convert_fusion.6), channel_id=1, source_target_pairs={{0,96},{96,0},{32,64},{64,32},{1,97},{97,1},{33,65},{65,33},{2,98}... | collective-permute-start | bytes 245768 | tf_op jit(solution)/shard_map/ppermute | solution.py:42
  (10 other events, 100.4 us)

commit v14 on v13

--- a/solution.py
+++ b/solution.py
@@ -315,7 +315,7 @@
 def add_cores(mine, other):
     return pl.pallas_call(
         add_kernel,
-        out_shape=[pltpu.HBM((2, 32, 1280), BF16)] * 4,
+        out_shape=[pltpu.VMEM((2, 32, 1280), BF16)] + [pltpu.HBM((2, 32, 1280), BF16)] * 3,
         cost_estimate=pl.CostEstimate(flops=327_680, bytes_accessed=2_000_000, transcendentals=0),
         compiler_params=SMALL,
         name="add_cores",

time: 85.9 us -> 86.5 us (level)
  no operation moved by 1% of the time
where the time goes in v14:
time: 86.5 us; the launch traced here: 85.7 us
  starting transfers between devices  40.9 us (47%)
  waiting for transfers between devices  16.4 us (19%)
  Pallas kernels  13.1 us (15%)
  matrix products  11.1 us (13%)
  other arithmetic  2.61 us (3%)
  between operations  0.97 us (1%)
    ppermute x7, starting transfers between devices, far(): return lax.ppermute(value, axis, [(0, 3), (3, 0), (1, 2), (2, 1)])  16.2 us
    ppermute x9, starting transfers between devices, shift(): return lax.ppermute(value, axis, [(i, (i + by) % 4) for i in range(4)])  15.6 us
    ppermute x7, starting transfers between devices, near(): return lax.ppermute(value, axis, [(0, 1), (1, 0), (2, 3), (3, 2)])  8.89 us
    ppermute x7, waiting for transfers between devices, far(): return lax.ppermute(value, axis, [(0, 3), (3, 0), (1, 2), (2, 1)])  7.86 us
    ppermute x7, waiting for transfers between devices, near(): return lax.ppermute(value, axis, [(0, 1), (1, 0), (2, 3), (3, 2)])  7.11 us
    pallas_call x1, Pallas kernels, local_softmax(): pl.pallas_call(softmax_kernel, grid=(1,), in_specs=[pl.BlockSpec((1, 256,...  5.11 us
    dot_general x1, matrix products, local(): jnp.einsum('sd,sh->dh', slot_late, grad_pre, preferred_element_type=F32)  3.67 us
    pallas_call x1, Pallas kernels, embed_grad(): pl.pallas_call(embed_grad_kernel, in_specs=[pl.BlockSpec(memory_space=pl....  2.78 us
  transfers between devices with their start and end apart: 25, of which 11 were waited for; matrix products, arithmetic and copies ran while one was open for 15% of the time, Pallas kernels for 6%

profile of v14, /device:TPU:0, one launch (start us, length us, event | category | flops | bytes accessed | tf_op | source)
XLA Modules:
  0.0 85.7 jit_solution(8317647364463373249)
XLA Ops:
  0.7 5.1 %local_softmax.1 = (f32[64,1024]{1,0:T(8,128)S(1)}, bf16[64,1408]{1,0:T(8,128)(2,1)S(1)}) custom-call(bf16[2,1024,1280]{2,1,0:T(8,128)(2,1)} %tok.3, bf16[2,1024,1280]{2,1,0:T(8,128)(2,1)} %tok.3, bf16[2,1024,1280]{2,1,0:T(8,128)(2,1)} %tok.3, bf16[2,1024,1280]{2,1,0:T(8,128)(2,1)} %tok.3, bf16[2,1024,1280]{2,1,0:T(8,128)(2,1)} %tok.3, ...), custom_call_target="tpu_custom_call" | custom-call | flops 700000000 | bytes 6000000 | tf_op jit(solution)/shard_map/local_softmax/pallas_call | solution.py:125
  5.8 2.1 %collective-permute-start = (bf16[64,1408]{1,0:T(8,128)(2,1)S(1)}, bf16[64,1408]{1,0:T(8,128)(2,1)S(1)}, u32[]{:S(2)}, u32[]{:S(2)}) collective-permute-start(bf16[64,1408]{1,0:T(8,128)(2,1)S(1)} %get-tuple-element.48.a), channel_id=1, source_target_pairs={{0,32},{32,0},{64,96},{96,64},{1,33},{33,1},{65,97},{97,65},{2,34}... | collective-permute-start | bytes 540680 | tf_op jit(solution)/shard_map/ppermute | solution.py:38
  8.9 2.6 %collective-permute-start.1 = (bf16[64,1280]{1,0:T(8,128)(2,1)S(1)}, bf16[64,1280]{1,0:T(8,128)(2,1)S(1)}, u32[]{:S(2)}, u32[]{:S(2)}) collective-permute-start(bf16[64,1280]{1,0:T(8,128)(2,1)S(1)} %bitcast.51), channel_id=1, source_target_pairs={{0,96},{96,0},{32,64},{64,32},{1,97},{97,1},{33,65},{65,33},{2,98}... | collective-permute-start | bytes 491528 | tf_op jit(solution)/shard_map/ppermute | solution.py:42
  12.7 3.9 %collective-permute-start.2 = (bf16[64,1408]{1,0:T(8,128)(2,1)S(1)}, bf16[64,1408]{1,0:T(8,128)(2,1)S(1)}, u32[]{:S(2)}, u32[]{:S(2)}) collective-permute-start(bf16[64,1408]{1,0:T(8,128)(2,1)S(1)} %merge_pair.1.one), channel_id=1, source_target_pairs={{0,96},{96,0},{32,64},{64,32},{1,97},{97,1},{33,65},{65,33},{2,98}... | collective-permute-start | bytes 540680 | tf_op jit(solution)/shard_map/ppermute | solution.py:42
  16.8 3.3 %collective-permute-start.6 = (bf16[224,256]{1,0:T(8,128)(2,1)S(1)}, bf16[224,256]{1,0:T(8,128)(2,1)S(1)}, u32[]{:S(2)}, u32[]{:S(2)}) collective-permute-start(bf16[224,256]{1,0:T(8,128)(2,1)S(1)} %get-tuple-element.56), channel_id=1, source_target_pairs={{0,16},{8,24},{16,0},{24,8},{1,17},{9,25},{17,1},{25,9},{2,18},{10... | collective-permute-start | bytes 344072 | tf_op jit(solution)/shard_map/ppermute | solution.py:30
  22.4 2.1 %collective-permute-start.4 = (bf16[64,1280]{1,0:T(8,128)(2,1)S(1)}, bf16[64,1280]{1,0:T(8,128)(2,1)S(1)}, u32[]{:S(2)}, u32[]{:S(2)}) collective-permute-start(bf16[64,1280]{1,0:T(8,128)(2,1)S(1)} %fusion.18), channel_id=1, source_target_pairs={{0,32},{32,0},{64,96},{96,64},{1,33},{33,1},{65,97},{97,65},{2,34}... | collective-permute-start | bytes 491528 | tf_op jit(solution)/shard_map/ppermute | solution.py:38
  24.5 2.6 %collective-permute-start.5 = (bf16[224,256]{1,0:T(8,128)(2,1)S(1)}, bf16[224,256]{1,0:T(8,128)(2,1)S(1)}, u32[]{:S(2)}, u32[]{:S(2)}) collective-permute-start(bf16[224,256]{1,0:T(8,128)(2,1)S(1)} %get-tuple-element.55), channel_id=1, source_target_pairs={{0,24},{8,0},{16,8},{24,16},{1,25},{9,1},{17,9},{25,17},{2,26},{10... | collective-permute-start | bytes 344072 | tf_op jit(solution)/shard_map/ppermute | solution.py:30
  29.5 1.8 %collective-permute-start.9 = (bf16[64,1280]{1,0:T(8,128)(2,1)S(1)}, bf16[64,1280]{1,0:T(8,128)(2,1)S(1)}, u32[]{:S(2)}, u32[]{:S(2)}) collective-permute-start(bf16[64,1280]{1,0:T(8,128)(2,1)S(1)} %add_convert_fusion.3.sum_a), channel_id=1, source_target_pairs={{0,96},{96,0},{32,64},{64,32},{1,97},{97,1},{33,65},{65,33},{2,98}... | collective-permute-start | bytes 491528 | tf_op jit(solution)/shard_map/ppermute | solution.py:42
  32.0 2.8 %convolution_convert_fusion.1 = bf16[1280,1280]{1,0:T(8,128)(2,1)} fusion(bf16[64,1280]{1,0:T(8,128)(2,1)S(1)} %get-tuple-element.60, bf16[64,1280]{1,0:T(8,128)(2,1)S(1)} %add_convert_fusion.4), kind=kOutput, calls=%fused_computation.1 | convolution fusion | flops 211353600 | bytes 3604480 | tf_op jit(solution)/shard_map/sh,sd->hd/dot_general | solution.py:370
  34.8 1.9 %collective-permute-done.8 = bf16[64,1280]{1,0:T(8,128)(2,1)S(1)} collective-permute-done((bf16[64,1280]{1,0:T(8,128)(2,1)S(1)}, bf16[64,1280]{1,0:T(8,128)(2,1)S(1)}, u32[]{:S(2)}, u32[]{:S(2)}) %collective-permute-start.8) | collective-permute-done | bytes 163872 | tf_op jit(solution)/shard_map/ppermute | solution.py:38
  41.1 2.2 %collective-permute-done.10 = bf16[64,1280]{1,0:T(8,128)(2,1)S(1)} collective-permute-done((bf16[64,1280]{1,0:T(8,128)(2,1)S(1)}, bf16[64,1280]{1,0:T(8,128)(2,1)S(1)}, u32[]{:S(2)}, u32[]{:S(2)}) %collective-permute-start.10) | collective-permute-done | bytes 163872 | tf_op jit(solution)/shard_map/ppermute | solution.py:42
  43.4 1.6 %dispatch_grad.1 = (f32[64,1024]{1,0:T(8,128)S(1)}, bf16[64,1792]{1,0:T(8,128)(2,1)S(1)}, bf16[64,1792]{1,0:T(8,128)(2,1)S(1)}, bf16[64,1792]{1,0:T(8,128)(2,1)S(1)}, bf16[64,1792]{1,0:T(8,128)(2,1)S(1)}) custom-call(bf16[2,1024,1280]{2,1,0:T(8,128)(2,1)S(1)} %bitcast.42, bf16[64,1280]{1,0:T(8,128)(2,1)S(1)} %add_convert_fusion.1.gslot, ...), custom_call_target="tpu_custom_call" | custom-call | flops 350000000 | bytes 7000000 | tf_op jit(solution)/shard_map/dispatch_grad/pallas_call | solution.py:216
  45.0 3.5 %collective-permute-start.12 = (bf16[64,1792]{1,0:T(8,128)(2,1)S(1)}, bf16[64,1792]{1,0:T(8,128)(2,1)S(1)}, u32[]{:S(2)}, u32[]{:S(2)}) collective-permute-start(bf16[64,1792]{1,0:T(8,128)(2,1)S(1)} %get-tuple-element.71), channel_id=1, source_target_pairs={{0,24},{8,0},{16,8},{24,16},{1,25},{9,1},{17,9},{25,17},{2,26},{10... | collective-permute-start | bytes 688136 | tf_op jit(solution)/shard_map/ppermute | solution.py:30
  51.2 2.2 %collective-permute-done.15 = f32[2,1,1024]{2,1,0:T(1,128)S(1)} collective-permute-done((f32[2,1,1024]{2,1,0:T(1,128)S(1)}, f32[2,1,1024]{2,1,0:T(1,128)S(1)}, u32[]{:S(2)}, u32[]{:S(2)}) %collective-permute-start.15) | collective-permute-done | bytes 8224 | tf_op jit(solution)/shard_map/ppermute | solution.py:38
  53.3 2.8 %collective-permute-start.16 = (f32[2,1,1024]{2,1,0:T(1,128)S(1)}, f32[2,1,1024]{2,1,0:T(1,128)S(1)}, u32[]{:S(2)}, u32[]{:S(2)}) collective-permute-start(f32[2,1,1024]{2,1,0:T(1,128)S(1)} %add.66), channel_id=1, source_target_pairs={{0,6},{6,0},{2,4},{4,2},{1,7},{7,1},{3,5},{5,3},{8,14},{14,8},{10,... | collective-permute-start | bytes 24584 | tf_op jit(solution)/shard_map/ppermute | solution.py:42
  56.2 2.1 %collective-permute-done.16 = f32[2,1,1024]{2,1,0:T(1,128)S(1)} collective-permute-done((f32[2,1,1024]{2,1,0:T(1,128)S(1)}, f32[2,1,1024]{2,1,0:T(1,128)S(1)}, u32[]{:S(2)}, u32[]{:S(2)}) %collective-permute-start.16) | collective-permute-done | bytes 8224 | tf_op jit(solution)/shard_map/ppermute | solution.py:42
  58.3 2.4 %collective-permute-start.17 = (f32[2,1,1024]{2,1,0:T(1,128)S(1)}, f32[2,1,1024]{2,1,0:T(1,128)S(1)}, u32[]{:S(2)}, u32[]{:S(2)}) collective-permute-start(f32[2,1,1024]{2,1,0:T(1,128)S(1)} %add.67), channel_id=1, source_target_pairs={{0,8},{8,0},{16,24},{24,16},{1,9},{9,1},{17,25},{25,17},{2,10},{10... | collective-permute-start | bytes 24584 | tf_op jit(solution)/shard_map/ppermute | solution.py:38
  60.7 1.6 %collective-permute-done.17 = f32[2,1,1024]{2,1,0:T(1,128)S(1)} collective-permute-done((f32[2,1,1024]{2,1,0:T(1,128)S(1)}, f32[2,1,1024]{2,1,0:T(1,128)S(1)}, u32[]{:S(2)}, u32[]{:S(2)}) %collective-permute-start.17) | collective-permute-done | bytes 8224 | tf_op jit(solution)/shard_map/ppermute | solution.py:38
  62.4 1.9 %collective-permute-start.18 = (f32[2,1,1024]{2,1,0:T(1,128)S(1)}, f32[2,1,1024]{2,1,0:T(1,128)S(1)}, u32[]{:S(2)}, u32[]{:S(2)}) collective-permute-start(f32[2,1,1024]{2,1,0:T(1,128)S(1)} %add.68), channel_id=1, source_target_pairs={{0,24},{24,0},{8,16},{16,8},{1,25},{25,1},{9,17},{17,9},{2,26},{26... | collective-permute-start | bytes 24584 | tf_op jit(solution)/shard_map/ppermute | solution.py:42
  64.2 3.1 %collective-permute-done.18 = f32[2,1,1024]{2,1,0:T(1,128)S(1)} collective-permute-done((f32[2,1,1024]{2,1,0:T(1,128)S(1)}, f32[2,1,1024]{2,1,0:T(1,128)S(1)}, u32[]{:S(2)}, u32[]{:S(2)}) %collective-permute-start.18) | collective-permute-done | bytes 8224 | tf_op jit(solution)/shard_map/ppermute | solution.py:42
  68.1 2.8 %embed_grad.1 = bf16[32,1280]{1,0:T(8,128)(2,1)S(1)} custom-call(bf16[2,1024,1280]{2,1,0:T(8,128)(2,1)} %tok.3, f32[64,1024]{1,0:T(8,128)S(1)} %get-tuple-element.77.partial_logits, bf16[64,1024]{1,0:T(8,128)(2,1)S(1)} %bitcast.47, f32[2,1,1024]{2,1,0:T(1,128)S(1)} %add.69.refs_8_.row_dot), custom_call_target="tpu_custom_call" | custom-call | flops 170000000 | bytes 6000000 | tf_op jit(solution)/shard_map/embed_grad/pallas_call | solution.py:260
  72.7 3.9 %collective-permute-start.21 = (bf16[2,32,1280]{2,1,0:T(8,128)(2,1)}, bf16[2,32,1280]{2,1,0:T(8,128)(2,1)S(1)}, u32[]{:S(2)}, u32[]{:S(2)}) collective-permute-start(bf16[2,32,1280]{2,1,0:T(8,128)(2,1)} %get-tuple-element.82), channel_id=1, source_target_pairs={{0,4},{2,6},{4,0},{6,2},{1,5},{3,7},{5,1},{7,3},{8,12},{10,14},{12... | collective-permute-start | bytes 491528 | tf_op jit(solution)/shard_map/ppermute | solution.py:30
  78.3 1.6 %collective-permute-start.24 = (bf16[32,1280]{1,0:T(8,128)(2,1)S(1)}, bf16[32,1280]{1,0:T(8,128)(2,1)S(1)}, u32[]{:S(2)}, u32[]{:S(2)}) collective-permute-start(bf16[32,1280]{1,0:T(8,128)(2,1)S(1)} %add_convert_fusion.6), channel_id=1, source_target_pairs={{0,96},{96,0},{32,64},{64,32},{1,97},{97,1},{33,65},{65,33},{2,98}... | collective-permute-start | bytes 245768 | tf_op jit(solution)/shard_map/ppermute | solution.py:42
  79.8 3.7 %fusion = bf16[1,1280,1280]{2,1,0:T(8,128)(2,1)} fusion(bf16[64,1280]{1,0:T(8,128)(2,1)S(1)} %get-tuple-element.85.slot_in, bf16[64,1280]{1,0:T(8,128)(2,1)} %copy-done.7), kind=kOutput, calls=%fused_computation.2 | convolution fusion | flops 211353600 | bytes 3604480 | tf_op jit(solution)/shard_map/sd,sh->dh/dot_general | solution.py:404
  (76 shorter events, 21.2 us)
Async XLA Ops:
  5.8 6.6 %collective-permute-start = (bf16[64,1408]{1,0:T(8,128)(2,1)S(1)}, bf16[64,1408]{1,0:T(8,128)(2,1)S(1)}, u32[]{:S(2)}, u32[]{:S(2)}) collective-permute-start(bf16[64,1408]{1,0:T(8,128)(2,1)S(1)} %get-tuple-element.48.a), channel_id=1, source_target_pairs={{0,32},{32,0},{64,96},{96,64},{1,33},{33,1},{65,97},{97,65},{2,34}... | collective-permute-start | bytes 540680 | tf_op jit(solution)/shard_map/ppermute | solution.py:38
  8.9 7.7 %collective-permute-start.1 = (bf16[64,1280]{1,0:T(8,128)(2,1)S(1)}, bf16[64,1280]{1,0:T(8,128)(2,1)S(1)}, u32[]{:S(2)}, u32[]{:S(2)}) collective-permute-start(bf16[64,1280]{1,0:T(8,128)(2,1)S(1)} %bitcast.51), channel_id=1, source_target_pairs={{0,96},{96,0},{32,64},{64,32},{1,97},{97,1},{33,65},{65,33},{2,98}... | collective-permute-start | bytes 491528 | tf_op jit(solution)/shard_map/ppermute | solution.py:42
  12.7 8.1 %collective-permute-start.2 = (bf16[64,1408]{1,0:T(8,128)(2,1)S(1)}, bf16[64,1408]{1,0:T(8,128)(2,1)S(1)}, u32[]{:S(2)}, u32[]{:S(2)}) collective-permute-start(bf16[64,1408]{1,0:T(8,128)(2,1)S(1)} %merge_pair.1.one), channel_id=1, source_target_pairs={{0,96},{96,0},{32,64},{64,32},{1,97},{97,1},{33,65},{65,33},{2,98}... | collective-permute-start | bytes 540680 | tf_op jit(solution)/shard_map/ppermute | solution.py:42
  16.6 10.4 %collective-permute-start.3 = (bf16[64,1280]{1,0:T(8,128)(2,1)S(1)}, bf16[64,1280]{1,0:T(8,128)(2,1)S(1)}, u32[]{:S(2)}, u32[]{:S(2)}) collective-permute-start(bf16[64,1280]{1,0:T(8,128)(2,1)S(1)} %add_convert_fusion.5), channel_id=1, source_target_pairs={{0,32},{32,0},{64,96},{96,64},{1,33},{33,1},{65,97},{97,65},{2,34}... | collective-permute-start | bytes 491528 | tf_op jit(solution)/shard_map/ppermute | solution.py:38
  16.8 12.7 %collective-permute-start.6 = (bf16[224,256]{1,0:T(8,128)(2,1)S(1)}, bf16[224,256]{1,0:T(8,128)(2,1)S(1)}, u32[]{:S(2)}, u32[]{:S(2)}) collective-permute-start(bf16[224,256]{1,0:T(8,128)(2,1)S(1)} %get-tuple-element.56), channel_id=1, source_target_pairs={{0,16},{8,24},{16,0},{24,8},{1,17},{9,25},{17,1},{25,9},{2,18},{10... | collective-permute-start | bytes 344072 | tf_op jit(solution)/shard_map/ppermute | solution.py:30
  20.1 9.4 %collective-permute-start.7 = (bf16[224,256]{1,0:T(8,128)(2,1)S(1)}, bf16[224,256]{1,0:T(8,128)(2,1)S(1)}, u32[]{:S(2)}, u32[]{:S(2)}) collective-permute-start(bf16[224,256]{1,0:T(8,128)(2,1)S(1)} %get-tuple-element.57), channel_id=1, source_target_pairs={{0,8},{8,16},{16,24},{24,0},{1,9},{9,17},{17,25},{25,1},{2,10},{10... | collective-permute-start | bytes 344072 | tf_op jit(solution)/shard_map/ppermute | solution.py:30
  22.4 7.0 %collective-permute-start.4 = (bf16[64,1280]{1,0:T(8,128)(2,1)S(1)}, bf16[64,1280]{1,0:T(8,128)(2,1)S(1)}, u32[]{:S(2)}, u32[]{:S(2)}) collective-permute-start(bf16[64,1280]{1,0:T(8,128)(2,1)S(1)} %fusion.18), channel_id=1, source_target_pairs={{0,32},{32,0},{64,96},{96,64},{1,33},{33,1},{65,97},{97,65},{2,34}... | collective-permute-start | bytes 491528 | tf_op jit(solution)/shard_map/ppermute | solution.py:38
  24.5 5.0 %collective-permute-start.5 = (bf16[224,256]{1,0:T(8,128)(2,1)S(1)}, bf16[224,256]{1,0:T(8,128)(2,1)S(1)}, u32[]{:S(2)}, u32[]{:S(2)}) collective-permute-start(bf16[224,256]{1,0:T(8,128)(2,1)S(1)} %get-tuple-element.55), channel_id=1, source_target_pairs={{0,24},{8,0},{16,8},{24,16},{1,25},{9,1},{17,9},{25,17},{2,26},{10... | collective-permute-start | bytes 344072 | tf_op jit(solution)/shard_map/ppermute | solution.py:30
  29.5 8.8 %collective-permute-start.9 = (bf16[64,1280]{1,0:T(8,128)(2,1)S(1)}, bf16[64,1280]{1,0:T(8,128)(2,1)S(1)}, u32[]{:S(2)}, u32[]{:S(2)}) collective-permute-start(bf16[64,1280]{1,0:T(8,128)(2,1)S(1)} %add_convert_fusion.3.sum_a), channel_id=1, source_target_pairs={{0,96},{96,0},{32,64},{64,32},{1,97},{97,1},{33,65},{65,33},{2,98}... | collective-permute-start | bytes 491528 | tf_op jit(solution)/shard_map/ppermute | solution.py:42
  31.3 5.3 %collective-permute-start.8 = (bf16[64,1280]{1,0:T(8,128)(2,1)S(1)}, bf16[64,1280]{1,0:T(8,128)(2,1)S(1)}, u32[]{:S(2)}, u32[]{:S(2)}) collective-permute-start(bf16[64,1280]{1,0:T(8,128)(2,1)S(1)} %fusion.15), channel_id=1, source_target_pairs={{0,32},{32,0},{64,96},{96,64},{1,33},{33,1},{65,97},{97,65},{2,34}... | collective-permute-start | bytes 491528 | tf_op jit(solution)/shard_map/ppermute | solution.py:38
  36.7 6.6 %collective-permute-start.10 = (bf16[64,1280]{1,0:T(8,128)(2,1)S(1)}, bf16[64,1280]{1,0:T(8,128)(2,1)S(1)}, u32[]{:S(2)}, u32[]{:S(2)}) collective-permute-start(bf16[64,1280]{1,0:T(8,128)(2,1)S(1)} %add_convert_fusion.2), channel_id=1, source_target_pairs={{0,96},{96,0},{32,64},{64,32},{1,97},{97,1},{33,65},{65,33},{2,98}... | collective-permute-start | bytes 491528 | tf_op jit(solution)/shard_map/ppermute | solution.py:42
  45.0 22.3 %collective-permute-start.12 = (bf16[64,1792]{1,0:T(8,128)(2,1)S(1)}, bf16[64,1792]{1,0:T(8,128)(2,1)S(1)}, u32[]{:S(2)}, u32[]{:S(2)}) collective-permute-start(bf16[64,1792]{1,0:T(8,128)(2,1)S(1)} %get-tuple-element.71), channel_id=1, source_target_pairs={{0,24},{8,0},{16,8},{24,16},{1,25},{9,1},{17,9},{25,17},{2,26},{10... | collective-permute-start | bytes 688136 | tf_op jit(solution)/shard_map/ppermute | solution.py:30
  48.5 18.8 %collective-permute-start.13 = (bf16[64,1792]{1,0:T(8,128)(2,1)S(1)}, bf16[64,1792]{1,0:T(8,128)(2,1)S(1)}, u32[]{:S(2)}, u32[]{:S(2)}) collective-permute-start(bf16[64,1792]{1,0:T(8,128)(2,1)S(1)} %get-tuple-element.72), channel_id=1, source_target_pairs={{0,16},{8,24},{16,0},{24,8},{1,17},{9,25},{17,1},{25,9},{2,18},{10... | collective-permute-start | bytes 688136 | tf_op jit(solution)/shard_map/ppermute | solution.py:30
  48.6 18.8 %collective-permute-start.14 = (bf16[64,1792]{1,0:T(8,128)(2,1)S(1)}, bf16[64,1792]{1,0:T(8,128)(2,1)S(1)}, u32[]{:S(2)}, u32[]{:S(2)}) collective-permute-start(bf16[64,1792]{1,0:T(8,128)(2,1)S(1)} %get-tuple-element.73), channel_id=1, source_target_pairs={{0,8},{8,16},{16,24},{24,0},{1,9},{9,17},{17,25},{25,1},{2,10},{10... | collective-permute-start | bytes 688136 | tf_op jit(solution)/shard_map/ppermute | solution.py:30
  49.7 3.7 %collective-permute-start.15 = (f32[2,1,1024]{2,1,0:T(1,128)S(1)}, f32[2,1,1024]{2,1,0:T(1,128)S(1)}, u32[]{:S(2)}, u32[]{:S(2)}) collective-permute-start(f32[2,1,1024]{2,1,0:T(1,128)S(1)} %add.65), channel_id=1, source_target_pairs={{0,2},{2,0},{4,6},{6,4},{1,3},{3,1},{5,7},{7,5},{8,10},{10,8},{12,... | collective-permute-start | bytes 24584 | tf_op jit(solution)/shard_map/ppermute | solution.py:38
  53.3 4.9 %collective-permute-start.16 = (f32[2,1,1024]{2,1,0:T(1,128)S(1)}, f32[2,1,1024]{2,1,0:T(1,128)S(1)}, u32[]{:S(2)}, u32[]{:S(2)}) collective-permute-start(f32[2,1,1024]{2,1,0:T(1,128)S(1)} %add.66), channel_id=1, source_target_pairs={{0,6},{6,0},{2,4},{4,2},{1,7},{7,1},{3,5},{5,3},{8,14},{14,8},{10,... | collective-permute-start | bytes 24584 | tf_op jit(solution)/shard_map/ppermute | solution.py:42
  58.3 4.1 %collective-permute-start.17 = (f32[2,1,1024]{2,1,0:T(1,128)S(1)}, f32[2,1,1024]{2,1,0:T(1,128)S(1)}, u32[]{:S(2)}, u32[]{:S(2)}) collective-permute-start(f32[2,1,1024]{2,1,0:T(1,128)S(1)} %add.67), channel_id=1, source_target_pairs={{0,8},{8,0},{16,24},{24,16},{1,9},{9,1},{17,25},{25,17},{2,10},{10... | collective-permute-start | bytes 24584 | tf_op jit(solution)/shard_map/ppermute | solution.py:38
  62.4 4.9 %collective-permute-start.18 = (f32[2,1,1024]{2,1,0:T(1,128)S(1)}, f32[2,1,1024]{2,1,0:T(1,128)S(1)}, u32[]{:S(2)}, u32[]{:S(2)}) collective-permute-start(f32[2,1,1024]{2,1,0:T(1,128)S(1)} %add.68), channel_id=1, source_target_pairs={{0,24},{24,0},{8,16},{16,8},{1,25},{25,1},{9,17},{17,9},{2,26},{26... | collective-permute-start | bytes 24584 | tf_op jit(solution)/shard_map/ppermute | solution.py:42
  68.0 2.9 %collective-permute-start.19 = (bf16[4,2,32,1280]{3,2,1,0:T(8,128)(2,1)S(1)}, bf16[4,2,32,1280]{3,2,1,0:T(8,128)(2,1)S(1)}, u32[]{:S(2)}, u32[]{:S(2)}) collective-permute-start(bf16[4,2,32,1280]{3,2,1,0:T(8,128)(2,1)S(1)} %get-tuple-element.79), channel_id=1, source_target_pairs={{0,1},{1,0},{2,3},{3,2},{4,5},{5,4},{6,7},{7,6},{8,9},{9,8},{10,11... | collective-permute-start | bytes 1966088 | tf_op jit(solution)/shard_map/ppermute | solution.py:34
  72.4 4.9 %collective-permute-start.23 = (bf16[32,1280]{1,0:T(8,128)(2,1)S(1)}, bf16[32,1280]{1,0:T(8,128)(2,1)}, u32[]{:S(2)}, u32[]{:S(2)}) collective-permute-start(bf16[32,1280]{1,0:T(8,128)(2,1)S(1)} %embed_grad.1), channel_id=1, source_target_pairs={{0,32},{32,0},{64,96},{96,64},{1,33},{33,1},{65,97},{97,65},{2,34}... | collective-permute-start | bytes 245768 | tf_op jit(solution)/shard_map/ppermute | solution.py:38
  72.4 12.3 %collective-permute-start.20 = (bf16[2,32,1280]{2,1,0:T(8,128)(2,1)}, bf16[2,32,1280]{2,1,0:T(8,128)(2,1)S(1)}, u32[]{:S(2)}, u32[]{:S(2)}) collective-permute-start(bf16[2,32,1280]{2,1,0:T(8,128)(2,1)} %get-tuple-element.81), channel_id=1, source_target_pairs={{0,2},{2,4},{4,6},{6,0},{1,3},{3,5},{5,7},{7,1},{8,10},{10,12},{12... | collective-permute-start | bytes 491528 | tf_op jit(solution)/shard_map/ppermute | solution.py:30
  72.7 12.2 %collective-permute-start.21 = (bf16[2,32,1280]{2,1,0:T(8,128)(2,1)}, bf16[2,32,1280]{2,1,0:T(8,128)(2,1)S(1)}, u32[]{:S(2)}, u32[]{:S(2)}) collective-permute-start(bf16[2,32,1280]{2,1,0:T(8,128)(2,1)} %get-tuple-element.82), channel_id=1, source_target_pairs={{0,4},{2,6},{4,0},{6,2},{1,5},{3,7},{5,1},{7,3},{8,12},{10,14},{12... | collective-permute-start | bytes 491528 | tf_op jit(solution)/shard_map/ppermute | solution.py:30
  76.6 8.3 %collective-permute-start.22 = (bf16[2,32,1280]{2,1,0:T(8,128)(2,1)}, bf16[2,32,1280]{2,1,0:T(8,128)(2,1)S(1)}, u32[]{:S(2)}, u32[]{:S(2)}) collective-permute-start(bf16[2,32,1280]{2,1,0:T(8,128)(2,1)} %get-tuple-element.83), channel_id=1, source_target_pairs={{0,6},{2,0},{4,2},{6,4},{1,7},{3,1},{5,3},{7,5},{8,14},{10,8},{12,... | collective-permute-start | bytes 491528 | tf_op jit(solution)/shard_map/ppermute | solution.py:30
  78.3 5.7 %collective-permute-start.24 = (bf16[32,1280]{1,0:T(8,128)(2,1)S(1)}, bf16[32,1280]{1,0:T(8,128)(2,1)S(1)}, u32[]{:S(2)}, u32[]{:S(2)}) collective-permute-start(bf16[32,1280]{1,0:T(8,128)(2,1)S(1)} %add_convert_fusion.6), channel_id=1, source_target_pairs={{0,96},{96,0},{32,64},{64,32},{1,97},{97,1},{33,65},{65,33},{2,98}... | collective-permute-start | bytes 245768 | tf_op jit(solution)/shard_map/ppermute | solution.py:42
  (11 other events, 101.1 us)
